TPU v7x, 32 devices: a whole 2x2x4 slice. The times are simulated.
32 devices in a mesh: dp: 8 (over z, y), tensor: 4 (over x, core).
Axes of the slice: x: 2, y: 2, z: 4, core: 2. Of those that a mesh axis runs over, the one named last changes fastest.
Arguments:
- audio_codes: int32 [24, 768, 4], P('dp'), may hold values from 0 to 2047
- delay_mask: int32 [24, 768, 4], P('dp'), may hold values from 0 to 1, as said below
- frame_mask: int32 [24, 768], P('dp'), may hold values from 0 to 1, as said below
- text_states: bfloat16 [24, 256, 768], P('dp'), may hold values from -6 to 6
- text_mask: int32 [24, 256], P('dp'), may hold values from 0 to 1, as said below
- attention: float32 [8, 1024, 1024], P(None, 'dp', 'tensor')
- feedforward: float32 [2, 1024, 4096], P(None, 'dp', 'tensor')
- tables: float32 [8, 1024, 2048], P(None, 'dp', 'tensor')
- text_proj: float32 [1024, 768], P('tensor', 'dp'), may hold values from -0.21875 to 0.21875
- norm_params: float32 [9, 1024], P(None, 'dp')
- attention_first: float32 [8, 1024, 1024], P(None, 'dp', 'tensor'), may hold values from -3.8146973e-06 to 3.8146973e-06
- attention_second: float32 [8, 1024, 1024], P(None, 'dp', 'tensor'), may hold values from 4.6591724e-13 to 1.863669e-12
- feedforward_first: float32 [2, 1024, 4096], P(None, 'dp', 'tensor'), may hold values from -3.8146973e-06 to 3.8146973e-06
- feedforward_second: float32 [2, 1024, 4096], P(None, 'dp', 'tensor'), may hold values from 4.6591724e-13 to 1.863669e-12
- tables_first: float32 [8, 1024, 2048], P(None, 'dp', 'tensor'), may hold values from -3.8146973e-06 to 3.8146973e-06
- tables_second: float32 [8, 1024, 2048], P(None, 'dp', 'tensor'), may hold values from 4.6591724e-13 to 1.863669e-12
- text_first: float32 [1024, 768], P('tensor', 'dp'), may hold values from -3.8146973e-06 to 3.8146973e-06
- text_second: float32 [1024, 768], P('tensor', 'dp'), may hold values from 4.6591724e-13 to 1.863669e-12
- norm_first: float32 [9, 1024], P(None, 'dp'), may hold values from -3.8146973e-05 to 3.8146973e-05
- norm_second: float32 [9, 1024], P(None, 'dp'), may hold values from 4.6591724e-11 to 1.863669e-10
Outputs:
- mean_loss: float32 [], replicated
- valid_count: float32 [], replicated
- grad_norm: float32 [], replicated
- new_attention: float32 [8, 1024, 1024], P(None, 'dp', 'tensor')
- low_attention: bfloat16 [8, 1024, 1024], P(None, 'dp', 'tensor')
- new_attention_first: float32 [8, 1024, 1024], P(None, 'dp', 'tensor')
- new_attention_second: float32 [8, 1024, 1024], P(None, 'dp', 'tensor')
- new_feedforward: float32 [2, 1024, 4096], P(None, 'dp', 'tensor')
- low_feedforward: bfloat16 [2, 1024, 4096], P(None, 'dp', 'tensor')
- new_feedforward_first: float32 [2, 1024, 4096], P(None, 'dp', 'tensor')
- new_feedforward_second: float32 [2, 1024, 4096], P(None, 'dp', 'tensor')
- new_tables: float32 [8, 1024, 2048], P(None, 'dp', 'tensor')
- low_tables: bfloat16 [8, 1024, 2048], P(None, 'dp', 'tensor')
- new_tables_first: float32 [8, 1024, 2048], P(None, 'dp', 'tensor')
- new_tables_second: float32 [8, 1024, 2048], P(None, 'dp', 'tensor')
- new_text_proj: float32 [1024, 768], P('tensor', 'dp')
- low_text_proj: bfloat16 [1024, 768], P('tensor', 'dp')
- new_text_first: float32 [1024, 768], P('tensor', 'dp')
- new_text_second: float32 [1024, 768], P('tensor', 'dp')
- new_norm_params: float32 [9, 1024], P(None, 'dp')
- new_norm_first: float32 [9, 1024], P(None, 'dp')
- new_norm_second: float32 [9, 1024], P(None, 'dp')
Inputs may be any that keep to these rules, and one draw needn't show every extreme that they name: Each clip's frame_mask is 1 on a prefix of at least 384 frames and 0 after it; some clip is full. delay_mask[c, s, k] is 1 exactly where k <= s < n_c + k, with n_c the length of clip c's prefix in frame_mask. Each clip's text_mask is 1 on a prefix of at least 64 positions and 0 after it; some clip is full.
All inputs are finite; a program needn't handle non-finite values.
Results may differ from a plain program's by a relative error of at most 0.017.
Values may be sent and summed in bfloat16 or wider, within the bound.
No kernel may reach another device: no remote copies, remote signals or barrier semaphores. Data moves between devices by JAX's collectives and lax.ppermute only.
A program may use at most 320 MiB of HBM per device.

v0:
```python
from functools import partial
import math

import jax
import jax.numpy as jnp
from jax import lax
from jax.sharding import PartitionSpec as P

HEAD_DIM = 64
QBLOCK = 768
STEP = 5


clip_limit = 0.004
stability_offset = 1e-08
weight_decay = 0.01
moment_decay = 0.5
rate_matrix = 0.03
rate_table = 0.05
rate_norm = 0.2


def combined_all(shard, axis, join):
    gathered = jax.tree.map(
        lambda a, kind: lax.all_gather(a.astype(kind), axis),
        shard,
        (jnp.bfloat16, jnp.bfloat16, jnp.bfloat16),
    )

    def take(source):
        return jax.tree.map(
            lambda a, own: lax.dynamic_index_in_dim(a, source, 0, False).astype(own.dtype),
            gathered,
            shard,
        )

    return lax.fori_loop(
        1, lax.axis_size(axis), lambda source, state: join(state, take(source)), take(0)
    )


def layer_norm(values, gain_row, shift_row):
    center = values - jnp.mean(values, axis=-1, keepdims=True)
    spread = jnp.mean(center * center, axis=-1, keepdims=True)
    return center * lax.rsqrt(spread + 1e-05) * gain_row + shift_row


def norm_backward(values, gain_row, shift_row, grad_normed):
    outputs, pullback = jax.vjp(layer_norm, values, gain_row, shift_row)
    return pullback(grad_normed)


def gelu_backward(inner_values, grad_activated):
    outputs, pullback = jax.vjp(partial(jax.nn.gelu, approximate=False), inner_values)
    return pullback(grad_activated)[0]


def positions_table(position_count, feature_count):
    half_width = feature_count // 2
    frequency = jnp.exp(
        jnp.arange(half_width, dtype=jnp.float32) * (-math.log(10000.0) / (half_width - 1))
    )
    angles = jnp.arange(position_count, dtype=jnp.float32)[:, None] * frequency[None, :]
    return jnp.concatenate([jnp.cos(angles), jnp.sin(angles)], axis=1)


def allowed_mask(block_start, key_valid, causal):
    key_count = key_valid.shape[0]
    allowed = jnp.broadcast_to(key_valid[None, :] > 0, (QBLOCK, key_count))
    if causal:
        row_index = block_start + jnp.arange(QBLOCK, dtype=jnp.int32)
        allowed = allowed & (row_index[:, None] >= jnp.arange(key_count, dtype=jnp.int32)[None, :])
    return allowed


def attend_forward(queries, key_rows, value_rows, key_valid, causal):
    frames = queries.shape[0]
    score_scale = queries.shape[2] ** (-0.5)

    def one_block(block_start):
        scores = (
            jnp.einsum("qhe,khe->hqk", queries, key_rows, preferred_element_type=jnp.float32)
            * score_scale
        )
        scores = jnp.where(allowed_mask(block_start, key_valid, causal)[None], scores, -1e30)
        highest_score = jnp.max(scores, axis=-1, keepdims=True)
        exponent = jnp.exp(scores - highest_score)
        row_total = jnp.sum(exponent, axis=-1, keepdims=True)
        weights = (exponent / row_total).astype(jnp.bfloat16)
        output = jnp.einsum("hqk,khe->qhe", weights, value_rows, preferred_element_type=jnp.float32)
        return (output, (highest_score + jnp.log(row_total))[..., 0])

    starts = jnp.arange(frames // QBLOCK, dtype=jnp.int32) * QBLOCK
    outputs, log_totals = lax.map(one_block, starts)
    return (outputs.reshape(frames, -1), log_totals)


def attend_backward(queries, key_rows, value_rows, key_valid, log_totals, grad_out, causal):
    frames = queries.shape[0]
    score_scale = queries.shape[2] ** (-0.5)

    def one_block(carried, inputs):
        grad_keys, grad_values = carried
        block_start, block_totals = inputs
        scores = (
            jnp.einsum("qhe,khe->hqk", queries, key_rows, preferred_element_type=jnp.float32)
            * score_scale
        )
        scores = jnp.where(allowed_mask(block_start, key_valid, causal)[None], scores, -1e30)
        weights = jnp.exp(scores - block_totals[..., None])
        grad_weights = jnp.einsum(
            "qhe,khe->hqk", grad_out, value_rows, preferred_element_type=jnp.float32
        )
        inner_sum = jnp.sum(weights * grad_weights, axis=-1, keepdims=True)
        grad_scores = (weights * (grad_weights - inner_sum)).astype(jnp.bfloat16)
        grad_query = (
            jnp.einsum("hqk,khe->qhe", grad_scores, key_rows, preferred_element_type=jnp.float32)
            * score_scale
        )
        grad_keys = (
            grad_keys
            + jnp.einsum("hqk,qhe->khe", grad_scores, queries, preferred_element_type=jnp.float32)
            * score_scale
        )
        grad_values = grad_values + jnp.einsum(
            "hqk,qhe->khe",
            weights.astype(jnp.bfloat16),
            grad_out,
            preferred_element_type=jnp.float32,
        )
        return ((grad_keys, grad_values), grad_query)

    starts = jnp.arange(frames // QBLOCK, dtype=jnp.int32) * QBLOCK
    zero_keys = jnp.zeros(key_rows.shape, jnp.float32)
    (grad_keys, grad_values), grad_queries = lax.scan(
        one_block, (zero_keys, zero_keys), (starts, log_totals)
    )
    key_count = key_rows.shape[0]
    return (
        grad_queries.reshape(frames, -1),
        grad_keys.reshape(key_count, -1),
        grad_values.reshape(key_count, -1),
    )


def merge_logits(first_part, second_part):
    peak_value = jnp.maximum(first_part[0], second_part[0])
    row_total = first_part[1] * jnp.exp(first_part[0] - peak_value) + second_part[1] * jnp.exp(
        second_part[0] - peak_value
    )
    return (peak_value, row_total, first_part[2] + second_part[2])


def gather_rows(values):
    return lax.all_gather(values, "tensor", axis=0, tiled=True)


def scatter_rows(partial_sum):
    return lax.psum_scatter(partial_sum, "tensor", scatter_dimension=0, tiled=True)


def gather_grad_rows(values):
    return lax.all_gather(values, "tensor", axis=0, tiled=True)


def scatter_grad_rows(partial_sum):
    return lax.psum_scatter(
        partial_sum.astype(jnp.bfloat16), "tensor", scatter_dimension=0, tiled=True
    ).astype(jnp.float32)


def adam_update(weight, gradient, first_moment, second_moment, step_rate, factor):
    clipped = gradient * factor
    new_first = moment_decay * first_moment + (1.0 - moment_decay) * clipped
    new_second = moment_decay * second_moment + (1.0 - moment_decay) * clipped * clipped
    first_hat = new_first / (1.0 - moment_decay**STEP)
    second_hat = new_second / (1.0 - moment_decay**STEP)
    new_weight = weight * (1.0 - step_rate * weight_decay) - step_rate * first_hat / (
        jnp.sqrt(second_hat) + stability_offset
    )
    return (new_weight, new_first, new_second)


def on_device(
    audio_codes,
    delay_mask,
    frame_mask,
    text_states,
    text_mask,
    attention,
    feedforward,
    tables,
    text_proj,
    norm_params,
    attention_first,
    attention_second,
    feedforward_first,
    feedforward_second,
    tables_first,
    tables_second,
    text_first,
    text_second,
    norm_first,
    norm_second,
):
    clip_count, frames, book_count = audio_codes.shape
    text_len = text_states.shape[1]
    tensor_size = lax.axis_size("tensor")
    tensor_index = lax.axis_index("tensor")
    row_count = clip_count * frames
    share_rows = row_count // tensor_size
    attn_low, ffn_low, table_low, text_low, norm_low = (
        lax.all_gather(attention.astype(jnp.bfloat16), "dp", axis=1, tiled=True),
        lax.all_gather(feedforward.astype(jnp.bfloat16), "dp", axis=1, tiled=True),
        lax.all_gather(tables.astype(jnp.bfloat16), "dp", axis=1, tiled=True),
        lax.all_gather(text_proj.astype(jnp.bfloat16), "dp", axis=1, tiled=True),
        lax.all_gather(norm_params.astype(jnp.bfloat16), "dp", axis=1, tiled=True),
    )
    norm_rows = norm_low.astype(jnp.float32)
    model_width = attn_low.shape[1]
    columns = attn_low.shape[2]
    local_heads = columns // HEAD_DIM
    vocab_local = table_low.shape[2]
    vocab_start = tensor_index * vocab_local
    vocab_index = jnp.arange(vocab_local, dtype=jnp.int32)
    head_shape = (clip_count, frames, local_heads, HEAD_DIM)
    text_shape = (clip_count, text_len, local_heads, HEAD_DIM)
    placed = jnp.tile(positions_table(frames, model_width), (clip_count, 1))
    placed = lax.dynamic_slice_in_dim(placed, tensor_index * share_rows, share_rows, 0)
    local_codes = audio_codes.reshape(row_count, book_count) - vocab_start
    code_table = (local_codes[:, :, None] == vocab_index[None, None, :]).astype(jnp.bfloat16)
    embed_part = jnp.einsum(
        "tkv,kdv->td", code_table, table_low[:book_count], preferred_element_type=jnp.float32
    )
    resid_zero = scatter_rows(embed_part) + placed
    self_in = gather_rows(layer_norm(resid_zero, norm_rows[0], norm_rows[4]).astype(jnp.bfloat16))
    projected = jnp.einsum(
        "td,ndc->ntc", self_in, attn_low[0:3], preferred_element_type=jnp.float32
    ).astype(jnp.bfloat16)
    self_valid = jnp.ones((clip_count, frames), jnp.int32)
    self_query = projected[0].reshape(head_shape)
    self_key = projected[1].reshape(head_shape)
    self_value = projected[2].reshape(head_shape)
    self_mixed, self_totals = jax.vmap(partial(attend_forward, causal=True))(
        self_query, self_key, self_value, self_valid
    )
    self_mixed = self_mixed.reshape(row_count, columns).astype(jnp.bfloat16)
    resid_one = resid_zero + scatter_rows(
        jnp.einsum("tc,dc->td", self_mixed, attn_low[6], preferred_element_type=jnp.float32)
    )
    cross_in = gather_rows(layer_norm(resid_one, norm_rows[1], norm_rows[5]).astype(jnp.bfloat16))
    cross_query = jnp.dot(cross_in, attn_low[3], preferred_element_type=jnp.float32).astype(
        jnp.bfloat16
    )
    text_rows = text_states.reshape(clip_count * text_len, text_states.shape[2])
    text_cols = text_low.shape[0]
    text_bias = lax.dynamic_slice_in_dim(norm_rows[8], tensor_index * text_cols, text_cols, 0)
    text_local = (
        jnp.einsum("ti,di->td", text_rows, text_low, preferred_element_type=jnp.float32) + text_bias
    ).astype(jnp.bfloat16)
    text_hidden = lax.all_gather(text_local, "tensor", axis=1, tiled=True)
    text_pair = jnp.einsum(
        "td,ndc->ntc", text_hidden, attn_low[4:6], preferred_element_type=jnp.float32
    ).astype(jnp.bfloat16)
    cross_heads = cross_query.reshape(head_shape)
    text_key = text_pair[0].reshape(text_shape)
    text_value = text_pair[1].reshape(text_shape)
    cross_mixed, cross_totals = jax.vmap(partial(attend_forward, causal=False))(
        cross_heads, text_key, text_value, text_mask
    )
    cross_mixed = cross_mixed.reshape(row_count, columns).astype(jnp.bfloat16)
    resid_two = resid_one + scatter_rows(
        jnp.einsum("tc,dc->td", cross_mixed, attn_low[7], preferred_element_type=jnp.float32)
    )
    normed_ffn = layer_norm(resid_two, norm_rows[2], norm_rows[6]).astype(jnp.bfloat16)
    ffn_in = gather_rows(normed_ffn)
    inner_values = jnp.dot(ffn_in, ffn_low[0], preferred_element_type=jnp.float32)
    activated = jax.nn.gelu(inner_values, approximate=False).astype(jnp.bfloat16)
    ffn_part = jnp.einsum("tf,df->td", activated, ffn_low[1], preferred_element_type=jnp.float32)
    resid_three = resid_two + scatter_rows(ffn_part)
    head_in = gather_rows(layer_norm(resid_three, norm_rows[3], norm_rows[7]).astype(jnp.bfloat16))
    output_logits = jnp.einsum(
        "td,kdv->tkv", head_in, table_low[book_count:], preferred_element_type=jnp.float32
    )
    local_high = jnp.max(output_logits, axis=-1)
    local_total = jnp.sum(jnp.exp(output_logits - local_high[..., None]), axis=-1)
    target_codes = jnp.roll(audio_codes, -1, axis=1).reshape(row_count, book_count) - vocab_start
    target_table = target_codes[:, :, None] == vocab_index[None, None, :]
    local_pick = jnp.sum(jnp.where(target_table, output_logits, 0.0), axis=-1)
    peak_value, row_total, picked = combined_all(
        (local_high, local_total, local_pick), "tensor", merge_logits
    )
    log_total = peak_value + jnp.log(row_total)
    frame_live = (jnp.arange(frames, dtype=jnp.int32) < frames - 1).astype(jnp.int32)
    loss_weight = (
        (delay_mask * frame_mask[:, :, None] * frame_live[None, :, None])
        .astype(jnp.float32)
        .reshape(row_count, book_count)
    )
    loss_sum, valid_count = lax.psum(
        (jnp.sum((log_total - picked) * loss_weight), jnp.sum(loss_weight)), "dp"
    )
    probabilities = jnp.exp(output_logits - log_total[..., None])
    grad_logits = (
        (probabilities - target_table.astype(jnp.float32)) * (loss_weight / valid_count)[..., None]
    ).astype(jnp.bfloat16)
    grad_heads = jnp.einsum("td,tkv->kdv", head_in, grad_logits, preferred_element_type=jnp.float32)
    grad_head_in = scatter_grad_rows(
        jnp.einsum(
            "tkv,kdv->td", grad_logits, table_low[book_count:], preferred_element_type=jnp.float32
        )
    )
    grad_resid, gain_three, shift_three = norm_backward(
        resid_three, norm_rows[3], norm_rows[7], grad_head_in
    )
    grad_branch = grad_resid.astype(jnp.bfloat16)
    grad_ffn_out = gather_grad_rows(grad_branch)
    grad_ffn_two = jnp.einsum(
        "td,tf->df", grad_ffn_out, activated, preferred_element_type=jnp.float32
    )
    grad_activated = jnp.dot(grad_ffn_out, ffn_low[1], preferred_element_type=jnp.float32)
    grad_inner = gelu_backward(inner_values, grad_activated).astype(jnp.bfloat16)
    grad_ffn_one = jnp.einsum("td,tf->df", ffn_in, grad_inner, preferred_element_type=jnp.float32)
    grad_ffn_in = jnp.einsum(
        "tf,df->td", grad_inner, ffn_low[0], preferred_element_type=jnp.float32
    )
    grad_normed = scatter_grad_rows(grad_ffn_in)
    grad_feedforward = jnp.stack([grad_ffn_one, grad_ffn_two])
    delta_norm, gain_two, shift_two = norm_backward(
        resid_two, norm_rows[2], norm_rows[6], grad_normed
    )
    grad_resid = grad_resid + delta_norm
    grad_branch = gather_grad_rows(grad_resid.astype(jnp.bfloat16))
    grad_cross_out = jnp.einsum(
        "td,tc->dc", grad_branch, cross_mixed, preferred_element_type=jnp.float32
    )
    grad_cross_mixed = jnp.dot(grad_branch, attn_low[7], preferred_element_type=jnp.float32).astype(
        jnp.bfloat16
    )
    grad_cross_heads, grad_text_key, grad_text_value = jax.vmap(
        partial(attend_backward, causal=False)
    )(
        cross_heads,
        text_key,
        text_value,
        text_mask,
        cross_totals,
        grad_cross_mixed.reshape(head_shape),
    )
    grad_cross_query = grad_cross_heads.reshape(row_count, columns).astype(jnp.bfloat16)
    grad_text_pair = jnp.stack(
        [
            grad_text_key.reshape(clip_count * text_len, columns),
            grad_text_value.reshape(clip_count * text_len, columns),
        ]
    ).astype(jnp.bfloat16)
    grad_cross_weight = jnp.einsum(
        "td,tc->dc", cross_in, grad_cross_query, preferred_element_type=jnp.float32
    )
    grad_text_weight = jnp.einsum(
        "td,ntc->ndc", text_hidden, grad_text_pair, preferred_element_type=jnp.float32
    )
    grad_text_part = jnp.einsum(
        "ntc,ndc->td", grad_text_pair, attn_low[4:6], preferred_element_type=jnp.float32
    )
    grad_normed = scatter_grad_rows(
        jnp.einsum("tc,dc->td", grad_cross_query, attn_low[3], preferred_element_type=jnp.float32)
    )
    delta_norm, gain_one, shift_one = norm_backward(
        resid_one, norm_rows[1], norm_rows[5], grad_normed
    )
    grad_resid = grad_resid + delta_norm
    grad_branch = gather_grad_rows(grad_resid.astype(jnp.bfloat16))
    grad_self_out = jnp.einsum(
        "td,tc->dc", grad_branch, self_mixed, preferred_element_type=jnp.float32
    )
    grad_self_mixed = jnp.dot(grad_branch, attn_low[6], preferred_element_type=jnp.float32).astype(
        jnp.bfloat16
    )
    grad_query, grad_key, grad_value = jax.vmap(partial(attend_backward, causal=True))(
        self_query,
        self_key,
        self_value,
        self_valid,
        self_totals,
        grad_self_mixed.reshape(head_shape),
    )
    grad_projected = jnp.stack(
        [
            grad_query.reshape(row_count, columns),
            grad_key.reshape(row_count, columns),
            grad_value.reshape(row_count, columns),
        ]
    ).astype(jnp.bfloat16)
    grad_self_in = jnp.einsum(
        "td,ntc->ndc", self_in, grad_projected, preferred_element_type=jnp.float32
    )
    grad_normed = scatter_grad_rows(
        jnp.einsum("ntc,ndc->td", grad_projected, attn_low[0:3], preferred_element_type=jnp.float32)
    )
    delta_norm, gain_zero, shift_zero = norm_backward(
        resid_zero, norm_rows[0], norm_rows[4], grad_normed
    )
    grad_resid = grad_resid + delta_norm
    grad_embed_in = gather_grad_rows(grad_resid.astype(jnp.bfloat16))
    grad_embed = jnp.einsum(
        "td,tkv->kdv", grad_embed_in, code_table, preferred_element_type=jnp.float32
    )
    norm_part = jnp.stack(
        [gain_zero, gain_one, gain_two, gain_three, shift_zero, shift_one, shift_two, shift_three]
    )
    grad_text_full, norm_total = (
        lax.psum(grad_text_part.astype(jnp.bfloat16), "tensor").astype(jnp.float32),
        lax.psum(norm_part.astype(jnp.bfloat16), "tensor").astype(jnp.float32),
    )
    grad_text_low = grad_text_full.astype(jnp.bfloat16)
    grad_text_local = lax.dynamic_slice_in_dim(
        grad_text_low, tensor_index * text_cols, text_cols, 1
    )
    grad_text_proj = jnp.einsum(
        "td,ti->di", grad_text_local, text_rows, preferred_element_type=jnp.float32
    )
    grad_text_bias = jnp.sum(grad_text_low.astype(jnp.float32), axis=0)
    grad_norm_rows = jnp.concatenate([norm_total, grad_text_bias[None, :]], 0)
    grad_attention = jnp.concatenate(
        [
            grad_self_in,
            grad_cross_weight[None],
            grad_text_weight,
            grad_self_out[None],
            grad_cross_out[None],
        ],
        0,
    )
    grad_tables = jnp.concatenate([grad_embed, grad_heads], 0)
    grad_attention, grad_feedforward, grad_tables, grad_text_proj, grad_norm_rows = (
        lax.psum_scatter(
            grad_attention.astype(jnp.bfloat16), "dp", scatter_dimension=1, tiled=True
        ).astype(jnp.float32),
        lax.psum_scatter(
            grad_feedforward.astype(jnp.bfloat16), "dp", scatter_dimension=1, tiled=True
        ).astype(jnp.float32),
        lax.psum_scatter(
            grad_tables.astype(jnp.bfloat16), "dp", scatter_dimension=1, tiled=True
        ).astype(jnp.float32),
        lax.psum_scatter(
            grad_text_proj.astype(jnp.bfloat16), "dp", scatter_dimension=1, tiled=True
        ).astype(jnp.float32),
        lax.psum_scatter(
            grad_norm_rows.astype(jnp.bfloat16), "dp", scatter_dimension=1, tiled=True
        ).astype(jnp.float32),
    )
    local_square = (
        jnp.sum(grad_attention * grad_attention)
        + jnp.sum(grad_feedforward * grad_feedforward)
        + jnp.sum(grad_tables * grad_tables)
        + jnp.sum(grad_text_proj * grad_text_proj)
        + jnp.sum(grad_norm_rows * grad_norm_rows) / tensor_size
    )
    grad_norm = jnp.sqrt(lax.psum(local_square, ("dp", "tensor")))
    factor = clip_limit / jnp.maximum(grad_norm, clip_limit)
    attn_new, attn_first_new, attn_second_new = adam_update(
        attention, grad_attention, attention_first, attention_second, rate_matrix, factor
    )
    ffn_new, updated_feedforward_first, ffn_second_new = adam_update(
        feedforward, grad_feedforward, feedforward_first, feedforward_second, rate_matrix, factor
    )
    table_new, table_first_new, table_second_new = adam_update(
        tables, grad_tables, tables_first, tables_second, rate_table, factor
    )
    text_new, text_first_new, text_second_new = adam_update(
        text_proj, grad_text_proj, text_first, text_second, rate_matrix, factor
    )
    norm_new, norm_first_new, norm_second_new = adam_update(
        norm_params, grad_norm_rows, norm_first, norm_second, rate_norm, factor
    )
    return (
        loss_sum / valid_count,
        valid_count,
        grad_norm,
        attn_new,
        attn_new.astype(jnp.bfloat16),
        attn_first_new,
        attn_second_new,
        ffn_new,
        ffn_new.astype(jnp.bfloat16),
        updated_feedforward_first,
        ffn_second_new,
        table_new,
        table_new.astype(jnp.bfloat16),
        table_first_new,
        table_second_new,
        text_new,
        text_new.astype(jnp.bfloat16),
        text_first_new,
        text_second_new,
        norm_new,
        norm_first_new,
        norm_second_new,
    )


def solution(mesh):
    placed = (
        P("dp", None, None),
        P("dp", None, None),
        P("dp", None),
        P("dp", None, None),
        P("dp", None),
        P(None, "dp", "tensor"),
        P(None, "dp", "tensor"),
        P(None, "dp", "tensor"),
        P("tensor", "dp"),
        P(None, "dp"),
        P(None, "dp", "tensor"),
        P(None, "dp", "tensor"),
        P(None, "dp", "tensor"),
        P(None, "dp", "tensor"),
        P(None, "dp", "tensor"),
        P(None, "dp", "tensor"),
        P("tensor", "dp"),
        P("tensor", "dp"),
        P(None, "dp"),
        P(None, "dp"),
    )
    return jax.shard_map(
        on_device,
        mesh=mesh,
        in_specs=placed,
        out_specs=(
            P(),
            P(),
            P(),
            P(None, "dp", "tensor"),
            P(None, "dp", "tensor"),
            P(None, "dp", "tensor"),
            P(None, "dp", "tensor"),
            P(None, "dp", "tensor"),
            P(None, "dp", "tensor"),
            P(None, "dp", "tensor"),
            P(None, "dp", "tensor"),
            P(None, "dp", "tensor"),
            P(None, "dp", "tensor"),
            P(None, "dp", "tensor"),
            P(None, "dp", "tensor"),
            P("tensor", "dp"),
            P("tensor", "dp"),
            P("tensor", "dp"),
            P("tensor", "dp"),
            P(None, "dp"),
            P(None, "dp"),
            P(None, "dp"),
        ),
        check_vma=False,
    )
```

profile of v0, /device:TPU:0, one launch (start us, length us, event | category | flops | bytes accessed | tf_op | source)
XLA Modules:
  0.0 2171.9 jit_solution(16739978658841873402)
XLA Ops:
  10.2 128.3 %all-gather.16.cloned.1.call-done = bf16[8,1024,512]{2,1,0:T(8,128)(2,1)} async-done(((bf16[8,128,512]{2,1,0:T(8,128)(2,1)}), bf16[8,1024,512]{2,1,0:T(8,128)(2,1)}) %all-gather.16.cloned.1.call-update) | async-done | bytes 8388624 | tf_op jit(solution)/shard_map/all_gather | solution.py:215
  154.8 26.2 %all_gather.55 = bf16[9,1024]{1,0:T(8,128)(2,1)S(1)} all-gather(bf16[9,128]{1,0:T(8,128)(2,1)S(1)} %convert_element_type.313), channel_id=1, replica_groups=mesh['dp'=8,'tensor'=4] {'dp'}, dimensions={1}, use_global_device_ids=true | all-gather | bytes 20736 | tf_op jit(solution)/shard_map/all_gather | solution.py:217
  189.3 40.2 %reduce-scatter.20.cloned.1.call-done = f32[576,1024]{1,0:T(8,128)} async-done(((f32[2304,1024]{1,0:T(8,128)}), f32[576,1024]{1,0:T(8,128)}) %reduce-scatter.20.cloned.1.call-update) | async-done | bytes 2359312 | tf_op jit(solution)/shard_map/reduce_scatter | solution.py:159
  237.5 68.1 %all-gather.20.cloned.1.call-done = bf16[8,1024,256]{2,1,0:T(8,128)(2,1)} async-done(((bf16[8,128,256]{2,1,0:T(8,128)(2,1)}), bf16[8,1024,256]{2,1,0:T(8,128)(2,1)}) %all-gather.20.cloned.1.call-update) | async-done | bytes 4194320 | tf_op jit(solution)/shard_map/all_gather | solution.py:213
  305.6 37.7 %all-gather.18.cloned.1.call-done = bf16[2304,1024]{1,0:T(8,128)(2,1)} async-done(((bf16[576,1024]{1,0:T(8,128)(2,1)}), bf16[2304,1024]{1,0:T(8,128)(2,1)}) %all-gather.18.cloned.1.call-update) | async-done | bytes 4718608 | tf_op jit(solution)/shard_map/all_gather | solution.py:155
  428.4 31.4 %all_gather.58 = bf16[256,768]{0,1:T(8,128)(2,1)S(1)} all-gather(bf16[256,96]{0,1:T(8,128)(2,1)} %convert_element_type.323), channel_id=1, replica_groups=mesh['dp'=8,'tensor'=4] {'dp'}, dimensions={1}, use_global_device_ids=true | all-gather | bytes 442368 | tf_op jit(solution)/shard_map/all_gather | solution.py:216
  461.2 43.5 %reduce-scatter.22.cloned.1.call-done = f32[576,1024]{1,0:T(8,128)} async-done(((f32[2304,1024]{1,0:T(8,128)}), f32[576,1024]{1,0:T(8,128)}) %reduce-scatter.22.cloned.1.call-update) | async-done | bytes 2359312 | tf_op jit(solution)/shard_map/reduce_scatter | solution.py:159
  530.9 35.3 %all-gather.24.cloned.1.call-done = bf16[2304,1024]{1,0:T(8,128)(2,1)} async-done(((bf16[576,1024]{1,0:T(8,128)(2,1)}), bf16[2304,1024]{1,0:T(8,128)(2,1)}) %all-gather.24.cloned.1.call-update) | async-done | bytes 4718608 | tf_op jit(solution)/shard_map/all_gather | solution.py:155
  595.9 76.2 %reduce-scatter.24.cloned.1.call-done = f32[576,1024]{1,0:T(8,128)} async-done(((f32[2304,1024]{1,0:T(8,128)}), f32[576,1024]{1,0:T(8,128)}) %reduce-scatter.24.cloned.1.call-update) | async-done | bytes 2359312 | tf_op jit(solution)/shard_map/reduce_scatter | solution.py:159
  677.4 70.9 %all-gather.28.cloned.1.call-done = bf16[2,1024,1024]{2,1,0:T(8,128)(2,1)} async-done(((bf16[2,128,1024]{2,1,0:T(8,128)(2,1)}), bf16[2,1024,1024]{2,1,0:T(8,128)(2,1)}) %all-gather.28.cloned.1.call-update) | async-done | bytes 4194320 | tf_op jit(solution)/shard_map/all_gather | solution.py:214
  748.3 37.7 %all-gather.26.cloned.1.call-done = bf16[2304,1024]{1,0:T(8,128)(2,1)} async-done(((bf16[576,1024]{1,0:T(8,128)(2,1)}), bf16[2304,1024]{1,0:T(8,128)(2,1)}) %all-gather.26.cloned.1.call-update) | async-done | bytes 4718608 | tf_op jit(solution)/shard_map/all_gather | solution.py:155
  786.1 28.8 %multiply_convert_fusion.3 = (bf16[2304,1024]{1,0:T(8,128)(2,1)S(1)}, f32[2304,1024]{1,0:T(8,128)}, f32[2304,1024]{1,0:T(8,128)}) fusion(bf16[2304,1024]{1,0:T(8,128)(2,1)} %all-gather.26.cloned.1.call-done, bf16[2,1024,1024]{2,1,0:T(8,128)(2,1)} %all-gather.28.cloned.1.call-done), kind=kOutput, calls=%fused_computation.33 | convolution fusion | flops 4985192448 | bytes 30408704 | tf_op jit(solution)/shard_map/dot_general | solution.py:277
  824.9 78.4 %reduce-scatter.26.cloned.1.call-done = f32[576,1024]{1,0:T(8,128)} async-done(((f32[2304,1024]{1,0:T(8,128)}), f32[576,1024]{1,0:T(8,128)}) %reduce-scatter.26.cloned.1.call-update) | async-done | bytes 2359312 | tf_op jit(solution)/shard_map/reduce_scatter | solution.py:159
  913.4 33.6 %all-gather.30.cloned.1.call-done = bf16[2304,1024]{1,0:T(8,128)(2,1)} async-done(((bf16[576,1024]{1,0:T(8,128)(2,1)}), bf16[2304,1024]{1,0:T(8,128)(2,1)}) %all-gather.30.cloned.1.call-update) | async-done | bytes 4718608 | tf_op jit(solution)/shard_map/all_gather | solution.py:155
  998.0 22.2 %all-reduce = (f32[]{:T(128)}, f32[]{:T(128)}) all-reduce(f32[]{:T(128)} %get-tuple-element.420, f32[]{:T(128)} %get-tuple-element.418), channel_id=1, replica_groups=mesh['dp'=8,'tensor'=4] {'dp'}, use_global_device_ids=true, to_apply=%region_22.23 | all-reduce | flops 2 | bytes 16 | tf_op jit(solution)/shard_map/psum | solution.py:300
  1022.2 19.7 bitcast_convert_fusion.1
  1042.0 44.3 %reduce-scatter.28.cloned.1.call-done = bf16[576,1024]{1,0:T(8,128)(2,1)} async-done(((bf16[2304,1024]{1,0:T(8,128)(2,1)}), bf16[576,1024]{1,0:T(8,128)(2,1)}) %reduce-scatter.28.cloned.1.call-update) | async-done | bytes 1179664 | tf_op jit(solution)/shard_map/reduce_scatter | solution.py:167
  1093.8 37.3 %all-gather.32.cloned.1.call-done = bf16[2304,1024]{1,0:T(8,128)(2,1)} async-done(((bf16[576,1024]{1,0:T(8,128)(2,1)}), bf16[2304,1024]{1,0:T(8,128)(2,1)}) %all-gather.32.cloned.1.call-update) | async-done | bytes 4718608 | tf_op jit(solution)/shard_map/all_gather | solution.py:163
  1155.7 47.9 %reduce-scatter.30.cloned.1.call-done = bf16[576,1024]{1,0:T(8,128)(2,1)} async-done(((bf16[2304,1024]{1,0:T(8,128)(2,1)}), bf16[576,1024]{1,0:T(8,128)(2,1)}) %reduce-scatter.30.cloned.1.call-update) | async-done | bytes 1179664 | tf_op jit(solution)/shard_map/reduce_scatter | solution.py:167
  1211.0 36.3 %all-gather.34.cloned.1.call-done = bf16[2304,1024]{1,0:T(8,128)(2,1)} async-done(((bf16[576,1024]{1,0:T(8,128)(2,1)}), bf16[2304,1024]{1,0:T(8,128)(2,1)}) %all-gather.34.cloned.1.call-update) | async-done | bytes 4718608 | tf_op jit(solution)/shard_map/all_gather | solution.py:163
  1275.6 47.9 %reduce-scatter.32.cloned.1.call-done = bf16[576,1024]{1,0:T(8,128)(2,1)} async-done(((bf16[2304,1024]{1,0:T(8,128)(2,1)}), bf16[576,1024]{1,0:T(8,128)(2,1)}) %reduce-scatter.32.cloned.1.call-update) | async-done | bytes 1179664 | tf_op jit(solution)/shard_map/reduce_scatter | solution.py:167
  1330.8 36.9 %all-gather.36.cloned.1.call-done = bf16[2304,1024]{1,0:T(8,128)(2,1)} async-done(((bf16[576,1024]{1,0:T(8,128)(2,1)}), bf16[2304,1024]{1,0:T(8,128)(2,1)}) %all-gather.36.cloned.1.call-update) | async-done | bytes 4718608 | tf_op jit(solution)/shard_map/all_gather | solution.py:163
  1390.8 22.4 %multiply_reduce_fusion = (f32[3,4,768]{2,1,0:T(4,128)}, f32[3,4,768,768]{2,3,1,0:T(8,128)}) fusion(f32[3,4,768,768]{2,3,1,0:T(8,128)} %get-tuple-element.450, f32[3,4,768]{2,1,0:T(4,128)} %log_add_fusion.1, bf16[3,768,4,64]{1,3,2,0:T(8,128)(2,1)S(1)} %copy.176, bf16[3,768,4,64]{1,3,2,0:T(8,128)(2,1)S(1)} %copy-done.38), kind=kOutput, calls=%fused_computation.7 | convolution fusion | flops 927194112 | bytes 59056128 | tf_op jit(solution)/shard_map/vmap()/while/body/eval_jaxpr/qhe,khe->hqk/dot_general | solution.py:111
  1413.3 23.4 %multiply_convert_fusion = bf16[3,4,768,768]{2,3,1,0:T(8,128)(2,1)} fusion(f32[3,4,768,768]{2,3,1,0:T(8,128)} %get-tuple-element.459, f32[3,4,768,768]{2,3,1,0:T(8,128)} %get-tuple-element.450, f32[3,4,768]{2,1,0:T(4,128)} %get-tuple-element.458, f32[3,4,768]{2,1,0:T(4,128)} %log_add_fusion.1), kind=kLoop, calls=%fused_computation.6 | loop fusion | flops 28311552 | bytes 70852608 | tf_op jit(solution)/shard_map/vmap()/while/body/eval_jaxpr/convert_element_type | solution.py:115
  1500.4 28.5 %reduce-scatter.36.cloned.1.call-done = bf16[576,1024]{1,0:T(8,128)(2,1)} async-done(((bf16[2304,1024]{1,0:T(8,128)(2,1)}), bf16[576,1024]{1,0:T(8,128)(2,1)}) %reduce-scatter.36.cloned.1.call-update) | async-done | bytes 1179664 | tf_op jit(solution)/shard_map/reduce_scatter | solution.py:167
  1556.6 18.0 all-reduce.3.cloned.1.call-done
  1613.1 17.0 convert_bitcast_fusion
  1711.1 60.2 %reduce-scatter.38.cloned.1.call-done = bf16[256,96]{0,1:T(8,128)(2,1)} async-done(((bf16[256,768]{0,1:T(8,128)(2,1)}), bf16[256,96]{0,1:T(8,128)(2,1)}) %reduce-scatter.38.cloned.1.call-update) | async-done | bytes 49168 | tf_op jit(solution)/shard_map/reduce_scatter | solution.py:446
  1772.7 89.6 %reduce-scatter.40.cloned.1.call-done = bf16[128,2048]{1,0:T(8,128)(2,1)} async-done(((bf16[1024,2048]{1,0:T(8,128)(2,1)}), bf16[128,2048]{1,0:T(8,128)(2,1)}) %reduce-scatter.40.cloned.1.call-update) | async-done | bytes 524304
  1866.1 61.2 %reduce-scatter.44.cloned.1.call-done = bf16[128,9]{1,0:T(8,128)(2,1)} async-done(((bf16[1024,9]{1,0:T(8,128)(2,1)}), bf16[128,9]{1,0:T(8,128)(2,1)}) %reduce-scatter.44.cloned.1.call-update) | async-done | bytes 2320
  1929.4 149.4 %reduce-scatter.42.cloned.1.call-done = bf16[128,4096]{1,0:T(8,128)(2,1)} async-done(((bf16[1024,4096]{1,0:T(8,128)(2,1)}), bf16[128,4096]{1,0:T(8,128)(2,1)}) %reduce-scatter.42.cloned.1.call-update) | async-done | bytes 1048592
  2087.1 39.3 %psum.39 = f32[]{:T(128)} all-reduce(f32[]{:T(128)S(6)} %add.371), channel_id=1, replica_groups=mesh['dp'=8,'tensor'=4] {'dp','tensor'}, use_global_device_ids=true, to_apply=%region_60.61 | all-reduce | flops 1 | bytes 8 | tf_op jit(solution)/shard_map/psum | solution.py:460
  (508 shorter events, 614.7 us)
Async XLA Ops:
  7.2 452.5 %copy-start = (bf16[3,256,768]{2,1,0:T(8,128)(2,1)S(1)}, bf16[3,256,768]{2,1,0:T(8,128)(2,1)}, u32[]{:S(2)}) copy-start(bf16[3,256,768]{2,1,0:T(8,128)(2,1)} %param.25) | copy-start | bytes 3538948
  7.2 131.2 %all-gather.16.cloned.1.call-start = ((), (), s32[]{:S(2)}) async-start(), calls=%async_computation.13 | async-start | bytes 9437184 | tf_op jit(solution)/shard_map/all_gather | solution.py:215
  10.1 219.4 %reduce-scatter.20.cloned.1.call-start = ((), (), s32[]{:S(2)}) async-start(), calls=%async_computation.14 | async-start | bytes 11796480 | tf_op jit(solution)/shard_map/reduce_scatter | solution.py:159
  10.1 142.5 %copy-start.96 = (s32[3,768,4]{1,2,0:T(4,128)}, s32[3,768,4]{1,2,0:T(4,128)S(1)}, u32[]{:S(2)}) copy-start(s32[3,768,4]{1,2,0:T(4,128)S(1)} %broadcast_subtract_fusion) | copy-start | bytes 110596
  152.7 153.0 %all-gather.20.cloned.1.call-start = ((), (), s32[]{:S(2)}) async-start(), calls=%async_computation.16 | async-start | bytes 4718592 | tf_op jit(solution)/shard_map/all_gather | solution.py:213
  154.7 188.6 %all-gather.18.cloned.1.call-start = ((), (), s32[]{:S(2)}) async-start(), calls=%async_computation.15 | async-start | bytes 5898240 | tf_op jit(solution)/shard_map/all_gather | solution.py:155
  189.3 318.7 %copy-start.78 = (f32[1,1024]{1,0:T(1,128)}, f32[1,1024]{1,0:T(1,128)S(1)}, u32[]{:S(2)}) copy-start(f32[1,1024]{1,0:T(1,128)S(1)} %get-tuple-element.442) | copy-start | bytes 12292
  189.3 486.6 %copy-start.75 = (f32[1,1024]{1,0:T(1,128)}, f32[1,1024]{1,0:T(1,128)S(1)}, u32[]{:S(2)}) copy-start(f32[1,1024]{1,0:T(1,128)S(1)} %get-tuple-element.440) | copy-start | bytes 12292
  233.0 271.7 %copy-start.2 = (f32[576,1024]{1,0:T(8,128)}, f32[576,1024]{1,0:T(8,128)S(1)}, u32[]{:S(2)}) copy-start(f32[576,1024]{1,0:T(8,128)S(1)} %get-tuple-element.431) | copy-start | bytes 7077892
  236.5 268.2 %reduce-scatter.22.cloned.1.call-start = ((), (), s32[]{:S(2)}) async-start(), calls=%async_computation.17 | async-start | bytes 11796480 | tf_op jit(solution)/shard_map/reduce_scatter | solution.py:159
  426.1 100.5 %all-gather.22.cloned.1.call-start = ((), (), s32[]{:S(2)}) async-start(), calls=%async_computation.18 | async-start | bytes 1966080 | tf_op jit(solution)/shard_map/all_gather | solution.py:261
  461.0 105.2 %all-gather.24.cloned.1.call-start = ((), (), s32[]{:S(2)}) async-start(), calls=%async_computation.19 | async-start | bytes 5898240 | tf_op jit(solution)/shard_map/all_gather | solution.py:155
  510.1 162.0 %reduce-scatter.24.cloned.1.call-start = ((), (), s32[]{:S(2)}) async-start(), calls=%async_computation.20 | async-start | bytes 11796480 | tf_op jit(solution)/shard_map/reduce_scatter | solution.py:159
  593.5 154.8 %all-gather.28.cloned.1.call-start = ((), (), s32[]{:S(2)}) async-start(), calls=%async_computation.22 | async-start | bytes 4718592 | tf_op jit(solution)/shard_map/all_gather | solution.py:214
  595.6 190.4 %all-gather.26.cloned.1.call-start = ((), (), s32[]{:S(2)}) async-start(), calls=%async_computation.21 | async-start | bytes 5898240 | tf_op jit(solution)/shard_map/all_gather | solution.py:155
  675.8 139.0 %copy-start.87 = (f32[576]{0:T(1024)}, f32[576]{0:T(1024)S(1)}, u32[]{:S(2)}) copy-start(f32[576]{0:T(1024)S(1)} %fusion.143) | copy-start | bytes 6916
  677.3 226.0 %reduce-scatter.26.cloned.1.call-start = ((), (), s32[]{:S(2)}) async-start(), calls=%async_computation.23 | async-start | bytes 11796480 | tf_op jit(solution)/shard_map/reduce_scatter | solution.py:159
  824.9 122.2 %all-gather.30.cloned.1.call-start = ((), (), s32[]{:S(2)}) async-start(), calls=%async_computation.24 | async-start | bytes 5898240 | tf_op jit(solution)/shard_map/all_gather | solution.py:155
  909.4 176.9 %reduce-scatter.28.cloned.1.call-start = ((), (), s32[]{:S(2)}) async-start(), calls=%async_computation.25 | async-start | bytes 5898240 | tf_op jit(solution)/shard_map/reduce_scatter | solution.py:167
  1042.0 89.2 %all-gather.32.cloned.1.call-start = ((), (), s32[]{:S(2)}) async-start(), calls=%async_computation.26 | async-start | bytes 5898240 | tf_op jit(solution)/shard_map/all_gather | solution.py:163
  1093.6 110.1 %reduce-scatter.30.cloned.1.call-start = ((), (), s32[]{:S(2)}) async-start(), calls=%async_computation.27 | async-start | bytes 5898240 | tf_op jit(solution)/shard_map/reduce_scatter | solution.py:167
  1155.6 91.7 %all-gather.34.cloned.1.call-start = ((), (), s32[]{:S(2)}) async-start(), calls=%async_computation.28 | async-start | bytes 5898240 | tf_op jit(solution)/shard_map/all_gather | solution.py:163
  1209.8 113.7 %reduce-scatter.32.cloned.1.call-start = ((), (), s32[]{:S(2)}) async-start(), calls=%async_computation.29 | async-start | bytes 5898240 | tf_op jit(solution)/shard_map/reduce_scatter | solution.py:167
  1275.5 92.2 %all-gather.36.cloned.1.call-start = ((), (), s32[]{:S(2)}) async-start(), calls=%async_computation.30 | async-start | bytes 5898240 | tf_op jit(solution)/shard_map/all_gather | solution.py:163
  1330.1 198.9 %reduce-scatter.36.cloned.1.call-start = ((), (), s32[]{:S(2)}) async-start(), calls=%async_computation.32 | async-start | bytes 5898240 | tf_op jit(solution)/shard_map/reduce_scatter | solution.py:167
  1480.9 93.7 %all-reduce.3.cloned.1.call-start = ((), (), s32[]{:S(2)}) async-start(), calls=%async_computation.34 | async-start | bytes 3145728 | tf_op jit(solution)/shard_map/psum | solution.py:413
  1500.4 148.5 %all-gather.38.cloned.1.call-start = ((), (), s32[]{:S(2)}) async-start(), calls=%async_computation.33 | async-start | bytes 5898240 | tf_op jit(solution)/shard_map/all_gather | solution.py:163
  1536.8 172.4 %reduce-scatter.34.cloned.1.call-start = ((), (), s32[]{:S(2)}) async-start(), calls=%async_computation.31 | async-start | bytes 4718592 | tf_op jit(solution)/shard_map/reduce_scatter | solution.py:440
  1556.5 214.8 %reduce-scatter.38.cloned.1.call-start = ((), (), s32[]{:S(2)}) async-start(), calls=%async_computation.35 | async-start | bytes 442368 | tf_op jit(solution)/shard_map/reduce_scatter | solution.py:446
  1577.0 285.4 %reduce-scatter.40.cloned.1.call-start = ((), (), s32[]{:S(2)}) async-start(), calls=%async_computation.36 | async-start | bytes 4718592
  1612.3 315.0 %reduce-scatter.44.cloned.1.call-start = ((), (), s32[]{:S(2)}) async-start(), calls=%async_computation.38 | async-start | bytes 294912
  1648.8 430.0 %reduce-scatter.42.cloned.1.call-start = ((), (), s32[]{:S(2)}) async-start(), calls=%async_computation.37 | async-start | bytes 9437184
  (117 other events, 1522.0 us)
Sparse Core Ops, SparseCore 0:
  10.8 127.6 all-gather.15
  152.8 76.5 reduce-scatter.19
  232.2 73.3 all-gather.19
  307.6 35.7 all-gather.17
  426.2 78.4 reduce-scatter.21
  506.7 19.8 all-gather.21
  528.7 37.4 all-gather.23
  593.7 78.4 reduce-scatter.23
  674.9 73.3 all-gather.27
  750.3 35.7 all-gather.25
  825.0 78.3 reduce-scatter.25
  909.5 37.4 all-gather.29
  1042.1 44.1 reduce-scatter.27
  1093.7 37.4 all-gather.31
  1155.8 47.8 reduce-scatter.29
  1209.9 37.4 all-gather.33
  1275.6 47.8 reduce-scatter.31
  1330.2 37.4 all-gather.35
  1481.1 47.8 reduce-scatter.35
  1531.7 42.8 all-reduce.2
  1576.7 37.5 all-gather.37
  1617.9 87.9 reduce-scatter.33
  1710.1 61.1 reduce-scatter.37
  1775.2 87.0 reduce-scatter.39
  1866.2 61.0 reduce-scatter.43
  1930.8 147.9 reduce-scatter.41
where the time goes:
time: 2180 us; the launch traced here: 2170 us
  waiting for transfers between devices  1320 us (61%)
  matrix products  333 us (15%)
  local copies, waits for them, and re-layouts  185 us (8%)
  other arithmetic  158 us (7%)
  blocking collectives  146 us (7%)
  between operations  23.6 us (1%)
    unnamed x29, waiting for transfers between devices  301 us
    reduce_scatter x4, waiting for transfers between devices, scatter_rows(): lax.psum_scatter(partial_sum, 'tensor', scatter_dimension=0, tiled=True)  238 us
    reduce_scatter x4, waiting for transfers between devices, scatter_grad_rows(): lax.psum_scatter(partial_sum.astype(jnp.bfloat16), 'tensor', scatter_dime...  169 us
    all_gather x4, waiting for transfers between devices, gather_rows(): return lax.all_gather(values, 'tensor', axis=0, tiled=True)  144 us
    all_gather x1, waiting for transfers between devices, on_device(): lax.all_gather(tables.astype(jnp.bfloat16), 'dp', axis=1, tiled=True)  128 us
    all_gather x4, waiting for transfers between devices, gather_grad_rows(): return lax.all_gather(values, 'tensor', axis=0, tiled=True)  111 us
    unnamed x274, local copies, waits for them, and re-layouts  106 us
    all_gather x1, waiting for transfers between devices, on_device(): lax.all_gather(feedforward.astype(jnp.bfloat16), 'dp', axis=1, tiled=True)  70.9 us
  transfers between devices with their start and end apart: 26, of which 24 were waited for; matrix products, arithmetic and copies ran while one was open for 10% of the time, Pallas kernels for 0%

commit v1 on v0

v1 whole, which is shorter than its diff:
```python
from functools import partial
import math

import jax
import jax.numpy as jnp
from jax import lax
from jax.experimental import pallas as pl
from jax.experimental.pallas import tpu as pltpu
from jax.sharding import PartitionSpec as P

HEAD_DIM = 64
STEP = 5
BLOCK = 256
NEG = -1e30
LOW = jnp.bfloat16
F32 = jnp.float32

clip_limit = 0.004
stability_offset = 1e-08
weight_decay = 0.01
moment_decay = 0.5
rate_matrix = 0.03
rate_table = 0.05
rate_norm = 0.2


def nn(a, b):
    return lax.dot_general(a, b, (((1,), (0,)), ((), ())), preferred_element_type=F32)


def nt(a, b):
    return lax.dot_general(a, b, (((1,), (1,)), ((), ())), preferred_element_type=F32)


def tn(a, b):
    return lax.dot_general(a, b, (((0,), (0,)), ((), ())), preferred_element_type=F32)


def sds(shape, kind):
    return jax.ShapeDtypeStruct(shape, kind)


def scalars():
    return pl.BlockSpec(memory_space=pltpu.SMEM)


def whole(a):
    rank = len(a.shape)
    return pl.BlockSpec(a.shape, lambda i: (0,) * rank)


def member(a, axis, size, index):
    block = a.shape[:axis] + (size,) + a.shape[axis + 1 :]
    place = tuple(index if d == axis else 0 for d in range(len(a.shape)))
    return pl.BlockSpec(block, lambda i: place)


def later(body, count, at):
    def ordered(*refs):
        return body(*refs[:at], *refs[at + count :])

    return ordered


def anywhere():
    return pl.BlockSpec(memory_space=pl.ANY)


def kernel(body, outs, operands, specs, flops=0, scratch=(), name=None, exps=0, after=(), limit=40):
    outs = tuple(outs)
    nbytes = sum(math.prod(o.shape) * jnp.dtype(o.dtype).itemsize for o in outs)
    for a, s in zip(operands, specs):
        shape = a.shape if s.block_shape is None else s.block_shape
        nbytes += math.prod(shape) * jnp.dtype(a.dtype).itemsize
    return pl.pallas_call(
        later(body, len(after), len(operands)),
        out_shape=outs,
        grid=(1,),
        in_specs=list(specs) + [anywhere()] * len(after),
        out_specs=tuple(whole(o) for o in outs),
        scratch_shapes=scratch,
        compiler_params=pltpu.CompilerParams(vmem_limit_bytes=limit << 20),
        cost_estimate=pl.CostEstimate(
            flops=int(flops), bytes_accessed=int(nbytes), transcendentals=int(exps)
        ),
        name=name,
    )(*operands, *after)


def flat(ref):
    w = ref[...]
    return w.reshape(-1, w.shape[-1])


def half_rows(core, height):
    return (
        pl.ds(pl.multiple_of(core * height, height), height),
        pl.ds(pl.multiple_of((1 - core) * height, height), height),
    )


def attend_block(query, keys, values, head_masks, diagonal, bias):
    rows, width = query.shape
    lane = lax.broadcasted_iota(jnp.int32, (rows, 128), 1)
    column = lax.broadcasted_iota(jnp.int32, (rows, width), 1) // HEAD_DIM
    mixed = jnp.zeros((rows, width), F32)
    totals = jnp.zeros((rows, 128), F32)
    count = keys.shape[0]
    for h, mask in enumerate(head_masks):
        s = nt(query * mask, keys)
        if diagonal is not None:
            last = jnp.where(diagonal, s[:, count - rows :], NEG)
            s = last if count == rows else jnp.concatenate([s[:, : count - rows], last], axis=1)
        if bias is not None:
            s = s + bias
        top = jnp.max(s, axis=1, keepdims=True)
        e = jnp.exp(s - top)
        total = jnp.sum(e, axis=1, keepdims=True)
        p = (e * (1.0 / total)).astype(LOW)
        mixed = jnp.where(column == h, nn(p, values), mixed)
        totals = jnp.where(lane == h, top + jnp.log(total), totals)
    return mixed, totals


def masks_of(width):
    head = lax.broadcasted_iota(jnp.int32, (1, width), 1) // HEAD_DIM
    return [(head == h).astype(F32).astype(LOW) for h in range(width // HEAD_DIM)]


def triangle(size):
    row = lax.broadcasted_iota(jnp.int32, (size, size), 0)
    col = lax.broadcasted_iota(jnp.int32, (size, size), 1)
    return row >= col


def self_forward_body(
    core_ref, own_ref, got_ref, wq_ref, wk_ref, wv_ref, wo_ref,
    q_ref, k_ref, v_ref, o_ref, lse_ref, keep_ref, send_ref, tot_ref,
):
    height = own_ref.shape[0]
    frames, width = q_ref.shape
    mine, other = half_rows(core_ref[0], height)
    for w_ref, to_ref in ((wq_ref, q_ref), (wk_ref, k_ref), (wv_ref, v_ref)):
        w = flat(w_ref)
        to_ref[mine, :] = nn(own_ref[...], w).astype(LOW)
        to_ref[other, :] = nn(got_ref[...], w).astype(LOW)
    scale = jnp.asarray(HEAD_DIM**-0.5, LOW)
    head_masks = masks_of(width)
    diagonal = triangle(BLOCK)
    for i in range(frames // BLOCK):
        rows = slice(i * BLOCK, (i + 1) * BLOCK)
        mixed, totals = attend_block(
            q_ref[rows, :] * scale,
            k_ref[: (i + 1) * BLOCK, :],
            v_ref[: (i + 1) * BLOCK, :],
            head_masks,
            diagonal,
            None,
        )
        o_ref[rows, :] = mixed.astype(LOW)
        tot_ref[rows, :] = totals
    lse_ref[...] = jnp.transpose(tot_ref[...])[:8, :]
    wo = flat(wo_ref)
    send_ref[...] = nt(o_ref[other, :], wo).astype(LOW)
    keep_ref[...] = nt(o_ref[mine, :], wo)


def cross_forward_body(
    core_ref, own_ref, got_ref, bias_ref, k_ref, v_ref, wq_ref, wo_ref,
    q_ref, o_ref, lse_ref, keep_ref, send_ref, tot_ref,
):
    height = own_ref.shape[0]
    frames, width = q_ref.shape
    mine, other = half_rows(core_ref[0], height)
    w = flat(wq_ref)
    q_ref[mine, :] = nn(own_ref[...], w).astype(LOW)
    q_ref[other, :] = nn(got_ref[...], w).astype(LOW)
    scale = jnp.asarray(HEAD_DIM**-0.5, LOW)
    head_masks = masks_of(width)
    for i in range(frames // BLOCK):
        rows = slice(i * BLOCK, (i + 1) * BLOCK)
        mixed, totals = attend_block(
            q_ref[rows, :] * scale, k_ref[...], v_ref[...], head_masks, None, bias_ref[...]
        )
        o_ref[rows, :] = mixed.astype(LOW)
        tot_ref[rows, :] = totals
    lse_ref[...] = jnp.transpose(tot_ref[...])[:8, :]
    wo = flat(wo_ref)
    send_ref[...] = nt(o_ref[other, :], wo).astype(LOW)
    keep_ref[...] = nt(o_ref[mine, :], wo)


def erf(x):
    return lax.erf(x)


def ffn_forward_body(
    core_ref, own_ref, got_ref, w1_ref, w2_ref, act_ref, slope_ref, keep_ref, send_ref
):
    height = own_ref.shape[0]
    mine, other = half_rows(core_ref[0], height)
    w1 = flat(w1_ref)
    w2 = flat(w2_ref)
    for source, rows, to_ref in ((got_ref, other, send_ref), (own_ref, mine, keep_ref)):
        u = nn(source[...], w1)
        phi = 0.5 * (1.0 + erf(u * (2.0**-0.5)))
        act = (u * phi).astype(LOW)
        density = jnp.exp(-0.5 * u * u) * ((2.0 * math.pi) ** -0.5)
        act_ref[rows, :] = act
        slope_ref[rows, :] = (phi + u * density).astype(LOW)
        to_ref[...] = nt(act, w2).astype(to_ref.dtype)


def head_forward_body(
    core_ref, own_ref, got_ref, target_ref, w_ref, logits_ref, stats_ref, tot_ref
):
    height = own_ref.shape[0]
    books, vocab = w_ref.shape[1], w_ref.shape[3]
    halves = half_rows(core_ref[0], height)
    lane = lax.broadcasted_iota(jnp.int32, (height, 128), 1)
    code = lax.broadcasted_iota(jnp.int32, (height, vocab), 1)
    for source, rows in zip((own_ref, got_ref), halves):
        target = target_ref[rows, :]
        y = source[...]
        totals = jnp.zeros((height, 128), F32)
        for k in range(books):
            w = w_ref[:, k].reshape(-1, vocab)
            s = nn(y, w)
            logits_ref[rows, k * vocab : (k + 1) * vocab] = s
            top = jnp.max(s, axis=1, keepdims=True)
            total = jnp.sum(jnp.exp(s - top), axis=1, keepdims=True)
            pick = jnp.sum(jnp.where(code == target[:, k : k + 1], s, 0.0), axis=1, keepdims=True)
            totals = jnp.where(lane == k, top + jnp.log(total), totals)
            totals = jnp.where(lane == books + k, pick, totals)
        tot_ref[rows, :] = totals
    stats_ref[...] = jnp.transpose(tot_ref[...])[: 2 * books, :]


def head_backward_body(
    core_ref, logits_ref, total_ref, weight_ref, target_ref, w_ref,
    grad_ref, keep_ref, send_ref, col_ref,
):
    height = keep_ref.shape[0]
    books, vocab = w_ref.shape[1], w_ref.shape[3]
    mine, other = half_rows(core_ref[0], height)
    frames = logits_ref.shape[0]
    wide = jnp.concatenate(
        [total_ref[...], jnp.zeros((128 - total_ref.shape[0], frames), F32)], axis=0
    )
    col_ref[...] = jnp.transpose(wide)
    code = lax.broadcasted_iota(jnp.int32, (height, vocab), 1)
    for rows, to_ref in ((other, send_ref), (mine, keep_ref)):
        target = target_ref[rows, :]
        weight = weight_ref[rows, :]
        total = col_ref[rows, :]
        acc = None
        for k in range(books):
            s = logits_ref[rows, k * vocab : (k + 1) * vocab]
            p = jnp.exp(s - total[:, k : k + 1])
            hit = jnp.where(code == target[:, k : k + 1], 1.0, 0.0)
            g = ((p - hit) * weight[:, k : k + 1]).astype(LOW)
            grad_ref[rows, k * vocab : (k + 1) * vocab] = g
            part = nt(g, w_ref[:, k].reshape(-1, vocab))
            acc = part if acc is None else acc + part
        to_ref[...] = acc.astype(to_ref.dtype)


def ffn_backward_body(
    core_ref, own_ref, got_ref, slope_ref, w1_ref, w2_ref, grad_ref, keep_ref, send_ref
):
    height = own_ref.shape[0]
    mine, other = half_rows(core_ref[0], height)
    w1 = flat(w1_ref)
    w2 = flat(w2_ref)
    for source, rows, to_ref in ((got_ref, other, send_ref), (own_ref, mine, keep_ref)):
        g = (nn(source[...], w2) * slope_ref[rows, :].astype(F32)).astype(LOW)
        grad_ref[rows, :] = g
        to_ref[...] = nt(g, w1).astype(to_ref.dtype)


def attend_back(
    q, k, v, g, lse, head_masks, scale, diagonal, bias, dq_ref, rows, dk_ref, dv_ref, first
):
    count, width = k.shape
    step = q.shape[0]
    dq = jnp.zeros((step, width), F32)
    dk = jnp.zeros((count, width), F32)
    dv = jnp.zeros((count, width), F32)
    for h, mask in enumerate(head_masks):
        qm = q * mask
        gm = g * mask
        s = nt(k, qm)
        if diagonal is not None:
            last = jnp.where(diagonal, s[count - step :, :], NEG)
            s = last if count == step else jnp.concatenate([s[: count - step, :], last], axis=0)
        if bias is not None:
            s = s + bias
        p = jnp.exp(s - lse[h : h + 1, :])
        dp = nt(v, gm)
        inner = jnp.sum(p * dp, axis=0, keepdims=True)
        ds = (p * (dp - inner)).astype(LOW)
        dq = dq + tn(ds, k * mask)
        dk = dk + nn(ds, qm)
        dv = dv + nn(p.astype(LOW), gm)
    dq_ref[rows, :] = (dq * scale).astype(LOW)
    dk_ref[:count, :] = dk if first else dk_ref[:count, :] + dk
    dv_ref[:count, :] = dv if first else dv_ref[:count, :] + dv


def self_backward_body(
    core_ref, own_ref, got_ref, q_ref, k_ref, v_ref, lse_ref, wq_ref, wk_ref, wv_ref, wo_ref,
    grad_ref, keep_ref, send_ref, g_ref, dq_ref, dk_acc, dv_acc,
):
    height = own_ref.shape[0]
    frames, width = q_ref.shape
    mine, other = half_rows(core_ref[0], height)
    wo = flat(wo_ref)
    g_ref[mine, :] = nn(own_ref[...], wo).astype(LOW)
    g_ref[other, :] = nn(got_ref[...], wo).astype(LOW)
    scale = HEAD_DIM**-0.5
    head_masks = masks_of(width)
    row = lax.broadcasted_iota(jnp.int32, (BLOCK, BLOCK), 0)
    col = lax.broadcasted_iota(jnp.int32, (BLOCK, BLOCK), 1)
    diagonal = col >= row
    blocks = frames // BLOCK
    for i in reversed(range(blocks)):
        rows = slice(i * BLOCK, (i + 1) * BLOCK)
        count = (i + 1) * BLOCK
        attend_back(
            q_ref[rows, :] * jnp.asarray(scale, LOW),
            k_ref[:count, :],
            v_ref[:count, :],
            g_ref[rows, :],
            lse_ref[:, rows],
            head_masks,
            scale,
            diagonal,
            None,
            dq_ref,
            rows,
            dk_acc,
            dv_acc,
            i == blocks - 1,
        )
    grad_ref[:, :width] = dq_ref[...]
    grad_ref[:, width : 2 * width] = dk_acc[...].astype(LOW)
    grad_ref[:, 2 * width :] = dv_acc[...].astype(LOW)
    for rows, to_ref in ((other, send_ref), (mine, keep_ref)):
        part = None
        for n, w_ref in enumerate((wq_ref, wk_ref, wv_ref)):
            term = nt(grad_ref[rows, n * width : (n + 1) * width], flat(w_ref))
            part = term if part is None else part + term
        to_ref[...] = part.astype(to_ref.dtype)


def cross_backward_body(
    core_ref, own_ref, got_ref, bias_ref, q_ref, k_ref, v_ref, lse_ref, wq_ref, wo_ref,
    dq_ref, dk_ref, dv_ref, keep_ref, send_ref, g_ref, dk_acc, dv_acc,
):
    height = own_ref.shape[0]
    frames, width = q_ref.shape
    mine, other = half_rows(core_ref[0], height)
    wo = flat(wo_ref)
    g_ref[mine, :] = nn(own_ref[...], wo).astype(LOW)
    g_ref[other, :] = nn(got_ref[...], wo).astype(LOW)
    scale = HEAD_DIM**-0.5
    head_masks = masks_of(width)
    for i in range(frames // BLOCK):
        rows = slice(i * BLOCK, (i + 1) * BLOCK)
        attend_back(
            q_ref[rows, :] * jnp.asarray(scale, LOW),
            k_ref[...],
            v_ref[...],
            g_ref[rows, :],
            lse_ref[:, rows],
            head_masks,
            scale,
            None,
            bias_ref[...],
            dq_ref,
            rows,
            dk_acc,
            dv_acc,
            i == 0,
        )
    dk_ref[...] = dk_acc[...].astype(LOW)
    dv_ref[...] = dv_acc[...].astype(LOW)
    wq = flat(wq_ref)
    for rows, to_ref in ((other, send_ref), (mine, keep_ref)):
        to_ref[...] = nt(dq_ref[rows, :], wq).astype(to_ref.dtype)


def normalize(values, gain, shift):
    center = values - jnp.mean(values, axis=1, keepdims=True)
    spread = jnp.mean(center * center, axis=1, keepdims=True)
    return center * lax.rsqrt(spread + 1e-05) * gain + shift


def norm_body(which, hidden_ref, part_ref, far_ref, norm_ref, new_ref, out_ref):
    new = hidden_ref[...] + (part_ref[...].astype(F32) + far_ref[...].astype(F32))
    new_ref[...] = new
    out_ref[...] = normalize(
        new, norm_ref[which : which + 1, :], norm_ref[which + 4 : which + 5, :]
    ).astype(LOW)


def embed_norm_body(side_ref, place_ref, norm_ref, *refs):
    *part_refs, new_ref, out_ref = refs
    side = side_ref[0]
    rows = part_refs[0].shape[0]
    for s, part in enumerate(part_refs):
        at = pl.ds(pl.multiple_of((side ^ s) * rows, rows), rows)
        new_ref[at, :] = part[...].astype(F32) + place_ref[at, :]
    out_ref[...] = normalize(new_ref[...], norm_ref[0:1, :], norm_ref[4:5, :]).astype(LOW)


def norm_back_body(which, hidden_ref, part_ref, far_ref, *refs):
    *before, norm_ref, new_ref, low_ref, sums_ref = refs
    values = hidden_ref[...]
    grad = part_ref[...].astype(F32) + far_ref[...].astype(F32)
    gain = norm_ref[which : which + 1, :]
    center = values - jnp.mean(values, axis=1, keepdims=True)
    spread = jnp.mean(center * center, axis=1, keepdims=True)
    inverse = lax.rsqrt(spread + 1e-05)
    unit = center * inverse
    scaled = grad * gain
    first = jnp.mean(scaled, axis=1, keepdims=True)
    second = jnp.mean(scaled * unit, axis=1, keepdims=True)
    new = inverse * (scaled - first - unit * second)
    if before:
        new = before[0][...] + new
    new_ref[...] = new
    low_ref[...] = new.astype(LOW)

    @pl.when(pl.program_id(0) == 0)
    def _():
        sums_ref[...] = jnp.zeros(sums_ref.shape, F32)

    sums_ref[0:1, :] += jnp.sum(grad * unit, axis=0, keepdims=True)
    sums_ref[1:2, :] += jnp.sum(grad, axis=0, keepdims=True)


def norm_rows_kernel(body, outs, operands, norm_rows, after, steps=4):
    height, width = operands[0].shape
    rows = height // steps

    def spec(a):
        if a.shape[0] == height:
            return pl.BlockSpec((rows, width), lambda i: (i, 0))
        return pl.BlockSpec(a.shape, lambda i: (0, 0))

    operands = list(operands) + [norm_rows]
    nbytes = sum(
        math.prod(a.shape) * jnp.dtype(a.dtype).itemsize for a in operands + list(outs)
    )
    return pl.pallas_call(
        later(body, len(after), len(operands)),
        out_shape=tuple(outs),
        grid=(steps,),
        in_specs=[spec(a) for a in operands] + [anywhere()] * len(after),
        out_specs=tuple(spec(o) for o in outs),
        compiler_params=pltpu.CompilerParams(vmem_limit_bytes=24 << 20),
        cost_estimate=pl.CostEstimate(
            flops=20 * height * width, bytes_accessed=nbytes, transcendentals=0
        ),
        name="norm",
    )(*operands, *after)


def weight_grad_body(clips, core_ref, *refs):
    pairs = refs[: 2 * clips]
    rights = refs[2 * clips : 3 * clips]
    out_ref, turned = refs[3 * clips :]
    height = pairs[0].shape[0]
    frames = rights[0].shape[0]

    @pl.when(pl.program_id(0) == 0)
    def _():
        core = core_ref[0]
        for c in range(clips):
            for j, at in ((0, core), (1, 1 - core)):
                place = pl.ds(pl.multiple_of(c * frames + at * height, 128), height)
                turned[:, place] = jnp.transpose(pairs[2 * c + j][...])

    total = None
    for c in range(clips):
        part = nn(turned[:, c * frames : (c + 1) * frames], rights[c][...])
        total = part if total is None else total + part
    out_ref[...] = total.astype(LOW).reshape(out_ref.shape)


def weight_grad(core, pairs, rights, dp, group, name, after):
    clips = len(pairs)
    width = pairs[0][0].shape[1]
    frames, columns = rights[0].shape
    lefts = [half for pair in pairs for half in pair]
    members = columns // group
    nbytes = 2 * (2 * clips * frames * (width + columns) // 2 + width * columns)
    return pl.pallas_call(
        later(partial(weight_grad_body, clips), 1, 1 + 3 * clips),
        out_shape=sds((dp, members, width // dp, group), LOW),
        grid=(members,),
        in_specs=[scalars()]
        + [pl.BlockSpec(a.shape, lambda i: (0, 0)) for a in lefts]
        + [pl.BlockSpec((frames, group), lambda i: (0, i)) for _ in rights]
        + [anywhere()],
        out_specs=pl.BlockSpec((dp, 1, width // dp, group), lambda i: (0, i, 0, 0)),
        scratch_shapes=[pltpu.VMEM((width, clips * frames), LOW)],
        compiler_params=pltpu.CompilerParams(vmem_limit_bytes=56 << 20),
        cost_estimate=pl.CostEstimate(
            flops=2 * clips * frames * width * columns, bytes_accessed=nbytes, transcendentals=0
        ),
        name=name,
    )(core, *lefts, *rights, after)


def embed_body(base_ref, codes_ref, *refs):
    *table_refs, out_ref = refs
    books, features, vocab = table_refs[0].shape
    rows = codes_ref.shape[1]
    chunk = min(256, vocab)
    code = lax.broadcasted_iota(jnp.int32, (rows, chunk), 1)
    acc = jnp.zeros((rows, features), F32)
    for k in range(books):
        column = codes_ref[0, :, k : k + 1]
        for b, table in enumerate(table_refs):
            local = column - base_ref[b]
            for v in range(0, vocab, chunk):
                hit = jnp.where(code == local - v, 1.0, 0.0).astype(LOW)
                acc = acc + nt(hit, table[k, :, v : v + chunk])
    out_ref[0] = acc.astype(LOW)


def embed(base, codes, tables, after):
    blocks, rows, books = codes.shape
    features = tables[0].shape[1]
    vocab = tables[0].shape[2] * len(tables)
    return pl.pallas_call(
        later(embed_body, len(after), 2 + len(tables)),
        out_shape=sds((blocks, rows, features), LOW),
        grid=(blocks,),
        in_specs=[scalars(), pl.BlockSpec((1, rows, books), lambda i: (i, 0, 0))]
        + [whole(t) for t in tables]
        + [anywhere()] * len(after),
        out_specs=pl.BlockSpec((1, rows, features), lambda i: (i, 0, 0)),
        compiler_params=pltpu.CompilerParams(vmem_limit_bytes=56 << 20),
        cost_estimate=pl.CostEstimate(
            flops=4 * blocks * rows * books * vocab * features,
            bytes_accessed=2 * books * vocab * features + blocks * rows * (features + 512),
            transcendentals=0,
        ),
        name="embed",
    )(base, codes, *tables, *after)


def embed_back_body(base_ref, codes_ref, *refs):
    *grad_refs, out_ref, all_ref = refs
    rows, features = grad_refs[0].shape
    vocab = out_ref.shape[3]
    book = pl.program_id(1)
    chunk = min(256, vocab)

    @pl.when((pl.program_id(0) == 0) & (book == 0))
    def _():
        for j, g in enumerate(grad_refs):
            all_ref[j * rows : (j + 1) * rows, :] = g[...]

    base = base_ref[pl.program_id(0)]
    line = codes_ref[0]
    line = line[0:1, :]
    code = lax.broadcasted_iota(jnp.int32, (chunk, line.shape[1]), 0)
    for v in range(0, vocab, chunk):
        hit = jnp.where(code == line - (base + v), 1.0, 0.0).astype(LOW)
        out_ref[0, 0, :, v : v + chunk] = jnp.transpose(nn(hit, all_ref[...])).astype(LOW)


def embed_back(base, lines, grads, vocab):
    parts = base.shape[0]
    books, _, total = lines.shape
    features = grads[0].shape[1]
    return pl.pallas_call(
        embed_back_body,
        out_shape=sds((parts, books, features, vocab), LOW),
        grid=(parts, books),
        in_specs=[scalars(), pl.BlockSpec((1, 8, total), lambda i, k: (k, 0, 0))]
        + [pl.BlockSpec(g.shape, lambda i, k: (0, 0)) for g in grads],
        out_specs=pl.BlockSpec((1, 1, features, vocab), lambda i, k: (i, k, 0, 0)),
        scratch_shapes=[pltpu.VMEM((total, features), LOW)],
        compiler_params=pltpu.CompilerParams(vmem_limit_bytes=56 << 20),
        cost_estimate=pl.CostEstimate(
            flops=4 * parts * books * vocab * features * total,
            bytes_accessed=2 * parts * books * features * vocab + 2 * total * features,
            transcendentals=0,
        ),
        name="embed_back",
    )(base, lines, *grads)


def gather_features_body(where_ref, *refs):
    *part_refs, out_ref = refs
    features = part_refs[0].shape[1]
    for m, part in enumerate(part_refs):
        at = pl.ds(pl.multiple_of(where_ref[m] * features, features), features)
        out_ref[:, at] = part[...]


def split_features_body(where_ref, side_ref, *refs):
    clips = side_ref.shape[0] - 1
    grads, outs = refs[:clips], refs[clips:]
    features = outs[0].shape[1]
    rows = outs[0].shape[0] // clips
    at_rows = pl.ds(pl.multiple_of(side_ref[0] * rows, rows), rows)
    for m, out_ref in enumerate(outs):
        at = pl.ds(pl.multiple_of(where_ref[m] * features, features), features)
        for c in range(clips):
            out_ref[c * rows : (c + 1) * rows, :] = grads[c][at_rows, at]


def text_body(where_ref, *refs):
    *part_refs, wk_ref, wv_ref, tp_ref, k_ref, v_ref = refs
    columns = part_refs[0].shape[1]
    for m, part in enumerate(part_refs):
        at = pl.ds(pl.multiple_of(where_ref[m] * columns, columns), columns)
        tp_ref[:, at] = part[...]
    tp = tp_ref[...]
    k_ref[...] = nn(tp, flat(wk_ref)).astype(LOW)
    v_ref[...] = nn(tp, flat(wv_ref)).astype(LOW)


def text_back_body(dk_ref, dv_ref, wk_ref, wv_ref, tp_ref, part_ref, gk_ref, gv_ref):
    dk, dv = dk_ref[...], dv_ref[...]
    part_ref[...] = (nt(dk, flat(wk_ref)) + nt(dv, flat(wv_ref))).astype(LOW)
    turned = jnp.transpose(tp_ref[...])
    gk_ref[...] = nn(turned, dk).astype(LOW).reshape(gk_ref.shape)
    gv_ref[...] = nn(turned, dv).astype(LOW).reshape(gv_ref.shape)


def positions_rows(start, count, feature_count):
    half_width = feature_count // 2
    frequency = jnp.exp(
        jnp.arange(half_width, dtype=F32) * (-math.log(10000.0) / (half_width - 1))
    )
    angles = (start + jnp.arange(count, dtype=jnp.int32)).astype(F32)[:, None] * frequency[None, :]
    return jnp.concatenate([jnp.cos(angles), jnp.sin(angles)], axis=1)


def adam_update(weight, gradient, first_moment, second_moment, step_rate, factor):
    clipped = gradient * factor
    new_first = moment_decay * first_moment + (1.0 - moment_decay) * clipped
    new_second = moment_decay * second_moment + (1.0 - moment_decay) * clipped * clipped
    first_hat = new_first / (1.0 - moment_decay**STEP)
    second_hat = new_second / (1.0 - moment_decay**STEP)
    new_weight = weight * (1.0 - step_rate * weight_decay) - step_rate * first_hat / (
        jnp.sqrt(second_hat) + stability_offset
    )
    return (new_weight, new_first, new_second)


def swap(values, axis, mask):
    size = lax.axis_size(axis)
    return lax.ppermute(values, axis, [(i, i ^ mask) for i in range(size)])


def on_device(
    audio_codes,
    delay_mask,
    frame_mask,
    text_states,
    text_mask,
    attention,
    feedforward,
    tables,
    text_proj,
    norm_params,
    attention_first,
    attention_second,
    feedforward_first,
    feedforward_second,
    tables_first,
    tables_second,
    text_first,
    text_second,
    norm_first,
    norm_second,
):
    clips, frames, books = audio_codes.shape
    text_len, text_width = text_states.shape[1:]
    dp = lax.axis_size("dp")
    tensor = lax.axis_size("tensor")
    group = lax.axis_index("dp")
    place = lax.axis_index("tensor")
    core = place & 1
    side = place >> 1
    sides = tensor // 2
    height = frames // 2
    strip = height // sides
    share = attention.shape[1]
    columns = attention.shape[2]
    width = share * dp
    vocab = tables.shape[2]
    text_share = text_proj.shape[1]
    core_arg = core.astype(jnp.int32).reshape(1)
    side_arg = side.astype(jnp.int32).reshape(1)
    swap_core = partial(swap, axis="tensor", mask=1)

    def spread_tensor(values):
        held = [values]
        mask = tensor // 2
        order = [0]
        while mask:
            held = held + [swap(v, "tensor", mask) for v in held]
            order = order + [o | mask for o in order]
            mask //= 2
        return [v for _, v in sorted(zip(order, held), key=lambda t: t[0])]

    def collect_tensor(parts):
        mask = 1
        live = {m: p for m, p in enumerate(parts)}
        while mask < tensor:
            fresh = {}
            for m in live:
                if not m & mask:
                    got = swap(live[m | mask].astype(LOW), "tensor", mask)
                    fresh[m] = live[m].astype(F32) + got.astype(F32)
            live = fresh
            mask *= 2
        return live[0]

    def across(values):
        own = values
        mask = 2
        rest = None
        while mask < tensor:
            got = swap(own, "tensor", mask)
            mask *= 2
            if mask < tensor:
                own = (own.astype(F32) + got.astype(F32)).astype(LOW)
            rest = got
        if rest is None:
            rest = jnp.zeros_like(own)
        return own, rest

    def total_over(values, axes):
        for axis in axes:
            mask = 1
            while mask < lax.axis_size(axis):
                values = values + swap(values, axis, mask)
                mask *= 2
        return values

    last = []

    def run(body, outs, operands, specs, after=(), **rest):
        results = kernel(body, outs, operands, specs, after=last + list(after), **rest)
        last[:] = [results[-1]]
        return results

    norm_pad = jnp.pad(norm_params.astype(LOW), ((0, 16 - norm_params.shape[0]), (0, columns - share)))
    attn_flat = jnp.concatenate(
        [attention.astype(LOW).reshape(-1, columns), text_proj.astype(LOW).T, norm_pad], axis=0
    )
    attn_all = lax.all_gather(attn_flat, "dp", axis=0)
    ffn_all = lax.all_gather(feedforward.astype(LOW), "dp", axis=0)
    head_all = lax.all_gather(tables[books:].astype(LOW), "dp", axis=0)

    frame_live = (jnp.arange(frames, dtype=jnp.int32) < frames - 1).astype(jnp.int32)
    weight_int = delay_mask * frame_mask[:, :, None] * frame_live[None, :, None]
    start = core * height + side * strip
    strip_codes = lax.dynamic_slice_in_dim(audio_codes, start, strip, 1)
    lines = jnp.transpose(strip_codes, (2, 0, 1)).reshape(books, clips * strip)
    count_line = jnp.broadcast_to(jnp.sum(weight_int), (1, clips * strip))
    packet = jnp.concatenate([lines, count_line], axis=0)[None]
    mask = 1
    while mask < dp:
        packet = jnp.concatenate([packet, swap(packet, "dp", mask)], axis=0)
        mask *= 2
    valid_count = jnp.sum(packet[:, books, 0]).astype(F32)
    all_lines = packet[:, :books]
    all_codes = jnp.transpose(all_lines, (0, 2, 1))
    back_lines = jnp.broadcast_to(
        jnp.transpose(all_lines, (1, 0, 2)).reshape(books, 1, dp * clips * strip),
        (books, 8, dp * clips * strip),
    )
    vocab_base = (place ^ jnp.arange(tensor, dtype=jnp.int32)) * vocab
    group_order = group ^ jnp.arange(dp, dtype=jnp.int32)
    place_order = place ^ jnp.arange(tensor, dtype=jnp.int32)

    table_parts = spread_tensor(tables[:books].astype(LOW))
    step = max(1, dp // 4)
    arrived = [None] * dp
    for low_end in reversed(range(0, dp, step)):
        embedded = embed(
            vocab_base, all_codes[low_end : low_end + step], table_parts, list(last)
        )
        last[:] = [embedded]
        for m in range(low_end, low_end + step):
            piece = embedded[m - low_end]
            arrived[m] = swap(piece, "dp", m) if m else piece
    aligned = share % 128 == 0
    if aligned:
        (strips,) = run(
            gather_features_body,
            [sds((clips * strip, width), LOW)],
            [group_order] + arrived,
            [scalars()] + [whole(a) for a in arrived],
            name="gather_features",
        )
    else:
        strips = jnp.take(jnp.stack(arrived), group_order, axis=0)
        strips = jnp.transpose(strips, (1, 0, 2)).reshape(clips * strip, width)
    placed = positions_rows(core * height, height, width)

    norm_rows = attn_all[:, 8 * share + text_share :, :share]
    norm_rows = jnp.transpose(norm_rows, (1, 0, 2)).reshape(16, width).astype(F32)

    def w_attn(n):
        return member(attn_all, 1, share, n)

    def w_ffn(n):
        return member(ffn_all, 1, 1, n)

    half_sds = sds((height, width), F32)
    half_low = sds((height, width), LOW)

    def norm_step(which, hidden, parts):
        new, out = norm_rows_kernel(
            partial(norm_body, which), [half_sds, half_low], [hidden, *parts], norm_rows, last
        )
        last[:] = [out]
        return new, (out, swap_core(out))

    def norm_back(which, hidden, parts, before):
        operands = [hidden, *parts] + ([before] if before is not None else [])
        new, out, sums = norm_rows_kernel(
            partial(norm_back_body, which),
            [half_sds, half_low, sds((8, width), F32)],
            operands,
            norm_rows,
            last,
        )
        last[:] = [out]
        return new, (out, swap_core(out)), sums

    def reduce_rows(keep, send):
        got = swap_core(send)
        return across((keep + got.astype(F32)).astype(LOW))

    text_rows = text_states.reshape(clips * text_len, text_width)
    text_weight = attn_all[:, 8 * share : 8 * share + text_share, :].reshape(text_width, columns)
    text_bias = lax.dynamic_slice_in_dim(norm_rows[8], place * columns, columns, 0)
    text_local = (nn(text_rows, text_weight) + text_bias).astype(LOW)
    text_parts = spread_tensor(text_local)
    text_bias_row = jnp.where(text_mask > 0, 0.0, NEG).astype(F32)
    bias_columns = jnp.transpose(text_bias_row)

    full = sds((frames, columns), LOW)
    lse_sds = sds((8, frames), F32)
    tot = [pltpu.VMEM((frames, 128), F32)]
    heads = columns // HEAD_DIM
    score_flops = 2 * heads * frames * HEAD_DIM
    units = feedforward.shape[2]
    inner = sds((frames, units), LOW)
    every = range(clips)

    def embed_step(c):
        mine = strips[c * strip : (c + 1) * strip]
        parts = [mine] + [swap(mine, "tensor", 2 * s) for s in range(1, sides)]
        operands = [side_arg, placed, norm_rows] + parts
        new, out = run(
            embed_norm_body,
            [half_sds, half_low],
            operands,
            [scalars()] + [whole(a) for a in operands[1:]],
            flops=10 * height * width,
            name="embed_norm",
        )
        return new, (out, swap_core(out))

    def self_step(pair):
        operands = [core_arg, *pair, attn_all, attn_all, attn_all, attn_all]
        *kept, keep, send = run(
            self_forward_body,
            [full, full, full, full, lse_sds, half_sds, half_low],
            operands,
            [scalars()] + [whole(a) for a in pair] + [w_attn(0), w_attn(1), w_attn(2), w_attn(6)],
            flops=8 * frames * width * columns + 4 * score_flops * frames,
            scratch=tot,
            name="self_forward",
        )
        return kept, reduce_rows(keep, send)

    def text_step():
        operands = [place_order] + text_parts + [attn_all, attn_all]
        return run(
            text_body,
            [
                sds((clips * text_len, width), LOW),
                sds((clips * text_len, columns), LOW),
                sds((clips * text_len, columns), LOW),
            ],
            operands,
            [scalars()] + [whole(a) for a in text_parts] + [w_attn(4), w_attn(5)],
            flops=4 * clips * text_len * width * columns,
            name="text",
        )

    def cross_step(c, pair):
        k = text_key[c * text_len : (c + 1) * text_len]
        v = text_value[c * text_len : (c + 1) * text_len]
        operands = [core_arg, *pair, text_bias_row[c : c + 1], k, v, attn_all, attn_all]
        q, o, lse, keep, send = run(
            cross_forward_body,
            [full, full, lse_sds, half_sds, half_low],
            operands,
            [scalars()] + [whole(a) for a in operands[1:6]] + [w_attn(3), w_attn(7)],
            flops=4 * frames * width * columns + 4 * score_flops * text_len,
            scratch=tot,
            name="cross_forward",
        )
        return (q, k, v, o, lse), reduce_rows(keep, send)

    def ffn_step(pair):
        *kept, keep, send = run(
            ffn_forward_body,
            [inner, inner, half_sds, half_low],
            [core_arg, *pair, ffn_all, ffn_all],
            [scalars()] + [whole(a) for a in pair] + [w_ffn(0), w_ffn(1)],
            flops=4 * frames * width * units,
            name="ffn_forward",
        )
        return kept, reduce_rows(keep, send)

    hidden = [[None] * clips for _ in range(4)]
    pairs = [[None] * clips for _ in range(4)]
    kept = [[None] * clips for _ in range(3)]
    moving = [None] * clips
    for c in every:
        hidden[0][c], pairs[0][c] = embed_step(c)
        kept[0][c], moving[c] = self_step(pairs[0][c])
    text_hidden, text_key, text_value = text_step()
    for c in every:
        hidden[1][c], pairs[1][c] = norm_step(1, hidden[0][c], moving[c])
        kept[1][c], moving[c] = cross_step(c, pairs[1][c])
    for c in every:
        hidden[2][c], pairs[2][c] = norm_step(2, hidden[1][c], moving[c])
        kept[2][c], moving[c] = ffn_step(pairs[2][c])

    targets = (jnp.roll(audio_codes, -1, axis=1) - place * vocab).astype(jnp.int32)
    loss_weight = weight_int.astype(F32)
    grad_weight = loss_weight / valid_count
    loss_part = [None] * clips
    sums = [[], [], [], []]

    def head_step(c, pair):
        operands = [core_arg, *pair, targets[c], head_all]
        logits, stats = run(
            head_forward_body,
            [sds((frames, books * vocab), F32), sds((2 * books, frames), F32)],
            operands,
            [scalars()] + [whole(a) for a in operands[1:]],
            flops=2 * frames * width * books * vocab,
            scratch=tot,
            name="head_forward",
        )
        total, pick = stats[:books], stats[books:]
        mask = 1
        while mask < tensor:
            far = swap(jnp.concatenate([total, pick], axis=0), "tensor", mask)
            high = jnp.maximum(total, far[:books])
            total = high + jnp.log(jnp.exp(total - high) + jnp.exp(far[:books] - high))
            pick = pick + far[books:]
            mask *= 2
        loss_part[c] = jnp.sum((total - pick) * jnp.transpose(loss_weight[c]))
        return logits, jnp.concatenate([total, total], axis=0)

    def head_back_step(c, logits, total):
        operands = [core_arg, logits, total, grad_weight[c], targets[c], head_all]
        grad, keep, send = run(
            head_backward_body,
            [sds((frames, books * vocab), LOW), half_sds, half_low],
            operands,
            [scalars()] + [whole(a) for a in operands[1:]],
            flops=2 * frames * width * books * vocab,
            scratch=tot,
            name="head_backward",
        )
        return grad, reduce_rows(keep, send)

    def weights(lefts, rights, group_columns, name):
        result = weight_grad(core_arg, lefts, rights, dp, group_columns, name, last[0])
        last[:] = [result]
        return result

    logit_grads = [None] * clips
    ready = [None] * clips
    for c in every:
        hidden[3][c], pairs[3][c] = norm_step(3, hidden[2][c], moving[c])
        ready[c] = head_step(c, pairs[3][c])
        if c:
            logit_grads[c - 1], moving[c - 1] = head_back_step(c - 1, *ready[c - 1])
    logit_grads[-1], moving[-1] = head_back_step(clips - 1, *ready[-1])
    head_grads = weights(pairs[3], logit_grads, vocab, "head_weights")
    head_sum = lax.psum_scatter(head_grads, "dp", scatter_dimension=0, tiled=False)

    def ffn_back_step(c, pair):
        slope = kept[2][c][1]
        grad, keep, send = run(
            ffn_backward_body,
            [inner, half_sds, half_low],
            [core_arg, *pair, slope, ffn_all, ffn_all],
            [scalars()] + [whole(a) for a in pair] + [whole(slope), w_ffn(0), w_ffn(1)],
            flops=4 * frames * width * units,
            name="ffn_backward",
        )
        return grad, reduce_rows(keep, send)

    grads = [None] * clips
    back_pairs = [[None] * clips for _ in range(4)]
    inner_grads = [None] * clips
    for c in every:
        grads[c], back_pairs[3][c], s = norm_back(3, hidden[3][c], moving[c], None)
        sums[3].append(s)
        inner_grads[c], moving[c] = ffn_back_step(c, back_pairs[3][c])
    ffn_two = weights(back_pairs[3], [k[0] for k in kept[2]], units, "ffn_two_weights")
    ffn_one = weights(pairs[2], inner_grads, units, "ffn_one_weights")
    ffn_sum = lax.psum_scatter(
        jnp.concatenate([ffn_one, ffn_two], axis=1), "dp", scatter_dimension=0, tiled=False
    )

    acc_text = [pltpu.VMEM((text_len, columns), F32)] * 2
    small = sds((text_len, columns), LOW)

    def cross_back_step(c, pair):
        q, k, v, o, lse = kept[1][c]
        bias = bias_columns[:, c : c + 1]
        operands = [core_arg, *pair, bias, q, k, v, lse, attn_all, attn_all]
        dq, dk, dv, keep, send = run(
            cross_backward_body,
            [full, small, small, half_sds, half_low],
            operands,
            [scalars()] + [whole(a) for a in operands[1:8]] + [w_attn(3), w_attn(7)],
            flops=4 * frames * width * columns + 10 * score_flops * text_len,
            scratch=[pltpu.VMEM((frames, columns), LOW)] + acc_text,
            name="cross_backward",
        )
        return (dq, dk, dv), reduce_rows(keep, send)

    cross_grads = [None] * clips
    for c in every:
        grads[c], back_pairs[2][c], s = norm_back(2, hidden[2][c], moving[c], grads[c])
        sums[2].append(s)
        cross_grads[c], moving[c] = cross_back_step(c, back_pairs[2][c])
    text_dk = jnp.concatenate([g[1] for g in cross_grads], axis=0)
    text_dv = jnp.concatenate([g[2] for g in cross_grads], axis=0)
    text_part, text_gk, text_gv = run(
        text_back_body,
        [
            sds((clips * text_len, width), LOW),
            sds((dp, 1, share, columns), LOW),
            sds((dp, 1, share, columns), LOW),
        ],
        [text_dk, text_dv, attn_all, attn_all, text_hidden],
        [whole(text_dk), whole(text_dv), w_attn(4), w_attn(5), whole(text_hidden)],
        flops=8 * clips * text_len * width * columns,
        name="text_back",
    )
    text_grad = collect_tensor(
        [
            lax.dynamic_slice_in_dim(text_part, place_order[m] * columns, columns, 1)
            for m in range(tensor)
        ]
    ).astype(LOW)
    text_proj_grad = tn(text_rows, text_grad).astype(LOW)
    bias_grad = jnp.sum(text_grad.astype(F32), axis=0)
    cross_out = weights(back_pairs[2], [k[3] for k in kept[1]], columns, "cross_out_weights")
    cross_query = weights(pairs[1], [g[0] for g in cross_grads], columns, "cross_query_weights")

    acc_self = [pltpu.VMEM((frames, columns), F32)] * 2

    def self_back_step(c, pair):
        q, k, v, o, lse = kept[0][c]
        operands = [core_arg, *pair, q, k, v, lse, attn_all, attn_all, attn_all, attn_all]
        grad, keep, send = run(
            self_backward_body,
            [sds((frames, 3 * columns), LOW), half_sds, half_low],
            operands,
            [scalars()]
            + [whole(a) for a in operands[1:7]]
            + [w_attn(0), w_attn(1), w_attn(2), w_attn(6)],
            flops=8 * frames * width * columns + 10 * score_flops * frames,
            scratch=[pltpu.VMEM((frames, columns), LOW)] * 2 + acc_self,
            name="self_backward",
        )
        return grad, reduce_rows(keep, send)

    self_grads = [None] * clips
    for c in every:
        grads[c], back_pairs[1][c], s = norm_back(1, hidden[1][c], moving[c], grads[c])
        sums[1].append(s)
        self_grads[c], moving[c] = self_back_step(c, back_pairs[1][c])
    self_out = weights(back_pairs[1], [k[3] for k in kept[0]], columns, "self_out_weights")
    self_in = weights(pairs[0], self_grads, columns, "self_in_weights")
    attn_grads = jnp.concatenate(
        [
            a.reshape(dp, -1, columns)
            for a in (
                self_in,
                cross_query,
                text_gk,
                text_gv,
                self_out,
                cross_out,
                text_proj_grad.reshape(dp, text_share, columns),
            )
        ],
        axis=1,
    )
    attn_sum = lax.psum_scatter(attn_grads, "dp", scatter_dimension=0, tiled=False)

    zero_lows = [None] * clips
    for c in every:
        _, (zero_lows[c], _), s = norm_back(0, hidden[0][c], moving[c], grads[c])
        sums[0].append(s)
    if aligned:
        pieces = run(
            split_features_body,
            [sds((clips * strip, share), LOW)] * dp,
            [group_order, jnp.broadcast_to(side_arg, (clips + 1,))] + zero_lows,
            [scalars(), scalars()] + [whole(a) for a in zero_lows],
            name="split_features",
        )
    else:
        rows = jnp.concatenate(
            [lax.dynamic_slice_in_dim(a, side * strip, strip, 0) for a in zero_lows], axis=0
        )
        rows = jnp.transpose(rows.reshape(clips * strip, dp, share), (1, 0, 2))
        pieces = list(jnp.take(rows, group_order, axis=0))
    rows_all = [pieces[0]] + [swap(pieces[m], "dp", m) for m in range(1, dp)]
    embed_parts = embed_back(vocab_base, back_lines, rows_all, vocab)
    grad_embed = collect_tensor([embed_parts[m] for m in range(tensor)])

    norm_part = jnp.concatenate(
        [sum(s)[0:1] for s in sums] + [sum(s)[1:2] for s in sums], axis=0
    ) * (1.0 / sides)
    bias_row = lax.dynamic_update_slice_in_dim(
        jnp.zeros((width,), F32), bias_grad, place * columns, 0
    )
    norm_total = total_over(
        jnp.concatenate([norm_part, bias_row[None]], axis=0), ("tensor", "dp")
    )
    grad_norm_rows = lax.dynamic_slice_in_dim(norm_total, group * share, share, 1)

    grad_attention = attn_sum[: 8 * share].reshape(attention.shape).astype(F32)
    grad_text_proj = jnp.transpose(attn_sum[8 * share :]).astype(F32)
    grad_feedforward = ffn_sum.astype(F32)
    grad_heads = head_sum.astype(F32)
    local_square = (
        jnp.sum(grad_attention * grad_attention)
        + jnp.sum(grad_feedforward * grad_feedforward)
        + jnp.sum(grad_heads * grad_heads)
        + jnp.sum(grad_embed * grad_embed)
        + jnp.sum(grad_text_proj * grad_text_proj)
        + jnp.sum(grad_norm_rows * grad_norm_rows) / tensor
    )
    both = total_over(
        jnp.stack([local_square, sum(loss_part) / tensor]).reshape(1, 2), ("tensor", "dp")
    )[0]
    grad_norm = jnp.sqrt(both[0])
    mean_loss = both[1] / valid_count
    factor = clip_limit / jnp.maximum(grad_norm, clip_limit)
    grad_tables = jnp.concatenate([grad_embed, grad_heads], 0)
    attn_new, attn_first_new, attn_second_new = adam_update(
        attention, grad_attention, attention_first, attention_second, rate_matrix, factor
    )
    ffn_new, ffn_first_new, ffn_second_new = adam_update(
        feedforward, grad_feedforward, feedforward_first, feedforward_second, rate_matrix, factor
    )
    table_new, table_first_new, table_second_new = adam_update(
        tables, grad_tables, tables_first, tables_second, rate_table, factor
    )
    text_new, text_first_new, text_second_new = adam_update(
        text_proj, grad_text_proj, text_first, text_second, rate_matrix, factor
    )
    norm_new, norm_first_new, norm_second_new = adam_update(
        norm_params, grad_norm_rows, norm_first, norm_second, rate_norm, factor
    )
    return (
        mean_loss,
        valid_count,
        grad_norm,
        attn_new,
        attn_new.astype(LOW),
        attn_first_new,
        attn_second_new,
        ffn_new,
        ffn_new.astype(LOW),
        ffn_first_new,
        ffn_second_new,
        table_new,
        table_new.astype(LOW),
        table_first_new,
        table_second_new,
        text_new,
        text_new.astype(LOW),
        text_first_new,
        text_second_new,
        norm_new,
        norm_first_new,
        norm_second_new,
    )


def solution(mesh):
    clip3 = P("dp", None, None)
    clip2 = P("dp", None)
    matrix = P(None, "dp", "tensor")
    text = P("tensor", "dp")
    norm = P(None, "dp")
    placed = (
        (clip3, clip3, clip2, clip3, clip2)
        + (matrix, matrix, matrix, text, norm)
        + (matrix,) * 6
        + (text, text, norm, norm)
    )
    return jax.shard_map(
        on_device,
        mesh=mesh,
        in_specs=placed,
        out_specs=(P(), P(), P()) + (matrix,) * 12 + (text,) * 4 + (norm,) * 3,
        check_vma=False,
    )
```

time: 2180 us -> 1030 us (0.47)
  waiting for transfers between devices: 1320 us -> 281 us
  Pallas kernels: 0 us -> 348 us
  matrix products: 333 us -> 1.73 us
  blocking collectives: 146 us -> 0 us
  starting transfers between devices: 2.49 us -> 96.5 us
  other arithmetic: 158 us -> 88.6 us
    all_gather x12 -> x3, waiting for transfers between devices: 539 us -> 0.02 us  [the longest x1 0.02 us: on_device(): attn_all = lax.all_gather(attn_flat, 'dp', axis=0)]
    reduce_scatter x10 -> x3, waiting for transfers between devices: 467 us -> 0.01 us  [the longest x1 0.01 us: on_device(): lax.psum_scatter(head_grads, 'dp', scatter_dimension=0, tiled=False)]
    pallas_call x0 -> x64, Pallas kernels: none -> 348 us  [the longest x31 152 us: kernel(): pl.pallas_call(later(body, len(after), len(operands)), out_shape=outs, gr...]
    dot_general x40 -> x2, matrix products: 333 us -> 1.73 us  [the longest x1 1.26 us: tn(): lax.dot_general(a, b, (((0,), (0,)), ((), ())), preferred_element_type=F32)]
    unnamed x29 -> x6, waiting for transfers between devices: 301 us -> 0.1 us
    ppermute x0 -> x111, waiting for transfers between devices: none -> 280 us  [swap(): return lax.ppermute(values, axis, [(i, i ^ mask) for i in range(size)])]
    ppermute x0 -> x111, starting transfers between devices: none -> 96.2 us  [swap(): return lax.ppermute(values, axis, [(i, i ^ mask) for i in range(size)])]
    all_gather x5 -> x0, blocking collectives: 73.4 us -> none  [the longest x1 31.4 us: on_device(): lax.all_gather(text_proj.astype(jnp.bfloat16), 'dp', axis=1, tiled=True)]
  transfers between devices with their start and end apart: 26 -> 117, of which waited for: 24 -> 49; matrix products, arithmetic and copies ran while one was open for 10% -> 11% of each run, Pallas kernels for 0% -> 31%
where the time goes in v1:
time: 1030 us; the launch traced here: 1020 us
  Pallas kernels  348 us (34%)
  waiting for transfers between devices  281 us (27%)
  local copies, waits for them, and re-layouts  171 us (17%)
  starting transfers between devices  96.5 us (9%)
  other arithmetic  88.6 us (9%)
  between operations  32 us (3%)
    ppermute x111, waiting for transfers between devices, swap(): return lax.ppermute(values, axis, [(i, i ^ mask) for i in range(size)])  280 us
    pallas_call x31, Pallas kernels, kernel(): pl.pallas_call(later(body, len(after), len(operands)), out_shape=outs, gr...  152 us
    unnamed x647, local copies, waits for them, and re-layouts  126 us
    ppermute x111, starting transfers between devices, swap(): return lax.ppermute(values, axis, [(i, i ^ mask) for i in range(size)])  96.2 us
    pallas_call x7, Pallas kernels, weight_grad(): pl.pallas_call(later(partial(weight_grad_body, clips), 1, 1 + 3 * clips),...  66.8 us
    pallas_call x21, Pallas kernels, norm_rows_kernel(): pl.pallas_call(later(body, len(after), len(operands)), out_shape=tuple(ou...  63.6 us
    pallas_call x4, Pallas kernels, embed(): pl.pallas_call(later(embed_body, len(after), 2 + len(tables)), out_shape=...  39.8 us
    convert_element_type x21, other arithmetic, reduce_rows(): return across((keep + got.astype(F32)).astype(LOW))  33.1 us
  transfers between devices with their start and end apart: 117, of which 49 were waited for; matrix products, arithmetic and copies ran while one was open for 11% of the time, Pallas kernels for 31%

profile of v1, /device:TPU:0, one launch (start us, length us, event | category | flops | bytes accessed | tf_op | source)
XLA Modules:
  0.0 1018.8 jit_solution(2762490731334545017)
XLA Ops:
  49.6 9.9 embed.4.refs_6_
  66.2 9.9 embed.5.refs_6_
  79.7 9.9 embed.6.refs_6_
  92.9 10.2 %embed.7.refs_9_ = bf16[2,576,128]{2,1,0:T(8,128)(2,1)} custom-call(s32[4]{0:T(128)} %broadcast_multiply_fusion.1.refs_0_.base_ref, s32[2,576,4]{2,1,0:T(8,128)} %get-tuple-element.395.refs_1_, bf16[4,128,512]{2,1,0:T(8,128)(2,1)} %copy-done.299, bf16[4,128,512]{2,1,0:T(8,128)(2,1)} %collective-permute-done.3.refs_3_, ...), custom_call_target="tpu_custom_call" | custom-call | flops 4831838208 | bytes 2834432 | tf_op jit(solution)/shard_map/embed/pallas_call | solution.py:538
  156.7 7.6 self_forward.4
  171.5 8.6 collective-permute-done.22.refs_3_
  182.7 7.5 self_forward.5
  215.0 9.0 collective-permute-done.30.refs_2_
  237.8 12.2 %collective-permute-done.28.refs_2_ = bf16[384,1024]{1,0:T(8,128)(2,1)} collective-permute-done((bf16[384,1024]{1,0:T(8,128)(2,1)}, bf16[384,1024]{1,0:T(8,128)(2,1)}, u32[]{:S(2)}, u32[]{:S(2)}) %collective-permute-start.28) | collective-permute-done | bytes 786464 | tf_op jit(solution)/shard_map/ppermute | solution.py:661
  263.4 12.4 %collective-permute-done.26.refs_2_ = bf16[384,1024]{1,0:T(8,128)(2,1)} collective-permute-done((bf16[384,1024]{1,0:T(8,128)(2,1)}, bf16[384,1024]{1,0:T(8,128)(2,1)}, u32[]{:S(2)}, u32[]{:S(2)}) %collective-permute-start.26) | collective-permute-done | bytes 786464 | tf_op jit(solution)/shard_map/ppermute | solution.py:661
  292.1 9.6 collective-permute-done.39.refs_2_
  394.1 8.5 collective-permute-done.44
  415.9 7.5 head_backward.3
  452.0 9.9 collective-permute-done.56
  479.8 7.7 head_backward.5
  491.2 16.0 %head_weights.1.refs_4_ = bf16[8,4,128,512]{3,2,1,0:T(8,128)(2,1)} custom-call(s32[1]{0:T(128)} %bitcast.refs_0_, bf16[384,1024]{1,0:T(8,128)(2,1)} %get-tuple-element.224.refs_1_.refs_5_, bf16[384,1024]{1,0:T(8,128)(2,1)} %collective-permute-done.42.refs_2_, bf16[384,1024]{1,0:T(8,128)(2,1)} %get-tuple-element.229.refs_1_.refs_5_.refs_3_, ...), custom_call_target="tpu_custom_call" | custom-call | flops 9663676416 | bytes 18350080 | tf_op jit(solution)/shard_map/head_weights/pallas_call | solution.py:499
  511.3 18.4 %collective-permute-done.49.refs_2_ = bf16[384,1024]{1,0:T(8,128)(2,1)S(1)} collective-permute-done((bf16[384,1024]{1,0:T(8,128)(2,1)S(1)}, bf16[384,1024]{1,0:T(8,128)(2,1)S(1)}, u32[]{:S(2)}, u32[]{:S(2)}) %collective-permute-start.49) | collective-permute-done | bytes 786464 | tf_op jit(solution)/shard_map/ppermute | solution.py:661
  541.4 12.7 %collective-permute-done.61.refs_2_ = bf16[384,1024]{1,0:T(8,128)(2,1)S(1)} collective-permute-done((bf16[384,1024]{1,0:T(8,128)(2,1)S(1)}, bf16[384,1024]{1,0:T(8,128)(2,1)S(1)}, u32[]{:S(2)}, u32[]{:S(2)}) %collective-permute-start.61) | collective-permute-done | bytes 786464 | tf_op jit(solution)/shard_map/ppermute | solution.py:661
  561.8 14.5 %collective-permute-done.64.refs_2_ = bf16[384,1024]{1,0:T(8,128)(2,1)S(1)} collective-permute-done((bf16[384,1024]{1,0:T(8,128)(2,1)S(1)}, bf16[384,1024]{1,0:T(8,128)(2,1)S(1)}, u32[]{:S(2)}, u32[]{:S(2)}) %collective-permute-start.64) | collective-permute-done | bytes 786464 | tf_op jit(solution)/shard_map/ppermute | solution.py:661
  587.5 11.4 %ffn_two_weights.1.refs_10_ = bf16[8,1,128,1024]{3,2,1,0:T(8,128)(2,1)} custom-call(s32[1]{0:T(128)} %bitcast.refs_0_, bf16[384,1024]{1,0:T(8,128)(2,1)} %copy-done.68, bf16[384,1024]{1,0:T(8,128)(2,1)} %copy-done.166, bf16[384,1024]{1,0:T(8,128)(2,1)} %copy-done.69, bf16[384,1024]{1,0:T(8,128)(2,1)} %copy-done.167, bf16[384,1024]{1,0:T(8,128)(2,1)} %copy-done.70, ...), custom_call_target="tpu_custom_call" | custom-call | flops 4831838208 | bytes 11534336 | tf_op jit(solution)/shard_map/ffn_two_weights/pallas_call | solution.py:499
  599.0 11.5 %ffn_one_weights.1.refs_5_ = bf16[8,1,128,1024]{3,2,1,0:T(8,128)(2,1)} custom-call(s32[1]{0:T(128)} %bitcast.refs_0_, bf16[384,1024]{1,0:T(8,128)(2,1)} %get-tuple-element.212.refs_1_.refs_5_, bf16[384,1024]{1,0:T(8,128)(2,1)} %collective-permute-done.33.refs_2_, bf16[384,1024]{1,0:T(8,128)(2,1)} %get-tuple-element.219.refs_1_.refs_5_.refs_3_, ...), custom_call_target="tpu_custom_call" | custom-call | flops 4831838208 | bytes 11534336 | tf_op jit(solution)/shard_map/ffn_one_weights/pallas_call | solution.py:499
  649.2 12.2 %collective-permute-done.73.refs_2_ = bf16[384,1024]{1,0:T(8,128)(2,1)S(1)} collective-permute-done((bf16[384,1024]{1,0:T(8,128)(2,1)S(1)}, bf16[384,1024]{1,0:T(8,128)(2,1)S(1)}, u32[]{:S(2)}, u32[]{:S(2)}) %collective-permute-start.73) | collective-permute-done | bytes 786464 | tf_op jit(solution)/shard_map/ppermute | solution.py:661
  705.6 8.6 self_backward.3
  736.0 8.6 self_backward.4
  763.7 8.6 self_backward.5
  781.3 9.4 self_in_weights.1.refs_5_
  807.2 16.5 %collective-permute-done.86.refs_2_ = bf16[384,1024]{1,0:T(8,128)(2,1)S(1)} collective-permute-done((bf16[384,1024]{1,0:T(8,128)(2,1)S(1)}, bf16[384,1024]{1,0:T(8,128)(2,1)S(1)}, u32[]{:S(2)}, u32[]{:S(2)}) %collective-permute-start.86) | collective-permute-done | bytes 786464 | tf_op jit(solution)/shard_map/ppermute | solution.py:661
  826.5 14.1 %collective-permute-done.88.refs_2_ = bf16[384,1024]{1,0:T(8,128)(2,1)S(1)} collective-permute-done((bf16[384,1024]{1,0:T(8,128)(2,1)S(1)}, bf16[384,1024]{1,0:T(8,128)(2,1)S(1)}, u32[]{:S(2)}, u32[]{:S(2)}) %collective-permute-start.88) | collective-permute-done | bytes 786464 | tf_op jit(solution)/shard_map/ppermute | solution.py:661
  843.3 13.6 %collective-permute-done.90.refs_2_ = bf16[384,1024]{1,0:T(8,128)(2,1)S(1)} collective-permute-done((bf16[384,1024]{1,0:T(8,128)(2,1)S(1)}, bf16[384,1024]{1,0:T(8,128)(2,1)S(1)}, u32[]{:S(2)}, u32[]{:S(2)}) %collective-permute-start.90) | collective-permute-done | bytes 786464 | tf_op jit(solution)/shard_map/ppermute | solution.py:661
  879.2 18.4 %collective-permute-done.95.refs_5_ = bf16[576,128]{1,0:T(8,128)(2,1)S(1)} collective-permute-done((bf16[576,128]{1,0:T(8,128)(2,1)S(1)}, bf16[576,128]{1,0:T(8,128)(2,1)S(1)}, u32[]{:S(2)}, u32[]{:S(2)}) %collective-permute-start.95) | collective-permute-done | bytes 147488 | tf_op jit(solution)/shard_map/ppermute | solution.py:661
  898.6 26.6 %embed_back.1 = bf16[4,4,128,512]{3,2,1,0:T(8,128)(2,1)} custom-call(s32[4]{0:T(128)} %broadcast_multiply_fusion.1.refs_0_.base_ref, s32[4,8,4608]{2,1,0:T(8,128)} %broadcast_in_dim.39.codes_ref, bf16[576,128]{1,0:T(8,128)(2,1)} %copy-done.253, bf16[576,128]{1,0:T(8,128)(2,1)} %copy-done.312, bf16[576,128]{1,0:T(8,128)(2,1)} %copy-done.313, ...), custom_call_target="tpu_custom_call" | custom-call | flops 19327352832 | bytes 3276800 | tf_op jit(solution)/shard_map/embed_back/pallas_call | solution.py:581
  937.2 15.3 %collective-permute-start.104 = (f32[9,1024]{1,0:T(8,128)S(1)}, f32[9,1024]{1,0:T(8,128)S(1)}, u32[]{:S(2)}, u32[]{:S(2)}) collective-permute-start(f32[9,1024]{1,0:T(8,128)S(1)} %add.402), channel_id=1, source_target_pairs={{0,8},{4,12},{8,0},{12,4},{16,24},{20,28},{24,16},{28,20},{1,9},{5... | collective-permute-start | bytes 110600 | tf_op jit(solution)/shard_map/ppermute | solution.py:661
  (1075 shorter events, 610.2 us)
Async XLA Ops:
  7.2 119.8 %all-gather.7.cloned.1.call-start = ((), (), s32[]{:S(2)}) async-start(), calls=%async_computation.6 | async-start | bytes 5234688 | tf_op jit(solution)/shard_map/all_gather | solution.py:762
  11.2 272.0 %all-gather.9.cloned.1.call-start = ((), (), s32[]{:S(2)}) async-start(), calls=%async_computation.7 | async-start | bytes 4718592 | tf_op jit(solution)/shard_map/all_gather | solution.py:763
  19.2 26.3 %collective-permute-start.4 = (bf16[4,128,512]{2,1,0:T(8,128)(2,1)S(1)}, bf16[4,128,512]{2,1,0:T(8,128)(2,1)}, u32[]{:S(2)}, u32[]{:S(2)}) collective-permute-start(bf16[4,128,512]{2,1,0:T(8,128)(2,1)S(1)} %get-tuple-element.410.refs_2_), channel_id=1, source_target_pairs={{0,2},{1,3},{2,0},{3,1},{4,6},{5,7},{6,4},{7,5},{8,10},{9,11},{10,... | collective-permute-start | bytes 1572872 | tf_op jit(solution)/shard_map/ppermute | solution.py:661
  20.7 28.0 %collective-permute-start.3 = (bf16[4,128,512]{2,1,0:T(8,128)(2,1)S(1)}, bf16[4,128,512]{2,1,0:T(8,128)(2,1)}, u32[]{:S(2)}, u32[]{:S(2)}) collective-permute-start(bf16[4,128,512]{2,1,0:T(8,128)(2,1)S(1)} %get-tuple-element.410.refs_2_), channel_id=1, source_target_pairs={{0,1},{1,0},{2,3},{3,2},{4,5},{5,4},{6,7},{7,6},{8,9},{9,8},{10,11... | collective-permute-start | bytes 1572872 | tf_op jit(solution)/shard_map/ppermute | solution.py:661
  21.6 345.3 %all-gather.11.cloned.1.call-start = ((), (), s32[]{:S(2)}) async-start(), calls=%async_computation.8 | async-start | bytes 4718592 | tf_op jit(solution)/shard_map/all_gather | solution.py:764
  60.4 43.7 %collective-permute-start.12 = (bf16[576,128]{1,0:T(8,128)(2,1)S(1)}, bf16[576,128]{1,0:T(8,128)(2,1)S(1)}, u32[]{:S(2)}, u32[]{:S(2)}) collective-permute-start(bf16[576,128]{1,0:T(8,128)(2,1)S(1)} %get-tuple-element.423), channel_id=1, source_target_pairs={{0,28},{4,24},{8,20},{12,16},{16,12},{20,8},{24,4},{28,0},{1,29},{... | collective-permute-start | bytes 442376 | tf_op jit(solution)/shard_map/ppermute | solution.py:661
  65.8 39.4 %collective-permute-start.11 = (bf16[576,128]{1,0:T(8,128)(2,1)S(1)}, bf16[576,128]{1,0:T(8,128)(2,1)S(1)}, u32[]{:S(2)}, u32[]{:S(2)}) collective-permute-start(bf16[576,128]{1,0:T(8,128)(2,1)S(1)} %get-tuple-element.424), channel_id=1, source_target_pairs={{0,24},{4,28},{8,16},{12,20},{16,8},{20,12},{24,0},{28,4},{1,25},{... | collective-permute-start | bytes 442376 | tf_op jit(solution)/shard_map/ppermute | solution.py:661
  77.1 33.3 %collective-permute-start.10 = (bf16[576,128]{1,0:T(8,128)(2,1)S(1)}, bf16[576,128]{1,0:T(8,128)(2,1)S(1)}, u32[]{:S(2)}, u32[]{:S(2)}) collective-permute-start(bf16[576,128]{1,0:T(8,128)(2,1)S(1)} %get-tuple-element.425), channel_id=1, source_target_pairs={{0,20},{4,16},{8,28},{12,24},{16,4},{20,0},{24,12},{28,8},{1,21},{... | collective-permute-start | bytes 442376 | tf_op jit(solution)/shard_map/ppermute | solution.py:661
  77.2 39.6 %collective-permute-start.9 = (bf16[576,128]{1,0:T(8,128)(2,1)S(1)}, bf16[576,128]{1,0:T(8,128)(2,1)S(1)}, u32[]{:S(2)}, u32[]{:S(2)}) collective-permute-start(bf16[576,128]{1,0:T(8,128)(2,1)S(1)} %get-tuple-element.426), channel_id=1, source_target_pairs={{0,16},{4,20},{8,24},{12,28},{16,0},{20,4},{24,8},{28,12},{1,17},{... | collective-permute-start | bytes 442376 | tf_op jit(solution)/shard_map/ppermute | solution.py:661
  90.6 26.2 %collective-permute-start.8 = (bf16[576,128]{1,0:T(8,128)(2,1)S(1)}, bf16[576,128]{1,0:T(8,128)(2,1)S(1)}, u32[]{:S(2)}, u32[]{:S(2)}) collective-permute-start(bf16[576,128]{1,0:T(8,128)(2,1)S(1)} %get-tuple-element.427), channel_id=1, source_target_pairs={{0,12},{4,8},{8,4},{12,0},{16,28},{20,24},{24,20},{28,16},{1,13},{... | collective-permute-start | bytes 442376 | tf_op jit(solution)/shard_map/ppermute | solution.py:661
  169.4 27.8 %collective-permute-start.20 = (bf16[384,1024]{1,0:T(8,128)(2,1)S(1)}, bf16[384,1024]{1,0:T(8,128)(2,1)}, u32[]{:S(2)}, u32[]{:S(2)}) collective-permute-start(bf16[384,1024]{1,0:T(8,128)(2,1)S(1)} %add_convert_fusion.20.refs_1_), channel_id=1, source_target_pairs={{0,2},{1,3},{2,0},{3,1},{4,6},{5,7},{6,4},{7,5},{8,10},{9,11},{10,... | collective-permute-start | bytes 2359304 | tf_op jit(solution)/shard_map/ppermute | solution.py:661
  170.8 30.3 %collective-permute-start.29 = (bf16[384,1024]{1,0:T(8,128)(2,1)}, bf16[384,1024]{1,0:T(8,128)(2,1)}, u32[]{:S(2)}, u32[]{:S(2)}) collective-permute-start(bf16[384,1024]{1,0:T(8,128)(2,1)} %get-tuple-element.192.refs_5_), channel_id=1, source_target_pairs={{0,1},{1,0},{2,3},{3,2},{4,5},{5,4},{6,7},{7,6},{8,9},{9,8},{10,11... | collective-permute-start | bytes 2359304 | tf_op jit(solution)/shard_map/ppermute | solution.py:661
  170.8 781.7 %reduce-scatter.8.cloned.1.call-start = ((), (), s32[]{:S(2)}) async-start(), calls=%async_computation.5 | async-start | bytes 4718592 | tf_op jit(solution)/shard_map/reduce_scatter | solution.py:1003
  194.1 33.0 %collective-permute-start.27 = (bf16[384,1024]{1,0:T(8,128)(2,1)}, bf16[384,1024]{1,0:T(8,128)(2,1)}, u32[]{:S(2)}, u32[]{:S(2)}) collective-permute-start(bf16[384,1024]{1,0:T(8,128)(2,1)} %get-tuple-element.196.refs_7_), channel_id=1, source_target_pairs={{0,1},{1,0},{2,3},{3,2},{4,5},{5,4},{6,7},{7,6},{8,9},{9,8},{10,11... | collective-permute-start | bytes 2359304 | tf_op jit(solution)/shard_map/ppermute | solution.py:661
  283.1 24.0 %collective-permute-start.36 = (bf16[384,1024]{1,0:T(8,128)(2,1)}, bf16[384,1024]{1,0:T(8,128)(2,1)}, u32[]{:S(2)}, u32[]{:S(2)}) collective-permute-start(bf16[384,1024]{1,0:T(8,128)(2,1)} %get-tuple-element.210.refs_4_), channel_id=1, source_target_pairs={{0,1},{1,0},{2,3},{3,2},{4,5},{5,4},{6,7},{7,6},{8,9},{9,8},{10,11... | collective-permute-start | bytes 2359304 | tf_op jit(solution)/shard_map/ppermute | solution.py:661
  366.9 24.6 %collective-permute-start.50 = (bf16[384,1024]{1,0:T(8,128)(2,1)}, bf16[384,1024]{1,0:T(8,128)(2,1)}, u32[]{:S(2)}, u32[]{:S(2)}) collective-permute-start(bf16[384,1024]{1,0:T(8,128)(2,1)} %get-tuple-element.222.refs_4_), channel_id=1, source_target_pairs={{0,1},{1,0},{2,3},{3,2},{4,5},{5,4},{6,7},{7,6},{8,9},{9,8},{10,11... | collective-permute-start | bytes 2359304 | tf_op jit(solution)/shard_map/ppermute | solution.py:661
  392.9 32.1 %collective-permute-start.51 = (bf16[384,1024]{1,0:T(8,128)(2,1)S(1)}, bf16[384,1024]{1,0:T(8,128)(2,1)}, u32[]{:S(2)}, u32[]{:S(2)}) collective-permute-start(bf16[384,1024]{1,0:T(8,128)(2,1)S(1)} %add_convert_fusion.11.refs_1_), channel_id=1, source_target_pairs={{0,2},{1,3},{2,0},{3,1},{4,6},{5,7},{6,4},{7,5},{8,10},{9,11},{10,... | collective-permute-start | bytes 2359304 | tf_op jit(solution)/shard_map/ppermute | solution.py:661
  507.2 458.9 %reduce-scatter.6.cloned.1.call-start = ((), (), s32[]{:S(2)}) async-start(), calls=%async_computation.4 | async-start | bytes 4718592 | tf_op jit(solution)/shard_map/reduce_scatter | solution.py:1026
  580.1 30.4 %collective-permute-start.59 = (bf16[384,1024]{1,0:T(8,128)(2,1)S(1)}, bf16[384,1024]{1,0:T(8,128)(2,1)S(1)}, u32[]{:S(2)}, u32[]{:S(2)}) collective-permute-start(bf16[384,1024]{1,0:T(8,128)(2,1)S(1)} %add_convert_fusion.10.refs_1_), channel_id=1, source_target_pairs={{0,2},{1,3},{2,0},{3,1},{4,6},{5,7},{6,4},{7,5},{8,10},{9,11},{10,... | collective-permute-start | bytes 2359304 | tf_op jit(solution)/shard_map/ppermute | solution.py:661
  581.1 33.3 %collective-permute-start.69 = (bf16[384,1024]{1,0:T(8,128)(2,1)S(1)}, bf16[384,1024]{1,0:T(8,128)(2,1)}, u32[]{:S(2)}, u32[]{:S(2)}) collective-permute-start(bf16[384,1024]{1,0:T(8,128)(2,1)S(1)} %get-tuple-element.257.refs_4_), channel_id=1, source_target_pairs={{0,1},{1,0},{2,3},{3,2},{4,5},{5,4},{6,7},{7,6},{8,9},{9,8},{10,11... | collective-permute-start | bytes 2359304 | tf_op jit(solution)/shard_map/ppermute | solution.py:661
  620.9 347.2 %reduce-scatter.4.cloned.1.call-start = ((), (), s32[]{:S(2)}) async-start(), calls=%async_computation.3 | async-start | bytes 5160960 | tf_op jit(solution)/shard_map/reduce_scatter | solution.py:1118
  663.5 30.6 %collective-permute-start.76 = (bf16[384,1024]{1,0:T(8,128)(2,1)}, bf16[384,1024]{1,0:T(8,128)(2,1)}, u32[]{:S(2)}, u32[]{:S(2)}) collective-permute-start(bf16[384,1024]{1,0:T(8,128)(2,1)} %get-tuple-element.280.refs_5_), channel_id=1, source_target_pairs={{0,1},{1,0},{2,3},{3,2},{4,5},{5,4},{6,7},{7,6},{8,9},{9,8},{10,11... | collective-permute-start | bytes 2359304 | tf_op jit(solution)/shard_map/ppermute | solution.py:661
  664.6 26.1 %collective-permute-start.68 = (bf16[384,1024]{1,0:T(8,128)(2,1)S(1)}, bf16[384,1024]{1,0:T(8,128)(2,1)S(1)}, u32[]{:S(2)}, u32[]{:S(2)}) collective-permute-start(bf16[384,1024]{1,0:T(8,128)(2,1)S(1)} %add_convert_fusion.7.refs_1_), channel_id=1, source_target_pairs={{0,2},{1,3},{2,0},{3,1},{4,6},{5,7},{6,4},{7,5},{8,10},{9,11},{10,... | collective-permute-start | bytes 2359304 | tf_op jit(solution)/shard_map/ppermute | solution.py:661
  698.0 24.5 %collective-permute-start.79 = (bf16[384,1024]{1,0:T(8,128)(2,1)}, bf16[384,1024]{1,0:T(8,128)(2,1)}, u32[]{:S(2)}, u32[]{:S(2)}) collective-permute-start(bf16[384,1024]{1,0:T(8,128)(2,1)} %get-tuple-element.295.refs_5_), channel_id=1, source_target_pairs={{0,1},{1,0},{2,3},{3,2},{4,5},{5,4},{6,7},{7,6},{8,9},{9,8},{10,11... | collective-permute-start | bytes 2359304 | tf_op jit(solution)/shard_map/ppermute | solution.py:661
  727.4 24.6 %collective-permute-start.82 = (bf16[768,256]{1,0:T(8,128)(2,1)}, bf16[768,256]{1,0:T(8,128)(2,1)}, u32[]{:S(2)}, u32[]{:S(2)}) collective-permute-start(bf16[768,256]{1,0:T(8,128)(2,1)} %get-tuple-element.398), channel_id=1, source_target_pairs={{0,1},{1,0},{2,3},{3,2},{4,5},{5,4},{6,7},{7,6},{8,9},{9,8},{10,11... | collective-permute-start | bytes 1179656 | tf_op jit(solution)/shard_map/ppermute | solution.py:661
  729.5 24.0 %collective-permute-start.84 = (bf16[768,256]{1,0:T(8,128)(2,1)}, bf16[768,256]{1,0:T(8,128)(2,1)}, u32[]{:S(2)}, u32[]{:S(2)}) collective-permute-start(bf16[768,256]{1,0:T(8,128)(2,1)} %add_convert_fusion.22), channel_id=1, source_target_pairs={{0,2},{1,3},{2,0},{3,1},{4,6},{5,7},{6,4},{7,5},{8,10},{9,11},{10,... | collective-permute-start | bytes 1179656 | tf_op jit(solution)/shard_map/ppermute | solution.py:661
  804.5 36.1 %collective-permute-start.88 = (bf16[384,1024]{1,0:T(8,128)(2,1)S(1)}, bf16[384,1024]{1,0:T(8,128)(2,1)S(1)}, u32[]{:S(2)}, u32[]{:S(2)}) collective-permute-start(bf16[384,1024]{1,0:T(8,128)(2,1)S(1)} %add_convert_fusion.1.refs_1_), channel_id=1, source_target_pairs={{0,2},{1,3},{2,0},{3,1},{4,6},{5,7},{6,4},{7,5},{8,10},{9,11},{10,... | collective-permute-start | bytes 2359304 | tf_op jit(solution)/shard_map/ppermute | solution.py:661
  806.1 50.8 %collective-permute-start.90 = (bf16[384,1024]{1,0:T(8,128)(2,1)S(1)}, bf16[384,1024]{1,0:T(8,128)(2,1)S(1)}, u32[]{:S(2)}, u32[]{:S(2)}) collective-permute-start(bf16[384,1024]{1,0:T(8,128)(2,1)S(1)} %add_convert_fusion.refs_1_), channel_id=1, source_target_pairs={{0,2},{1,3},{2,0},{3,1},{4,6},{5,7},{6,4},{7,5},{8,10},{9,11},{10,... | collective-permute-start | bytes 2359304 | tf_op jit(solution)/shard_map/ppermute | solution.py:661
  866.8 30.7 %collective-permute-start.95 = (bf16[576,128]{1,0:T(8,128)(2,1)S(1)}, bf16[576,128]{1,0:T(8,128)(2,1)S(1)}, u32[]{:S(2)}, u32[]{:S(2)}) collective-permute-start(bf16[576,128]{1,0:T(8,128)(2,1)S(1)} %get-tuple-element.341), channel_id=1, source_target_pairs={{0,20},{4,16},{8,28},{12,24},{16,4},{20,0},{24,12},{28,8},{1,21},{... | collective-permute-start | bytes 442376 | tf_op jit(solution)/shard_map/ppermute | solution.py:661
  868.4 29.1 %collective-permute-start.96 = (bf16[576,128]{1,0:T(8,128)(2,1)S(1)}, bf16[576,128]{1,0:T(8,128)(2,1)S(1)}, u32[]{:S(2)}, u32[]{:S(2)}) collective-permute-start(bf16[576,128]{1,0:T(8,128)(2,1)S(1)} %get-tuple-element.342), channel_id=1, source_target_pairs={{0,24},{4,28},{8,16},{12,20},{16,8},{20,12},{24,0},{28,4},{1,25},{... | collective-permute-start | bytes 442376 | tf_op jit(solution)/shard_map/ppermute | solution.py:661
  933.0 29.9 %collective-permute-start.98 = (bf16[4,128,512]{2,1,0:T(8,128)(2,1)S(1)}, bf16[4,128,512]{2,1,0:T(8,128)(2,1)}, u32[]{:S(2)}, u32[]{:S(2)}) collective-permute-start(bf16[4,128,512]{2,1,0:T(8,128)(2,1)S(1)} %get-tuple-element.396), channel_id=1, source_target_pairs={{0,1},{1,0},{2,3},{3,2},{4,5},{5,4},{6,7},{7,6},{8,9},{9,8},{10,11... | collective-permute-start | bytes 1572872 | tf_op jit(solution)/shard_map/ppermute | solution.py:661
  934.2 28.7 %collective-permute-start.100 = (bf16[4,128,512]{2,1,0:T(8,128)(2,1)S(1)}, bf16[4,128,512]{2,1,0:T(8,128)(2,1)}, u32[]{:S(2)}, u32[]{:S(2)}) collective-permute-start(bf16[4,128,512]{2,1,0:T(8,128)(2,1)S(1)} %fusion.10), channel_id=1, source_target_pairs={{0,2},{1,3},{2,0},{3,1},{4,6},{5,7},{6,4},{7,5},{8,10},{9,11},{10,... | collective-permute-start | bytes 1572872 | tf_op jit(solution)/shard_map/ppermute | solution.py:661
  (405 other events, 3099.5 us)
Sparse Core Ops, SparseCore 0:
  11.3 106.7 all-gather.6
  120.7 72.4 all-gather.8
  195.9 71.6 all-gather.10
  507.3 87.8 reduce-scatter.7
  621.0 87.8 reduce-scatter.5
  798.6 113.3 reduce-scatter.3

commit v2 on v1

--- a/solution.py
+++ b/solution.py
@@ -44,17 +44,23 @@
     return pl.BlockSpec(memory_space=pltpu.SMEM)
 
 
+def anywhere():
+    return pl.BlockSpec(memory_space=pl.ANY)
+
+
+def in_hbm():
+    return pl.BlockSpec(memory_space=pltpu.HBM)
+
+
+def in_vmem():
+    return pl.BlockSpec(memory_space=pltpu.VMEM)
+
+
 def whole(a):
     rank = len(a.shape)
     return pl.BlockSpec(a.shape, lambda i: (0,) * rank)
 
 
-def member(a, axis, size, index):
-    block = a.shape[:axis] + (size,) + a.shape[axis + 1 :]
-    place = tuple(index if d == axis else 0 for d in range(len(a.shape)))
-    return pl.BlockSpec(block, lambda i: place)
-
-
 def later(body, count, at):
     def ordered(*refs):
         return body(*refs[:at], *refs[at + count :])
@@ -62,29 +68,171 @@
     return ordered
 
 
-def anywhere():
-    return pl.BlockSpec(memory_space=pl.ANY)
-
-
-def kernel(body, outs, operands, specs, flops=0, scratch=(), name=None, exps=0, after=(), limit=40):
-    outs = tuple(outs)
-    nbytes = sum(math.prod(o.shape) * jnp.dtype(o.dtype).itemsize for o in outs)
-    for a, s in zip(operands, specs):
-        shape = a.shape if s.block_shape is None else s.block_shape
-        nbytes += math.prod(shape) * jnp.dtype(a.dtype).itemsize
-    return pl.pallas_call(
-        later(body, len(after), len(operands)),
-        out_shape=outs,
-        grid=(1,),
-        in_specs=list(specs) + [anywhere()] * len(after),
-        out_specs=tuple(whole(o) for o in outs),
-        scratch_shapes=scratch,
+class Scalar:
+    def __init__(self, array):
+        self.array = array
+
+
+class Window:
+    def __init__(self, array, shape, pick):
+        self.array, self.shape, self.pick = array, tuple(shape), pick
+
+
+class Flow:
+    def __init__(self, shape):
+        self.shape = shape
+
+
+class Copy:
+    def __init__(self, i):
+        self.i = i
+
+
+class Shared:
+    def __init__(self, shape, kind):
+        self.full, self.array = sds(shape, kind), None
+
+
+class Into:
+    def __init__(self, shared, shape, pick):
+        self.shared, self.shape, self.pick = shared, tuple(shape), pick
+
+
+def everything(ref):
+    return ref
+
+
+def nbytes_of(shape, kind):
+    return math.prod(shape) * jnp.dtype(kind).itemsize
+
+
+def kernel(body, outs, operands, flops=0, scratch=(), name=None, exps=0, after=(), limit=32):
+    arrays, specs, windows = [], [], []
+    for a in operands:
+        if isinstance(a, Scalar):
+            arrays.append(a.array)
+            specs.append(scalars())
+            windows.append(None)
+        elif isinstance(a, Window):
+            arrays.append(a.array)
+            specs.append(in_hbm())
+            windows.append(a)
+        else:
+            arrays.append(a)
+            specs.append(in_vmem())
+            windows.append(None)
+    aliases, out_shapes, out_specs, out_parts, owners = {}, [], [], [], []
+    extra = []
+    for o in outs:
+        if isinstance(o, Into):
+            if o.shared not in owners:
+                if o.shared.array is not None:
+                    aliases[len(arrays) + len(extra)] = len(out_shapes)
+                    extra.append(o.shared.array)
+                out_shapes.append(o.shared.full)
+                out_specs.append(in_hbm())
+                owners.append(o.shared)
+            out_parts.append(("put", o.shape, o.shared.full.dtype, o.pick, owners.index(o.shared)))
+            continue
+        if isinstance(o, Flow):
+            out_parts.append(("flow", None, None, None, len(out_shapes)))
+            out_shapes.append(o.shape)
+            out_specs.append(in_vmem())
+        elif isinstance(o, Copy):
+            a = operands[o.i]
+            out_parts.append(("copy", o.i, None, None, len(out_shapes)))
+            out_shapes.append(sds(a.shape, a.dtype))
+            out_specs.append(in_hbm())
+        else:
+            out_parts.append(("put", o.shape, o.dtype, everything, len(out_shapes)))
+            out_shapes.append(o)
+            out_specs.append(in_hbm())
+        owners.append(None)
+    moved = [w for w in windows if w is not None]
+    made = [p for p in out_parts if p[0] == "put"]
+    count_in, count_extra, count_after = len(arrays), len(extra), len(after)
+    count_out, count_moved, count_arrays = len(outs), len(moved), len(out_shapes)
+
+    def run_body(*refs):
+        refs = list(refs)
+        ins = refs[:count_in]
+        at = count_in + count_extra + count_after
+        out_refs = refs[at : at + count_arrays]
+        at += count_arrays
+        in_buffers = refs[at : at + count_moved]
+        at += count_moved
+        made_buffers = refs[at : at + len(made)]
+        at += len(made)
+        in_sems, out_sems = refs[at], refs[at + 1]
+        rest = refs[at + 2 :]
+        views, copies, waited = [], {}, set()
+        n = 0
+        for i, (ref, w) in enumerate(zip(ins, windows)):
+            if w is None:
+                views.append(ref)
+            else:
+                copies[i] = pltpu.make_async_copy(w.pick(ref), in_buffers[n], in_sems.at[n])
+                copies[i].start()
+                views.append(in_buffers[n])
+                n += 1
+        sent, sources = {}, {}
+
+        def need(*which):
+            for i in which:
+                if i in copies and i not in waited:
+                    waited.add(i)
+                    copies[i].wait()
+
+        def put(*which):
+            for j in which:
+                if j in sources:
+                    source, target = sources[j]
+                    sent[j] = pltpu.make_async_copy(source, target, out_sems.at[j])
+                    sent[j].start()
+
+        body_outs = []
+        n = 0
+        for j, (kind, what, _, pick, owner) in enumerate(out_parts):
+            if kind == "put":
+                sources[j] = (made_buffers[n], pick(out_refs[owner]))
+                body_outs.append(made_buffers[n])
+                n += 1
+            elif kind == "copy":
+                sources[j] = (ins[what], out_refs[owner])
+                put(j)
+            else:
+                body_outs.append(out_refs[owner])
+        body(need, put, *views, *body_outs, *rest)
+        need(*copies)
+        put(*(j for j in sources if j not in sent))
+        for copy in sent.values():
+            copy.wait()
+
+    nbytes = sum(nbytes_of(w.shape, w.array.dtype) for w in moved)
+    nbytes += sum(nbytes_of(p[1], p[2]) for p in made)
+    results = pl.pallas_call(
+        run_body,
+        out_shape=tuple(out_shapes),
+        in_specs=specs + [anywhere()] * (count_extra + count_after),
+        out_specs=tuple(out_specs),
+        input_output_aliases=aliases,
+        scratch_shapes=[pltpu.VMEM(w.shape, w.array.dtype) for w in moved]
+        + [pltpu.VMEM(p[1], p[2]) for p in made]
+        + [
+            pltpu.SemaphoreType.DMA((max(1, count_moved),)),
+            pltpu.SemaphoreType.DMA((max(1, count_out),)),
+        ]
+        + list(scratch),
         compiler_params=pltpu.CompilerParams(vmem_limit_bytes=limit << 20),
         cost_estimate=pl.CostEstimate(
             flops=int(flops), bytes_accessed=int(nbytes), transcendentals=int(exps)
         ),
         name=name,
-    )(*operands, *after)
+    )(*arrays, *extra, *after)
+    for owner, result in zip(owners, results):
+        if owner is not None:
+            owner.array = result
+    return [r for owner, r in zip(owners, results) if owner is None] or [results[-1]]
 
 
 def flat(ref):
@@ -134,16 +282,20 @@
 
 
 def self_forward_body(
-    core_ref, own_ref, got_ref, wq_ref, wk_ref, wv_ref, wo_ref,
+    need, put, core_ref, own_ref, wq_ref, got_ref, wk_ref, wv_ref, wo_ref,
     q_ref, k_ref, v_ref, o_ref, lse_ref, keep_ref, send_ref, tot_ref,
 ):
     height = own_ref.shape[0]
     frames, width = q_ref.shape
     mine, other = half_rows(core_ref[0], height)
-    for w_ref, to_ref in ((wq_ref, q_ref), (wk_ref, k_ref), (wv_ref, v_ref)):
+    need(1)
+    for i, w_ref, to_ref in ((2, wq_ref, q_ref), (4, wk_ref, k_ref), (5, wv_ref, v_ref)):
+        need(i)
         w = flat(w_ref)
         to_ref[mine, :] = nn(own_ref[...], w).astype(LOW)
+        need(3)
         to_ref[other, :] = nn(got_ref[...], w).astype(LOW)
+    put(0, 1, 2)
     scale = jnp.asarray(HEAD_DIM**-0.5, LOW)
     head_masks = masks_of(width)
     diagonal = triangle(BLOCK)
@@ -159,24 +311,32 @@
         )
         o_ref[rows, :] = mixed.astype(LOW)
         tot_ref[rows, :] = totals
-    lse_ref[...] = jnp.transpose(tot_ref[...])[:8, :]
+    put(3)
+    need(6)
     wo = flat(wo_ref)
     send_ref[...] = nt(o_ref[other, :], wo).astype(LOW)
-    keep_ref[...] = nt(o_ref[mine, :], wo)
+    put(6)
+    keep_ref[...] = nt(o_ref[mine, :], wo).astype(LOW)
+    put(5)
+    lse_ref[...] = jnp.transpose(tot_ref[...])[:8, :]
 
 
 def cross_forward_body(
-    core_ref, own_ref, got_ref, bias_ref, k_ref, v_ref, wq_ref, wo_ref,
+    need, put, core_ref, own_ref, wq_ref, got_ref, bias_ref, k_ref, v_ref, wo_ref,
     q_ref, o_ref, lse_ref, keep_ref, send_ref, tot_ref,
 ):
     height = own_ref.shape[0]
     frames, width = q_ref.shape
     mine, other = half_rows(core_ref[0], height)
+    need(1, 2)
     w = flat(wq_ref)
     q_ref[mine, :] = nn(own_ref[...], w).astype(LOW)
+    need(3)
     q_ref[other, :] = nn(got_ref[...], w).astype(LOW)
+    put(0)
     scale = jnp.asarray(HEAD_DIM**-0.5, LOW)
     head_masks = masks_of(width)
+    need(4, 5, 6)
     for i in range(frames // BLOCK):
         rows = slice(i * BLOCK, (i + 1) * BLOCK)
         mixed, totals = attend_block(
@@ -184,98 +344,120 @@
         )
         o_ref[rows, :] = mixed.astype(LOW)
         tot_ref[rows, :] = totals
-    lse_ref[...] = jnp.transpose(tot_ref[...])[:8, :]
+    put(1)
+    need(7)
     wo = flat(wo_ref)
     send_ref[...] = nt(o_ref[other, :], wo).astype(LOW)
-    keep_ref[...] = nt(o_ref[mine, :], wo)
-
-
-def erf(x):
-    return lax.erf(x)
+    put(4)
+    keep_ref[...] = nt(o_ref[mine, :], wo).astype(LOW)
+    put(3)
+    lse_ref[...] = jnp.transpose(tot_ref[...])[:8, :]
 
 
 def ffn_forward_body(
-    core_ref, own_ref, got_ref, w1_ref, w2_ref, act_ref, slope_ref, keep_ref, send_ref
+    need, put, core_ref, own_ref, got_ref, w1_ref, w2_ref,
+    act_ref, slope_ref, keep_ref, send_ref,
 ):
     height = own_ref.shape[0]
     mine, other = half_rows(core_ref[0], height)
+    need(1, 2, 3)
     w1 = flat(w1_ref)
-    w2 = flat(w2_ref)
-    for source, rows, to_ref in ((got_ref, other, send_ref), (own_ref, mine, keep_ref)):
+    for j, source, rows, to_ref in (
+        (3, got_ref, other, send_ref),
+        (2, own_ref, mine, keep_ref),
+    ):
         u = nn(source[...], w1)
-        phi = 0.5 * (1.0 + erf(u * (2.0**-0.5)))
+        phi = 0.5 * (1.0 + lax.erf(u * (2.0**-0.5)))
         act = (u * phi).astype(LOW)
         density = jnp.exp(-0.5 * u * u) * ((2.0 * math.pi) ** -0.5)
         act_ref[rows, :] = act
         slope_ref[rows, :] = (phi + u * density).astype(LOW)
-        to_ref[...] = nt(act, w2).astype(to_ref.dtype)
+        need(4)
+        to_ref[...] = nt(act, flat(w2_ref)).astype(to_ref.dtype)
+        put(j)
 
 
 def head_forward_body(
-    core_ref, own_ref, got_ref, target_ref, w_ref, logits_ref, stats_ref, tot_ref
+    need, put, core_ref, own_ref, target_ref, got_ref, *refs
 ):
+    *w_refs, logits_ref, stats_ref, tot_ref = refs
     height = own_ref.shape[0]
-    books, vocab = w_ref.shape[1], w_ref.shape[3]
+    books = len(w_refs)
+    vocab = w_refs[0].shape[2]
     halves = half_rows(core_ref[0], height)
     lane = lax.broadcasted_iota(jnp.int32, (height, 128), 1)
     code = lax.broadcasted_iota(jnp.int32, (height, vocab), 1)
-    for source, rows in zip((own_ref, got_ref), halves):
-        target = target_ref[rows, :]
-        y = source[...]
-        totals = jnp.zeros((height, 128), F32)
-        for k in range(books):
-            w = w_ref[:, k].reshape(-1, vocab)
-            s = nn(y, w)
+    need(1, 2)
+    totals = [jnp.zeros((height, 128), F32)] * 2
+    for k, w_ref in enumerate(w_refs):
+        need(4 + k)
+        w = flat(w_ref)
+        for j, (source, rows) in enumerate(zip((own_ref, got_ref), halves)):
+            need(1 + 2 * j)
+            s = nn(source[...], w)
             logits_ref[rows, k * vocab : (k + 1) * vocab] = s
             top = jnp.max(s, axis=1, keepdims=True)
             total = jnp.sum(jnp.exp(s - top), axis=1, keepdims=True)
-            pick = jnp.sum(jnp.where(code == target[:, k : k + 1], s, 0.0), axis=1, keepdims=True)
-            totals = jnp.where(lane == k, top + jnp.log(total), totals)
-            totals = jnp.where(lane == books + k, pick, totals)
-        tot_ref[rows, :] = totals
+            hit = code == target_ref[rows, k : k + 1]
+            pick = jnp.sum(jnp.where(hit, s, 0.0), axis=1, keepdims=True)
+            totals[j] = jnp.where(lane == k, top + jnp.log(total), totals[j])
+            totals[j] = jnp.where(lane == books + k, pick, totals[j])
+    put(0)
+    for rows, t in zip(halves, totals):
+        tot_ref[rows, :] = t
     stats_ref[...] = jnp.transpose(tot_ref[...])[: 2 * books, :]
 
 
 def head_backward_body(
-    core_ref, logits_ref, total_ref, weight_ref, target_ref, w_ref,
-    grad_ref, keep_ref, send_ref, col_ref,
+    need, put, core_ref, total_ref, weight_ref, target_ref, logits_ref, *refs
 ):
+    *w_refs, grad_ref, keep_ref, send_ref, col_ref = refs
     height = keep_ref.shape[0]
-    books, vocab = w_ref.shape[1], w_ref.shape[3]
+    books = len(w_refs)
+    vocab = w_refs[0].shape[2]
     mine, other = half_rows(core_ref[0], height)
     frames = logits_ref.shape[0]
+    need(1, 2, 3)
     wide = jnp.concatenate(
         [total_ref[...], jnp.zeros((128 - total_ref.shape[0], frames), F32)], axis=0
     )
     col_ref[...] = jnp.transpose(wide)
     code = lax.broadcasted_iota(jnp.int32, (height, vocab), 1)
-    for rows, to_ref in ((other, send_ref), (mine, keep_ref)):
-        target = target_ref[rows, :]
+    need(4)
+    for j, rows, to_ref in ((2, other, send_ref), (1, mine, keep_ref)):
         weight = weight_ref[rows, :]
         total = col_ref[rows, :]
         acc = None
-        for k in range(books):
+        for k, w_ref in enumerate(w_refs):
             s = logits_ref[rows, k * vocab : (k + 1) * vocab]
             p = jnp.exp(s - total[:, k : k + 1])
-            hit = jnp.where(code == target[:, k : k + 1], 1.0, 0.0)
+            hit = jnp.where(code == target_ref[rows, k : k + 1], 1.0, 0.0)
             g = ((p - hit) * weight[:, k : k + 1]).astype(LOW)
             grad_ref[rows, k * vocab : (k + 1) * vocab] = g
-            part = nt(g, w_ref[:, k].reshape(-1, vocab))
+            need(5 + k)
+            part = nt(g, flat(w_ref))
             acc = part if acc is None else acc + part
         to_ref[...] = acc.astype(to_ref.dtype)
+        put(j)
 
 
 def ffn_backward_body(
-    core_ref, own_ref, got_ref, slope_ref, w1_ref, w2_ref, grad_ref, keep_ref, send_ref
+    need, put, core_ref, own_ref, got_ref, w2_ref, slope_ref, w1_ref,
+    grad_ref, keep_ref, send_ref,
 ):
     height = own_ref.shape[0]
     mine, other = half_rows(core_ref[0], height)
-    w1 = flat(w1_ref)
+    need(1, 2, 3, 4)
     w2 = flat(w2_ref)
-    for source, rows, to_ref in ((got_ref, other, send_ref), (own_ref, mine, keep_ref)):
+    for j, source, rows, to_ref in (
+        (2, got_ref, other, send_ref),
+        (1, own_ref, mine, keep_ref),
+    ):
         g = (nn(source[...], w2) * slope_ref[rows, :].astype(F32)).astype(LOW)
         grad_ref[rows, :] = g
-        to_ref[...] = nt(g, w1).astype(to_ref.dtype)
+        need(5)
+        to_ref[...] = nt(g, flat(w1_ref)).astype(to_ref.dtype)
+        put(j)
 
 
 def attend_back(
@@ -302,20 +484,22 @@
         dq = dq + tn(ds, k * mask)
         dk = dk + nn(ds, qm)
         dv = dv + nn(p.astype(LOW), gm)
-    dq_ref[rows, :] = (dq * scale).astype(LOW)
+    dq_ref[rows, :width] = (dq * scale).astype(LOW)
     dk_ref[:count, :] = dk if first else dk_ref[:count, :] + dk
     dv_ref[:count, :] = dv if first else dv_ref[:count, :] + dv
 
 
 def self_backward_body(
-    core_ref, own_ref, got_ref, q_ref, k_ref, v_ref, lse_ref, wq_ref, wk_ref, wv_ref, wo_ref,
-    grad_ref, keep_ref, send_ref, g_ref, dq_ref, dk_acc, dv_acc,
+    need, put, core_ref, own_ref, wo_ref, got_ref, q_ref, k_ref, v_ref, lse_ref,
+    wq_ref, wk_ref, wv_ref, grad_ref, keep_ref, send_ref, g_ref, dk_acc, dv_acc,
 ):
     height = own_ref.shape[0]
     frames, width = q_ref.shape
     mine, other = half_rows(core_ref[0], height)
+    need(1, 2)
     wo = flat(wo_ref)
     g_ref[mine, :] = nn(own_ref[...], wo).astype(LOW)
+    need(3)
     g_ref[other, :] = nn(got_ref[...], wo).astype(LOW)
     scale = HEAD_DIM**-0.5
     head_masks = masks_of(width)
@@ -323,6 +507,7 @@
     col = lax.broadcasted_iota(jnp.int32, (BLOCK, BLOCK), 1)
     diagonal = col >= row
     blocks = frames // BLOCK
+    need(4, 5, 6, 7)
     for i in reversed(range(blocks)):
         rows = slice(i * BLOCK, (i + 1) * BLOCK)
         count = (i + 1) * BLOCK
@@ -336,35 +521,40 @@
             scale,
             diagonal,
             None,
-            dq_ref,
+            grad_ref,
             rows,
             dk_acc,
             dv_acc,
             i == blocks - 1,
         )
-    grad_ref[:, :width] = dq_ref[...]
     grad_ref[:, width : 2 * width] = dk_acc[...].astype(LOW)
     grad_ref[:, 2 * width :] = dv_acc[...].astype(LOW)
-    for rows, to_ref in ((other, send_ref), (mine, keep_ref)):
+    put(0)
+    need(8, 9, 10)
+    for j, rows, to_ref in ((2, other, send_ref), (1, mine, keep_ref)):
         part = None
         for n, w_ref in enumerate((wq_ref, wk_ref, wv_ref)):
             term = nt(grad_ref[rows, n * width : (n + 1) * width], flat(w_ref))
             part = term if part is None else part + term
         to_ref[...] = part.astype(to_ref.dtype)
+        put(j)
 
 
 def cross_backward_body(
-    core_ref, own_ref, got_ref, bias_ref, q_ref, k_ref, v_ref, lse_ref, wq_ref, wo_ref,
+    need, put, core_ref, own_ref, wo_ref, got_ref, bias_ref, q_ref, k_ref, v_ref, lse_ref, wq_ref,
     dq_ref, dk_ref, dv_ref, keep_ref, send_ref, g_ref, dk_acc, dv_acc,
 ):
     height = own_ref.shape[0]
     frames, width = q_ref.shape
     mine, other = half_rows(core_ref[0], height)
+    need(1, 2)
     wo = flat(wo_ref)
     g_ref[mine, :] = nn(own_ref[...], wo).astype(LOW)
+    need(3)
     g_ref[other, :] = nn(got_ref[...], wo).astype(LOW)
     scale = HEAD_DIM**-0.5
     head_masks = masks_of(width)
+    need(4, 5, 6, 7, 8)
     for i in range(frames // BLOCK):
         rows = slice(i * BLOCK, (i + 1) * BLOCK)
         attend_back(
@@ -383,17 +573,24 @@
             dv_acc,
             i == 0,
         )
+    put(0)
+    need(9)
+    wq = flat(wq_ref)
+    for j, rows, to_ref in ((4, other, send_ref), (3, mine, keep_ref)):
+        to_ref[...] = nt(dq_ref[rows, :], wq).astype(to_ref.dtype)
+        put(j)
     dk_ref[...] = dk_acc[...].astype(LOW)
     dv_ref[...] = dv_acc[...].astype(LOW)
-    wq = flat(wq_ref)
-    for rows, to_ref in ((other, send_ref), (mine, keep_ref)):
-        to_ref[...] = nt(dq_ref[rows, :], wq).astype(to_ref.dtype)
 
 
 def normalize(values, gain, shift):
     center = values - jnp.mean(values, axis=1, keepdims=True)
     spread = jnp.mean(center * center, axis=1, keepdims=True)
     return center * lax.rsqrt(spread + 1e-05) * gain + shift
+
+
+def add_body(keep_ref, got_ref, out_ref):
+    out_ref[...] = (keep_ref[...].astype(F32) + got_ref[...].astype(F32)).astype(LOW)
 
 
 def norm_body(which, hidden_ref, part_ref, far_ref, norm_ref, new_ref, out_ref):
@@ -404,14 +601,18 @@
     ).astype(LOW)
 
 
-def embed_norm_body(side_ref, place_ref, norm_ref, *refs):
+def embed_norm_body(need, put, side_ref, place_ref, norm_ref, *refs):
     *part_refs, new_ref, out_ref = refs
     side = side_ref[0]
     rows = part_refs[0].shape[0]
+    need(1, 2)
     for s, part in enumerate(part_refs):
+        need(3 + s)
         at = pl.ds(pl.multiple_of((side ^ s) * rows, rows), rows)
-        new_ref[at, :] = part[...].astype(F32) + place_ref[at, :]
-    out_ref[...] = normalize(new_ref[...], norm_ref[0:1, :], norm_ref[4:5, :]).astype(LOW)
+        new = part[...].astype(F32) + place_ref[at, :]
+        new_ref[at, :] = new
+        out_ref[at, :] = normalize(new, norm_ref[0:1, :], norm_ref[4:5, :]).astype(LOW)
+    put(1, 0)
 
 
 def norm_back_body(which, hidden_ref, part_ref, far_ref, *refs):
@@ -431,87 +632,75 @@
         new = before[0][...] + new
     new_ref[...] = new
     low_ref[...] = new.astype(LOW)
-
-    @pl.when(pl.program_id(0) == 0)
-    def _():
-        sums_ref[...] = jnp.zeros(sums_ref.shape, F32)
-
-    sums_ref[0:1, :] += jnp.sum(grad * unit, axis=0, keepdims=True)
-    sums_ref[1:2, :] += jnp.sum(grad, axis=0, keepdims=True)
-
-
-def norm_rows_kernel(body, outs, operands, norm_rows, after, steps=4):
+    sums_ref[...] = jnp.concatenate(
+        [
+            jnp.sum(grad * unit, axis=0, keepdims=True),
+            jnp.sum(grad, axis=0, keepdims=True),
+            jnp.zeros((6, values.shape[1]), F32),
+        ],
+        axis=0,
+    )
+
+
+def weight_grad_body(clips, turn_left, need, put, core_ref, *refs):
+    lefts = refs[: 2 * clips]
+    rights = refs[2 * clips : 3 * clips]
+    outs = refs[3 * clips : -1]
+    turned = refs[-1]
+    height, width = lefts[0].shape
+    frames = rights[0].shape[0]
+    group = outs[0].shape[2]
+    core = core_ref[0]
+
+    def place(c, at):
+        return pl.ds(pl.multiple_of(c * frames + at * height, 128), height)
+
+    if turn_left:
+        for m, out_ref in enumerate(outs):
+            total = None
+            for c in range(clips):
+                if m == 0:
+                    for j, at in ((0, core), (1, 1 - core)):
+                        need(1 + 2 * c + j)
+                        turned[:, place(c, at)] = jnp.transpose(lefts[2 * c + j][...])
+                    need(1 + 2 * clips + c)
+                part = nn(
+                    turned[:, c * frames : (c + 1) * frames],
+                    rights[c][:, m * group : (m + 1) * group],
+                )
+                total = part if total is None else total + part
+            out_ref[...] = total.astype(LOW).reshape(out_ref.shape)
+            put(m)
+    else:
+        total = None
+        for c in range(clips):
+            need(1 + 2 * clips + c)
+            turned[:, c * frames : (c + 1) * frames] = jnp.transpose(rights[c][...])
+            for j, at in ((0, core), (1, 1 - core)):
+                need(1 + 2 * c + j)
+                part = nn(turned[:, place(c, at)], lefts[2 * c + j][...])
+                total = part if total is None else total + part
+        for m, out_ref in enumerate(outs):
+            member = total[m * group : (m + 1) * group, :]
+            out_ref[...] = jnp.transpose(member).astype(LOW).reshape(out_ref.shape)
+            put(m)
+
+
+def norm_rows_kernel(body, outs, operands, norm_rows, after, name="norm"):
     height, width = operands[0].shape
-    rows = height // steps
-
-    def spec(a):
-        if a.shape[0] == height:
-            return pl.BlockSpec((rows, width), lambda i: (i, 0))
-        return pl.BlockSpec(a.shape, lambda i: (0, 0))
-
-    operands = list(operands) + [norm_rows]
-    nbytes = sum(
-        math.prod(a.shape) * jnp.dtype(a.dtype).itemsize for a in operands + list(outs)
-    )
+    operands = list(operands) + ([] if norm_rows is None else [norm_rows])
+    nbytes = sum(nbytes_of(a.shape, a.dtype) for a in operands + list(outs))
     return pl.pallas_call(
         later(body, len(after), len(operands)),
         out_shape=tuple(outs),
-        grid=(steps,),
-        in_specs=[spec(a) for a in operands] + [anywhere()] * len(after),
-        out_specs=tuple(spec(o) for o in outs),
-        compiler_params=pltpu.CompilerParams(vmem_limit_bytes=24 << 20),
+        in_specs=[in_vmem()] * len(operands) + [anywhere()] * len(after),
+        out_specs=tuple(in_vmem() for _ in outs),
+        compiler_params=pltpu.CompilerParams(vmem_limit_bytes=16 << 20),
         cost_estimate=pl.CostEstimate(
-            flops=20 * height * width, bytes_accessed=nbytes, transcendentals=0
-        ),
-        name="norm",
-    )(*operands, *after)
-
-
-def weight_grad_body(clips, core_ref, *refs):
-    pairs = refs[: 2 * clips]
-    rights = refs[2 * clips : 3 * clips]
-    out_ref, turned = refs[3 * clips :]
-    height = pairs[0].shape[0]
-    frames = rights[0].shape[0]
-
-    @pl.when(pl.program_id(0) == 0)
-    def _():
-        core = core_ref[0]
-        for c in range(clips):
-            for j, at in ((0, core), (1, 1 - core)):
-                place = pl.ds(pl.multiple_of(c * frames + at * height, 128), height)
-                turned[:, place] = jnp.transpose(pairs[2 * c + j][...])
-
-    total = None
-    for c in range(clips):
-        part = nn(turned[:, c * frames : (c + 1) * frames], rights[c][...])
-        total = part if total is None else total + part
-    out_ref[...] = total.astype(LOW).reshape(out_ref.shape)
-
-
-def weight_grad(core, pairs, rights, dp, group, name, after):
-    clips = len(pairs)
-    width = pairs[0][0].shape[1]
-    frames, columns = rights[0].shape
-    lefts = [half for pair in pairs for half in pair]
-    members = columns // group
-    nbytes = 2 * (2 * clips * frames * (width + columns) // 2 + width * columns)
-    return pl.pallas_call(
-        later(partial(weight_grad_body, clips), 1, 1 + 3 * clips),
-        out_shape=sds((dp, members, width // dp, group), LOW),
-        grid=(members,),
-        in_specs=[scalars()]
-        + [pl.BlockSpec(a.shape, lambda i: (0, 0)) for a in lefts]
-        + [pl.BlockSpec((frames, group), lambda i: (0, i)) for _ in rights]
-        + [anywhere()],
-        out_specs=pl.BlockSpec((dp, 1, width // dp, group), lambda i: (0, i, 0, 0)),
-        scratch_shapes=[pltpu.VMEM((width, clips * frames), LOW)],
-        compiler_params=pltpu.CompilerParams(vmem_limit_bytes=56 << 20),
-        cost_estimate=pl.CostEstimate(
-            flops=2 * clips * frames * width * columns, bytes_accessed=nbytes, transcendentals=0
+            flops=20 * height * width, bytes_accessed=nbytes // 4, transcendentals=0
         ),
         name=name,
-    )(core, *lefts, *rights, after)
+    )(*operands, *after)
 
 
 def embed_body(base_ref, codes_ref, *refs):
@@ -540,10 +729,10 @@
         out_shape=sds((blocks, rows, features), LOW),
         grid=(blocks,),
         in_specs=[scalars(), pl.BlockSpec((1, rows, books), lambda i: (i, 0, 0))]
-        + [whole(t) for t in tables]
+        + [in_vmem() for t in tables]
         + [anywhere()] * len(after),
         out_specs=pl.BlockSpec((1, rows, features), lambda i: (i, 0, 0)),
-        compiler_params=pltpu.CompilerParams(vmem_limit_bytes=56 << 20),
+        compiler_params=pltpu.CompilerParams(vmem_limit_bytes=32 << 20),
         cost_estimate=pl.CostEstimate(
             flops=4 * blocks * rows * books * vocab * features,
             bytes_accessed=2 * books * vocab * features + blocks * rows * (features + 512),
@@ -586,7 +775,7 @@
         + [pl.BlockSpec(g.shape, lambda i, k: (0, 0)) for g in grads],
         out_specs=pl.BlockSpec((1, 1, features, vocab), lambda i, k: (i, k, 0, 0)),
         scratch_shapes=[pltpu.VMEM((total, features), LOW)],
-        compiler_params=pltpu.CompilerParams(vmem_limit_bytes=56 << 20),
+        compiler_params=pltpu.CompilerParams(vmem_limit_bytes=32 << 20),
         cost_estimate=pl.CostEstimate(
             flops=4 * parts * books * vocab * features * total,
             bytes_accessed=2 * parts * books * features * vocab + 2 * total * features,
@@ -596,43 +785,72 @@
     )(base, lines, *grads)
 
 
-def gather_features_body(where_ref, *refs):
+def gather_features_body(need, put, where_ref, *refs):
     *part_refs, out_ref = refs
     features = part_refs[0].shape[1]
     for m, part in enumerate(part_refs):
+        need(1 + m)
         at = pl.ds(pl.multiple_of(where_ref[m] * features, features), features)
         out_ref[:, at] = part[...]
 
 
-def split_features_body(where_ref, side_ref, *refs):
+def split_features_body(need, put, where_ref, side_ref, *refs):
     clips = side_ref.shape[0] - 1
     grads, outs = refs[:clips], refs[clips:]
     features = outs[0].shape[1]
     rows = outs[0].shape[0] // clips
     at_rows = pl.ds(pl.multiple_of(side_ref[0] * rows, rows), rows)
-    for m, out_ref in enumerate(outs):
+    need(*range(2, 2 + clips))
+    for m, out_ref in reversed(list(enumerate(outs))):
         at = pl.ds(pl.multiple_of(where_ref[m] * features, features), features)
         for c in range(clips):
             out_ref[c * rows : (c + 1) * rows, :] = grads[c][at_rows, at]
-
-
-def text_body(where_ref, *refs):
+        put(m)
+
+
+def text_body(need, put, where_ref, *refs):
     *part_refs, wk_ref, wv_ref, tp_ref, k_ref, v_ref = refs
     columns = part_refs[0].shape[1]
     for m, part in enumerate(part_refs):
+        need(1 + m)
         at = pl.ds(pl.multiple_of(where_ref[m] * columns, columns), columns)
         tp_ref[:, at] = part[...]
-    tp = tp_ref[...]
-    k_ref[...] = nn(tp, flat(wk_ref)).astype(LOW)
-    v_ref[...] = nn(tp, flat(wv_ref)).astype(LOW)
-
-
-def text_back_body(dk_ref, dv_ref, wk_ref, wv_ref, tp_ref, part_ref, gk_ref, gv_ref):
-    dk, dv = dk_ref[...], dv_ref[...]
-    part_ref[...] = (nt(dk, flat(wk_ref)) + nt(dv, flat(wv_ref))).astype(LOW)
+    put(0)
+    for j, w_ref, to_ref in ((1, wk_ref, k_ref), (2, wv_ref, v_ref)):
+        need(len(part_refs) + j)
+        to_ref[...] = nn(tp_ref[...], flat(w_ref)).astype(LOW)
+        put(j)
+
+
+def text_back_body(clips, need, put, where_ref, *refs):
+    dks, dvs = refs[:clips], refs[clips : 2 * clips]
+    wk_ref, wv_ref, tp_ref = refs[2 * clips : 2 * clips + 3]
+    *part_refs, gk_ref, gv_ref, full_ref = refs[2 * clips + 3 :]
+    columns = part_refs[0].shape[1]
+    length = dks[0].shape[0]
+    need(*range(1, 1 + 2 * clips + 2))
+    wk, wv = flat(wk_ref), flat(wv_ref)
+    for c in range(clips):
+        tp_rows = slice(c * length, (c + 1) * length)
+        full_ref[tp_rows, :] = (nt(dks[c][...], wk) + nt(dvs[c][...], wv)).astype(LOW)
+    for m, part_ref in enumerate(part_refs):
+        at = pl.ds(pl.multiple_of(where_ref[m] * columns, columns), columns)
+        part_ref[...] = full_ref[:, at]
+    put(*range(len(part_refs)))
+    need(3 + 2 * clips)
     turned = jnp.transpose(tp_ref[...])
-    gk_ref[...] = nn(turned, dk).astype(LOW).reshape(gk_ref.shape)
-    gv_ref[...] = nn(turned, dv).astype(LOW).reshape(gv_ref.shape)
+    for j, grads, to_ref in ((0, dks, gk_ref), (1, dvs, gv_ref)):
+        total = None
+        for c in range(clips):
+            part = nn(turned[:, c * length : (c + 1) * length], grads[c][...])
+            total = part if total is None else total + part
+        to_ref[...] = total.astype(LOW).reshape(to_ref.shape)
+        put(len(part_refs) + j)
+
+
+def text_weight_body(need, put, rows_ref, grad_ref, out_ref):
+    need(0, 1)
+    out_ref[...] = tn(rows_ref[...], grad_ref[...]).astype(LOW).reshape(out_ref.shape)
 
 
 def positions_rows(start, count, feature_count):
@@ -699,8 +917,8 @@
     width = share * dp
     vocab = tables.shape[2]
     text_share = text_proj.shape[1]
-    core_arg = core.astype(jnp.int32).reshape(1)
-    side_arg = side.astype(jnp.int32).reshape(1)
+    core_arg = Scalar(core.astype(jnp.int32).reshape(1))
+    side_arg = Scalar(side.astype(jnp.int32).reshape(1))
     swap_core = partial(swap, axis="tensor", mask=1)
 
     def spread_tensor(values):
@@ -750,8 +968,10 @@
 
     last = []
 
-    def run(body, outs, operands, specs, after=(), **rest):
-        results = kernel(body, outs, operands, specs, after=last + list(after), **rest)
+    def run(body, outs, operands, **rest):
+        shared = [o.shared.array for o in outs if isinstance(o, Into)]
+        wait_for = [a for a in last if not any(a is b for b in shared)]
+        results = kernel(body, outs, operands, after=wait_for, **rest)
         last[:] = [results[-1]]
         return results
 
@@ -800,9 +1020,8 @@
     if aligned:
         (strips,) = run(
             gather_features_body,
-            [sds((clips * strip, width), LOW)],
-            [group_order] + arrived,
-            [scalars()] + [whole(a) for a in arrived],
+            [Flow(sds((clips * strip, width), LOW))],
+            [Scalar(group_order)] + arrived,
             name="gather_features",
         )
     else:
@@ -814,13 +1033,20 @@
     norm_rows = jnp.transpose(norm_rows, (1, 0, 2)).reshape(16, width).astype(F32)
 
     def w_attn(n):
-        return member(attn_all, 1, share, n)
-
-    def w_ffn(n):
-        return member(ffn_all, 1, 1, n)
+        return Window(
+            attn_all, (dp, share, columns), lambda ref: ref.at[:, pl.ds(n * share, share), :]
+        )
+
+    def w_member(array, n):
+        return Window(array, (dp,) + array.shape[2:], lambda ref: ref.at[:, n])
 
     half_sds = sds((height, width), F32)
     half_low = sds((height, width), LOW)
+    flow = Flow(half_low)
+
+    def fetch(a):
+        return Window(a, a.shape, everything)
+
 
     def norm_step(which, hidden, parts):
         new, out = norm_rows_kernel(
@@ -841,9 +1067,18 @@
         last[:] = [out]
         return new, (out, swap_core(out)), sums
 
-    def reduce_rows(keep, send):
-        got = swap_core(send)
-        return across((keep + got.astype(F32)).astype(LOW))
+    waiting = []
+    moving = [None] * clips
+
+    def flush():
+        if waiting:
+            c, keep, got = waiting.pop()
+            (part,) = norm_rows_kernel(add_body, [half_low], [keep, got], None, last, name="add")
+            last[:] = [part]
+            moving[c] = across(part)
+
+    def reduce_rows(c, keep, send):
+        waiting.append((c, keep, swap_core(send)))
 
     text_rows = text_states.reshape(clips * text_len, text_width)
     text_weight = attn_all[:, 8 * share : 8 * share + text_share, :].reshape(text_width, columns)
@@ -865,85 +1100,89 @@
     def embed_step(c):
         mine = strips[c * strip : (c + 1) * strip]
         parts = [mine] + [swap(mine, "tensor", 2 * s) for s in range(1, sides)]
-        operands = [side_arg, placed, norm_rows] + parts
         new, out = run(
             embed_norm_body,
-            [half_sds, half_low],
-            operands,
-            [scalars()] + [whole(a) for a in operands[1:]],
+            [Flow(half_sds), Flow(half_low)],
+            [side_arg, placed, norm_rows] + parts,
             flops=10 * height * width,
             name="embed_norm",
         )
         return new, (out, swap_core(out))
 
-    def self_step(pair):
-        operands = [core_arg, *pair, attn_all, attn_all, attn_all, attn_all]
-        *kept, keep, send = run(
+    def self_step(c, pair):
+        own, got = pair
+        *saved, keep, send, left, right = run(
             self_forward_body,
-            [full, full, full, full, lse_sds, half_sds, half_low],
-            operands,
-            [scalars()] + [whole(a) for a in pair] + [w_attn(0), w_attn(1), w_attn(2), w_attn(6)],
+            [full, full, full, full, lse_sds, flow, flow, Copy(1), Copy(3)],
+            [core_arg, own, w_attn(0), got, w_attn(1), w_attn(2), w_attn(6)],
             flops=8 * frames * width * columns + 4 * score_flops * frames,
             scratch=tot,
             name="self_forward",
         )
-        return kept, reduce_rows(keep, send)
+        pairs[0][c] = (left, right)
+        reduce_rows(c, keep, send)
+        return saved
+
+    text_full = sds((clips * text_len, width), LOW)
+    text_cols = sds((clips * text_len, columns), LOW)
 
     def text_step():
-        operands = [place_order] + text_parts + [attn_all, attn_all]
         return run(
             text_body,
-            [
-                sds((clips * text_len, width), LOW),
-                sds((clips * text_len, columns), LOW),
-                sds((clips * text_len, columns), LOW),
-            ],
-            operands,
-            [scalars()] + [whole(a) for a in text_parts] + [w_attn(4), w_attn(5)],
+            [text_full, text_cols, text_cols],
+            [Scalar(place_order)] + text_parts + [w_attn(4), w_attn(5)],
             flops=4 * clips * text_len * width * columns,
             name="text",
         )
 
+    def text_rows_of(array, c):
+        return Window(
+            array, (text_len, columns), lambda ref: ref.at[pl.ds(c * text_len, text_len), :]
+        )
+
     def cross_step(c, pair):
-        k = text_key[c * text_len : (c + 1) * text_len]
-        v = text_value[c * text_len : (c + 1) * text_len]
-        operands = [core_arg, *pair, text_bias_row[c : c + 1], k, v, attn_all, attn_all]
-        q, o, lse, keep, send = run(
+        own, got = pair
+        k, v = text_rows_of(text_key, c), text_rows_of(text_value, c)
+        q, o, lse, keep, send, left, right = run(
             cross_forward_body,
-            [full, full, lse_sds, half_sds, half_low],
-            operands,
-            [scalars()] + [whole(a) for a in operands[1:6]] + [w_attn(3), w_attn(7)],
+            [full, full, lse_sds, flow, flow, Copy(1), Copy(3)],
+            [core_arg, own, w_attn(3), got, text_bias_row[c : c + 1], k, v, w_attn(7)],
             flops=4 * frames * width * columns + 4 * score_flops * text_len,
             scratch=tot,
             name="cross_forward",
         )
-        return (q, k, v, o, lse), reduce_rows(keep, send)
-
-    def ffn_step(pair):
-        *kept, keep, send = run(
+        pairs[1][c] = (left, right)
+        reduce_rows(c, keep, send)
+        return (q, k, v, o, lse)
+
+    def ffn_step(c, pair):
+        *saved, keep, send, left, right = run(
             ffn_forward_body,
-            [inner, inner, half_sds, half_low],
-            [core_arg, *pair, ffn_all, ffn_all],
-            [scalars()] + [whole(a) for a in pair] + [w_ffn(0), w_ffn(1)],
+            [inner, inner, flow, flow, Copy(1), Copy(2)],
+            [core_arg, *pair, w_member(ffn_all, 0), w_member(ffn_all, 1)],
             flops=4 * frames * width * units,
             name="ffn_forward",
         )
-        return kept, reduce_rows(keep, send)
+        pairs[2][c] = (left, right)
+        reduce_rows(c, keep, send)
+        return saved
 
     hidden = [[None] * clips for _ in range(4)]
     pairs = [[None] * clips for _ in range(4)]
     kept = [[None] * clips for _ in range(3)]
-    moving = [None] * clips
     for c in every:
         hidden[0][c], pairs[0][c] = embed_step(c)
-        kept[0][c], moving[c] = self_step(pairs[0][c])
+        flush()
+        kept[0][c] = self_step(c, pairs[0][c])
     text_hidden, text_key, text_value = text_step()
     for c in every:
         hidden[1][c], pairs[1][c] = norm_step(1, hidden[0][c], moving[c])
-        kept[1][c], moving[c] = cross_step(c, pairs[1][c])
+        flush()
+        kept[1][c] = cross_step(c, pairs[1][c])
     for c in every:
         hidden[2][c], pairs[2][c] = norm_step(2, hidden[1][c], moving[c])
-        kept[2][c], moving[c] = ffn_step(pairs[2][c])
+        flush()
+        kept[2][c] = ffn_step(c, pairs[2][c])
 
     targets = (jnp.roll(audio_codes, -1, axis=1) - place * vocab).astype(jnp.int32)
     loss_weight = weight_int.astype(F32)
@@ -952,16 +1191,21 @@
     sums = [[], [], [], []]
 
     def head_step(c, pair):
-        operands = [core_arg, *pair, targets[c], head_all]
-        logits, stats = run(
+        own, got = pair
+        logits, stats, left, right = run(
             head_forward_body,
-            [sds((frames, books * vocab), F32), sds((2 * books, frames), F32)],
-            operands,
-            [scalars()] + [whole(a) for a in operands[1:]],
+            [
+                sds((frames, books * vocab), F32),
+                Flow(sds((2 * books, frames), F32)),
+                Copy(1),
+                Copy(3),
+            ],
+            [core_arg, own, targets[c], got] + [w_member(head_all, k) for k in range(books)],
             flops=2 * frames * width * books * vocab,
             scratch=tot,
             name="head_forward",
         )
+        pairs[3][c] = (left, right)
         total, pick = stats[:books], stats[books:]
         mask = 1
         while mask < tensor:
@@ -974,45 +1218,69 @@
         return logits, jnp.concatenate([total, total], axis=0)
 
     def head_back_step(c, logits, total):
-        operands = [core_arg, logits, total, grad_weight[c], targets[c], head_all]
         grad, keep, send = run(
             head_backward_body,
-            [sds((frames, books * vocab), LOW), half_sds, half_low],
-            operands,
-            [scalars()] + [whole(a) for a in operands[1:]],
+            [sds((frames, books * vocab), LOW), flow, flow],
+            [core_arg, total, grad_weight[c], targets[c], fetch(logits)]
+            + [w_member(head_all, k) for k in range(books)],
             flops=2 * frames * width * books * vocab,
             scratch=tot,
             name="head_backward",
         )
-        return grad, reduce_rows(keep, send)
-
-    def weights(lefts, rights, group_columns, name):
-        result = weight_grad(core_arg, lefts, rights, dp, group_columns, name, last[0])
-        last[:] = [result]
-        return result
+        reduce_rows(c, keep, send)
+        return grad
+
+    attn_shared = Shared((dp, 8 * share + text_share, columns), LOW)
+    ffn_shared = Shared((dp,) + feedforward.shape, LOW)
+    head_shared = Shared((dp, books, share, vocab), LOW)
+
+    def attn_into(n):
+        return Into(
+            attn_shared,
+            (dp, share, columns),
+            lambda ref: ref.at[:, pl.ds(n * share, share), :],
+        )
+
+    def member_into(shared, n):
+        return Into(shared, (dp,) + shared.full.shape[2:], lambda ref: ref.at[:, n])
+
+    def weights(lefts, rights, outs, name):
+        total = rights[0].shape[1]
+        turn_left = 2 * total > width
+        run(
+            partial(weight_grad_body, clips, turn_left),
+            outs,
+            [core_arg] + [fetch(half) for pair in lefts for half in pair] + [fetch(a) for a in rights],
+            flops=2 * clips * frames * width * total,
+            scratch=[pltpu.VMEM((width if turn_left else total, clips * frames), LOW)],
+            name=name,
+            limit=48,
+        )
 
     logit_grads = [None] * clips
     ready = [None] * clips
     for c in every:
         hidden[3][c], pairs[3][c] = norm_step(3, hidden[2][c], moving[c])
+        flush()
         ready[c] = head_step(c, pairs[3][c])
         if c:
-            logit_grads[c - 1], moving[c - 1] = head_back_step(c - 1, *ready[c - 1])
-    logit_grads[-1], moving[-1] = head_back_step(clips - 1, *ready[-1])
-    head_grads = weights(pairs[3], logit_grads, vocab, "head_weights")
-    head_sum = lax.psum_scatter(head_grads, "dp", scatter_dimension=0, tiled=False)
+            flush()
+            logit_grads[c - 1] = head_back_step(c - 1, *ready[c - 1])
+    flush()
+    logit_grads[-1] = head_back_step(clips - 1, *ready[-1])
 
     def ffn_back_step(c, pair):
-        slope = kept[2][c][1]
-        grad, keep, send = run(
+        own, got = pair
+        grad, keep, send, left, right = run(
             ffn_backward_body,
-            [inner, half_sds, half_low],
-            [core_arg, *pair, slope, ffn_all, ffn_all],
-            [scalars()] + [whole(a) for a in pair] + [whole(slope), w_ffn(0), w_ffn(1)],
+            [inner, flow, flow, Copy(1), Copy(2)],
+            [core_arg, own, got, w_member(ffn_all, 1), fetch(kept[2][c][1]), w_member(ffn_all, 0)],
             flops=4 * frames * width * units,
             name="ffn_backward",
         )
-        return grad, reduce_rows(keep, send)
+        back_pairs[3][c] = (left, right)
+        reduce_rows(c, keep, send)
+        return grad
 
     grads = [None] * clips
     back_pairs = [[None] * clips for _ in range(4)]
@@ -1020,113 +1288,127 @@
     for c in every:
         grads[c], back_pairs[3][c], s = norm_back(3, hidden[3][c], moving[c], None)
         sums[3].append(s)
-        inner_grads[c], moving[c] = ffn_back_step(c, back_pairs[3][c])
-    ffn_two = weights(back_pairs[3], [k[0] for k in kept[2]], units, "ffn_two_weights")
-    ffn_one = weights(pairs[2], inner_grads, units, "ffn_one_weights")
-    ffn_sum = lax.psum_scatter(
-        jnp.concatenate([ffn_one, ffn_two], axis=1), "dp", scatter_dimension=0, tiled=False
-    )
+        flush()
+        inner_grads[c] = ffn_back_step(c, back_pairs[3][c])
+        if c == 0:
+            head_into = [member_into(head_shared, k) for k in range(books)]
+            weights(pairs[3], logit_grads, head_into, "head_weights")
+    head_sum = lax.psum_scatter(head_shared.array, "dp", scatter_dimension=0, tiled=False)
 
     acc_text = [pltpu.VMEM((text_len, columns), F32)] * 2
     small = sds((text_len, columns), LOW)
 
     def cross_back_step(c, pair):
+        own, got = pair
         q, k, v, o, lse = kept[1][c]
         bias = bias_columns[:, c : c + 1]
-        operands = [core_arg, *pair, bias, q, k, v, lse, attn_all, attn_all]
-        dq, dk, dv, keep, send = run(
+        dq, dk, dv, keep, send, left, right = run(
             cross_backward_body,
-            [full, small, small, half_sds, half_low],
-            operands,
-            [scalars()] + [whole(a) for a in operands[1:8]] + [w_attn(3), w_attn(7)],
+            [full, small, small, flow, flow, Copy(1), Copy(3)],
+            [core_arg, own, w_attn(7), got, bias, fetch(q), k, v, fetch(lse), w_attn(3)],
             flops=4 * frames * width * columns + 10 * score_flops * text_len,
             scratch=[pltpu.VMEM((frames, columns), LOW)] + acc_text,
             name="cross_backward",
         )
-        return (dq, dk, dv), reduce_rows(keep, send)
+        back_pairs[2][c] = (left, right)
+        reduce_rows(c, keep, send)
+        return (dq, dk, dv)
 
     cross_grads = [None] * clips
     for c in every:
         grads[c], back_pairs[2][c], s = norm_back(2, hidden[2][c], moving[c], grads[c])
         sums[2].append(s)
-        cross_grads[c], moving[c] = cross_back_step(c, back_pairs[2][c])
-    text_dk = jnp.concatenate([g[1] for g in cross_grads], axis=0)
-    text_dv = jnp.concatenate([g[2] for g in cross_grads], axis=0)
-    text_part, text_gk, text_gv = run(
-        text_back_body,
-        [
-            sds((clips * text_len, width), LOW),
-            sds((dp, 1, share, columns), LOW),
-            sds((dp, 1, share, columns), LOW),
-        ],
-        [text_dk, text_dv, attn_all, attn_all, text_hidden],
-        [whole(text_dk), whole(text_dv), w_attn(4), w_attn(5), whole(text_hidden)],
-        flops=8 * clips * text_len * width * columns,
-        name="text_back",
-    )
-    text_grad = collect_tensor(
-        [
-            lax.dynamic_slice_in_dim(text_part, place_order[m] * columns, columns, 1)
-            for m in range(tensor)
-        ]
-    ).astype(LOW)
-    text_proj_grad = tn(text_rows, text_grad).astype(LOW)
-    bias_grad = jnp.sum(text_grad.astype(F32), axis=0)
-    cross_out = weights(back_pairs[2], [k[3] for k in kept[1]], columns, "cross_out_weights")
-    cross_query = weights(pairs[1], [g[0] for g in cross_grads], columns, "cross_query_weights")
+        flush()
+        cross_grads[c] = cross_back_step(c, back_pairs[2][c])
+        if c == 0:
+            weights(
+                back_pairs[3], [k[0] for k in kept[2]], [member_into(ffn_shared, 1)], "ffn_two"
+            )
+        if c == min(1, clips - 1):
+            weights(pairs[2], inner_grads, [member_into(ffn_shared, 0)], "ffn_one")
+    ffn_sum = lax.psum_scatter(ffn_shared.array, "dp", scatter_dimension=0, tiled=False)
+
+    def text_back_step():
+        results = run(
+            partial(text_back_body, clips),
+            [Flow(text_cols)] * tensor + [attn_into(4), attn_into(5)],
+            [Scalar(place_order)]
+            + [fetch(g[1]) for g in cross_grads]
+            + [fetch(g[2]) for g in cross_grads]
+            + [w_attn(4), w_attn(5), fetch(text_hidden)],
+            flops=8 * clips * text_len * width * columns,
+            scratch=[pltpu.VMEM((clips * text_len, width), LOW)],
+            name="text_back",
+        )
+        return collect_tensor(results).astype(LOW)
 
     acc_self = [pltpu.VMEM((frames, columns), F32)] * 2
 
     def self_back_step(c, pair):
+        own, got = pair
         q, k, v, o, lse = kept[0][c]
-        operands = [core_arg, *pair, q, k, v, lse, attn_all, attn_all, attn_all, attn_all]
-        grad, keep, send = run(
+        grad, keep, send, left, right = run(
             self_backward_body,
-            [sds((frames, 3 * columns), LOW), half_sds, half_low],
-            operands,
-            [scalars()]
-            + [whole(a) for a in operands[1:7]]
-            + [w_attn(0), w_attn(1), w_attn(2), w_attn(6)],
+            [sds((frames, 3 * columns), LOW), flow, flow, Copy(1), Copy(3)],
+            [core_arg, own, w_attn(6), got]
+            + [fetch(a) for a in (q, k, v, lse)]
+            + [w_attn(0), w_attn(1), w_attn(2)],
             flops=8 * frames * width * columns + 10 * score_flops * frames,
-            scratch=[pltpu.VMEM((frames, columns), LOW)] * 2 + acc_self,
+            scratch=[pltpu.VMEM((frames, columns), LOW)] + acc_self,
             name="self_backward",
         )
-        return grad, reduce_rows(keep, send)
+        back_pairs[1][c] = (left, right)
+        reduce_rows(c, keep, send)
+        return grad
 
     self_grads = [None] * clips
     for c in every:
         grads[c], back_pairs[1][c], s = norm_back(1, hidden[1][c], moving[c], grads[c])
         sums[1].append(s)
-        self_grads[c], moving[c] = self_back_step(c, back_pairs[1][c])
-    self_out = weights(back_pairs[1], [k[3] for k in kept[0]], columns, "self_out_weights")
-    self_in = weights(pairs[0], self_grads, columns, "self_in_weights")
-    attn_grads = jnp.concatenate(
-        [
-            a.reshape(dp, -1, columns)
-            for a in (
-                self_in,
-                cross_query,
-                text_gk,
-                text_gv,
-                self_out,
-                cross_out,
-                text_proj_grad.reshape(dp, text_share, columns),
-            )
-        ],
-        axis=1,
-    )
-    attn_sum = lax.psum_scatter(attn_grads, "dp", scatter_dimension=0, tiled=False)
+        flush()
+        self_grads[c] = self_back_step(c, back_pairs[1][c])
+        if c == 0:
+            text_grad = text_back_step()
+            weights(back_pairs[2], [k[3] for k in kept[1]], [attn_into(7)], "cross_out")
+        if c == min(1, clips - 1):
+            weights(pairs[1], [g[0] for g in cross_grads], [attn_into(3)], "cross_query")
+    bias_grad = jnp.sum(text_grad.astype(F32), axis=0)
 
     zero_lows = [None] * clips
-    for c in every:
+
+    def zero_step(c):
         _, (zero_lows[c], _), s = norm_back(0, hidden[0][c], moving[c], grads[c])
         sums[0].append(s)
+
+    zero_step(0)
+    flush()
+    text_into = Into(
+        attn_shared,
+        (dp, text_share, columns),
+        lambda ref: ref.at[:, pl.ds(8 * share, text_share), :],
+    )
+    run(
+        text_weight_body,
+        [text_into],
+        [text_rows, text_grad],
+        flops=2 * clips * text_len * text_width * columns,
+        name="text_weight",
+    )
+    weights(back_pairs[1], [k[3] for k in kept[0]], [attn_into(6)], "self_out")
+    weights(pairs[0], self_grads, [attn_into(n) for n in range(3)], "self_in")
+    attn_sum = lax.psum_scatter(attn_shared.array, "dp", scatter_dimension=0, tiled=False)
+    for c in range(1, clips):
+        zero_step(c)
+
     if aligned:
         pieces = run(
             split_features_body,
-            [sds((clips * strip, share), LOW)] * dp,
-            [group_order, jnp.broadcast_to(side_arg, (clips + 1,))] + zero_lows,
-            [scalars(), scalars()] + [whole(a) for a in zero_lows],
+            [Flow(sds((clips * strip, share), LOW))] * dp,
+            [
+                Scalar(group_order),
+                Scalar(jnp.broadcast_to(side.astype(jnp.int32), (clips + 1,))),
+            ]
+            + zero_lows,
             name="split_features",
         )
     else:

time: 1030 us -> 1010 us (0.981)
  other arithmetic: 88.6 us -> 52 us
  starting transfers between devices: 96.5 us -> 77 us
  local copies, waits for them, and re-layouts: 171 us -> 185 us
  Pallas kernels: 348 us -> 361 us
    unnamed x647 -> x737, local copies, waits for them, and re-layouts: 126 us -> 160 us
    convert_element_type x21 -> x0, other arithmetic: 33.1 us -> none  [reduce_rows(): return across((keep + got.astype(F32)).astype(LOW))]
    pallas_call x38 -> x39, Pallas kernels: 218 us -> 245 us  [kernel(): pl.pallas_call(run_body, out_shape=tuple(out_shapes), in_specs=specs + [a...]
    ppermute x111, starting transfers between devices: 96.2 us -> 76.8 us  [swap(): return lax.ppermute(values, axis, [(i, i ^ mask) for i in range(size)])]
    pallas_call x21 -> x42, Pallas kernels: 63.6 us -> 59.3 us  [norm_rows_kernel(): pl.pallas_call(later(body, len(after), len(operands)), out_shape=tuple(ou...]
  transfers between devices with their start and end apart: 117 -> 117, of which waited for: 49 -> 51; matrix products, arithmetic and copies ran while one was open for 11% -> 5% of each run, Pallas kernels for 31% -> 34%
where the time goes in v2:
time: 1010 us; the launch traced here: 994 us
  Pallas kernels  361 us (36%)
  waiting for transfers between devices  288 us (29%)
  local copies, waits for them, and re-layouts  185 us (18%)
  starting transfers between devices  77 us (8%)
  other arithmetic  52 us (5%)
  between operations  29.6 us (3%)
    ppermute x111, waiting for transfers between devices, swap(): return lax.ppermute(values, axis, [(i, i ^ mask) for i in range(size)])  283 us
    pallas_call x39, Pallas kernels, kernel(): pl.pallas_call(run_body, out_shape=tuple(out_shapes), in_specs=specs + [a...  245 us
    unnamed x737, local copies, waits for them, and re-layouts  160 us
    ppermute x111, starting transfers between devices, swap(): return lax.ppermute(values, axis, [(i, i ^ mask) for i in range(size)])  76.8 us
    pallas_call x42, Pallas kernels, norm_rows_kernel(): pl.pallas_call(later(body, len(after), len(operands)), out_shape=tuple(ou...  59.3 us
    pallas_call x4, Pallas kernels, embed(): pl.pallas_call(later(embed_body, len(after), 2 + len(tables)), out_shape=...  32.7 us
    pallas_call x1, Pallas kernels, embed_back(): pl.pallas_call(embed_back_body, out_shape=sds((parts, books, features, vo...  24.4 us
  transfers between devices with their start and end apart: 117, of which 51 were waited for; matrix products, arithmetic and copies ran while one was open for 5% of the time, Pallas kernels for 34%

profile of v2, /device:TPU:0, one launch (start us, length us, event | category | flops | bytes accessed | tf_op | source)
XLA Modules:
  0.0 994.2 jit_solution(12680376128631799733)
XLA Ops:
  40.5 8.1 embed.4.refs_6_
  54.0 8.1 embed.5.refs_6_
  65.2 8.1 embed.6.refs_6_
  75.7 8.3 embed.7.refs_9_
  91.3 13.5 %collective-permute-done.9.refs_5_ = bf16[576,128]{1,0:T(8,128)(2,1)S(1)} collective-permute-done((bf16[576,128]{1,0:T(8,128)(2,1)S(1)}, bf16[576,128]{1,0:T(8,128)(2,1)S(1)}, u32[]{:S(2)}, u32[]{:S(2)}) %collective-permute-start.9) | collective-permute-done | bytes 147488 | tf_op jit(solution)/shard_map/ppermute | solution.py:879
  124.7 8.3 self_forward.3
  144.9 9.0 self_forward.4
  161.7 10.1 %collective-permute-done.23.refs_3_ = bf16[768,256]{1,0:T(8,128)(2,1)} collective-permute-done((bf16[768,256]{1,0:T(8,128)(2,1)}, bf16[768,256]{1,0:T(8,128)(2,1)}, u32[]{:S(2)}, u32[]{:S(2)}) %collective-permute-start.23) | collective-permute-done | bytes 393248 | tf_op jit(solution)/shard_map/ppermute | solution.py:879
  178.8 8.0 self_forward.5
  257.4 7.7 collective-permute-done.29.refs_2_
  300.4 10.4 %collective-permute-done.39.refs_2_ = bf16[384,1024]{1,0:T(8,128)(2,1)S(1)} collective-permute-done((bf16[384,1024]{1,0:T(8,128)(2,1)S(1)}, bf16[384,1024]{1,0:T(8,128)(2,1)S(1)}, u32[]{:S(2)}, u32[]{:S(2)}) %collective-permute-start.39) | collective-permute-done | bytes 786464 | tf_op jit(solution)/shard_map/ppermute | solution.py:879
  348.0 7.6 head_forward.3
  374.0 8.9 collective-permute-done.46
  439.5 10.4 %collective-permute-done.54 = f32[8,768]{0,1:T(8,128)S(1)} collective-permute-done((f32[8,768]{0,1:T(8,128)S(1)}, f32[8,768]{0,1:T(8,128)S(1)}, u32[]{:S(2)}, u32[]{:S(2)}) %collective-permute-start.54) | collective-permute-done | bytes 24608 | tf_op jit(solution)/shard_map/ppermute | solution.py:879
  503.4 14.7 %head_weights.1.refs_4_ = bf16[8,4,128,512]{3,2,1,0:T(8,128)(2,1)} custom-call(s32[1]{0:T(128)} %bitcast.refs_0_, bf16[384,1024]{1,0:T(8,128)(2,1)S(1)} %copy-done.292, bf16[384,1024]{1,0:T(8,128)(2,1)S(1)} %copy-done.197, bf16[384,1024]{1,0:T(8,128)(2,1)S(1)} %copy-done.294, bf16[384,1024]{1,0:T(8,128)(2,1)S(1)} %copy-done.147, ...), custom_call_target="tpu_custom_call" | custom-call | flops 9663676416 | bytes 18350080 | tf_op jit(solution)/shard_map/head_weights/pallas_call | solution.py:213
  519.9 18.9 %collective-permute-done.61.refs_2_ = bf16[384,1024]{1,0:T(8,128)(2,1)S(1)} collective-permute-done((bf16[384,1024]{1,0:T(8,128)(2,1)S(1)}, bf16[384,1024]{1,0:T(8,128)(2,1)S(1)}, u32[]{:S(2)}, u32[]{:S(2)}) %collective-permute-start.61) | collective-permute-done | bytes 786464 | tf_op jit(solution)/shard_map/ppermute | solution.py:879
  550.9 12.9 %collective-permute-done.63.refs_2_ = bf16[384,1024]{1,0:T(8,128)(2,1)S(1)} collective-permute-done((bf16[384,1024]{1,0:T(8,128)(2,1)S(1)}, bf16[384,1024]{1,0:T(8,128)(2,1)S(1)}, u32[]{:S(2)}, u32[]{:S(2)}) %collective-permute-start.63) | collective-permute-done | bytes 786464 | tf_op jit(solution)/shard_map/ppermute | solution.py:879
  573.1 13.1 %collective-permute-done.62.refs_2_ = bf16[384,1024]{1,0:T(8,128)(2,1)S(1)} collective-permute-done((bf16[384,1024]{1,0:T(8,128)(2,1)S(1)}, bf16[384,1024]{1,0:T(8,128)(2,1)S(1)}, u32[]{:S(2)}, u32[]{:S(2)}) %collective-permute-start.62) | collective-permute-done | bytes 786464 | tf_op jit(solution)/shard_map/ppermute | solution.py:879
  591.2 8.0 cross_backward.3
  602.5 9.9 ffn_two.1.refs_5_.refs_10_
  630.9 9.6 ffn_one.1.refs_5_
  642.4 18.9 %collective-permute-done.72.refs_2_ = bf16[384,1024]{1,0:T(8,128)(2,1)S(1)} collective-permute-done((bf16[384,1024]{1,0:T(8,128)(2,1)S(1)}, bf16[384,1024]{1,0:T(8,128)(2,1)S(1)}, u32[]{:S(2)}, u32[]{:S(2)}) %collective-permute-start.72) | collective-permute-done | bytes 786464 | tf_op jit(solution)/shard_map/ppermute | solution.py:879
  679.6 8.2 collective-permute-done.71.refs_2_
  692.7 11.3 %self_backward.3 = (bf16[768,768]{1,0:T(8,128)(2,1)S(1)}, bf16[384,1024]{1,0:T(8,128)(2,1)S(1)}, bf16[384,1024]{1,0:T(8,128)(2,1)}, bf16[384,1024]{1,0:T(8,128)(2,1)S(1)}, bf16[384,1024]{1,0:T(8,128)(2,1)S(1)}) custom-call(s32[1]{0:T(128)} %bitcast.refs_0_, bf16[384,1024]{1,0:T(8,128)(2,1)S(1)} %get-tuple-element.357.refs_2_.refs_1_, ...), custom_call_target="tpu_custom_call" | custom-call | flops 4630511616 | bytes 4481024 | tf_op jit(solution)/shard_map/self_backward/pallas_call | solution.py:213
  730.5 10.9 %self_backward.4 = (bf16[768,768]{1,0:T(8,128)(2,1)S(1)}, bf16[384,1024]{1,0:T(8,128)(2,1)S(1)}, bf16[384,1024]{1,0:T(8,128)(2,1)}, bf16[384,1024]{1,0:T(8,128)(2,1)S(1)}, bf16[384,1024]{1,0:T(8,128)(2,1)S(1)}) custom-call(s32[1]{0:T(128)} %bitcast.refs_0_, bf16[384,1024]{1,0:T(8,128)(2,1)S(1)} %get-tuple-element.382.refs_2_.refs_1_, ...), custom_call_target="tpu_custom_call" | custom-call | flops 4630511616 | bytes 4481024 | tf_op jit(solution)/shard_map/self_backward/pallas_call | solution.py:213
  761.5 10.1 %self_backward.5 = (bf16[768,768]{1,0:T(8,128)(2,1)S(1)}, bf16[384,1024]{1,0:T(8,128)(2,1)S(1)}, bf16[384,1024]{1,0:T(8,128)(2,1)S(1)}, bf16[384,1024]{1,0:T(8,128)(2,1)S(1)}, bf16[384,1024]{1,0:T(8,128)(2,1)S(1)}) custom-call(s32[1]{0:T(128)} %bitcast.refs_0_, bf16[384,1024]{1,0:T(8,128)(2,1)S(1)} %get-tuple-element.398.refs_2_.refs_1_, ...), custom_call_target="tpu_custom_call" | custom-call | flops 4630511616 | bytes 4481024 | tf_op jit(solution)/shard_map/self_backward/pallas_call | solution.py:213
  772.8 14.0 %collective-permute-done.86 = bf16[768,256]{1,0:T(8,128)(2,1)S(1)} collective-permute-done((bf16[768,256]{1,0:T(8,128)(2,1)S(1)}, bf16[768,256]{1,0:T(8,128)(2,1)S(1)}, u32[]{:S(2)}, u32[]{:S(2)}) %collective-permute-start.86) | collective-permute-done | bytes 393248 | tf_op jit(solution)/shard_map/ppermute | solution.py:879
  798.7 8.2 self_in.1.refs_5_
  812.4 18.4 %collective-permute-done.89.refs_2_ = bf16[384,1024]{1,0:T(8,128)(2,1)S(1)} collective-permute-done((bf16[384,1024]{1,0:T(8,128)(2,1)S(1)}, bf16[384,1024]{1,0:T(8,128)(2,1)S(1)}, u32[]{:S(2)}, u32[]{:S(2)}) %collective-permute-start.89) | collective-permute-done | bytes 786464 | tf_op jit(solution)/shard_map/ppermute | solution.py:879
  837.0 8.7 collective-permute-done.90.refs_2_
  855.2 7.6 collective-permute-done.91.refs_1_
  878.3 24.4 %embed_back.1 = bf16[4,4,128,512]{3,2,1,0:T(8,128)(2,1)S(1)} custom-call(s32[4]{0:T(128)S(1)} %copy-done.314, s32[4,8,4608]{2,1,0:T(8,128)S(1)} %broadcast_in_dim.37.codes_ref, bf16[576,128]{1,0:T(8,128)(2,1)S(1)} %get-tuple-element.424.refs_0_, bf16[576,128]{1,0:T(8,128)(2,1)S(1)} %collective-permute-done.91.refs_1_, ...), custom_call_target="tpu_custom_call" | custom-call | flops 19327352832 | bytes 3276800 | tf_op jit(solution)/shard_map/embed_back/pallas_call | solution.py:770
  (1158 shorter events, 609.9 us)
Async XLA Ops:
  7.2 108.9 %all-gather.7.cloned.1.call-start = ((), (), s32[]{:S(2)}) async-start(), calls=%async_computation.6 | async-start | bytes 5234688 | tf_op jit(solution)/shard_map/all_gather | solution.py:982
  11.1 258.8 %all-gather.9.cloned.1.call-start = ((), (), s32[]{:S(2)}) async-start(), calls=%async_computation.7 | async-start | bytes 4718592 | tf_op jit(solution)/shard_map/all_gather | solution.py:983
  16.8 21.7 %collective-permute-start.4 = (bf16[4,128,512]{2,1,0:T(8,128)(2,1)S(1)}, bf16[4,128,512]{2,1,0:T(8,128)(2,1)S(1)}, u32[]{:S(2)}, u32[]{:S(2)}) collective-permute-start(bf16[4,128,512]{2,1,0:T(8,128)(2,1)S(1)} %get-tuple-element.496.refs_2_), channel_id=1, source_target_pairs={{0,2},{1,3},{2,0},{3,1},{4,6},{5,7},{6,4},{7,5},{8,10},{9,11},{10,... | collective-permute-start | bytes 1572872 | tf_op jit(solution)/shard_map/ppermute | solution.py:879
  18.3 22.1 %collective-permute-start.3 = (bf16[4,128,512]{2,1,0:T(8,128)(2,1)S(1)}, bf16[4,128,512]{2,1,0:T(8,128)(2,1)S(1)}, u32[]{:S(2)}, u32[]{:S(2)}) collective-permute-start(bf16[4,128,512]{2,1,0:T(8,128)(2,1)S(1)} %get-tuple-element.496.refs_2_), channel_id=1, source_target_pairs={{0,1},{1,0},{2,3},{3,2},{4,5},{5,4},{6,7},{7,6},{8,9},{9,8},{10,11... | collective-permute-start | bytes 1572872 | tf_op jit(solution)/shard_map/ppermute | solution.py:879
  19.2 325.6 %all-gather.11.cloned.1.call-start = ((), (), s32[]{:S(2)}) async-start(), calls=%async_computation.8 | async-start | bytes 4718592 | tf_op jit(solution)/shard_map/all_gather | solution.py:984
  48.6 35.5 %collective-permute-start.12 = (bf16[576,128]{1,0:T(8,128)(2,1)S(1)}, bf16[576,128]{1,0:T(8,128)(2,1)S(1)}, u32[]{:S(2)}, u32[]{:S(2)}) collective-permute-start(bf16[576,128]{1,0:T(8,128)(2,1)S(1)} %get-tuple-element.503), channel_id=1, source_target_pairs={{0,28},{4,24},{8,20},{12,16},{16,12},{20,8},{24,4},{28,0},{1,29},{... | collective-permute-start | bytes 442376 | tf_op jit(solution)/shard_map/ppermute | solution.py:879
  54.0 30.8 %collective-permute-start.11 = (bf16[576,128]{1,0:T(8,128)(2,1)S(1)}, bf16[576,128]{1,0:T(8,128)(2,1)S(1)}, u32[]{:S(2)}, u32[]{:S(2)}) collective-permute-start(bf16[576,128]{1,0:T(8,128)(2,1)S(1)} %get-tuple-element.504), channel_id=1, source_target_pairs={{0,24},{4,28},{8,16},{12,20},{16,8},{20,12},{24,0},{28,4},{1,25},{... | collective-permute-start | bytes 442376 | tf_op jit(solution)/shard_map/ppermute | solution.py:879
  62.1 29.1 %collective-permute-start.10 = (bf16[576,128]{1,0:T(8,128)(2,1)S(1)}, bf16[576,128]{1,0:T(8,128)(2,1)S(1)}, u32[]{:S(2)}, u32[]{:S(2)}) collective-permute-start(bf16[576,128]{1,0:T(8,128)(2,1)S(1)} %get-tuple-element.505), channel_id=1, source_target_pairs={{0,20},{4,16},{8,28},{12,24},{16,4},{20,0},{24,12},{28,8},{1,21},{... | collective-permute-start | bytes 442376 | tf_op jit(solution)/shard_map/ppermute | solution.py:879
  62.2 42.6 %collective-permute-start.9 = (bf16[576,128]{1,0:T(8,128)(2,1)S(1)}, bf16[576,128]{1,0:T(8,128)(2,1)S(1)}, u32[]{:S(2)}, u32[]{:S(2)}) collective-permute-start(bf16[576,128]{1,0:T(8,128)(2,1)S(1)} %get-tuple-element.506), channel_id=1, source_target_pairs={{0,16},{4,20},{8,24},{12,28},{16,0},{20,4},{24,8},{28,12},{1,17},{... | collective-permute-start | bytes 442376 | tf_op jit(solution)/shard_map/ppermute | solution.py:879
  73.4 31.5 %collective-permute-start.8 = (bf16[576,128]{1,0:T(8,128)(2,1)S(1)}, bf16[576,128]{1,0:T(8,128)(2,1)S(1)}, u32[]{:S(2)}, u32[]{:S(2)}) collective-permute-start(bf16[576,128]{1,0:T(8,128)(2,1)S(1)} %get-tuple-element.507), channel_id=1, source_target_pairs={{0,12},{4,8},{8,4},{12,0},{16,28},{20,24},{24,20},{28,16},{1,13},{... | collective-permute-start | bytes 442376 | tf_op jit(solution)/shard_map/ppermute | solution.py:879
  84.1 20.7 %collective-permute-start.7 = (bf16[576,128]{1,0:T(8,128)(2,1)S(1)}, bf16[576,128]{1,0:T(8,128)(2,1)S(1)}, u32[]{:S(2)}, u32[]{:S(2)}) collective-permute-start(bf16[576,128]{1,0:T(8,128)(2,1)S(1)} %get-tuple-element.508), channel_id=1, source_target_pairs={{0,8},{4,12},{8,0},{12,4},{16,24},{20,28},{24,16},{28,20},{1,9},{5... | collective-permute-start | bytes 442376 | tf_op jit(solution)/shard_map/ppermute | solution.py:879
  84.7 20.1 %collective-permute-start.6 = (bf16[576,128]{1,0:T(8,128)(2,1)S(1)}, bf16[576,128]{1,0:T(8,128)(2,1)S(1)}, u32[]{:S(2)}, u32[]{:S(2)}) collective-permute-start(bf16[576,128]{1,0:T(8,128)(2,1)S(1)} %get-tuple-element.509), channel_id=1, source_target_pairs={{0,4},{4,0},{8,12},{12,8},{16,20},{20,16},{24,28},{28,24},{1,5},{5... | collective-permute-start | bytes 442376 | tf_op jit(solution)/shard_map/ppermute | solution.py:879
  160.1 35.2 %collective-permute-start.21 = (bf16[384,1024]{1,0:T(8,128)(2,1)S(1)}, bf16[384,1024]{1,0:T(8,128)(2,1)}, u32[]{:S(2)}, u32[]{:S(2)}) collective-permute-start(bf16[384,1024]{1,0:T(8,128)(2,1)S(1)} %add.490.refs_7_.refs_1_), channel_id=1, source_target_pairs={{0,2},{1,3},{2,0},{3,1},{4,6},{5,7},{6,4},{7,5},{8,10},{9,11},{10,... | collective-permute-start | bytes 2359304 | tf_op jit(solution)/shard_map/ppermute | solution.py:879
  161.5 766.5 %reduce-scatter.8.cloned.1.call-start = ((), (), s32[]{:S(2)}) async-start(), calls=%async_computation.5 | async-start | bytes 4718592 | tf_op jit(solution)/shard_map/reduce_scatter | solution.py:1296
  161.6 29.7 %collective-permute-start.22 = (bf16[768,256]{1,0:T(8,128)(2,1)}, bf16[768,256]{1,0:T(8,128)(2,1)S(1)}, u32[]{:S(2)}, u32[]{:S(2)}) collective-permute-start(bf16[768,256]{1,0:T(8,128)(2,1)} %fusion.2.refs_1_), channel_id=1, source_target_pairs={{0,1},{1,0},{2,3},{3,2},{4,5},{5,4},{6,7},{7,6},{8,9},{9,8},{10,11... | collective-permute-start | bytes 1179656 | tf_op jit(solution)/shard_map/ppermute | solution.py:879
  312.5 20.1 %collective-permute-start.38 = (bf16[384,1024]{1,0:T(8,128)(2,1)S(1)}, bf16[384,1024]{1,0:T(8,128)(2,1)}, u32[]{:S(2)}, u32[]{:S(2)}) collective-permute-start(bf16[384,1024]{1,0:T(8,128)(2,1)S(1)} %add.496.refs_5_.refs_1_), channel_id=1, source_target_pairs={{0,2},{1,3},{2,0},{3,1},{4,6},{5,7},{6,4},{7,5},{8,10},{9,11},{10,... | collective-permute-start | bytes 2359304 | tf_op jit(solution)/shard_map/ppermute | solution.py:879
  339.5 23.3 %collective-permute-start.47 = (bf16[384,1024]{1,0:T(8,128)(2,1)}, bf16[384,1024]{1,0:T(8,128)(2,1)}, u32[]{:S(2)}, u32[]{:S(2)}) collective-permute-start(bf16[384,1024]{1,0:T(8,128)(2,1)} %add.497.refs_5_.refs_1_), channel_id=1, source_target_pairs={{0,2},{1,3},{2,0},{3,1},{4,6},{5,7},{6,4},{7,5},{8,10},{9,11},{10,... | collective-permute-start | bytes 2359304 | tf_op jit(solution)/shard_map/ppermute | solution.py:879
  373.3 36.6 %collective-permute-start.50 = (bf16[384,1024]{1,0:T(8,128)(2,1)S(1)}, bf16[384,1024]{1,0:T(8,128)(2,1)}, u32[]{:S(2)}, u32[]{:S(2)}) collective-permute-start(bf16[384,1024]{1,0:T(8,128)(2,1)S(1)} %add.498.refs_8_.refs_1_), channel_id=1, source_target_pairs={{0,2},{1,3},{2,0},{3,1},{4,6},{5,7},{6,4},{7,5},{8,10},{9,11},{10,... | collective-permute-start | bytes 2359304 | tf_op jit(solution)/shard_map/ppermute | solution.py:879
  469.9 20.1 %collective-permute-start.51 = (bf16[384,1024]{1,0:T(8,128)(2,1)S(1)}, bf16[384,1024]{1,0:T(8,128)(2,1)}, u32[]{:S(2)}, u32[]{:S(2)}) collective-permute-start(bf16[384,1024]{1,0:T(8,128)(2,1)S(1)} %add.499.refs_8_.refs_1_), channel_id=1, source_target_pairs={{0,2},{1,3},{2,0},{3,1},{4,6},{5,7},{6,4},{7,5},{8,10},{9,11},{10,... | collective-permute-start | bytes 2359304 | tf_op jit(solution)/shard_map/ppermute | solution.py:879
  519.1 422.5 %reduce-scatter.6.cloned.1.call-start = ((), (), s32[]{:S(2)}) async-start(), calls=%async_computation.4 | async-start | bytes 4718592 | tf_op jit(solution)/shard_map/reduce_scatter | solution.py:1329
  519.9 24.6 %collective-permute-start.60 = (bf16[384,1024]{1,0:T(8,128)(2,1)}, bf16[384,1024]{1,0:T(8,128)(2,1)S(1)}, u32[]{:S(2)}, u32[]{:S(2)}) collective-permute-start(bf16[384,1024]{1,0:T(8,128)(2,1)} %copy-done.306), channel_id=1, source_target_pairs={{0,1},{1,0},{2,3},{3,2},{4,5},{5,4},{6,7},{7,6},{8,9},{9,8},{10,11... | collective-permute-start | bytes 2359304 | tf_op jit(solution)/shard_map/ppermute | solution.py:879
  588.8 23.7 %collective-permute-start.70 = (bf16[384,1024]{1,0:T(8,128)(2,1)S(1)}, bf16[384,1024]{1,0:T(8,128)(2,1)}, u32[]{:S(2)}, u32[]{:S(2)}) collective-permute-start(bf16[384,1024]{1,0:T(8,128)(2,1)S(1)} %add.503.refs_6_.refs_1_), channel_id=1, source_target_pairs={{0,2},{1,3},{2,0},{3,1},{4,6},{5,7},{6,4},{7,5},{8,10},{9,11},{10,... | collective-permute-start | bytes 2359304 | tf_op jit(solution)/shard_map/ppermute | solution.py:879
  641.4 302.1 %reduce-scatter.4.cloned.1.call-start = ((), (), s32[]{:S(2)}) async-start(), calls=%async_computation.3 | async-start | bytes 5160960 | tf_op jit(solution)/shard_map/reduce_scatter | solution.py:1399
  642.4 26.3 %collective-permute-start.75 = (bf16[384,1024]{1,0:T(8,128)(2,1)}, bf16[384,1024]{1,0:T(8,128)(2,1)S(1)}, u32[]{:S(2)}, u32[]{:S(2)}) collective-permute-start(bf16[384,1024]{1,0:T(8,128)(2,1)} %copy-done.305), channel_id=1, source_target_pairs={{0,1},{1,0},{2,3},{3,2},{4,5},{5,4},{6,7},{7,6},{8,9},{9,8},{10,11... | collective-permute-start | bytes 2359304 | tf_op jit(solution)/shard_map/ppermute | solution.py:879
  690.3 32.2 %collective-permute-start.78 = (bf16[384,1024]{1,0:T(8,128)(2,1)S(1)}, bf16[384,1024]{1,0:T(8,128)(2,1)}, u32[]{:S(2)}, u32[]{:S(2)}) collective-permute-start(bf16[384,1024]{1,0:T(8,128)(2,1)S(1)} %add.506.refs_10_.refs_1_), channel_id=1, source_target_pairs={{0,2},{1,3},{2,0},{3,1},{4,6},{5,7},{6,4},{7,5},{8,10},{9,11},{10,... | collective-permute-start | bytes 2359304 | tf_op jit(solution)/shard_map/ppermute | solution.py:879
  706.0 22.9 %collective-permute-start.80 = (bf16[384,1024]{1,0:T(8,128)(2,1)}, bf16[384,1024]{1,0:T(8,128)(2,1)}, u32[]{:S(2)}, u32[]{:S(2)}) collective-permute-start(bf16[384,1024]{1,0:T(8,128)(2,1)} %get-tuple-element.388), channel_id=1, source_target_pairs={{0,1},{1,0},{2,3},{3,2},{4,5},{5,4},{6,7},{7,6},{8,9},{9,8},{10,11... | collective-permute-start | bytes 2359304 | tf_op jit(solution)/shard_map/ppermute | solution.py:879
  727.9 25.0 %collective-permute-start.81 = (bf16[384,1024]{1,0:T(8,128)(2,1)S(1)}, bf16[384,1024]{1,0:T(8,128)(2,1)}, u32[]{:S(2)}, u32[]{:S(2)}) collective-permute-start(bf16[384,1024]{1,0:T(8,128)(2,1)S(1)} %add.507.refs_11_.refs_1_), channel_id=1, source_target_pairs={{0,2},{1,3},{2,0},{3,1},{4,6},{5,7},{6,4},{7,5},{8,10},{9,11},{10,... | collective-permute-start | bytes 2359304 | tf_op jit(solution)/shard_map/ppermute | solution.py:879
  758.9 28.2 %collective-permute-start.88 = (bf16[384,1024]{1,0:T(8,128)(2,1)S(1)}, bf16[384,1024]{1,0:T(8,128)(2,1)S(1)}, u32[]{:S(2)}, u32[]{:S(2)}) collective-permute-start(bf16[384,1024]{1,0:T(8,128)(2,1)S(1)} %add.508.refs_11_.refs_1_), channel_id=1, source_target_pairs={{0,2},{1,3},{2,0},{3,1},{4,6},{5,7},{6,4},{7,5},{8,10},{9,11},{10,... | collective-permute-start | bytes 2359304 | tf_op jit(solution)/shard_map/ppermute | solution.py:879
  810.2 20.6 %collective-permute-start.89 = (bf16[384,1024]{1,0:T(8,128)(2,1)S(1)}, bf16[384,1024]{1,0:T(8,128)(2,1)S(1)}, u32[]{:S(2)}, u32[]{:S(2)}) collective-permute-start(bf16[384,1024]{1,0:T(8,128)(2,1)S(1)} %add.509.refs_11_.refs_1_), channel_id=1, source_target_pairs={{0,2},{1,3},{2,0},{3,1},{4,6},{5,7},{6,4},{7,5},{8,10},{9,11},{10,... | collective-permute-start | bytes 2359304 | tf_op jit(solution)/shard_map/ppermute | solution.py:879
  811.3 34.4 %collective-permute-start.90 = (bf16[384,1024]{1,0:T(8,128)(2,1)S(1)}, bf16[384,1024]{1,0:T(8,128)(2,1)S(1)}, u32[]{:S(2)}, u32[]{:S(2)}) collective-permute-start(bf16[384,1024]{1,0:T(8,128)(2,1)S(1)} %add.510.refs_3_.refs_1_), channel_id=1, source_target_pairs={{0,2},{1,3},{2,0},{3,1},{4,6},{5,7},{6,4},{7,5},{8,10},{9,11},{10,... | collective-permute-start | bytes 2359304 | tf_op jit(solution)/shard_map/ppermute | solution.py:879
  852.7 20.3 %collective-permute-start.94 = (bf16[576,128]{1,0:T(8,128)(2,1)S(1)}, bf16[576,128]{1,0:T(8,128)(2,1)S(1)}, u32[]{:S(2)}, u32[]{:S(2)}) collective-permute-start(bf16[576,128]{1,0:T(8,128)(2,1)S(1)} %get-tuple-element.428), channel_id=1, source_target_pairs={{0,16},{4,20},{8,24},{12,28},{16,0},{20,4},{24,8},{28,12},{1,17},{... | collective-permute-start | bytes 442376 | tf_op jit(solution)/shard_map/ppermute | solution.py:879
  852.7 23.0 %collective-permute-start.95 = (bf16[576,128]{1,0:T(8,128)(2,1)S(1)}, bf16[576,128]{1,0:T(8,128)(2,1)S(1)}, u32[]{:S(2)}, u32[]{:S(2)}) collective-permute-start(bf16[576,128]{1,0:T(8,128)(2,1)S(1)} %get-tuple-element.429), channel_id=1, source_target_pairs={{0,20},{4,16},{8,28},{12,24},{16,4},{20,0},{24,12},{28,8},{1,21},{... | collective-permute-start | bytes 442376 | tf_op jit(solution)/shard_map/ppermute | solution.py:879
  (453 other events, 3183.9 us)
Sparse Core Ops, SparseCore 0:
  11.2 104.8 all-gather.6
  118.8 71.2 all-gather.8
  192.8 71.6 all-gather.10
  519.2 84.7 reduce-scatter.7
  641.6 84.9 reduce-scatter.5
  807.1 101.3 reduce-scatter.3

commit v3 on v2

--- a/solution.py
+++ b/solution.py
@@ -78,6 +78,14 @@
         self.array, self.shape, self.pick = array, tuple(shape), pick
 
 
+def hold(array, space):
+    return pltpu.with_memory_space_constraint(array, space)
+
+
+def free(array):
+    return pltpu.with_memory_space_constraint(array, pl.ANY)
+
+
 class Flow:
     def __init__(self, shape):
         self.shape = shape
@@ -88,6 +96,11 @@
         self.i = i
 
 
+class Carry:
+    def __init__(self, array):
+        self.array = array
+
+
 class Shared:
     def __init__(self, shape, kind):
         self.full, self.array = sds(shape, kind), None
@@ -106,19 +119,26 @@
     return math.prod(shape) * jnp.dtype(kind).itemsize
 
 
-def kernel(body, outs, operands, flops=0, scratch=(), name=None, exps=0, after=(), limit=32):
-    arrays, specs, windows = [], [], []
-    for a in operands:
-        if isinstance(a, Scalar):
+def kernel(body, outs, operands, flops=0, scratch=(), name=None, exps=0, after=(), margin=12):
+    arrays, specs, windows, shown = [], [], [], []
+    outs = list(outs)
+    for i, a in enumerate(operands):
+        shown.append(not isinstance(a, Carry))
+        if isinstance(a, Carry):
+            arrays.append(hold(a.array, pltpu.VMEM))
+            specs.append(in_vmem())
+            windows.append(None)
+            outs.append(Copy(i))
+        elif isinstance(a, Scalar):
             arrays.append(a.array)
             specs.append(scalars())
             windows.append(None)
         elif isinstance(a, Window):
-            arrays.append(a.array)
+            arrays.append(hold(a.array, pltpu.HBM))
             specs.append(in_hbm())
             windows.append(a)
         else:
-            arrays.append(a)
+            arrays.append(hold(a, pltpu.VMEM))
             specs.append(in_vmem())
             windows.append(None)
     aliases, out_shapes, out_specs, out_parts, owners = {}, [], [], [], []
@@ -129,23 +149,23 @@
                 if o.shared.array is not None:
                     aliases[len(arrays) + len(extra)] = len(out_shapes)
                     extra.append(o.shared.array)
-                out_shapes.append(o.shared.full)
+                out_shapes.append(pltpu.HBM(o.shared.full.shape, o.shared.full.dtype))
                 out_specs.append(in_hbm())
                 owners.append(o.shared)
             out_parts.append(("put", o.shape, o.shared.full.dtype, o.pick, owners.index(o.shared)))
             continue
         if isinstance(o, Flow):
             out_parts.append(("flow", None, None, None, len(out_shapes)))
-            out_shapes.append(o.shape)
+            out_shapes.append(pltpu.VMEM(o.shape.shape, o.shape.dtype))
             out_specs.append(in_vmem())
         elif isinstance(o, Copy):
-            a = operands[o.i]
+            a = arrays[o.i]
             out_parts.append(("copy", o.i, None, None, len(out_shapes)))
-            out_shapes.append(sds(a.shape, a.dtype))
+            out_shapes.append(pltpu.HBM(a.shape, a.dtype))
             out_specs.append(in_hbm())
         else:
             out_parts.append(("put", o.shape, o.dtype, everything, len(out_shapes)))
-            out_shapes.append(o)
+            out_shapes.append(pltpu.HBM(o.shape, o.dtype))
             out_specs.append(in_hbm())
         owners.append(None)
     moved = [w for w in windows if w is not None]
@@ -168,6 +188,8 @@
         views, copies, waited = [], {}, set()
         n = 0
         for i, (ref, w) in enumerate(zip(ins, windows)):
+            if not shown[i]:
+                continue
             if w is None:
                 views.append(ref)
             else:
@@ -210,6 +232,7 @@
 
     nbytes = sum(nbytes_of(w.shape, w.array.dtype) for w in moved)
     nbytes += sum(nbytes_of(p[1], p[2]) for p in made)
+    held = nbytes + sum(nbytes_of(m.shape, m.dtype) for m in scratch)
     results = pl.pallas_call(
         run_body,
         out_shape=tuple(out_shapes),
@@ -223,7 +246,7 @@
             pltpu.SemaphoreType.DMA((max(1, count_out),)),
         ]
         + list(scratch),
-        compiler_params=pltpu.CompilerParams(vmem_limit_bytes=limit << 20),
+        compiler_params=pltpu.CompilerParams(vmem_limit_bytes=held + (margin << 20)),
         cost_estimate=pl.CostEstimate(
             flops=int(flops), bytes_accessed=int(nbytes), transcendentals=int(exps)
         ),
@@ -411,7 +434,7 @@
 def head_backward_body(
     need, put, core_ref, total_ref, weight_ref, target_ref, logits_ref, *refs
 ):
-    *w_refs, grad_ref, keep_ref, send_ref, col_ref = refs
+    *w_refs, grad_ref, keep_ref, send_ref, loss_ref, col_ref = refs
     height = keep_ref.shape[0]
     books = len(w_refs)
     vocab = w_refs[0].shape[2]
@@ -422,6 +445,8 @@
         [total_ref[...], jnp.zeros((128 - total_ref.shape[0], frames), F32)], axis=0
     )
     col_ref[...] = jnp.transpose(wide)
+    gap = (col_ref[:, :books] - col_ref[:, books : 2 * books]) * weight_ref[...]
+    loss_ref[...] = jnp.broadcast_to(jnp.sum(gap).reshape(1, 1), loss_ref.shape)
     code = lax.broadcasted_iota(jnp.int32, (height, vocab), 1)
     need(4)
     for j, rows, to_ref in ((2, other, send_ref), (1, mine, keep_ref)):
@@ -589,6 +614,20 @@
     return center * lax.rsqrt(spread + 1e-05) * gain + shift
 
 
+def merge_body(books, own_ref, far_ref, out_ref):
+    own, far = own_ref[:books, :], far_ref[:books, :]
+    high = jnp.maximum(own, far)
+    out_ref[:books, :] = high + jnp.log(jnp.exp(own - high) + jnp.exp(far - high))
+    out_ref[books:, :] = own_ref[books:, :] + far_ref[books:, :]
+
+
+def text_in_body(need, put, place_ref, norm_ref, rows_ref, w_ref, out_ref):
+    columns = out_ref.shape[1]
+    at = pl.ds(pl.multiple_of(place_ref[0] * columns, columns), columns)
+    need(2, 3)
+    out_ref[...] = (nn(rows_ref[...], flat(w_ref)) + norm_ref[8:9, at]).astype(LOW)
+
+
 def add_body(keep_ref, got_ref, out_ref):
     out_ref[...] = (keep_ref[...].astype(F32) + got_ref[...].astype(F32)).astype(LOW)
 
@@ -692,15 +731,15 @@
     nbytes = sum(nbytes_of(a.shape, a.dtype) for a in operands + list(outs))
     return pl.pallas_call(
         later(body, len(after), len(operands)),
-        out_shape=tuple(outs),
+        out_shape=tuple(pltpu.VMEM(o.shape, o.dtype) for o in outs),
         in_specs=[in_vmem()] * len(operands) + [anywhere()] * len(after),
         out_specs=tuple(in_vmem() for _ in outs),
-        compiler_params=pltpu.CompilerParams(vmem_limit_bytes=16 << 20),
+        compiler_params=pltpu.CompilerParams(vmem_limit_bytes=12 << 20),
         cost_estimate=pl.CostEstimate(
             flops=20 * height * width, bytes_accessed=nbytes // 4, transcendentals=0
         ),
         name=name,
-    )(*operands, *after)
+    )(*(hold(a, pltpu.VMEM) for a in operands), *after)
 
 
 def embed_body(base_ref, codes_ref, *refs):
@@ -732,7 +771,7 @@
         + [in_vmem() for t in tables]
         + [anywhere()] * len(after),
         out_specs=pl.BlockSpec((1, rows, features), lambda i: (i, 0, 0)),
-        compiler_params=pltpu.CompilerParams(vmem_limit_bytes=32 << 20),
+        compiler_params=pltpu.CompilerParams(vmem_limit_bytes=12 << 20),
         cost_estimate=pl.CostEstimate(
             flops=4 * blocks * rows * books * vocab * features,
             bytes_accessed=2 * books * vocab * features + blocks * rows * (features + 512),
@@ -775,7 +814,7 @@
         + [pl.BlockSpec(g.shape, lambda i, k: (0, 0)) for g in grads],
         out_specs=pl.BlockSpec((1, 1, features, vocab), lambda i, k: (i, k, 0, 0)),
         scratch_shapes=[pltpu.VMEM((total, features), LOW)],
-        compiler_params=pltpu.CompilerParams(vmem_limit_bytes=32 << 20),
+        compiler_params=pltpu.CompilerParams(vmem_limit_bytes=12 << 20),
         cost_estimate=pl.CostEstimate(
             flops=4 * parts * books * vocab * features * total,
             bytes_accessed=2 * parts * books * features * vocab + 2 * total * features,
@@ -786,12 +825,14 @@
 
 
 def gather_features_body(need, put, where_ref, *refs):
-    *part_refs, out_ref = refs
+    clips = sum(r.shape[1] != refs[0].shape[1] for r in refs)
+    part_refs, outs = refs[:-clips], refs[-clips:]
     features = part_refs[0].shape[1]
+    strip = outs[0].shape[0]
     for m, part in enumerate(part_refs):
-        need(1 + m)
         at = pl.ds(pl.multiple_of(where_ref[m] * features, features), features)
-        out_ref[:, at] = part[...]
+        for c, out_ref in enumerate(outs):
+            out_ref[:, at] = part[c * strip : (c + 1) * strip, :]
 
 
 def split_features_body(need, put, where_ref, side_ref, *refs):
@@ -848,9 +889,13 @@
         put(len(part_refs) + j)
 
 
-def text_weight_body(need, put, rows_ref, grad_ref, out_ref):
-    need(0, 1)
-    out_ref[...] = tn(rows_ref[...], grad_ref[...]).astype(LOW).reshape(out_ref.shape)
+def text_weight_body(need, put, rows_ref, own_ref, far_ref, out_ref, bias_ref):
+    need(0)
+    grad = (own_ref[...].astype(F32) + far_ref[...].astype(F32)).astype(LOW)
+    out_ref[...] = tn(rows_ref[...], grad).astype(LOW).reshape(out_ref.shape)
+    bias_ref[...] = jnp.broadcast_to(
+        jnp.sum(grad.astype(F32), axis=0, keepdims=True), bias_ref.shape
+    )
 
 
 def positions_rows(start, count, feature_count):
@@ -1005,6 +1050,16 @@
     group_order = group ^ jnp.arange(dp, dtype=jnp.int32)
     place_order = place ^ jnp.arange(tensor, dtype=jnp.int32)
 
+    text_bias_row = jnp.where(text_mask > 0, 0.0, NEG).astype(F32)
+    bias_lines = [text_bias_row[c : c + 1] for c in range(clips)]
+    bias_columns = [jnp.transpose(line) for line in bias_lines]
+    targets = (jnp.roll(audio_codes, -1, axis=1) - place * vocab).astype(jnp.int32)
+    targets = [targets[c] for c in range(clips)]
+    grad_weight = weight_int.astype(F32) / valid_count
+    grad_weight = [grad_weight[c] for c in range(clips)]
+    placed = positions_rows(core * height, height, width)
+    last[:] = bias_lines + bias_columns + targets + grad_weight + [placed, back_lines]
+
     table_parts = spread_tensor(tables[:books].astype(LOW))
     step = max(1, dp // 4)
     arrived = [None] * dp
@@ -1018,16 +1073,16 @@
             arrived[m] = swap(piece, "dp", m) if m else piece
     aligned = share % 128 == 0
     if aligned:
-        (strips,) = run(
+        strips = run(
             gather_features_body,
-            [Flow(sds((clips * strip, width), LOW))],
+            [Flow(sds((strip, width), LOW))] * clips,
             [Scalar(group_order)] + arrived,
             name="gather_features",
         )
+        strips = [free(a) for a in strips]
     else:
         strips = jnp.take(jnp.stack(arrived), group_order, axis=0)
-        strips = jnp.transpose(strips, (1, 0, 2)).reshape(clips * strip, width)
-    placed = positions_rows(core * height, height, width)
+        strips = jnp.transpose(strips, (1, 0, 2)).reshape(clips, strip, width)
 
     norm_rows = attn_all[:, 8 * share + text_share :, :share]
     norm_rows = jnp.transpose(norm_rows, (1, 0, 2)).reshape(16, width).astype(F32)
@@ -1053,7 +1108,7 @@
             partial(norm_body, which), [half_sds, half_low], [hidden, *parts], norm_rows, last
         )
         last[:] = [out]
-        return new, (out, swap_core(out))
+        return new, (out, swap_core(free(out)))
 
     def norm_back(which, hidden, parts, before):
         operands = [hidden, *parts] + ([before] if before is not None else [])
@@ -1065,7 +1120,7 @@
             last,
         )
         last[:] = [out]
-        return new, (out, swap_core(out)), sums
+        return new, (out, swap_core(free(out))), free(sums)
 
     waiting = []
     moving = [None] * clips
@@ -1075,18 +1130,30 @@
             c, keep, got = waiting.pop()
             (part,) = norm_rows_kernel(add_body, [half_low], [keep, got], None, last, name="add")
             last[:] = [part]
-            moving[c] = across(part)
+            moving[c] = (part, *across(free(part))[1:])
 
     def reduce_rows(c, keep, send):
-        waiting.append((c, keep, swap_core(send)))
+        waiting.append((c, keep, swap_core(free(send))))
 
     text_rows = text_states.reshape(clips * text_len, text_width)
-    text_weight = attn_all[:, 8 * share : 8 * share + text_share, :].reshape(text_width, columns)
-    text_bias = lax.dynamic_slice_in_dim(norm_rows[8], place * columns, columns, 0)
-    text_local = (nn(text_rows, text_weight) + text_bias).astype(LOW)
-    text_parts = spread_tensor(text_local)
-    text_bias_row = jnp.where(text_mask > 0, 0.0, NEG).astype(F32)
-    bias_columns = jnp.transpose(text_bias_row)
+    def text_in_step():
+        (result,) = run(
+            text_in_body,
+            [Flow(sds((clips * text_len, columns), LOW))],
+            [
+                Scalar(place.astype(jnp.int32).reshape(1)),
+                norm_rows,
+                fetch(text_rows),
+                Window(
+                    attn_all,
+                    (dp, text_share, columns),
+                    lambda ref: ref.at[:, pl.ds(8 * share, text_share), :],
+                ),
+            ],
+            flops=2 * clips * text_len * text_width * columns,
+            name="text_in",
+        )
+        return spread_tensor(free(result))
 
     full = sds((frames, columns), LOW)
     lse_sds = sds((8, frames), F32)
@@ -1098,7 +1165,7 @@
     every = range(clips)
 
     def embed_step(c):
-        mine = strips[c * strip : (c + 1) * strip]
+        mine = strips[c]
         parts = [mine] + [swap(mine, "tensor", 2 * s) for s in range(1, sides)]
         new, out = run(
             embed_norm_body,
@@ -1107,14 +1174,15 @@
             flops=10 * height * width,
             name="embed_norm",
         )
-        return new, (out, swap_core(out))
+        return new, (out, swap_core(free(out)))
 
     def self_step(c, pair):
         own, got = pair
-        *saved, keep, send, left, right = run(
+        *saved, keep, send, left, right, hidden[0][c] = run(
             self_forward_body,
             [full, full, full, full, lse_sds, flow, flow, Copy(1), Copy(3)],
-            [core_arg, own, w_attn(0), got, w_attn(1), w_attn(2), w_attn(6)],
+            [core_arg, own, w_attn(0), got, w_attn(1), w_attn(2), w_attn(6)]
+            + [Carry(hidden[0][c])],
             flops=8 * frames * width * columns + 4 * score_flops * frames,
             scratch=tot,
             name="self_forward",
@@ -1143,10 +1211,11 @@
     def cross_step(c, pair):
         own, got = pair
         k, v = text_rows_of(text_key, c), text_rows_of(text_value, c)
-        q, o, lse, keep, send, left, right = run(
+        q, o, lse, keep, send, left, right, hidden[1][c] = run(
             cross_forward_body,
             [full, full, lse_sds, flow, flow, Copy(1), Copy(3)],
-            [core_arg, own, w_attn(3), got, text_bias_row[c : c + 1], k, v, w_attn(7)],
+            [core_arg, own, w_attn(3), got, bias_lines[c], k, v, w_attn(7)]
+            + [Carry(hidden[1][c])],
             flops=4 * frames * width * columns + 4 * score_flops * text_len,
             scratch=tot,
             name="cross_forward",
@@ -1156,10 +1225,10 @@
         return (q, k, v, o, lse)
 
     def ffn_step(c, pair):
-        *saved, keep, send, left, right = run(
+        *saved, keep, send, left, right, hidden[2][c] = run(
             ffn_forward_body,
             [inner, inner, flow, flow, Copy(1), Copy(2)],
-            [core_arg, *pair, w_member(ffn_all, 0), w_member(ffn_all, 1)],
+            [core_arg, *pair, w_member(ffn_all, 0), w_member(ffn_all, 1), Carry(hidden[2][c])],
             flops=4 * frames * width * units,
             name="ffn_forward",
         )
@@ -1174,6 +1243,8 @@
         hidden[0][c], pairs[0][c] = embed_step(c)
         flush()
         kept[0][c] = self_step(c, pairs[0][c])
+        if c == 0:
+            text_parts = text_in_step()
     text_hidden, text_key, text_value = text_step()
     for c in every:
         hidden[1][c], pairs[1][c] = norm_step(1, hidden[0][c], moving[c])
@@ -1184,15 +1255,12 @@
         flush()
         kept[2][c] = ffn_step(c, pairs[2][c])
 
-    targets = (jnp.roll(audio_codes, -1, axis=1) - place * vocab).astype(jnp.int32)
-    loss_weight = weight_int.astype(F32)
-    grad_weight = loss_weight / valid_count
     loss_part = [None] * clips
     sums = [[], [], [], []]
 
     def head_step(c, pair):
         own, got = pair
-        logits, stats, left, right = run(
+        logits, stats, left, right, hidden[3][c] = run(
             head_forward_body,
             [
                 sds((frames, books * vocab), F32),
@@ -1200,33 +1268,43 @@
                 Copy(1),
                 Copy(3),
             ],
-            [core_arg, own, targets[c], got] + [w_member(head_all, k) for k in range(books)],
+            [core_arg, own, targets[c], got]
+            + [w_member(head_all, k) for k in range(books)]
+            + [Carry(hidden[3][c])],
             flops=2 * frames * width * books * vocab,
             scratch=tot,
             name="head_forward",
         )
         pairs[3][c] = (left, right)
-        total, pick = stats[:books], stats[books:]
+        return logits, stats
+
+    def merge_step(stats):
         mask = 1
         while mask < tensor:
-            far = swap(jnp.concatenate([total, pick], axis=0), "tensor", mask)
-            high = jnp.maximum(total, far[:books])
-            total = high + jnp.log(jnp.exp(total - high) + jnp.exp(far[:books] - high))
-            pick = pick + far[books:]
+            far = swap(free(stats), "tensor", mask)
+            (stats,) = norm_rows_kernel(
+                partial(merge_body, books),
+                [sds((2 * books, frames), F32)],
+                [stats, far],
+                None,
+                last,
+                name="merge",
+            )
+            last[:] = [stats]
             mask *= 2
-        loss_part[c] = jnp.sum((total - pick) * jnp.transpose(loss_weight[c]))
-        return logits, jnp.concatenate([total, total], axis=0)
+        return stats
 
     def head_back_step(c, logits, total):
-        grad, keep, send = run(
+        grad, keep, send, loss = run(
             head_backward_body,
-            [sds((frames, books * vocab), LOW), flow, flow],
+            [sds((frames, books * vocab), LOW), flow, flow, Flow(sds((8, 128), F32))],
             [core_arg, total, grad_weight[c], targets[c], fetch(logits)]
             + [w_member(head_all, k) for k in range(books)],
             flops=2 * frames * width * books * vocab,
             scratch=tot,
             name="head_backward",
         )
+        loss_part[c] = free(loss)[0, 0]
         reduce_rows(c, keep, send)
         return grad
 
@@ -1254,7 +1332,7 @@
             flops=2 * clips * frames * width * total,
             scratch=[pltpu.VMEM((width if turn_left else total, clips * frames), LOW)],
             name=name,
-            limit=48,
+            margin=26,
         )
 
     logit_grads = [None] * clips
@@ -1265,16 +1343,20 @@
         ready[c] = head_step(c, pairs[3][c])
         if c:
             flush()
-            logit_grads[c - 1] = head_back_step(c - 1, *ready[c - 1])
+            logits, stats = ready[c - 1]
+            logit_grads[c - 1] = head_back_step(c - 1, logits, merge_step(stats))
+    logits, stats = ready[-1]
+    stats = merge_step(stats)
     flush()
-    logit_grads[-1] = head_back_step(clips - 1, *ready[-1])
+    logit_grads[-1] = head_back_step(clips - 1, logits, stats)
 
     def ffn_back_step(c, pair):
         own, got = pair
-        grad, keep, send, left, right = run(
+        grad, keep, send, left, right, grads[c] = run(
             ffn_backward_body,
             [inner, flow, flow, Copy(1), Copy(2)],
-            [core_arg, own, got, w_member(ffn_all, 1), fetch(kept[2][c][1]), w_member(ffn_all, 0)],
+            [core_arg, own, got, w_member(ffn_all, 1), fetch(kept[2][c][1]), w_member(ffn_all, 0)]
+            + [Carry(grads[c])],
             flops=4 * frames * width * units,
             name="ffn_backward",
         )
@@ -1293,7 +1375,7 @@
         if c == 0:
             head_into = [member_into(head_shared, k) for k in range(books)]
             weights(pairs[3], logit_grads, head_into, "head_weights")
-    head_sum = lax.psum_scatter(head_shared.array, "dp", scatter_dimension=0, tiled=False)
+    head_sum = lax.psum_scatter(free(head_shared.array), "dp", scatter_dimension=0, tiled=False)
 
     acc_text = [pltpu.VMEM((text_len, columns), F32)] * 2
     small = sds((text_len, columns), LOW)
@@ -1301,11 +1383,12 @@
     def cross_back_step(c, pair):
         own, got = pair
         q, k, v, o, lse = kept[1][c]
-        bias = bias_columns[:, c : c + 1]
-        dq, dk, dv, keep, send, left, right = run(
+        bias = bias_columns[c]
+        dq, dk, dv, keep, send, left, right, grads[c] = run(
             cross_backward_body,
             [full, small, small, flow, flow, Copy(1), Copy(3)],
-            [core_arg, own, w_attn(7), got, bias, fetch(q), k, v, fetch(lse), w_attn(3)],
+            [core_arg, own, w_attn(7), got, bias, fetch(q), k, v, fetch(lse), w_attn(3)]
+            + [Carry(grads[c])],
             flops=4 * frames * width * columns + 10 * score_flops * text_len,
             scratch=[pltpu.VMEM((frames, columns), LOW)] + acc_text,
             name="cross_backward",
@@ -1326,7 +1409,7 @@
             )
         if c == min(1, clips - 1):
             weights(pairs[2], inner_grads, [member_into(ffn_shared, 0)], "ffn_one")
-    ffn_sum = lax.psum_scatter(ffn_shared.array, "dp", scatter_dimension=0, tiled=False)
+    ffn_sum = lax.psum_scatter(free(ffn_shared.array), "dp", scatter_dimension=0, tiled=False)
 
     def text_back_step():
         results = run(
@@ -1340,19 +1423,34 @@
             scratch=[pltpu.VMEM((clips * text_len, width), LOW)],
             name="text_back",
         )
-        return collect_tensor(results).astype(LOW)
+        live = dict(enumerate(results))
+        mask = 1
+        while mask < tensor:
+            fresh = {}
+            for m in live:
+                if not m & mask:
+                    fresh[m] = (live[m], swap(free(live[m | mask]), "tensor", mask))
+            mask *= 2
+            if mask < tensor:
+                for m, both in fresh.items():
+                    (fresh[m],) = norm_rows_kernel(
+                        add_body, [text_cols], list(both), None, last, name="add"
+                    )
+                    last[:] = [fresh[m]]
+            live = fresh
+        return live[0]
 
     acc_self = [pltpu.VMEM((frames, columns), F32)] * 2
 
     def self_back_step(c, pair):
         own, got = pair
         q, k, v, o, lse = kept[0][c]
-        grad, keep, send, left, right = run(
+        grad, keep, send, left, right, grads[c] = run(
             self_backward_body,
             [sds((frames, 3 * columns), LOW), flow, flow, Copy(1), Copy(3)],
             [core_arg, own, w_attn(6), got]
             + [fetch(a) for a in (q, k, v, lse)]
-            + [w_attn(0), w_attn(1), w_attn(2)],
+            + [w_attn(0), w_attn(1), w_attn(2), Carry(grads[c])],
             flops=8 * frames * width * columns + 10 * score_flops * frames,
             scratch=[pltpu.VMEM((frames, columns), LOW)] + acc_self,
             name="self_backward",
@@ -1372,7 +1470,6 @@
             weights(back_pairs[2], [k[3] for k in kept[1]], [attn_into(7)], "cross_out")
         if c == min(1, clips - 1):
             weights(pairs[1], [g[0] for g in cross_grads], [attn_into(3)], "cross_query")
-    bias_grad = jnp.sum(text_grad.astype(F32), axis=0)
 
     zero_lows = [None] * clips
 
@@ -1387,21 +1484,21 @@
         (dp, text_share, columns),
         lambda ref: ref.at[:, pl.ds(8 * share, text_share), :],
     )
-    run(
+    (bias_grad,) = run(
         text_weight_body,
-        [text_into],
-        [text_rows, text_grad],
+        [text_into, Flow(sds((8, columns), F32))],
+        [fetch(text_rows), *text_grad],
         flops=2 * clips * text_len * text_width * columns,
         name="text_weight",
     )
     weights(back_pairs[1], [k[3] for k in kept[0]], [attn_into(6)], "self_out")
     weights(pairs[0], self_grads, [attn_into(n) for n in range(3)], "self_in")
-    attn_sum = lax.psum_scatter(attn_shared.array, "dp", scatter_dimension=0, tiled=False)
+    attn_sum = lax.psum_scatter(free(attn_shared.array), "dp", scatter_dimension=0, tiled=False)
     for c in range(1, clips):
         zero_step(c)
 
     if aligned:
-        pieces = run(
+        pieces = list(map(free, run(
             split_features_body,
             [Flow(sds((clips * strip, share), LOW))] * dp,
             [
@@ -1410,10 +1507,10 @@
             ]
             + zero_lows,
             name="split_features",
-        )
+        )))
     else:
         rows = jnp.concatenate(
-            [lax.dynamic_slice_in_dim(a, side * strip, strip, 0) for a in zero_lows], axis=0
+            [lax.dynamic_slice_in_dim(free(a), side * strip, strip, 0) for a in zero_lows], axis=0
         )
         rows = jnp.transpose(rows.reshape(clips * strip, dp, share), (1, 0, 2))
         pieces = list(jnp.take(rows, group_order, axis=0))
@@ -1425,7 +1522,7 @@
         [sum(s)[0:1] for s in sums] + [sum(s)[1:2] for s in sums], axis=0
     ) * (1.0 / sides)
     bias_row = lax.dynamic_update_slice_in_dim(
-        jnp.zeros((width,), F32), bias_grad, place * columns, 0
+        jnp.zeros((width,), F32), free(bias_grad)[0], place * columns, 0
     )
     norm_total = total_over(
         jnp.concatenate([norm_part, bias_row[None]], axis=0), ("tensor", "dp")
@@ -1448,7 +1545,7 @@
         jnp.stack([local_square, sum(loss_part) / tensor]).reshape(1, 2), ("tensor", "dp")
     )[0]
     grad_norm = jnp.sqrt(both[0])
-    mean_loss = both[1] / valid_count
+    mean_loss = both[1]
     factor = clip_limit / jnp.maximum(grad_norm, clip_limit)
     grad_tables = jnp.concatenate([grad_embed, grad_heads], 0)
     attn_new, attn_first_new, attn_second_new = adam_update(

time: 1010 us -> 981 us (0.971)
  local copies, waits for them, and re-layouts: 185 us -> 108 us
  Pallas kernels: 361 us -> 403 us
  starting transfers between devices: 77 us -> 100 us
    unnamed x737 -> x318, local copies, waits for them, and re-layouts: 160 us -> 86.1 us
    pallas_call x39 -> x40, Pallas kernels: 245 us -> 289 us  [kernel(): pl.pallas_call(run_body, out_shape=tuple(out_shapes), in_specs=specs + [a...]
    ppermute x111, starting transfers between devices: 76.8 us -> 99.7 us  [swap(): return lax.ppermute(values, axis, [(i, i ^ mask) for i in range(size)])]
    pallas_call x42 -> x50, Pallas kernels: 59.3 us -> 41.3 us  [norm_rows_kernel(): pl.pallas_call(later(body, len(after), len(operands)), out_shape=tuple((p...]
    pallas_call x4, Pallas kernels: 32.7 us -> 49.2 us  [embed(): pl.pallas_call(later(embed_body, len(after), 2 + len(tables)), out_shape=...]
  transfers between devices with their start and end apart: 117 -> 117, of which waited for: 51 -> 60; matrix products, arithmetic and copies ran while one was open for 5% -> 4% of each run, Pallas kernels for 34% -> 38%
where the time goes in v3:
time: 981 us; the launch traced here: 970 us
  Pallas kernels  403 us (41%)
  waiting for transfers between devices  289 us (29%)
  local copies, waits for them, and re-layouts  108 us (11%)
  starting transfers between devices  100 us (10%)
  other arithmetic  43.5 us (4%)
  between operations  25.9 us (3%)
    ppermute x111, waiting for transfers between devices, swap(): return lax.ppermute(values, axis, [(i, i ^ mask) for i in range(size)])  289 us
    pallas_call x40, Pallas kernels, kernel(): pl.pallas_call(run_body, out_shape=tuple(out_shapes), in_specs=specs + [a...  289 us
    ppermute x111, starting transfers between devices, swap(): return lax.ppermute(values, axis, [(i, i ^ mask) for i in range(size)])  99.7 us
    unnamed x318, local copies, waits for them, and re-layouts  86.1 us
    pallas_call x4, Pallas kernels, embed(): pl.pallas_call(later(embed_body, len(after), 2 + len(tables)), out_shape=...  49.2 us
    pallas_call x50, Pallas kernels, norm_rows_kernel(): pl.pallas_call(later(body, len(after), len(operands)), out_shape=tuple((p...  41.3 us
    pallas_call x1, Pallas kernels, embed_back(): pl.pallas_call(embed_back_body, out_shape=sds((parts, books, features, vo...  24.2 us
  transfers between devices with their start and end apart: 117, of which 60 were waited for; matrix products, arithmetic and copies ran while one was open for 4% of the time, Pallas kernels for 38%

profile of v3, /device:TPU:0, one launch (start us, length us, event | category | flops | bytes accessed | tf_op | source)
XLA Modules:
  0.0 969.8 jit_solution(677787606945820493)
XLA Ops:
  58.0 9.2 embed.4.refs_6_
  67.2 9.0 embed.5.refs_6_
  76.3 21.9 %embed.6.refs_6_ = bf16[2,576,128]{2,1,0:T(8,128)(2,1)S(1)} custom-call(s32[4]{0:T(128)S(1)} %broadcast_multiply_fusion.1.refs_0_.base_ref, s32[2,576,4]{2,1,0:T(8,128)S(1)} %get-tuple-element.529.refs_1_, bf16[4,128,512]{2,1,0:T(8,128)(2,1)} %get-tuple-element.540.refs_2_, bf16[4,128,512]{2,1,0:T(8,128)(2,1)} %collective-permute-done.3.refs_3_, ...), custom_call_target="tpu_custom_call" | custom-call | flops 4831838208 | bytes 2834432 | tf_op jit(solution)/shard_map/embed/pallas_call | solution.py:766
  98.2 9.0 embed.7.refs_9_
  120.4 9.5 collective-permute-done.7.refs_3_
  180.1 9.0 self_forward.4
  196.0 9.8 %collective-permute-done.23.refs_3_ = bf16[768,256]{1,0:T(8,128)(2,1)S(1)} collective-permute-done((bf16[768,256]{1,0:T(8,128)(2,1)S(1)}, bf16[768,256]{1,0:T(8,128)(2,1)S(1)}, u32[]{:S(2)}, u32[]{:S(2)}) %collective-permute-start.23) | collective-permute-done | bytes 393248 | tf_op jit(solution)/shard_map/ppermute | solution.py:924
  208.7 9.1 self_forward.5
  235.3 12.2 %collective-permute-done.28.refs_2_ = bf16[384,1024]{1,0:T(8,128)(2,1)S(1)} collective-permute-done((bf16[384,1024]{1,0:T(8,128)(2,1)S(1)}, bf16[384,1024]{1,0:T(8,128)(2,1)S(1)}, u32[]{:S(2)}, u32[]{:S(2)}) %collective-permute-start.28) | collective-permute-done | bytes 786464 | tf_op jit(solution)/shard_map/ppermute | solution.py:924
  257.6 12.0 %collective-permute-done.30.refs_2_ = bf16[384,1024]{1,0:T(8,128)(2,1)S(1)} collective-permute-done((bf16[384,1024]{1,0:T(8,128)(2,1)S(1)}, bf16[384,1024]{1,0:T(8,128)(2,1)S(1)}, u32[]{:S(2)}, u32[]{:S(2)}) %collective-permute-start.30) | collective-permute-done | bytes 786464 | tf_op jit(solution)/shard_map/ppermute | solution.py:924
  279.8 11.9 %collective-permute-done.29.refs_2_ = bf16[384,1024]{1,0:T(8,128)(2,1)S(1)} collective-permute-done((bf16[384,1024]{1,0:T(8,128)(2,1)S(1)}, bf16[384,1024]{1,0:T(8,128)(2,1)S(1)}, u32[]{:S(2)}, u32[]{:S(2)}) %collective-permute-start.29) | collective-permute-done | bytes 786464 | tf_op jit(solution)/shard_map/ppermute | solution.py:924
  329.4 9.5 collective-permute-done.39.refs_2_
  353.2 9.0 collective-permute-done.38.refs_2_
  371.3 11.4 %head_forward.3 = (f32[768,2048]{1,0:T(8,128)}, f32[8,768]{1,0:T(8,128)S(1)}, bf16[384,1024]{1,0:T(8,128)(2,1)}, bf16[384,1024]{1,0:T(8,128)(2,1)}, f32[384,1024]{1,0:T(8,128)}) custom-call(s32[1]{0:T(128)} %bitcast.refs_0_, bf16[384,1024]{1,0:T(8,128)(2,1)} %get-tuple-element.316.refs_2_.refs_1_, s32[768,4]{1,0:T(8,128)S(1)} %copy-done.65, ...), custom_call_target="tpu_custom_call" | custom-call | flops 3221225472 | bytes 10485760 | tf_op jit(solution)/shard_map/head_forward/pallas_call | solution.py:236
  392.4 9.6 head_forward.4
  424.0 9.3 head_forward.5
  451.3 16.7 %collective-permute-done.56.refs_1_ = f32[8,768]{1,0:T(8,128)S(1)} collective-permute-done((f32[8,768]{1,0:T(8,128)S(1)}, f32[8,768]{1,0:T(8,128)S(1)}, u32[]{:S(2)}, u32[]{:S(2)}) %collective-permute-start.56) | collective-permute-done | bytes 24608 | tf_op jit(solution)/shard_map/ppermute | solution.py:924
  468.3 9.2 head_backward.5
  491.7 15.8 %head_weights.1.refs_4_ = bf16[8,4,128,512]{3,2,1,0:T(8,128)(2,1)} custom-call(s32[1]{0:T(128)} %bitcast.refs_0_, bf16[384,1024]{1,0:T(8,128)(2,1)} %get-tuple-element.347.refs_1_, bf16[384,1024]{1,0:T(8,128)(2,1)} %get-tuple-element.348.refs_2_, bf16[384,1024]{1,0:T(8,128)(2,1)} %get-tuple-element.349.refs_3_, ...), custom_call_target="tpu_custom_call" | custom-call | flops 9663676416 | bytes 18350080 | tf_op jit(solution)/shard_map/head_weights/pallas_call | solution.py:236
  509.6 18.5 %collective-permute-done.61.refs_2_ = bf16[384,1024]{1,0:T(8,128)(2,1)S(1)} collective-permute-done((bf16[384,1024]{1,0:T(8,128)(2,1)}, bf16[384,1024]{1,0:T(8,128)(2,1)S(1)}, u32[]{:S(2)}, u32[]{:S(2)}) %collective-permute-start.61) | collective-permute-done | bytes 786464 | tf_op jit(solution)/shard_map/ppermute | solution.py:924
  544.0 10.2 %collective-permute-done.63.refs_2_ = bf16[384,1024]{1,0:T(8,128)(2,1)S(1)} collective-permute-done((bf16[384,1024]{1,0:T(8,128)(2,1)S(1)}, bf16[384,1024]{1,0:T(8,128)(2,1)S(1)}, u32[]{:S(2)}, u32[]{:S(2)}) %collective-permute-start.63) | collective-permute-done | bytes 786464 | tf_op jit(solution)/shard_map/ppermute | solution.py:924
  566.8 10.1 %collective-permute-done.62.refs_2_ = bf16[384,1024]{1,0:T(8,128)(2,1)S(1)} collective-permute-done((bf16[384,1024]{1,0:T(8,128)(2,1)S(1)}, bf16[384,1024]{1,0:T(8,128)(2,1)S(1)}, u32[]{:S(2)}, u32[]{:S(2)}) %collective-permute-start.62) | collective-permute-done | bytes 786464 | tf_op jit(solution)/shard_map/ppermute | solution.py:924
  591.5 10.9 %ffn_two.1.refs_5_.refs_10_ = bf16[8,2,128,1024]{3,2,1,0:T(8,128)(2,1)} custom-call(s32[1]{0:T(128)} %bitcast.refs_0_, bf16[384,1024]{1,0:T(8,128)(2,1)} %get-tuple-element.375.refs_1_, bf16[384,1024]{1,0:T(8,128)(2,1)} %get-tuple-element.376.refs_2_, bf16[384,1024]{1,0:T(8,128)(2,1)} %get-tuple-element.377.refs_3_, ...), custom_call_target="tpu_custom_call" | custom-call | flops 4831838208 | bytes 11534336 | tf_op jit(solution)/shard_map/ffn_two/pallas_call | solution.py:236
  619.6 10.7 %ffn_one.1.refs_5_ = bf16[8,2,128,1024]{3,2,1,0:T(8,128)(2,1)} custom-call(s32[1]{0:T(128)} %bitcast.refs_0_, bf16[384,1024]{1,0:T(8,128)(2,1)} %get-tuple-element.386.refs_1_, bf16[384,1024]{1,0:T(8,128)(2,1)} %get-tuple-element.387.refs_2_, bf16[384,1024]{1,0:T(8,128)(2,1)} %get-tuple-element.388.refs_3_, ...), custom_call_target="tpu_custom_call", output_to_operand_aliasing={{}: (10, {})} | custom-call | flops 4831838208 | bytes 11534336 | tf_op jit(solution)/shard_map/ffn_one/pallas_call | solution.py:236
  631.7 18.7 %collective-permute-done.72.refs_2_ = bf16[384,1024]{1,0:T(8,128)(2,1)S(1)} collective-permute-done((bf16[384,1024]{1,0:T(8,128)(2,1)}, bf16[384,1024]{1,0:T(8,128)(2,1)S(1)}, u32[]{:S(2)}, u32[]{:S(2)}) %collective-permute-start.72) | collective-permute-done | bytes 786464 | tf_op jit(solution)/shard_map/ppermute | solution.py:924
  668.3 9.7 %collective-permute-done.71.refs_2_ = bf16[384,1024]{1,0:T(8,128)(2,1)S(1)} collective-permute-done((bf16[384,1024]{1,0:T(8,128)(2,1)S(1)}, bf16[384,1024]{1,0:T(8,128)(2,1)S(1)}, u32[]{:S(2)}, u32[]{:S(2)}) %collective-permute-start.71) | collective-permute-done | bytes 786464 | tf_op jit(solution)/shard_map/ppermute | solution.py:924
  683.1 11.1 %self_backward.3 = (bf16[768,768]{1,0:T(8,128)(2,1)}, bf16[384,1024]{1,0:T(8,128)(2,1)S(1)}, bf16[384,1024]{1,0:T(8,128)(2,1)S(1)}, bf16[384,1024]{1,0:T(8,128)(...) custom-call(s32[1]{0:T(128)} %bitcast.refs_0_, bf16[384,1024]{1,0:T(8,128)(2,1)S(1)} %get-tuple-element.406.refs_2_.refs_1_, ...), custom_call_target="tpu_custom_call" | custom-call | flops 4630511616 | bytes 4481024 | tf_op jit(solution)/shard_map/self_backward/pallas_call | solution.py:236
  715.7 11.1 %self_backward.4 = (bf16[768,768]{1,0:T(8,128)(2,1)}, bf16[384,1024]{1,0:T(8,128)(2,1)S(1)}, bf16[384,1024]{1,0:T(8,128)(2,1)S(1)}, bf16[384,1024]{1,0:T(8,128)(...) custom-call(s32[1]{0:T(128)} %bitcast.refs_0_, bf16[384,1024]{1,0:T(8,128)(2,1)S(1)} %get-tuple-element.437.refs_2_.refs_1_, ...), custom_call_target="tpu_custom_call" | custom-call | flops 4630511616 | bytes 4481024 | tf_op jit(solution)/shard_map/self_backward/pallas_call | solution.py:236
  740.6 11.4 %self_backward.5 = (bf16[768,768]{1,0:T(8,128)(2,1)}, bf16[384,1024]{1,0:T(8,128)(2,1)S(1)}, bf16[384,1024]{1,0:T(8,128)(2,1)S(1)}, bf16[384,1024]{1,0:T(8,128)(...) custom-call(s32[1]{0:T(128)} %bitcast.refs_0_, bf16[384,1024]{1,0:T(8,128)(2,1)S(1)} %get-tuple-element.456.refs_2_.refs_1_, ...), custom_call_target="tpu_custom_call" | custom-call | flops 4630511616 | bytes 4481024 | tf_op jit(solution)/shard_map/self_backward/pallas_call | solution.py:236
  775.3 9.6 self_in.1.refs_5_
  787.7 17.7 %collective-permute-done.89.refs_2_ = bf16[384,1024]{1,0:T(8,128)(2,1)S(1)} collective-permute-done((bf16[384,1024]{1,0:T(8,128)(2,1)S(1)}, bf16[384,1024]{1,0:T(8,128)(2,1)S(1)}, u32[]{:S(2)}, u32[]{:S(2)}) %collective-permute-start.89) | collective-permute-done | bytes 786464 | tf_op jit(solution)/shard_map/ppermute | solution.py:924
  863.3 24.2 %embed_back.1 = bf16[4,4,128,512]{3,2,1,0:T(8,128)(2,1)S(1)} custom-call(s32[4]{0:T(128)S(1)} %copy-done.130, s32[4,8,4608]{2,1,0:T(8,128)S(1)} %copy-done.96, bf16[576,128]{1,0:T(8,128)(2,1)S(1)} %get-tuple-element.482.refs_0_, bf16[576,128]{1,0:T(8,128)(2,1)S(1)} %collective-permute-done.91.refs_1_, bf16[576,128]{1,0:T(8,128)(2,1)S(1)} %copy-done.118, ...), custom_call_target="tpu_custom_call" | custom-call | flops 19327352832 | bytes 3276800 | tf_op jit(solution)/shard_map/embed_back/pallas_call | solution.py:809
  (713 shorter events, 556.9 us)
Async XLA Ops:
  7.2 146.8 %all-gather.7.cloned.1.call-start = ((), (), s32[]{:S(2)}) async-start(), calls=%async_computation.6 | async-start | bytes 5234688 | tf_op jit(solution)/shard_map/all_gather | solution.py:1027
  11.2 286.3 %all-gather.9.cloned.1.call-start = ((), (), s32[]{:S(2)}) async-start(), calls=%async_computation.7 | async-start | bytes 4718592 | tf_op jit(solution)/shard_map/all_gather | solution.py:1028
  12.4 45.4 %collective-permute-start.3 = (bf16[4,128,512]{2,1,0:T(8,128)(2,1)}, bf16[4,128,512]{2,1,0:T(8,128)(2,1)}, u32[]{:S(2)}, u32[]{:S(2)}) collective-permute-start(bf16[4,128,512]{2,1,0:T(8,128)(2,1)} %get-tuple-element.540.refs_2_), channel_id=1, source_target_pairs={{0,1},{1,0},{2,3},{3,2},{4,5},{5,4},{6,7},{7,6},{8,9},{9,8},{10,11... | collective-permute-start | bytes 1572872 | tf_op jit(solution)/shard_map/ppermute | solution.py:924
  12.9 42.7 %collective-permute-start.4 = (bf16[4,128,512]{2,1,0:T(8,128)(2,1)}, bf16[4,128,512]{2,1,0:T(8,128)(2,1)}, u32[]{:S(2)}, u32[]{:S(2)}) collective-permute-start(bf16[4,128,512]{2,1,0:T(8,128)(2,1)} %get-tuple-element.540.refs_2_), channel_id=1, source_target_pairs={{0,2},{1,3},{2,0},{3,1},{4,6},{5,7},{6,4},{7,5},{8,10},{9,11},{10,... | collective-permute-start | bytes 1572872 | tf_op jit(solution)/shard_map/ppermute | solution.py:924
  19.5 349.3 %all-gather.11.cloned.1.call-start = ((), (), s32[]{:S(2)}) async-start(), calls=%async_computation.8 | async-start | bytes 4718592 | tf_op jit(solution)/shard_map/all_gather | solution.py:1029
  109.5 20.4 %collective-permute-start.7 = (bf16[576,128]{1,0:T(8,128)(2,1)S(1)}, bf16[576,128]{1,0:T(8,128)(2,1)S(1)}, u32[]{:S(2)}, u32[]{:S(2)}) collective-permute-start(bf16[576,128]{1,0:T(8,128)(2,1)S(1)} %get-tuple-element.546), channel_id=1, source_target_pairs={{0,8},{4,12},{8,0},{12,4},{16,24},{20,28},{24,16},{28,20},{1,9},{5... | collective-permute-start | bytes 442376 | tf_op jit(solution)/shard_map/ppermute | solution.py:924
  110.3 26.3 %collective-permute-start.8 = (bf16[576,128]{1,0:T(8,128)(2,1)S(1)}, bf16[576,128]{1,0:T(8,128)(2,1)S(1)}, u32[]{:S(2)}, u32[]{:S(2)}) collective-permute-start(bf16[576,128]{1,0:T(8,128)(2,1)S(1)} %get-tuple-element.545), channel_id=1, source_target_pairs={{0,12},{4,8},{8,4},{12,0},{16,28},{20,24},{24,20},{28,16},{1,13},{... | collective-permute-start | bytes 442376 | tf_op jit(solution)/shard_map/ppermute | solution.py:924
  111.7 24.9 %collective-permute-start.9 = (bf16[576,128]{1,0:T(8,128)(2,1)}, bf16[576,128]{1,0:T(8,128)(2,1)S(1)}, u32[]{:S(2)}, u32[]{:S(2)}) collective-permute-start(bf16[576,128]{1,0:T(8,128)(2,1)} %get-tuple-element.544), channel_id=1, source_target_pairs={{0,16},{4,20},{8,24},{12,28},{16,0},{20,4},{24,8},{28,12},{1,17},{... | collective-permute-start | bytes 442376 | tf_op jit(solution)/shard_map/ppermute | solution.py:924
  114.4 31.0 %collective-permute-start.10 = (bf16[576,128]{1,0:T(8,128)(2,1)S(1)}, bf16[576,128]{1,0:T(8,128)(2,1)S(1)}, u32[]{:S(2)}, u32[]{:S(2)}) collective-permute-start(bf16[576,128]{1,0:T(8,128)(2,1)S(1)} %get-tuple-element.543), channel_id=1, source_target_pairs={{0,20},{4,16},{8,28},{12,24},{16,4},{20,0},{24,12},{28,8},{1,21},{... | collective-permute-start | bytes 442376 | tf_op jit(solution)/shard_map/ppermute | solution.py:924
  116.8 29.2 %collective-permute-start.11 = (bf16[576,128]{1,0:T(8,128)(2,1)}, bf16[576,128]{1,0:T(8,128)(2,1)S(1)}, u32[]{:S(2)}, u32[]{:S(2)}) collective-permute-start(bf16[576,128]{1,0:T(8,128)(2,1)} %get-tuple-element.542), channel_id=1, source_target_pairs={{0,24},{4,28},{8,16},{12,20},{16,8},{20,12},{24,0},{28,4},{1,25},{... | collective-permute-start | bytes 442376 | tf_op jit(solution)/shard_map/ppermute | solution.py:924
  195.3 29.3 %collective-permute-start.21 = (bf16[384,1024]{1,0:T(8,128)(2,1)S(1)}, bf16[384,1024]{1,0:T(8,128)(2,1)}, u32[]{:S(2)}, u32[]{:S(2)}) collective-permute-start(bf16[384,1024]{1,0:T(8,128)(2,1)S(1)} %add.350.refs_8_.refs_1_), channel_id=1, source_target_pairs={{0,2},{1,3},{2,0},{3,1},{4,6},{5,7},{6,4},{7,5},{8,10},{9,11},{10,... | collective-permute-start | bytes 2359304 | tf_op jit(solution)/shard_map/ppermute | solution.py:924
  195.9 711.2 %reduce-scatter.8.cloned.1.call-start = ((), (), s32[]{:S(2)}) async-start(), calls=%async_computation.5 | async-start | bytes 4718592 | tf_op jit(solution)/shard_map/reduce_scatter | solution.py:1378
  195.9 22.5 %collective-permute-start.22 = (bf16[768,256]{1,0:T(8,128)(2,1)S(1)}, bf16[768,256]{1,0:T(8,128)(2,1)S(1)}, u32[]{:S(2)}, u32[]{:S(2)}) collective-permute-start(bf16[768,256]{1,0:T(8,128)(2,1)S(1)} %text_in.1.refs_5_.refs_1_), channel_id=1, source_target_pairs={{0,1},{1,0},{2,3},{3,2},{4,5},{5,4},{6,7},{7,6},{8,9},{9,8},{10,11... | collective-permute-start | bytes 1179656 | tf_op jit(solution)/shard_map/ppermute | solution.py:924
  295.0 20.3 %collective-permute-start.37 = (bf16[384,1024]{1,0:T(8,128)(2,1)}, bf16[384,1024]{1,0:T(8,128)(2,1)}, u32[]{:S(2)}, u32[]{:S(2)}) collective-permute-start(bf16[384,1024]{1,0:T(8,128)(2,1)} %add.354.refs_9_.refs_1_), channel_id=1, source_target_pairs={{0,2},{1,3},{2,0},{3,1},{4,6},{5,7},{6,4},{7,5},{8,10},{9,11},{10,... | collective-permute-start | bytes 2359304 | tf_op jit(solution)/shard_map/ppermute | solution.py:924
  318.8 20.2 %collective-permute-start.39 = (bf16[384,1024]{1,0:T(8,128)(2,1)}, bf16[384,1024]{1,0:T(8,128)(2,1)S(1)}, u32[]{:S(2)}, u32[]{:S(2)}) collective-permute-start(bf16[384,1024]{1,0:T(8,128)(2,1)} %add.355.refs_6_.refs_1_), channel_id=1, source_target_pairs={{0,2},{1,3},{2,0},{3,1},{4,6},{5,7},{6,4},{7,5},{8,10},{9,11},{10,... | collective-permute-start | bytes 2359304 | tf_op jit(solution)/shard_map/ppermute | solution.py:924
  366.3 20.3 %collective-permute-start.46 = (bf16[384,1024]{1,0:T(8,128)(2,1)}, bf16[384,1024]{1,0:T(8,128)(2,1)}, u32[]{:S(2)}, u32[]{:S(2)}) collective-permute-start(bf16[384,1024]{1,0:T(8,128)(2,1)} %add.357.refs_6_.refs_1_), channel_id=1, source_target_pairs={{0,2},{1,3},{2,0},{3,1},{4,6},{5,7},{6,4},{7,5},{8,10},{9,11},{10,... | collective-permute-start | bytes 2359304 | tf_op jit(solution)/shard_map/ppermute | solution.py:924
  390.1 29.6 %collective-permute-start.50 = (bf16[384,1024]{1,0:T(8,128)(2,1)}, bf16[384,1024]{1,0:T(8,128)(2,1)S(1)}, u32[]{:S(2)}, u32[]{:S(2)}) collective-permute-start(bf16[384,1024]{1,0:T(8,128)(2,1)} %add.358.refs_9_.refs_1_), channel_id=1, source_target_pairs={{0,2},{1,3},{2,0},{3,1},{4,6},{5,7},{6,4},{7,5},{8,10},{9,11},{10,... | collective-permute-start | bytes 2359304 | tf_op jit(solution)/shard_map/ppermute | solution.py:924
  447.4 20.6 %collective-permute-start.57 = (bf16[384,1024]{1,0:T(8,128)(2,1)S(1)}, bf16[384,1024]{1,0:T(8,128)(2,1)S(1)}, u32[]{:S(2)}, u32[]{:S(2)}) collective-permute-start(bf16[384,1024]{1,0:T(8,128)(2,1)S(1)} %get-tuple-element.338), channel_id=1, source_target_pairs={{0,1},{1,0},{2,3},{3,2},{4,5},{5,4},{6,7},{7,6},{8,9},{9,8},{10,11... | collective-permute-start | bytes 2359304 | tf_op jit(solution)/shard_map/ppermute | solution.py:924
  447.5 30.1 %collective-permute-start.51 = (bf16[384,1024]{1,0:T(8,128)(2,1)S(1)}, bf16[384,1024]{1,0:T(8,128)(2,1)S(1)}, u32[]{:S(2)}, u32[]{:S(2)}) collective-permute-start(bf16[384,1024]{1,0:T(8,128)(2,1)S(1)} %add.359.refs_9_.refs_1_), channel_id=1, source_target_pairs={{0,2},{1,3},{2,0},{3,1},{4,6},{5,7},{6,4},{7,5},{8,10},{9,11},{10,... | collective-permute-start | bytes 2359304 | tf_op jit(solution)/shard_map/ppermute | solution.py:924
  507.5 412.0 %reduce-scatter.6.cloned.1.call-start = ((), (), s32[]{:S(2)}) async-start(), calls=%async_computation.4 | async-start | bytes 4718592 | tf_op jit(solution)/shard_map/reduce_scatter | solution.py:1412
  509.5 26.2 %collective-permute-start.60 = (bf16[384,1024]{1,0:T(8,128)(2,1)}, bf16[384,1024]{1,0:T(8,128)(2,1)S(1)}, u32[]{:S(2)}, u32[]{:S(2)}) collective-permute-start(bf16[384,1024]{1,0:T(8,128)(2,1)} %copy-done.116), channel_id=1, source_target_pairs={{0,1},{1,0},{2,3},{3,2},{4,5},{5,4},{6,7},{7,6},{8,9},{9,8},{10,11... | collective-permute-start | bytes 2359304 | tf_op jit(solution)/shard_map/ppermute | solution.py:924
  579.8 22.7 %collective-permute-start.70 = (bf16[384,1024]{1,0:T(8,128)(2,1)S(1)}, bf16[384,1024]{1,0:T(8,128)(2,1)S(1)}, u32[]{:S(2)}, u32[]{:S(2)}) collective-permute-start(bf16[384,1024]{1,0:T(8,128)(2,1)S(1)} %add.363.refs_7_.refs_1_), channel_id=1, source_target_pairs={{0,2},{1,3},{2,0},{3,1},{4,6},{5,7},{6,4},{7,5},{8,10},{9,11},{10,... | collective-permute-start | bytes 2359304 | tf_op jit(solution)/shard_map/ppermute | solution.py:924
  630.3 291.2 %reduce-scatter.4.cloned.1.call-start = ((), (), s32[]{:S(2)}) async-start(), calls=%async_computation.3 | async-start | bytes 5160960 | tf_op jit(solution)/shard_map/reduce_scatter | solution.py:1496
  631.7 27.7 %collective-permute-start.75 = (bf16[384,1024]{1,0:T(8,128)(2,1)}, bf16[384,1024]{1,0:T(8,128)(2,1)S(1)}, u32[]{:S(2)}, u32[]{:S(2)}) collective-permute-start(bf16[384,1024]{1,0:T(8,128)(2,1)} %copy-done.115), channel_id=1, source_target_pairs={{0,1},{1,0},{2,3},{3,2},{4,5},{5,4},{6,7},{7,6},{8,9},{9,8},{10,11... | collective-permute-start | bytes 2359304 | tf_op jit(solution)/shard_map/ppermute | solution.py:924
  680.8 28.8 %collective-permute-start.78 = (bf16[384,1024]{1,0:T(8,128)(2,1)S(1)}, bf16[384,1024]{1,0:T(8,128)(2,1)S(1)}, u32[]{:S(2)}, u32[]{:S(2)}) collective-permute-start(bf16[384,1024]{1,0:T(8,128)(2,1)S(1)} %add.366.refs_11_.refs_1_), channel_id=1, source_target_pairs={{0,2},{1,3},{2,0},{3,1},{4,6},{5,7},{6,4},{7,5},{8,10},{9,11},{10,... | collective-permute-start | bytes 2359304 | tf_op jit(solution)/shard_map/ppermute | solution.py:924
  713.6 21.0 %collective-permute-start.83 = (bf16[384,1024]{1,0:T(8,128)(2,1)S(1)}, bf16[384,1024]{1,0:T(8,128)(2,1)S(1)}, u32[]{:S(2)}, u32[]{:S(2)}) collective-permute-start(bf16[384,1024]{1,0:T(8,128)(2,1)S(1)} %add.367.refs_12_.refs_1_), channel_id=1, source_target_pairs={{0,2},{1,3},{2,0},{3,1},{4,6},{5,7},{6,4},{7,5},{8,10},{9,11},{10,... | collective-permute-start | bytes 2359304 | tf_op jit(solution)/shard_map/ppermute | solution.py:924
  738.6 20.4 %collective-permute-start.88 = (bf16[384,1024]{1,0:T(8,128)(2,1)S(1)}, bf16[384,1024]{1,0:T(8,128)(2,1)S(1)}, u32[]{:S(2)}, u32[]{:S(2)}) collective-permute-start(bf16[384,1024]{1,0:T(8,128)(2,1)S(1)} %add.370.refs_12_.refs_1_), channel_id=1, source_target_pairs={{0,2},{1,3},{2,0},{3,1},{4,6},{5,7},{6,4},{7,5},{8,10},{9,11},{10,... | collective-permute-start | bytes 2359304 | tf_op jit(solution)/shard_map/ppermute | solution.py:924
  784.9 20.5 %collective-permute-start.89 = (bf16[384,1024]{1,0:T(8,128)(2,1)S(1)}, bf16[384,1024]{1,0:T(8,128)(2,1)S(1)}, u32[]{:S(2)}, u32[]{:S(2)}) collective-permute-start(bf16[384,1024]{1,0:T(8,128)(2,1)S(1)} %add.371.refs_12_.refs_1_), channel_id=1, source_target_pairs={{0,2},{1,3},{2,0},{3,1},{4,6},{5,7},{6,4},{7,5},{8,10},{9,11},{10,... | collective-permute-start | bytes 2359304 | tf_op jit(solution)/shard_map/ppermute | solution.py:924
  786.2 34.4 %collective-permute-start.90 = (bf16[384,1024]{1,0:T(8,128)(2,1)S(1)}, bf16[384,1024]{1,0:T(8,128)(2,1)S(1)}, u32[]{:S(2)}, u32[]{:S(2)}) collective-permute-start(bf16[384,1024]{1,0:T(8,128)(2,1)S(1)} %add.372.refs_4_.refs_1_), channel_id=1, source_target_pairs={{0,2},{1,3},{2,0},{3,1},{4,6},{5,7},{6,4},{7,5},{8,10},{9,11},{10,... | collective-permute-start | bytes 2359304 | tf_op jit(solution)/shard_map/ppermute | solution.py:924
  833.6 22.3 %collective-permute-start.95 = (bf16[576,128]{1,0:T(8,128)(2,1)S(1)}, bf16[576,128]{1,0:T(8,128)(2,1)S(1)}, u32[]{:S(2)}, u32[]{:S(2)}) collective-permute-start(bf16[576,128]{1,0:T(8,128)(2,1)S(1)} %get-tuple-element.487), channel_id=1, source_target_pairs={{0,20},{4,16},{8,28},{12,24},{16,4},{20,0},{24,12},{28,8},{1,21},{... | collective-permute-start | bytes 442376 | tf_op jit(solution)/shard_map/ppermute | solution.py:924
  834.5 22.1 %collective-permute-start.96 = (bf16[576,128]{1,0:T(8,128)(2,1)S(1)}, bf16[576,128]{1,0:T(8,128)(2,1)S(1)}, u32[]{:S(2)}, u32[]{:S(2)}) collective-permute-start(bf16[576,128]{1,0:T(8,128)(2,1)S(1)} %get-tuple-element.488), channel_id=1, source_target_pairs={{0,24},{4,28},{8,16},{12,20},{16,8},{20,12},{24,0},{28,4},{1,25},{... | collective-permute-start | bytes 442376 | tf_op jit(solution)/shard_map/ppermute | solution.py:924
  895.6 21.0 %collective-permute-start.98 = (bf16[4,128,512]{2,1,0:T(8,128)(2,1)}, bf16[4,128,512]{2,1,0:T(8,128)(2,1)}, u32[]{:S(2)}, u32[]{:S(2)}) collective-permute-start(bf16[4,128,512]{2,1,0:T(8,128)(2,1)} %get-tuple-element.531), channel_id=1, source_target_pairs={{0,1},{1,0},{2,3},{3,2},{4,5},{5,4},{6,7},{7,6},{8,9},{9,8},{10,11... | collective-permute-start | bytes 1572872 | tf_op jit(solution)/shard_map/ppermute | solution.py:924
  (245 other events, 1948.5 us)
Sparse Core Ops, SparseCore 0:
  11.3 83.9 all-gather.6
  97.4 91.3 all-gather.8
  196.0 76.4 all-gather.10
  507.7 90.7 reduce-scatter.7
  630.4 90.7 reduce-scatter.5
  785.0 106.8 reduce-scatter.3

commit v4 on v3

--- a/solution.py
+++ b/solution.py
@@ -14,6 +14,10 @@
 NEG = -1e30
 LOW = jnp.bfloat16
 F32 = jnp.float32
+
+SMALL = pl.CostEstimate(flops=1024, bytes_accessed=1024, transcendentals=0)
+
+PIECES = 2
 
 clip_limit = 0.004
 stability_offset = 1e-08
@@ -247,9 +251,7 @@
         ]
         + list(scratch),
         compiler_params=pltpu.CompilerParams(vmem_limit_bytes=held + (margin << 20)),
-        cost_estimate=pl.CostEstimate(
-            flops=int(flops), bytes_accessed=int(nbytes), transcendentals=int(exps)
-        ),
+        cost_estimate=SMALL,
         name=name,
     )(*arrays, *extra, *after)
     for owner, result in zip(owners, results):
@@ -434,7 +436,7 @@
 def head_backward_body(
     need, put, core_ref, total_ref, weight_ref, target_ref, logits_ref, *refs
 ):
-    *w_refs, grad_ref, keep_ref, send_ref, loss_ref, col_ref = refs
+    *w_refs, valid_ref, grad_ref, keep_ref, send_ref, loss_ref, col_ref = refs
     height = keep_ref.shape[0]
     books = len(w_refs)
     vocab = w_refs[0].shape[2]
@@ -445,12 +447,13 @@
         [total_ref[...], jnp.zeros((128 - total_ref.shape[0], frames), F32)], axis=0
     )
     col_ref[...] = jnp.transpose(wide)
-    gap = (col_ref[:, :books] - col_ref[:, books : 2 * books]) * weight_ref[...]
+    share = 1.0 / valid_ref[0]
+    gap = (col_ref[:, :books] - col_ref[:, books : 2 * books]) * (weight_ref[...] * share)
     loss_ref[...] = jnp.broadcast_to(jnp.sum(gap).reshape(1, 1), loss_ref.shape)
     code = lax.broadcasted_iota(jnp.int32, (height, vocab), 1)
     need(4)
     for j, rows, to_ref in ((2, other, send_ref), (1, mine, keep_ref)):
-        weight = weight_ref[rows, :]
+        weight = weight_ref[rows, :] * share
         total = col_ref[rows, :]
         acc = None
         for k, w_ref in enumerate(w_refs):
@@ -632,8 +635,22 @@
     out_ref[...] = (keep_ref[...].astype(F32) + got_ref[...].astype(F32)).astype(LOW)
 
 
-def norm_body(which, hidden_ref, part_ref, far_ref, norm_ref, new_ref, out_ref):
-    new = hidden_ref[...] + (part_ref[...].astype(F32) + far_ref[...].astype(F32))
+def add_parts_body(keep_ref, got_ref, *out_refs):
+    rows = out_refs[0].shape[0]
+    for j, out_ref in enumerate(out_refs):
+        at = slice(j * rows, (j + 1) * rows)
+        out_ref[...] = (keep_ref[at, :].astype(F32) + got_ref[at, :].astype(F32)).astype(LOW)
+
+
+def joined(refs):
+    half = len(refs) // 2
+    sums = [a[...].astype(F32) + b[...].astype(F32) for a, b in zip(refs[:half], refs[half:])]
+    return jnp.concatenate(sums, axis=0)
+
+
+def norm_body(which, hidden_ref, *refs):
+    *part_refs, norm_ref, new_ref, out_ref = refs
+    new = hidden_ref[...] + joined(part_refs)
     new_ref[...] = new
     out_ref[...] = normalize(
         new, norm_ref[which : which + 1, :], norm_ref[which + 4 : which + 5, :]
@@ -654,10 +671,10 @@
     put(1, 0)
 
 
-def norm_back_body(which, hidden_ref, part_ref, far_ref, *refs):
-    *before, norm_ref, new_ref, low_ref, sums_ref = refs
+def norm_back_body(which, parts, hidden_ref, *refs):
+    *before, norm_ref, new_ref, low_ref, sums_ref = refs[parts:]
     values = hidden_ref[...]
-    grad = part_ref[...].astype(F32) + far_ref[...].astype(F32)
+    grad = joined(refs[:parts])
     gain = norm_ref[which : which + 1, :]
     center = values - jnp.mean(values, axis=1, keepdims=True)
     spread = jnp.mean(center * center, axis=1, keepdims=True)
@@ -735,93 +752,93 @@
         in_specs=[in_vmem()] * len(operands) + [anywhere()] * len(after),
         out_specs=tuple(in_vmem() for _ in outs),
         compiler_params=pltpu.CompilerParams(vmem_limit_bytes=12 << 20),
-        cost_estimate=pl.CostEstimate(
-            flops=20 * height * width, bytes_accessed=nbytes // 4, transcendentals=0
-        ),
+        cost_estimate=SMALL,
         name=name,
     )(*(hold(a, pltpu.VMEM) for a in operands), *after)
 
 
-def embed_body(base_ref, codes_ref, *refs):
-    *table_refs, out_ref = refs
-    books, features, vocab = table_refs[0].shape
-    rows = codes_ref.shape[1]
+def turned_codes(packet):
+    lines = packet.astype(F32)
+    wide = jnp.concatenate([lines, jnp.zeros((120, lines.shape[1]), F32)], axis=0)
+    return jnp.transpose(wide)
+
+
+def embed_body(count, books, base_ref, *refs):
+    packets, tables, outs = refs[:count], refs[count : len(refs) - count], refs[len(refs) - count :]
+    features, vocab = tables[0].shape[1:]
+    rows = outs[0].shape[0]
     chunk = min(256, vocab)
-    code = lax.broadcasted_iota(jnp.int32, (rows, chunk), 1)
-    acc = jnp.zeros((rows, features), F32)
-    for k in range(books):
-        column = codes_ref[0, :, k : k + 1]
-        for b, table in enumerate(table_refs):
-            local = column - base_ref[b]
-            for v in range(0, vocab, chunk):
-                hit = jnp.where(code == local - v, 1.0, 0.0).astype(LOW)
-                acc = acc + nt(hit, table[k, :, v : v + chunk])
-    out_ref[0] = acc.astype(LOW)
-
-
-def embed(base, codes, tables, after):
-    blocks, rows, books = codes.shape
-    features = tables[0].shape[1]
-    vocab = tables[0].shape[2] * len(tables)
+    code = lax.broadcasted_iota(jnp.int32, (rows, chunk), 1).astype(F32)
+    for packet, out_ref in zip(packets, outs):
+        columns = turned_codes(packet[...])
+        acc = jnp.zeros((rows, features), F32)
+        for k in range(books):
+            column = columns[:rows, k : k + 1]
+            for b, table in enumerate(tables):
+                local = column - base_ref[b].astype(F32)
+                for v in range(0, vocab, chunk):
+                    hit = jnp.where(code == local - float(v), 1.0, 0.0).astype(LOW)
+                    acc = acc + nt(hit, table[k, :, v : v + chunk])
+        out_ref[...] = acc.astype(LOW)
+
+
+def embed(base, packets, tables, rows, after):
+    books, features = tables[0].shape[:2]
+    count = len(packets)
     return pl.pallas_call(
-        later(embed_body, len(after), 2 + len(tables)),
-        out_shape=sds((blocks, rows, features), LOW),
-        grid=(blocks,),
-        in_specs=[scalars(), pl.BlockSpec((1, rows, books), lambda i: (i, 0, 0))]
-        + [in_vmem() for t in tables]
+        later(partial(embed_body, count, books), len(after), 1 + count + len(tables)),
+        out_shape=[sds((rows, features), LOW)] * count,
+        in_specs=[scalars()]
+        + [in_vmem()] * (count + len(tables))
         + [anywhere()] * len(after),
-        out_specs=pl.BlockSpec((1, rows, features), lambda i: (i, 0, 0)),
-        compiler_params=pltpu.CompilerParams(vmem_limit_bytes=12 << 20),
-        cost_estimate=pl.CostEstimate(
-            flops=4 * blocks * rows * books * vocab * features,
-            bytes_accessed=2 * books * vocab * features + blocks * rows * (features + 512),
-            transcendentals=0,
-        ),
+        out_specs=[in_vmem()] * count,
+        compiler_params=pltpu.CompilerParams(vmem_limit_bytes=16 << 20),
+        cost_estimate=SMALL,
         name="embed",
-    )(base, codes, *tables, *after)
-
-
-def embed_back_body(base_ref, codes_ref, *refs):
-    *grad_refs, out_ref, all_ref = refs
-    rows, features = grad_refs[0].shape
+    )(base, *packets, *tables, *after)
+
+
+def embed_back_body(groups, base_ref, *refs):
+    packets, grads = refs[:groups], refs[groups : 2 * groups]
+    out_ref, all_ref = refs[-2:]
+    rows, features = grads[0].shape
+    padded = packets[0].shape[1]
     vocab = out_ref.shape[3]
+    chunk = min(256, vocab)
     book = pl.program_id(1)
-    chunk = min(256, vocab)
 
     @pl.when((pl.program_id(0) == 0) & (book == 0))
     def _():
-        for j, g in enumerate(grad_refs):
-            all_ref[j * rows : (j + 1) * rows, :] = g[...]
+        for j, g in enumerate(grads):
+            all_ref[j * padded : j * padded + rows, :] = g[...]
+            if padded > rows:
+                all_ref[j * padded + rows : (j + 1) * padded, :] = jnp.zeros(
+                    (padded - rows, features), LOW
+                )
 
     base = base_ref[pl.program_id(0)]
-    line = codes_ref[0]
-    line = line[0:1, :]
+    line = jnp.concatenate([p[pl.ds(book, 1), :] for p in packets], axis=1)
     code = lax.broadcasted_iota(jnp.int32, (chunk, line.shape[1]), 0)
     for v in range(0, vocab, chunk):
         hit = jnp.where(code == line - (base + v), 1.0, 0.0).astype(LOW)
         out_ref[0, 0, :, v : v + chunk] = jnp.transpose(nn(hit, all_ref[...])).astype(LOW)
 
 
-def embed_back(base, lines, grads, vocab):
+def embed_back(base, packets, grads, books, vocab, after):
     parts = base.shape[0]
-    books, _, total = lines.shape
+    groups = len(packets)
     features = grads[0].shape[1]
     return pl.pallas_call(
-        embed_back_body,
+        later(partial(embed_back_body, groups), len(after), 1 + 2 * groups),
         out_shape=sds((parts, books, features, vocab), LOW),
         grid=(parts, books),
-        in_specs=[scalars(), pl.BlockSpec((1, 8, total), lambda i, k: (k, 0, 0))]
-        + [pl.BlockSpec(g.shape, lambda i, k: (0, 0)) for g in grads],
+        in_specs=[scalars()] + [in_vmem()] * (2 * groups) + [anywhere()] * len(after),
         out_specs=pl.BlockSpec((1, 1, features, vocab), lambda i, k: (i, k, 0, 0)),
-        scratch_shapes=[pltpu.VMEM((total, features), LOW)],
-        compiler_params=pltpu.CompilerParams(vmem_limit_bytes=12 << 20),
-        cost_estimate=pl.CostEstimate(
-            flops=4 * parts * books * vocab * features * total,
-            bytes_accessed=2 * parts * books * features * vocab + 2 * total * features,
-            transcendentals=0,
-        ),
+        scratch_shapes=[pltpu.VMEM((groups * packets[0].shape[1], features), LOW)],
+        compiler_params=pltpu.CompilerParams(vmem_limit_bytes=24 << 20),
+        cost_estimate=SMALL,
         name="embed_back",
-    )(base, lines, *grads)
+    )(base, *packets, *grads, *after)
 
 
 def gather_features_body(need, put, where_ref, *refs):
@@ -1032,20 +1049,14 @@
     weight_int = delay_mask * frame_mask[:, :, None] * frame_live[None, :, None]
     start = core * height + side * strip
     strip_codes = lax.dynamic_slice_in_dim(audio_codes, start, strip, 1)
-    lines = jnp.transpose(strip_codes, (2, 0, 1)).reshape(books, clips * strip)
-    count_line = jnp.broadcast_to(jnp.sum(weight_int), (1, clips * strip))
-    packet = jnp.concatenate([lines, count_line], axis=0)[None]
-    mask = 1
-    while mask < dp:
-        packet = jnp.concatenate([packet, swap(packet, "dp", mask)], axis=0)
-        mask *= 2
-    valid_count = jnp.sum(packet[:, books, 0]).astype(F32)
-    all_lines = packet[:, :books]
-    all_codes = jnp.transpose(all_lines, (0, 2, 1))
-    back_lines = jnp.broadcast_to(
-        jnp.transpose(all_lines, (1, 0, 2)).reshape(books, 1, dp * clips * strip),
-        (books, 8, dp * clips * strip),
-    )
+    count = clips * strip
+    padded = -(-count // 128) * 128
+    lines = jnp.transpose(strip_codes, (2, 0, 1)).reshape(books, count)
+    lines = jnp.pad(lines, ((0, 0), (0, padded - count)), constant_values=-1)
+    count_line = jnp.broadcast_to(jnp.sum(weight_int), (8 - books, padded))
+    packet = jnp.concatenate([lines, count_line], axis=0)
+    packets = [packet] + [swap(packet, "dp", m) for m in range(1, dp)]
+    valid_count = sum(p[books, 0] for p in packets).astype(F32)
     vocab_base = (place ^ jnp.arange(tensor, dtype=jnp.int32)) * vocab
     group_order = group ^ jnp.arange(dp, dtype=jnp.int32)
     place_order = place ^ jnp.arange(tensor, dtype=jnp.int32)
@@ -1055,22 +1066,22 @@
     bias_columns = [jnp.transpose(line) for line in bias_lines]
     targets = (jnp.roll(audio_codes, -1, axis=1) - place * vocab).astype(jnp.int32)
     targets = [targets[c] for c in range(clips)]
-    grad_weight = weight_int.astype(F32) / valid_count
-    grad_weight = [grad_weight[c] for c in range(clips)]
+    valid_arg = Scalar(valid_count.reshape(1))
+    loss_weight = [weight_int[c].astype(F32) for c in range(clips)]
     placed = positions_rows(core * height, height, width)
-    last[:] = bias_lines + bias_columns + targets + grad_weight + [placed, back_lines]
 
     table_parts = spread_tensor(tables[:books].astype(LOW))
     step = max(1, dp // 4)
     arrived = [None] * dp
     for low_end in reversed(range(0, dp, step)):
         embedded = embed(
-            vocab_base, all_codes[low_end : low_end + step], table_parts, list(last)
-        )
-        last[:] = [embedded]
-        for m in range(low_end, low_end + step):
-            piece = embedded[m - low_end]
+            vocab_base, packets[low_end : low_end + step], table_parts, count, list(last)
+        )
+        last[:] = [embedded[-1]]
+        for m, piece in enumerate(embedded, low_end):
             arrived[m] = swap(piece, "dp", m) if m else piece
+        last += [a for a in arrived[low_end + step : low_end + 2 * step] if a is not None]
+    last += bias_lines + bias_columns + targets + loss_weight + [placed]
     aligned = share % 128 == 0
     if aligned:
         strips = run(
@@ -1105,32 +1116,47 @@
 
     def norm_step(which, hidden, parts):
         new, out = norm_rows_kernel(
-            partial(norm_body, which), [half_sds, half_low], [hidden, *parts], norm_rows, last
-        )
+            partial(norm_body, which),
+            [half_sds, half_low],
+            [hidden, *parts],
+            norm_rows,
+            last + soon,
+        )
+        soon[:] = []
         last[:] = [out]
         return new, (out, swap_core(free(out)))
 
     def norm_back(which, hidden, parts, before):
         operands = [hidden, *parts] + ([before] if before is not None else [])
         new, out, sums = norm_rows_kernel(
-            partial(norm_back_body, which),
+            partial(norm_back_body, which, len(parts)),
             [half_sds, half_low, sds((8, width), F32)],
             operands,
             norm_rows,
-            last,
-        )
+            last + soon,
+        )
+        soon[:] = []
         last[:] = [out]
         return new, (out, swap_core(free(out))), free(sums)
 
-    waiting = []
+    waiting, soon = [], []
     moving = [None] * clips
 
     def flush():
         if waiting:
             c, keep, got = waiting.pop()
-            (part,) = norm_rows_kernel(add_body, [half_low], [keep, got], None, last, name="add")
-            last[:] = [part]
-            moving[c] = (part, *across(free(part))[1:])
+            parts = norm_rows_kernel(
+                add_parts_body,
+                [sds((height // PIECES, width), LOW)] * PIECES,
+                [keep, got],
+                None,
+                last,
+                name="add",
+            )
+            last[:] = [parts[-1]]
+            fars = [across(free(part))[1] for part in parts]
+            moving[c] = (*parts, *fars)
+            soon[:] = fars[:-1]
 
     def reduce_rows(c, keep, send):
         waiting.append((c, keep, swap_core(free(send))))
@@ -1294,12 +1320,13 @@
             mask *= 2
         return stats
 
-    def head_back_step(c, logits, total):
+    def head_back_step(c, logits, stats):
         grad, keep, send, loss = run(
             head_backward_body,
             [sds((frames, books * vocab), LOW), flow, flow, Flow(sds((8, 128), F32))],
-            [core_arg, total, grad_weight[c], targets[c], fetch(logits)]
-            + [w_member(head_all, k) for k in range(books)],
+            [core_arg, stats, loss_weight[c], targets[c], fetch(logits)]
+            + [w_member(head_all, k) for k in range(books)]
+            + [valid_arg],
             flops=2 * frames * width * books * vocab,
             scratch=tot,
             name="head_backward",
@@ -1515,7 +1542,7 @@
         rows = jnp.transpose(rows.reshape(clips * strip, dp, share), (1, 0, 2))
         pieces = list(jnp.take(rows, group_order, axis=0))
     rows_all = [pieces[0]] + [swap(pieces[m], "dp", m) for m in range(1, dp)]
-    embed_parts = embed_back(vocab_base, back_lines, rows_all, vocab)
+    embed_parts = embed_back(vocab_base, packets, rows_all, books, vocab, list(last))
     grad_embed = collect_tensor([embed_parts[m] for m in range(tensor)])
 
     norm_part = jnp.concatenate(

time: 981 us -> 994 us (1.013)
  starting transfers between devices: 100 us -> 137 us
  Pallas kernels: 403 us -> 390 us
    ppermute x111 -> x136, starting transfers between devices: 99.7 us -> 136 us  [swap(): return lax.ppermute(values, axis, [(i, i ^ mask) for i in range(size)])]
    pallas_call x5, Pallas kernels: 73.4 us -> 62.5 us  [the longest x4 35.7 us: embed(): pl.pallas_call(later(partial(embed_body, count, books), len(after), 1 + c...]
    ppermute x111 -> x136, waiting for transfers between devices: 289 us -> 281 us  [swap(): return lax.ppermute(values, axis, [(i, i ^ mask) for i in range(size)])]
    unnamed x318 -> x398, local copies, waits for them, and re-layouts: 86.1 us -> 85.8 us
  transfers between devices with their start and end apart: 117 -> 142, of which waited for: 60 -> 61; matrix products, arithmetic and copies ran while one was open for 4% -> 4% of each run, Pallas kernels for 38% -> 36%
where the time goes in v4:
time: 994 us; the launch traced here: 988 us
  Pallas kernels  390 us (39%)
  waiting for transfers between devices  281 us (28%)
  starting transfers between devices  137 us (14%)
  local copies, waits for them, and re-layouts  108 us (11%)
  other arithmetic  40.7 us (4%)
  between operations  30.8 us (3%)
    pallas_call x40, Pallas kernels, kernel(): pl.pallas_call(run_body, out_shape=tuple(out_shapes), in_specs=specs + [a...  289 us
    ppermute x136, waiting for transfers between devices, swap(): return lax.ppermute(values, axis, [(i, i ^ mask) for i in range(size)])  281 us
    ppermute x136, starting transfers between devices, swap(): return lax.ppermute(values, axis, [(i, i ^ mask) for i in range(size)])  136 us
    unnamed x398, local copies, waits for them, and re-layouts  85.8 us
    pallas_call x50, Pallas kernels, norm_rows_kernel(): pl.pallas_call(later(body, len(after), len(operands)), out_shape=tuple((p...  39 us
    pallas_call x4, Pallas kernels, embed(): pl.pallas_call(later(partial(embed_body, count, books), len(after), 1 + c...  35.7 us
    pallas_call x1, Pallas kernels, embed_back(): pl.pallas_call(later(partial(embed_back_body, groups), len(after), 1 + 2...  26.8 us
  transfers between devices with their start and end apart: 142, of which 61 were waited for; matrix products, arithmetic and copies ran while one was open for 4% of the time, Pallas kernels for 36%

profile of v4, /device:TPU:0, one launch (start us, length us, event | category | flops | bytes accessed | tf_op | source)
XLA Modules:
  0.0 988.2 jit_solution(10231243475385237078)
XLA Ops:
  40.2 9.0 embed.4
  53.0 9.2 embed.5
  71.1 8.4 embed.6
  79.5 22.5 %collective-permute-start.16 = (bf16[576,128]{1,0:T(8,128)(2,1)S(1)}, bf16[576,128]{1,0:T(8,128)(2,1)S(1)}, u32[]{:S(2)}, u32[]{:S(2)}) collective-permute-start(bf16[576,128]{1,0:T(8,128)(2,1)S(1)} %get-tuple-element.315.refs_7_), channel_id=1, source_target_pairs={{0,12},{4,8},{8,4},{12,0},{16,28},{20,24},{24,20},{28,16},{1,13},{... | collective-permute-start | bytes 442376 | tf_op jit(solution)/shard_map/ppermute | solution.py:941
  108.0 9.0 embed.7
  155.4 8.8 self_forward.4
  169.3 11.1 %collective-permute-done.28.refs_3_ = bf16[768,256]{1,0:T(8,128)(2,1)} collective-permute-done((bf16[768,256]{1,0:T(8,128)(2,1)S(1)}, bf16[768,256]{1,0:T(8,128)(2,1)}, u32[]{:S(2)}, u32[]{:S(2)}) %collective-permute-start.28) | collective-permute-done | bytes 393248 | tf_op jit(solution)/shard_map/ppermute | solution.py:941
  185.2 8.8 self_forward.5
  284.4 8.1 ffn_forward.3
  303.7 8.2 ffn_forward.4
  327.9 8.2 ffn_forward.5
  354.6 11.2 %head_forward.3 = (f32[768,2048]{1,0:T(8,128)}, f32[8,768]{1,0:T(8,128)S(1)}, bf16[384,1024]{1,0:T(8,128)(2,1)}, bf16[384,1024]{1,0:T(8,128)(2,1)}, f32[384,1024]{1,0:T(8,128)}) custom-call(s32[1]{0:T(128)} %bitcast.refs_0_, bf16[384,1024]{1,0:T(8,128)(2,1)} %get-tuple-element.390.refs_2_.refs_1_, s32[768,4]{1,0:T(8,128)S(1)} %copy-done.62, ...), custom_call_target="tpu_custom_call" | custom-call | flops 1024 | bytes 1024 | tf_op jit(solution)/shard_map/head_forward/pallas_call | solution.py:240
  375.0 9.5 head_forward.4
  402.5 8.8 head_backward.3
  416.3 9.7 head_forward.5
  431.4 8.8 head_backward.4
  448.8 9.0 head_backward.5
  486.2 16.2 %head_weights.1.refs_6_ = bf16[8,4,128,512]{3,2,1,0:T(8,128)(2,1)} custom-call(s32[1]{0:T(128)} %bitcast.refs_0_, bf16[384,1024]{1,0:T(8,128)(2,1)} %get-tuple-element.428.refs_1_, bf16[384,1024]{1,0:T(8,128)(2,1)} %get-tuple-element.429.refs_2_, bf16[384,1024]{1,0:T(8,128)(2,1)} %get-tuple-element.430.refs_3_, ...), custom_call_target="tpu_custom_call" | custom-call | flops 1024 | bytes 1024 | tf_op jit(solution)/shard_map/head_weights/pallas_call | solution.py:240
  504.6 10.1 %collective-permute-done.76.refs_4_ = bf16[192,1024]{1,0:T(8,128)(2,1)S(1)} collective-permute-done((bf16[192,1024]{1,0:T(8,128)(2,1)}, bf16[192,1024]{1,0:T(8,128)(2,1)S(1)}, u32[]{:S(2)}, u32[]{:S(2)}) %collective-permute-start.76) | collective-permute-done | bytes 393248 | tf_op jit(solution)/shard_map/ppermute | solution.py:941
  588.1 10.9 %ffn_two.1.refs_7_.refs_10_ = bf16[8,2,128,1024]{3,2,1,0:T(8,128)(2,1)} custom-call(s32[1]{0:T(128)} %bitcast.refs_0_, bf16[384,1024]{1,0:T(8,128)(2,1)} %get-tuple-element.462.refs_1_, bf16[384,1024]{1,0:T(8,128)(2,1)} %get-tuple-element.463.refs_2_, bf16[384,1024]{1,0:T(8,128)(2,1)} %get-tuple-element.464.refs_3_, ...), custom_call_target="tpu_custom_call" | custom-call | flops 1024 | bytes 1024 | tf_op jit(solution)/shard_map/ffn_two/pallas_call | solution.py:240
  616.1 10.8 %ffn_one.1.refs_7_ = bf16[8,2,128,1024]{3,2,1,0:T(8,128)(2,1)} custom-call(s32[1]{0:T(128)} %bitcast.refs_0_, bf16[384,1024]{1,0:T(8,128)(2,1)} %get-tuple-element.476.refs_1_, bf16[384,1024]{1,0:T(8,128)(2,1)} %get-tuple-element.477.refs_2_, bf16[384,1024]{1,0:T(8,128)(2,1)} %get-tuple-element.478.refs_3_, ...), custom_call_target="tpu_custom_call", output_to_operand_aliasing={{}: (10, {})} | custom-call | flops 1024 | bytes 1024 | tf_op jit(solution)/shard_map/ffn_one/pallas_call | solution.py:240
  629.5 10.1 %collective-permute-done.92.refs_4_ = bf16[192,1024]{1,0:T(8,128)(2,1)S(1)} collective-permute-done((bf16[192,1024]{1,0:T(8,128)(2,1)}, bf16[192,1024]{1,0:T(8,128)(2,1)S(1)}, u32[]{:S(2)}, u32[]{:S(2)}) %collective-permute-start.92) | collective-permute-done | bytes 393248 | tf_op jit(solution)/shard_map/ppermute | solution.py:941
  682.0 11.1 %self_backward.3 = (bf16[768,768]{1,0:T(8,128)(2,1)}, bf16[384,1024]{1,0:T(8,128)(2,1)S(1)}, bf16[384,1024]{1,0:T(8,128)(2,1)S(1)}, bf16[384,1024]{1,0:T(8,128)(...) custom-call(s32[1]{0:T(128)} %bitcast.refs_0_, bf16[384,1024]{1,0:T(8,128)(2,1)S(1)} %get-tuple-element.498.refs_2_.refs_1_, ...), custom_call_target="tpu_custom_call" | custom-call | flops 1024 | bytes 1024 | tf_op jit(solution)/shard_map/self_backward/pallas_call | solution.py:240
  726.3 11.1 %self_backward.4 = (bf16[768,768]{1,0:T(8,128)(2,1)}, bf16[384,1024]{1,0:T(8,128)(2,1)S(1)}, bf16[384,1024]{1,0:T(8,128)(2,1)S(1)}, bf16[384,1024]{1,0:T(8,128)(...) custom-call(s32[1]{0:T(128)} %bitcast.refs_0_, bf16[384,1024]{1,0:T(8,128)(2,1)S(1)} %get-tuple-element.531.refs_2_.refs_1_, ...), custom_call_target="tpu_custom_call" | custom-call | flops 1024 | bytes 1024 | tf_op jit(solution)/shard_map/self_backward/pallas_call | solution.py:240
  751.1 11.4 %self_backward.5 = (bf16[768,768]{1,0:T(8,128)(2,1)}, bf16[384,1024]{1,0:T(8,128)(2,1)S(1)}, bf16[384,1024]{1,0:T(8,128)(2,1)S(1)}, bf16[384,1024]{1,0:T(8,128)(...) custom-call(s32[1]{0:T(128)} %bitcast.refs_0_, bf16[384,1024]{1,0:T(8,128)(2,1)S(1)} %get-tuple-element.552.refs_2_.refs_1_, ...), custom_call_target="tpu_custom_call" | custom-call | flops 1024 | bytes 1024 | tf_op jit(solution)/shard_map/self_backward/pallas_call | solution.py:240
  766.2 8.8 collective-permute-done.111.refs_4_
  774.9 8.4 collective-permute-done.112.refs_8_.refs_3_
  799.6 9.7 self_in.1.refs_7_
  815.2 8.4 collective-permute-done.113.refs_4_
  823.7 15.1 %collective-permute-done.114.refs_8_.refs_3_ = bf16[192,1024]{1,0:T(8,128)(2,1)S(1)} collective-permute-done((bf16[192,1024]{1,0:T(8,128)(2,1)}, bf16[192,1024]{1,0:T(8,128)(2,1)S(1)}, u32[]{:S(2)}, u32[]{:S(2)}) %collective-permute-start.114) | collective-permute-done | bytes 393248 | tf_op jit(solution)/shard_map/ppermute | solution.py:941
  869.2 8.4 collective-permute-done.120.refs_14_
  877.7 26.8 %embed_back.1 = bf16[4,4,128,512]{3,2,1,0:T(8,128)(2,1)S(1)} custom-call(s32[4]{0:T(128)S(1)} %copy-done.156, s32[8,640]{1,0:T(8,128)} %pad_select_fusion.refs_1_, s32[8,640]{1,0:T(8,128)} %collective-permute-done.refs_2_, s32[8,640]{1,0:T(8,128)S(1)} %copy-done.133, s32[8,640]{1,0:T(8,128)S(1)} %copy-done.144, s32[8,640]{1,0:T(8,128)S(1)} %copy-done.139, ...), custom_call_target="tpu_custom_call" | custom-call | flops 1024 | bytes 1024 | tf_op jit(solution)/shard_map/embed_back/pallas_call | solution.py:831
  (840 shorter events, 611.6 us)
Async XLA Ops:
  7.2 121.1 %all-gather.7.cloned.1.call-start = ((), (), s32[]{:S(2)}) async-start(), calls=%async_computation.6 | async-start | bytes 5234688 | tf_op jit(solution)/shard_map/all_gather | solution.py:1044
  11.1 269.9 %all-gather.9.cloned.1.call-start = ((), (), s32[]{:S(2)}) async-start(), calls=%async_computation.7 | async-start | bytes 4718592 | tf_op jit(solution)/shard_map/all_gather | solution.py:1045
  12.1 340.1 %all-gather.11.cloned.1.call-start = ((), (), s32[]{:S(2)}) async-start(), calls=%async_computation.8 | async-start | bytes 4718592 | tf_op jit(solution)/shard_map/all_gather | solution.py:1046
  13.9 25.1 %collective-permute-start.1 = (bf16[4,128,512]{2,1,0:T(8,128)(2,1)S(1)}, bf16[4,128,512]{2,1,0:T(8,128)(2,1)S(1)}, u32[]{:S(2)}, u32[]{:S(2)}) collective-permute-start(bf16[4,128,512]{2,1,0:T(8,128)(2,1)S(1)} %get-tuple-element.633.refs_3_), channel_id=1, source_target_pairs={{0,1},{1,0},{2,3},{3,2},{4,5},{5,4},{6,7},{7,6},{8,9},{9,8},{10,11... | collective-permute-start | bytes 1572872 | tf_op jit(solution)/shard_map/ppermute | solution.py:941
  14.4 20.8 %collective-permute-start.2 = (bf16[4,128,512]{2,1,0:T(8,128)(2,1)S(1)}, bf16[4,128,512]{2,1,0:T(8,128)(2,1)S(1)}, u32[]{:S(2)}, u32[]{:S(2)}) collective-permute-start(bf16[4,128,512]{2,1,0:T(8,128)(2,1)S(1)} %get-tuple-element.633.refs_3_), channel_id=1, source_target_pairs={{0,2},{1,3},{2,0},{3,1},{4,6},{5,7},{6,4},{7,5},{8,10},{9,11},{10,... | collective-permute-start | bytes 1572872 | tf_op jit(solution)/shard_map/ppermute | solution.py:941
  18.9 44.4 %collective-permute-start.4 = (s32[8,640]{1,0:T(8,128)}, s32[8,640]{1,0:T(8,128)S(1)}, u32[]{:S(2)}, u32[]{:S(2)}) collective-permute-start(s32[8,640]{1,0:T(8,128)} %pad_select_fusion.refs_1_), channel_id=1, source_target_pairs={{0,8},{4,12},{8,0},{12,4},{16,24},{20,28},{24,16},{28,20},{1,9},{5... | collective-permute-start | bytes 61448 | tf_op jit(solution)/shard_map/ppermute | solution.py:941
  39.0 27.8 %collective-permute-start.5 = (s32[8,640]{1,0:T(8,128)}, s32[8,640]{1,0:T(8,128)S(1)}, u32[]{:S(2)}, u32[]{:S(2)}) collective-permute-start(s32[8,640]{1,0:T(8,128)} %pad_select_fusion.refs_1_), channel_id=1, source_target_pairs={{0,12},{4,8},{8,4},{12,0},{16,28},{20,24},{24,20},{28,16},{1,13},{... | collective-permute-start | bytes 61448 | tf_op jit(solution)/shard_map/ppermute | solution.py:941
  62.3 39.7 %collective-permute-start.12 = (bf16[576,128]{1,0:T(8,128)(2,1)}, bf16[576,128]{1,0:T(8,128)(2,1)}, u32[]{:S(2)}, u32[]{:S(2)}) collective-permute-start(bf16[576,128]{1,0:T(8,128)(2,1)} %get-tuple-element.316), channel_id=1, source_target_pairs={{0,16},{4,20},{8,24},{12,28},{16,0},{20,4},{24,8},{28,12},{1,17},{... | collective-permute-start | bytes 442376 | tf_op jit(solution)/shard_map/ppermute | solution.py:941
  63.3 44.7 %collective-permute-start.13 = (bf16[576,128]{1,0:T(8,128)(2,1)}, bf16[576,128]{1,0:T(8,128)(2,1)}, u32[]{:S(2)}, u32[]{:S(2)}) collective-permute-start(bf16[576,128]{1,0:T(8,128)(2,1)} %get-tuple-element.313.refs_7_), channel_id=1, source_target_pairs={{0,20},{4,16},{8,28},{12,24},{16,4},{20,0},{24,12},{28,8},{1,21},{... | collective-permute-start | bytes 442376 | tf_op jit(solution)/shard_map/ppermute | solution.py:941
  66.8 35.2 %collective-permute-start = (s32[8,640]{1,0:T(8,128)}, s32[8,640]{1,0:T(8,128)}, u32[]{:S(2)}, u32[]{:S(2)}) collective-permute-start(s32[8,640]{1,0:T(8,128)} %pad_select_fusion.refs_1_), channel_id=1, source_target_pairs={{0,4},{4,0},{8,12},{12,8},{16,20},{20,16},{24,28},{28,24},{1,5},{5... | collective-permute-start | bytes 61448 | tf_op jit(solution)/shard_map/ppermute | solution.py:941
  79.5 44.4 %collective-permute-start.16 = (bf16[576,128]{1,0:T(8,128)(2,1)S(1)}, bf16[576,128]{1,0:T(8,128)(2,1)S(1)}, u32[]{:S(2)}, u32[]{:S(2)}) collective-permute-start(bf16[576,128]{1,0:T(8,128)(2,1)S(1)} %get-tuple-element.315.refs_7_), channel_id=1, source_target_pairs={{0,12},{4,8},{8,4},{12,0},{16,28},{20,24},{24,20},{28,16},{1,13},{... | collective-permute-start | bytes 442376 | tf_op jit(solution)/shard_map/ppermute | solution.py:941
  169.2 24.8 %collective-permute-start.27 = (bf16[768,256]{1,0:T(8,128)(2,1)S(1)}, bf16[768,256]{1,0:T(8,128)(2,1)}, u32[]{:S(2)}, u32[]{:S(2)}) collective-permute-start(bf16[768,256]{1,0:T(8,128)(2,1)S(1)} %text_in.1.refs_5_.refs_1_), channel_id=1, source_target_pairs={{0,1},{1,0},{2,3},{3,2},{4,5},{5,4},{6,7},{7,6},{8,9},{9,8},{10,11... | collective-permute-start | bytes 1179656 | tf_op jit(solution)/shard_map/ppermute | solution.py:941
  169.2 756.2 %reduce-scatter.8.cloned.1.call-start = ((), (), s32[]{:S(2)}) async-start(), calls=%async_computation.5 | async-start | bytes 4718592 | tf_op jit(solution)/shard_map/reduce_scatter | solution.py:1405
  184.8 23.9 %collective-permute-start.30 = (bf16[192,1024]{1,0:T(8,128)(2,1)S(1)}, bf16[192,1024]{1,0:T(8,128)(2,1)S(1)}, u32[]{:S(2)}, u32[]{:S(2)}) collective-permute-start(bf16[192,1024]{1,0:T(8,128)(2,1)S(1)} %get-tuple-element.346.refs_1_), channel_id=1, source_target_pairs={{0,2},{1,3},{2,0},{3,1},{4,6},{5,7},{6,4},{7,5},{8,10},{9,11},{10,... | collective-permute-start | bytes 1179656 | tf_op jit(solution)/shard_map/ppermute | solution.py:941
  372.7 38.7 %collective-permute-start.63 = (bf16[192,1024]{1,0:T(8,128)(2,1)}, bf16[192,1024]{1,0:T(8,128)(2,1)}, u32[]{:S(2)}, u32[]{:S(2)}) collective-permute-start(bf16[192,1024]{1,0:T(8,128)(2,1)} %get-tuple-element.394.refs_9_.refs_2_), channel_id=1, source_target_pairs={{0,2},{1,3},{2,0},{3,1},{4,6},{5,7},{6,4},{7,5},{8,10},{9,11},{10,... | collective-permute-start | bytes 1179656 | tf_op jit(solution)/shard_map/ppermute | solution.py:941
  444.4 20.4 %collective-permute-start.65 = (bf16[192,1024]{1,0:T(8,128)(2,1)S(1)}, bf16[192,1024]{1,0:T(8,128)(2,1)S(1)}, u32[]{:S(2)}, u32[]{:S(2)}) collective-permute-start(bf16[192,1024]{1,0:T(8,128)(2,1)S(1)} %get-tuple-element.407.refs_9_.refs_2_), channel_id=1, source_target_pairs={{0,2},{1,3},{2,0},{3,1},{4,6},{5,7},{6,4},{7,5},{8,10},{9,11},{10,... | collective-permute-start | bytes 1179656 | tf_op jit(solution)/shard_map/ppermute | solution.py:941
  446.8 25.4 %collective-permute-start.72 = (bf16[192,1024]{1,0:T(8,128)(2,1)S(1)}, bf16[192,1024]{1,0:T(8,128)(2,1)S(1)}, u32[]{:S(2)}, u32[]{:S(2)}) collective-permute-start(bf16[192,1024]{1,0:T(8,128)(2,1)S(1)} %get-tuple-element.419.refs_1_), channel_id=1, source_target_pairs={{0,2},{1,3},{2,0},{3,1},{4,6},{5,7},{6,4},{7,5},{8,10},{9,11},{10,... | collective-permute-start | bytes 1179656 | tf_op jit(solution)/shard_map/ppermute | solution.py:941
  502.5 435.4 %reduce-scatter.6.cloned.1.call-start = ((), (), s32[]{:S(2)}) async-start(), calls=%async_computation.4 | async-start | bytes 4718592 | tf_op jit(solution)/shard_map/reduce_scatter | solution.py:1439
  504.6 26.6 %collective-permute-start.75 = (bf16[384,1024]{1,0:T(8,128)(2,1)}, bf16[384,1024]{1,0:T(8,128)(2,1)S(1)}, u32[]{:S(2)}, u32[]{:S(2)}) collective-permute-start(bf16[384,1024]{1,0:T(8,128)(2,1)} %copy-done.162), channel_id=1, source_target_pairs={{0,1},{1,0},{2,3},{3,2},{4,5},{5,4},{6,7},{7,6},{8,9},{9,8},{10,11... | collective-permute-start | bytes 2359304 | tf_op jit(solution)/shard_map/ppermute | solution.py:941
  576.4 22.6 %collective-permute-start.88 = (bf16[192,1024]{1,0:T(8,128)(2,1)S(1)}, bf16[192,1024]{1,0:T(8,128)(2,1)S(1)}, u32[]{:S(2)}, u32[]{:S(2)}) collective-permute-start(bf16[192,1024]{1,0:T(8,128)(2,1)S(1)} %get-tuple-element.450.refs_7_.refs_2_), channel_id=1, source_target_pairs={{0,2},{1,3},{2,0},{3,1},{4,6},{5,7},{6,4},{7,5},{8,10},{9,11},{10,... | collective-permute-start | bytes 1179656 | tf_op jit(solution)/shard_map/ppermute | solution.py:941
  577.5 21.5 %collective-permute-start.89 = (bf16[192,1024]{1,0:T(8,128)(2,1)S(1)}, bf16[192,1024]{1,0:T(8,128)(2,1)S(1)}, u32[]{:S(2)}, u32[]{:S(2)}) collective-permute-start(bf16[192,1024]{1,0:T(8,128)(2,1)S(1)} %get-tuple-element.472.refs_1_), channel_id=1, source_target_pairs={{0,2},{1,3},{2,0},{3,1},{4,6},{5,7},{6,4},{7,5},{8,10},{9,11},{10,... | collective-permute-start | bytes 1179656 | tf_op jit(solution)/shard_map/ppermute | solution.py:941
  626.9 313.0 %reduce-scatter.4.cloned.1.call-start = ((), (), s32[]{:S(2)}) async-start(), calls=%async_computation.3 | async-start | bytes 5160960 | tf_op jit(solution)/shard_map/reduce_scatter | solution.py:1523
  629.5 28.4 %collective-permute-start.95 = (bf16[384,1024]{1,0:T(8,128)(2,1)}, bf16[384,1024]{1,0:T(8,128)(2,1)S(1)}, u32[]{:S(2)}, u32[]{:S(2)}) collective-permute-start(bf16[384,1024]{1,0:T(8,128)(2,1)} %copy-done.161), channel_id=1, source_target_pairs={{0,1},{1,0},{2,3},{3,2},{4,5},{5,4},{6,7},{7,6},{8,9},{9,8},{10,11... | collective-permute-start | bytes 2359304 | tf_op jit(solution)/shard_map/ppermute | solution.py:941
  702.6 22.6 %collective-permute-start.104 = (bf16[384,1024]{1,0:T(8,128)(2,1)S(1)}, bf16[384,1024]{1,0:T(8,128)(2,1)S(1)}, u32[]{:S(2)}, u32[]{:S(2)}) collective-permute-start(bf16[384,1024]{1,0:T(8,128)(2,1)S(1)} %get-tuple-element.538), channel_id=1, source_target_pairs={{0,1},{1,0},{2,3},{3,2},{4,5},{5,4},{6,7},{7,6},{8,9},{9,8},{10,11... | collective-permute-start | bytes 2359304 | tf_op jit(solution)/shard_map/ppermute | solution.py:941
  723.9 21.1 %collective-permute-start.105 = (bf16[192,1024]{1,0:T(8,128)(2,1)S(1)}, bf16[192,1024]{1,0:T(8,128)(2,1)S(1)}, u32[]{:S(2)}, u32[]{:S(2)}) collective-permute-start(bf16[192,1024]{1,0:T(8,128)(2,1)S(1)} %get-tuple-element.506.refs_12_.refs_2_), channel_id=1, source_target_pairs={{0,2},{1,3},{2,0},{3,1},{4,6},{5,7},{6,4},{7,5},{8,10},{9,11},{10,... | collective-permute-start | bytes 1179656 | tf_op jit(solution)/shard_map/ppermute | solution.py:941
  762.5 24.9 %collective-permute-start.110 = (bf16[384,1024]{1,0:T(8,128)(2,1)S(1)}, bf16[384,1024]{1,0:T(8,128)(2,1)S(1)}, u32[]{:S(2)}, u32[]{:S(2)}) collective-permute-start(bf16[384,1024]{1,0:T(8,128)(2,1)S(1)} %get-tuple-element.572), channel_id=1, source_target_pairs={{0,1},{1,0},{2,3},{3,2},{4,5},{5,4},{6,7},{7,6},{8,9},{9,8},{10,11... | collective-permute-start | bytes 2359304 | tf_op jit(solution)/shard_map/ppermute | solution.py:941
  765.0 26.0 %collective-permute-start.109 = (bf16[768,256]{1,0:T(8,128)(2,1)S(1)}, bf16[768,256]{1,0:T(8,128)(2,1)S(1)}, u32[]{:S(2)}, u32[]{:S(2)}) collective-permute-start(bf16[768,256]{1,0:T(8,128)(2,1)S(1)} %add.381.refs_11_), channel_id=1, source_target_pairs={{0,2},{1,3},{2,0},{3,1},{4,6},{5,7},{6,4},{7,5},{8,10},{9,11},{10,... | collective-permute-start | bytes 1179656 | tf_op jit(solution)/shard_map/ppermute | solution.py:941
  812.6 34.1 %collective-permute-start.115 = (bf16[192,1024]{1,0:T(8,128)(2,1)}, bf16[192,1024]{1,0:T(8,128)(2,1)S(1)}, u32[]{:S(2)}, u32[]{:S(2)}) collective-permute-start(bf16[192,1024]{1,0:T(8,128)(2,1)} %copy-done.97), channel_id=1, source_target_pairs={{0,2},{1,3},{2,0},{3,1},{4,6},{5,7},{6,4},{7,5},{8,10},{9,11},{10,... | collective-permute-start | bytes 1179656 | tf_op jit(solution)/shard_map/ppermute | solution.py:941
  813.4 25.3 %collective-permute-start.114 = (bf16[192,1024]{1,0:T(8,128)(2,1)}, bf16[192,1024]{1,0:T(8,128)(2,1)S(1)}, u32[]{:S(2)}, u32[]{:S(2)}) collective-permute-start(bf16[192,1024]{1,0:T(8,128)(2,1)} %copy-done.125), channel_id=1, source_target_pairs={{0,2},{1,3},{2,0},{3,1},{4,6},{5,7},{6,4},{7,5},{8,10},{9,11},{10,... | collective-permute-start | bytes 1179656 | tf_op jit(solution)/shard_map/ppermute | solution.py:941
  856.4 21.3 %collective-permute-start.120 = (bf16[576,128]{1,0:T(8,128)(2,1)S(1)}, bf16[576,128]{1,0:T(8,128)(2,1)S(1)}, u32[]{:S(2)}, u32[]{:S(2)}) collective-permute-start(bf16[576,128]{1,0:T(8,128)(2,1)S(1)} %get-tuple-element.587), channel_id=1, source_target_pairs={{0,20},{4,16},{8,28},{12,24},{16,4},{20,0},{24,12},{28,8},{1,21},{... | collective-permute-start | bytes 442376 | tf_op jit(solution)/shard_map/ppermute | solution.py:941
  913.2 21.7 %collective-permute-start.123 = (bf16[4,128,512]{2,1,0:T(8,128)(2,1)}, bf16[4,128,512]{2,1,0:T(8,128)(2,1)}, u32[]{:S(2)}, u32[]{:S(2)}) collective-permute-start(bf16[4,128,512]{2,1,0:T(8,128)(2,1)} %get-tuple-element.627), channel_id=1, source_target_pairs={{0,1},{1,0},{2,3},{3,2},{4,5},{5,4},{6,7},{7,6},{8,9},{9,8},{10,11... | collective-permute-start | bytes 1572872 | tf_op jit(solution)/shard_map/ppermute | solution.py:941
  914.1 20.8 %collective-permute-start.125 = (bf16[4,128,512]{2,1,0:T(8,128)(2,1)}, bf16[4,128,512]{2,1,0:T(8,128)(2,1)}, u32[]{:S(2)}, u32[]{:S(2)}) collective-permute-start(bf16[4,128,512]{2,1,0:T(8,128)(2,1)} %fusion.7), channel_id=1, source_target_pairs={{0,2},{1,3},{2,0},{3,1},{4,6},{5,7},{6,4},{7,5},{8,10},{9,11},{10,... | collective-permute-start | bytes 1572872 | tf_op jit(solution)/shard_map/ppermute | solution.py:941
  (310 other events, 3077.0 us)
Sparse Core Ops, SparseCore 0:
  11.2 105.1 all-gather.6
  119.1 71.7 all-gather.8
  193.6 71.6 all-gather.10
  502.6 88.0 reduce-scatter.7
  627.0 88.1 reduce-scatter.5
  809.5 104.9 reduce-scatter.3

commit v5 on v4

--- a/solution.py
+++ b/solution.py
@@ -15,9 +15,13 @@
 LOW = jnp.bfloat16
 F32 = jnp.float32
 
+SELF = (0, 1, 2, 6)
+CROSS = (3, 4, 5, 7)
+
 SMALL = pl.CostEstimate(flops=1024, bytes_accessed=1024, transcendentals=0)
 
-PIECES = 2
+PIECES = (2, 1)
+MORE_PIECES = (1, 1, 1)
 
 clip_limit = 0.004
 stability_offset = 1e-08
@@ -105,6 +109,11 @@
         self.array = array
 
 
+class Ahead:
+    def __init__(self, array):
+        self.array = array
+
+
 class Shared:
     def __init__(self, shape, kind):
         self.full, self.array = sds(shape, kind), None
@@ -124,11 +133,17 @@
 
 
 def kernel(body, outs, operands, flops=0, scratch=(), name=None, exps=0, after=(), margin=12):
-    arrays, specs, windows, shown = [], [], [], []
+    arrays, specs, windows, shown, fetched = [], [], [], [], {}
     outs = list(outs)
     for i, a in enumerate(operands):
-        shown.append(not isinstance(a, Carry))
-        if isinstance(a, Carry):
+        shown.append(not isinstance(a, (Carry, Ahead)))
+        if isinstance(a, Ahead):
+            arrays.append(hold(a.array, pltpu.HBM))
+            specs.append(in_hbm())
+            windows.append(None)
+            outs.append(Flow(sds(a.array.shape, a.array.dtype)))
+            fetched[len(outs) - 1] = i
+        elif isinstance(a, Carry):
             arrays.append(hold(a.array, pltpu.VMEM))
             specs.append(in_vmem())
             windows.append(None)
@@ -172,10 +187,14 @@
             out_shapes.append(pltpu.HBM(o.shape, o.dtype))
             out_specs.append(in_hbm())
         owners.append(None)
+    out_parts.append(("token", None, None, None, len(out_shapes)))
+    out_shapes.append(pltpu.VMEM((8, 128), F32))
+    out_specs.append(in_vmem())
+    owners.append(None)
     moved = [w for w in windows if w is not None]
     made = [p for p in out_parts if p[0] == "put"]
     count_in, count_extra, count_after = len(arrays), len(extra), len(after)
-    count_out, count_moved, count_arrays = len(outs), len(moved), len(out_shapes)
+    count_out, count_moved, count_arrays = len(out_parts), len(moved), len(out_shapes)
 
     def run_body(*refs):
         refs = list(refs)
@@ -226,6 +245,11 @@
             elif kind == "copy":
                 sources[j] = (ins[what], out_refs[owner])
                 put(j)
+            elif kind == "token":
+                out_refs[owner][...] = jnp.zeros((8, 128), F32)
+            elif j in fetched:
+                sources[j] = (ins[fetched[j]], out_refs[owner])
+                put(j)
             else:
                 body_outs.append(out_refs[owner])
         body(need, put, *views, *body_outs, *rest)
@@ -257,7 +281,7 @@
     for owner, result in zip(owners, results):
         if owner is not None:
             owner.array = result
-    return [r for owner, r in zip(owners, results) if owner is None] or [results[-1]]
+    return [r for owner, r in zip(owners, results) if owner is None]
 
 
 def flat(ref):
@@ -447,7 +471,7 @@
         [total_ref[...], jnp.zeros((128 - total_ref.shape[0], frames), F32)], axis=0
     )
     col_ref[...] = jnp.transpose(wide)
-    share = 1.0 / valid_ref[0]
+    share = 1.0 / valid_ref[0:1, 0:1]
     gap = (col_ref[:, :books] - col_ref[:, books : 2 * books]) * (weight_ref[...] * share)
     loss_ref[...] = jnp.broadcast_to(jnp.sum(gap).reshape(1, 1), loss_ref.shape)
     code = lax.broadcasted_iota(jnp.int32, (height, vocab), 1)
@@ -617,6 +641,12 @@
     return center * lax.rsqrt(spread + 1e-05) * gain + shift
 
 
+def count_body(books, *refs):
+    *packet_refs, out_ref = refs
+    total = sum(p[books : books + 1, 0:128] for p in packet_refs)
+    out_ref[...] = jnp.broadcast_to(total, out_ref.shape).astype(F32)
+
+
 def merge_body(books, own_ref, far_ref, out_ref):
     own, far = own_ref[:books, :], far_ref[:books, :]
     high = jnp.maximum(own, far)
@@ -636,9 +666,10 @@
 
 
 def add_parts_body(keep_ref, got_ref, *out_refs):
-    rows = out_refs[0].shape[0]
-    for j, out_ref in enumerate(out_refs):
-        at = slice(j * rows, (j + 1) * rows)
+    start = 0
+    for out_ref in out_refs:
+        at = slice(start, start + out_ref.shape[0])
+        start += out_ref.shape[0]
         out_ref[...] = (keep_ref[at, :].astype(F32) + got_ref[at, :].astype(F32)).astype(LOW)
 
 
@@ -1030,18 +1061,25 @@
 
     last = []
 
-    def run(body, outs, operands, **rest):
-        shared = [o.shared.array for o in outs if isinstance(o, Into)]
-        wait_for = [a for a in last if not any(a is b for b in shared)]
-        results = kernel(body, outs, operands, after=wait_for, **rest)
-        last[:] = [results[-1]]
+    def run(body, outs, operands, after=(), **rest):
+        *results, token = kernel(body, outs, operands, after=last + list(after), **rest)
+        last[:] = [token]
         return results
 
+    def run_block(*args, **rest):
+        return run(*args, **rest)
+
+    def run_weight(*args, **rest):
+        results = run(*args, after=soon[:1], **rest)
+        del soon[:1]
+        return results
+
     norm_pad = jnp.pad(norm_params.astype(LOW), ((0, 16 - norm_params.shape[0]), (0, columns - share)))
-    attn_flat = jnp.concatenate(
-        [attention.astype(LOW).reshape(-1, columns), text_proj.astype(LOW).T, norm_pad], axis=0
-    )
-    attn_all = lax.all_gather(attn_flat, "dp", axis=0)
+    attn_rows = attention.astype(LOW)
+    self_flat = jnp.concatenate([attn_rows[n] for n in SELF] + [norm_pad], axis=0)
+    cross_flat = jnp.concatenate([attn_rows[n] for n in CROSS] + [text_proj.astype(LOW).T], axis=0)
+    self_all = lax.all_gather(self_flat, "dp", axis=0)
+    cross_all = lax.all_gather(cross_flat, "dp", axis=0)
     ffn_all = lax.all_gather(feedforward.astype(LOW), "dp", axis=0)
     head_all = lax.all_gather(tables[books:].astype(LOW), "dp", axis=0)
 
@@ -1056,7 +1094,6 @@
     count_line = jnp.broadcast_to(jnp.sum(weight_int), (8 - books, padded))
     packet = jnp.concatenate([lines, count_line], axis=0)
     packets = [packet] + [swap(packet, "dp", m) for m in range(1, dp)]
-    valid_count = sum(p[books, 0] for p in packets).astype(F32)
     vocab_base = (place ^ jnp.arange(tensor, dtype=jnp.int32)) * vocab
     group_order = group ^ jnp.arange(dp, dtype=jnp.int32)
     place_order = place ^ jnp.arange(tensor, dtype=jnp.int32)
@@ -1066,7 +1103,6 @@
     bias_columns = [jnp.transpose(line) for line in bias_lines]
     targets = (jnp.roll(audio_codes, -1, axis=1) - place * vocab).astype(jnp.int32)
     targets = [targets[c] for c in range(clips)]
-    valid_arg = Scalar(valid_count.reshape(1))
     loss_weight = [weight_int[c].astype(F32) for c in range(clips)]
     placed = positions_rows(core * height, height, width)
 
@@ -1081,7 +1117,11 @@
         for m, piece in enumerate(embedded, low_end):
             arrived[m] = swap(piece, "dp", m) if m else piece
         last += [a for a in arrived[low_end + step : low_end + 2 * step] if a is not None]
-    last += bias_lines + bias_columns + targets + loss_weight + [placed]
+    (counted,) = norm_rows_kernel(
+        partial(count_body, books), [sds((8, 128), F32)], packets, None, last, name="count"
+    )
+    last[:] = bias_lines + bias_columns + targets + loss_weight + [placed, counted]
+    last += [a for a in arrived if a is not None]
     aligned = share % 128 == 0
     if aligned:
         strips = run(
@@ -1095,12 +1135,13 @@
         strips = jnp.take(jnp.stack(arrived), group_order, axis=0)
         strips = jnp.transpose(strips, (1, 0, 2)).reshape(clips, strip, width)
 
-    norm_rows = attn_all[:, 8 * share + text_share :, :share]
+    norm_rows = self_all[:, 4 * share :, :share]
     norm_rows = jnp.transpose(norm_rows, (1, 0, 2)).reshape(16, width).astype(F32)
 
     def w_attn(n):
+        array, at = (self_all, SELF.index(n)) if n in SELF else (cross_all, CROSS.index(n))
         return Window(
-            attn_all, (dp, share, columns), lambda ref: ref.at[:, pl.ds(n * share, share), :]
+            array, (dp, share, columns), lambda ref: ref.at[:, pl.ds(at * share, share), :]
         )
 
     def w_member(array, n):
@@ -1126,8 +1167,11 @@
         last[:] = [out]
         return new, (out, swap_core(free(out)))
 
-    def norm_back(which, hidden, parts, before):
-        operands = [hidden, *parts] + ([before] if before is not None else [])
+    def norm_back(which, c, parts, before):
+        rows = near.get((which, c, "back"), hidden[which][c])
+        if before is not None:
+            before = near_grad.get((which, c), before)
+        operands = [rows, *parts] + ([before] if before is not None else [])
         new, out, sums = norm_rows_kernel(
             partial(norm_back_body, which, len(parts)),
             [half_sds, half_low, sds((8, width), F32)],
@@ -1139,24 +1183,25 @@
         last[:] = [out]
         return new, (out, swap_core(free(out))), free(sums)
 
-    waiting, soon = [], []
+    waiting, soon, middle = [], [], []
     moving = [None] * clips
 
-    def flush():
+    def flush(pieces=PIECES):
         if waiting:
             c, keep, got = waiting.pop()
             parts = norm_rows_kernel(
                 add_parts_body,
-                [sds((height // PIECES, width), LOW)] * PIECES,
+                [sds((height * part // sum(pieces), width), LOW) for part in pieces],
                 [keep, got],
                 None,
-                last,
+                last + middle,
                 name="add",
             )
             last[:] = [parts[-1]]
             fars = [across(free(part))[1] for part in parts]
             moving[c] = (*parts, *fars)
             soon[:] = fars[:-1]
+            middle[:] = fars[-1:]
 
     def reduce_rows(c, keep, send):
         waiting.append((c, keep, swap_core(free(send))))
@@ -1171,9 +1216,9 @@
                 norm_rows,
                 fetch(text_rows),
                 Window(
-                    attn_all,
+                    cross_all,
                     (dp, text_share, columns),
-                    lambda ref: ref.at[:, pl.ds(8 * share, text_share), :],
+                    lambda ref: ref.at[:, pl.ds(4 * share, text_share), :],
                 ),
             ],
             flops=2 * clips * text_len * text_width * columns,
@@ -1189,6 +1234,38 @@
     units = feedforward.shape[2]
     inner = sds((frames, units), LOW)
     every = range(clips)
+
+    near, near_grad = {}, {}
+
+    def ahead(phase, c):
+        at, clip = (phase - 1, c + 1) if c + 1 < clips else (phase, 0)
+        if at < 0 or (phase == 3 and clip == 0) or (clip == c):
+            return []
+        return [Ahead(hidden[at][clip])]
+
+    def took(phase, c, results):
+        at, clip = (phase - 1, c + 1) if c + 1 < clips else (phase, 0)
+        if ahead(phase, c):
+            *results, near[at, clip] = results
+        return results
+
+    def ahead_back(phase, c):
+        at, clip = (phase, c + 1) if c + 1 < clips else (phase - 1, 0)
+        if clip == c:
+            return []
+        found = [Ahead(hidden[at][clip])]
+        if at < 3:
+            found.append(Ahead(grads[clip]))
+        return found
+
+    def took_back(phase, c, results):
+        at, clip = (phase, c + 1) if c + 1 < clips else (phase - 1, 0)
+        count = len(ahead_back(phase, c))
+        if count == 2:
+            near_grad[at, clip] = results[-1]
+        if count:
+            near[at, clip, "back"] = results[len(results) - count]
+        return results[: len(results) - count]
 
     def embed_step(c):
         mine = strips[c]
@@ -1204,15 +1281,16 @@
 
     def self_step(c, pair):
         own, got = pair
-        *saved, keep, send, left, right, hidden[0][c] = run(
+        *saved, keep, send, left, right, hidden[0][c] = took(0, c, run_block(
             self_forward_body,
             [full, full, full, full, lse_sds, flow, flow, Copy(1), Copy(3)],
             [core_arg, own, w_attn(0), got, w_attn(1), w_attn(2), w_attn(6)]
-            + [Carry(hidden[0][c])],
+            + [Carry(hidden[0][c])]
+            + ahead(0, c),
             flops=8 * frames * width * columns + 4 * score_flops * frames,
             scratch=tot,
             name="self_forward",
-        )
+        ))
         pairs[0][c] = (left, right)
         reduce_rows(c, keep, send)
         return saved
@@ -1237,27 +1315,29 @@
     def cross_step(c, pair):
         own, got = pair
         k, v = text_rows_of(text_key, c), text_rows_of(text_value, c)
-        q, o, lse, keep, send, left, right, hidden[1][c] = run(
+        q, o, lse, keep, send, left, right, hidden[1][c] = took(1, c, run_block(
             cross_forward_body,
             [full, full, lse_sds, flow, flow, Copy(1), Copy(3)],
             [core_arg, own, w_attn(3), got, bias_lines[c], k, v, w_attn(7)]
-            + [Carry(hidden[1][c])],
+            + [Carry(hidden[1][c])]
+            + ahead(1, c),
             flops=4 * frames * width * columns + 4 * score_flops * text_len,
             scratch=tot,
             name="cross_forward",
-        )
+        ))
         pairs[1][c] = (left, right)
         reduce_rows(c, keep, send)
         return (q, k, v, o, lse)
 
     def ffn_step(c, pair):
-        *saved, keep, send, left, right, hidden[2][c] = run(
+        *saved, keep, send, left, right, hidden[2][c] = took(2, c, run_block(
             ffn_forward_body,
             [inner, inner, flow, flow, Copy(1), Copy(2)],
-            [core_arg, *pair, w_member(ffn_all, 0), w_member(ffn_all, 1), Carry(hidden[2][c])],
+            [core_arg, *pair, w_member(ffn_all, 0), w_member(ffn_all, 1), Carry(hidden[2][c])]
+            + ahead(2, c),
             flops=4 * frames * width * units,
             name="ffn_forward",
-        )
+        ))
         pairs[2][c] = (left, right)
         reduce_rows(c, keep, send)
         return saved
@@ -1273,11 +1353,11 @@
             text_parts = text_in_step()
     text_hidden, text_key, text_value = text_step()
     for c in every:
-        hidden[1][c], pairs[1][c] = norm_step(1, hidden[0][c], moving[c])
+        hidden[1][c], pairs[1][c] = norm_step(1, near.get((0, c), hidden[0][c]), moving[c])
         flush()
         kept[1][c] = cross_step(c, pairs[1][c])
     for c in every:
-        hidden[2][c], pairs[2][c] = norm_step(2, hidden[1][c], moving[c])
+        hidden[2][c], pairs[2][c] = norm_step(2, near.get((1, c), hidden[1][c]), moving[c])
         flush()
         kept[2][c] = ffn_step(c, pairs[2][c])
 
@@ -1286,7 +1366,7 @@
 
     def head_step(c, pair):
         own, got = pair
-        logits, stats, left, right, hidden[3][c] = run(
+        logits, stats, left, right, hidden[3][c] = took(3, c, run_block(
             head_forward_body,
             [
                 sds((frames, books * vocab), F32),
@@ -1296,11 +1376,12 @@
             ],
             [core_arg, own, targets[c], got]
             + [w_member(head_all, k) for k in range(books)]
-            + [Carry(hidden[3][c])],
+            + [Carry(hidden[3][c])]
+            + ahead(3, c),
             flops=2 * frames * width * books * vocab,
             scratch=tot,
             name="head_forward",
-        )
+        ))
         pairs[3][c] = (left, right)
         return logits, stats
 
@@ -1321,12 +1402,12 @@
         return stats
 
     def head_back_step(c, logits, stats):
-        grad, keep, send, loss = run(
+        grad, keep, send, loss = run_block(
             head_backward_body,
             [sds((frames, books * vocab), LOW), flow, flow, Flow(sds((8, 128), F32))],
             [core_arg, stats, loss_weight[c], targets[c], fetch(logits)]
             + [w_member(head_all, k) for k in range(books)]
-            + [valid_arg],
+            + [counted],
             flops=2 * frames * width * books * vocab,
             scratch=tot,
             name="head_backward",
@@ -1335,15 +1416,17 @@
         reduce_rows(c, keep, send)
         return grad
 
-    attn_shared = Shared((dp, 8 * share + text_share, columns), LOW)
+    self_shared = Shared((dp, 4 * share + text_share, columns), LOW)
+    cross_shared = Shared((dp, 4 * share, columns), LOW)
     ffn_shared = Shared((dp,) + feedforward.shape, LOW)
     head_shared = Shared((dp, books, share, vocab), LOW)
 
     def attn_into(n):
+        shared, at = (
+            (self_shared, SELF.index(n)) if n in SELF else (cross_shared, CROSS.index(n))
+        )
         return Into(
-            attn_shared,
-            (dp, share, columns),
-            lambda ref: ref.at[:, pl.ds(n * share, share), :],
+            shared, (dp, share, columns), lambda ref: ref.at[:, pl.ds(at * share, share), :]
         )
 
     def member_into(shared, n):
@@ -1352,7 +1435,7 @@
     def weights(lefts, rights, outs, name):
         total = rights[0].shape[1]
         turn_left = 2 * total > width
-        run(
+        run_weight(
             partial(weight_grad_body, clips, turn_left),
             outs,
             [core_arg] + [fetch(half) for pair in lefts for half in pair] + [fetch(a) for a in rights],
@@ -1365,7 +1448,7 @@
     logit_grads = [None] * clips
     ready = [None] * clips
     for c in every:
-        hidden[3][c], pairs[3][c] = norm_step(3, hidden[2][c], moving[c])
+        hidden[3][c], pairs[3][c] = norm_step(3, near.get((2, c), hidden[2][c]), moving[c])
         flush()
         ready[c] = head_step(c, pairs[3][c])
         if c:
@@ -1379,14 +1462,15 @@
 
     def ffn_back_step(c, pair):
         own, got = pair
-        grad, keep, send, left, right, grads[c] = run(
+        grad, keep, send, left, right, grads[c] = took_back(3, c, run_block(
             ffn_backward_body,
             [inner, flow, flow, Copy(1), Copy(2)],
             [core_arg, own, got, w_member(ffn_all, 1), fetch(kept[2][c][1]), w_member(ffn_all, 0)]
-            + [Carry(grads[c])],
+            + [Carry(grads[c])]
+            + ahead_back(3, c),
             flops=4 * frames * width * units,
             name="ffn_backward",
-        )
+        ))
         back_pairs[3][c] = (left, right)
         reduce_rows(c, keep, send)
         return grad
@@ -1395,9 +1479,9 @@
     back_pairs = [[None] * clips for _ in range(4)]
     inner_grads = [None] * clips
     for c in every:
-        grads[c], back_pairs[3][c], s = norm_back(3, hidden[3][c], moving[c], None)
+        grads[c], back_pairs[3][c], s = norm_back(3, c, moving[c], None)
         sums[3].append(s)
-        flush()
+        flush(MORE_PIECES if c == 0 else PIECES)
         inner_grads[c] = ffn_back_step(c, back_pairs[3][c])
         if c == 0:
             head_into = [member_into(head_shared, k) for k in range(books)]
@@ -1411,24 +1495,25 @@
         own, got = pair
         q, k, v, o, lse = kept[1][c]
         bias = bias_columns[c]
-        dq, dk, dv, keep, send, left, right, grads[c] = run(
+        dq, dk, dv, keep, send, left, right, grads[c] = took_back(2, c, run_block(
             cross_backward_body,
             [full, small, small, flow, flow, Copy(1), Copy(3)],
             [core_arg, own, w_attn(7), got, bias, fetch(q), k, v, fetch(lse), w_attn(3)]
-            + [Carry(grads[c])],
+            + [Carry(grads[c])]
+            + ahead_back(2, c),
             flops=4 * frames * width * columns + 10 * score_flops * text_len,
             scratch=[pltpu.VMEM((frames, columns), LOW)] + acc_text,
             name="cross_backward",
-        )
+        ))
         back_pairs[2][c] = (left, right)
         reduce_rows(c, keep, send)
         return (dq, dk, dv)
 
     cross_grads = [None] * clips
     for c in every:
-        grads[c], back_pairs[2][c], s = norm_back(2, hidden[2][c], moving[c], grads[c])
+        grads[c], back_pairs[2][c], s = norm_back(2, c, moving[c], grads[c])
         sums[2].append(s)
-        flush()
+        flush(MORE_PIECES if c < 2 else PIECES)
         cross_grads[c] = cross_back_step(c, back_pairs[2][c])
         if c == 0:
             weights(
@@ -1472,44 +1557,48 @@
     def self_back_step(c, pair):
         own, got = pair
         q, k, v, o, lse = kept[0][c]
-        grad, keep, send, left, right, grads[c] = run(
+        grad, keep, send, left, right, grads[c] = took_back(1, c, run_block(
             self_backward_body,
             [sds((frames, 3 * columns), LOW), flow, flow, Copy(1), Copy(3)],
             [core_arg, own, w_attn(6), got]
             + [fetch(a) for a in (q, k, v, lse)]
-            + [w_attn(0), w_attn(1), w_attn(2), Carry(grads[c])],
+            + [w_attn(0), w_attn(1), w_attn(2), Carry(grads[c])]
+            + ahead_back(1, c),
             flops=8 * frames * width * columns + 10 * score_flops * frames,
             scratch=[pltpu.VMEM((frames, columns), LOW)] + acc_self,
             name="self_backward",
-        )
+        ))
         back_pairs[1][c] = (left, right)
         reduce_rows(c, keep, send)
         return grad
 
     self_grads = [None] * clips
     for c in every:
-        grads[c], back_pairs[1][c], s = norm_back(1, hidden[1][c], moving[c], grads[c])
+        grads[c], back_pairs[1][c], s = norm_back(1, c, moving[c], grads[c])
         sums[1].append(s)
-        flush()
+        flush(MORE_PIECES if c < 2 else PIECES)
         self_grads[c] = self_back_step(c, back_pairs[1][c])
         if c == 0:
             text_grad = text_back_step()
             weights(back_pairs[2], [k[3] for k in kept[1]], [attn_into(7)], "cross_out")
         if c == min(1, clips - 1):
             weights(pairs[1], [g[0] for g in cross_grads], [attn_into(3)], "cross_query")
+            cross_sum = lax.psum_scatter(
+                free(cross_shared.array), "dp", scatter_dimension=0, tiled=False
+            )
 
     zero_lows = [None] * clips
 
     def zero_step(c):
-        _, (zero_lows[c], _), s = norm_back(0, hidden[0][c], moving[c], grads[c])
+        _, (zero_lows[c], _), s = norm_back(0, c, moving[c], grads[c])
         sums[0].append(s)
 
     zero_step(0)
-    flush()
+    flush(MORE_PIECES)
     text_into = Into(
-        attn_shared,
+        self_shared,
         (dp, text_share, columns),
-        lambda ref: ref.at[:, pl.ds(8 * share, text_share), :],
+        lambda ref: ref.at[:, pl.ds(4 * share, text_share), :],
     )
     (bias_grad,) = run(
         text_weight_body,
@@ -1520,7 +1609,7 @@
     )
     weights(back_pairs[1], [k[3] for k in kept[0]], [attn_into(6)], "self_out")
     weights(pairs[0], self_grads, [attn_into(n) for n in range(3)], "self_in")
-    attn_sum = lax.psum_scatter(free(attn_shared.array), "dp", scatter_dimension=0, tiled=False)
+    self_sum = lax.psum_scatter(free(self_shared.array), "dp", scatter_dimension=0, tiled=False)
     for c in range(1, clips):
         zero_step(c)
 
@@ -1556,8 +1645,13 @@
     )
     grad_norm_rows = lax.dynamic_slice_in_dim(norm_total, group * share, share, 1)
 
-    grad_attention = attn_sum[: 8 * share].reshape(attention.shape).astype(F32)
-    grad_text_proj = jnp.transpose(attn_sum[8 * share :]).astype(F32)
+    parts = [None] * attention.shape[0]
+    for at, n in enumerate(SELF):
+        parts[n] = self_sum[at * share : (at + 1) * share]
+    for at, n in enumerate(CROSS):
+        parts[n] = cross_sum[at * share : (at + 1) * share]
+    grad_attention = jnp.stack(parts).astype(F32)
+    grad_text_proj = jnp.transpose(self_sum[4 * share :]).astype(F32)
     grad_feedforward = ffn_sum.astype(F32)
     grad_heads = head_sum.astype(F32)
     local_square = (
@@ -1592,7 +1686,7 @@
     )
     return (
         mean_loss,
-        valid_count,
+        free(counted)[0, 0],
         grad_norm,
         attn_new,
         attn_new.astype(LOW),

time: 994 us -> 1010 us (1.016)
  waiting for transfers between devices: 281 us -> 356 us
  local copies, waits for them, and re-layouts: 108 us -> 58.9 us
    unnamed x398 -> x367, local copies, waits for them, and re-layouts: 85.8 us -> 43.1 us
    reduce_scatter x1 -> x2, waiting for transfers between devices: 0.01 us -> 37.9 us  [the longest x1 37.9 us: on_device(): lax.psum_scatter(free(cross_shared.array), 'dp', scatter_dimension=0, til...]
    ppermute x136 -> x142, waiting for transfers between devices: 281 us -> 317 us  [swap(): return lax.ppermute(values, axis, [(i, i ^ mask) for i in range(size)])]
    ppermute x136 -> x142, starting transfers between devices: 136 us -> 139 us  [swap(): return lax.ppermute(values, axis, [(i, i ^ mask) for i in range(size)])]
    pallas_call x50 -> x51, Pallas kernels: 39 us -> 38.2 us  [norm_rows_kernel(): pl.pallas_call(later(body, len(after), len(operands)), out_shape=tuple((p...]
  transfers between devices with their start and end apart: 142 -> 150, of which waited for: 61 -> 63; matrix products, arithmetic and copies ran while one was open for 4% -> 4% of each run, Pallas kernels for 36% -> 36%
where the time goes in v5:
time: 1010 us
  Pallas kernels  392 us (39%)
  waiting for transfers between devices  356 us (35%)
  starting transfers between devices  140 us (14%)
  local copies, waits for them, and re-layouts  58.9 us (6%)
  other arithmetic  38.3 us (4%)
  between operations  24.8 us (2%)
    ppermute x142, waiting for transfers between devices, swap(): return lax.ppermute(values, axis, [(i, i ^ mask) for i in range(size)])  317 us
    pallas_call x40, Pallas kernels, kernel(): pl.pallas_call(run_body, out_shape=tuple(out_shapes), in_specs=specs + [a...  291 us
    ppermute x142, starting transfers between devices, swap(): return lax.ppermute(values, axis, [(i, i ^ mask) for i in range(size)])  139 us
    unnamed x367, local copies, waits for them, and re-layouts  43.1 us
    pallas_call x51, Pallas kernels, norm_rows_kernel(): pl.pallas_call(later(body, len(after), len(operands)), out_shape=tuple((p...  38.2 us
    reduce_scatter x1, waiting for transfers between devices, on_device(): lax.psum_scatter(free(cross_shared.array), 'dp', scatter_dimension=0, til...  37.9 us
    pallas_call x4, Pallas kernels, embed(): pl.pallas_call(later(partial(embed_body, count, books), len(after), 1 + c...  35.7 us
    pallas_call x1, Pallas kernels, embed_back(): pl.pallas_call(later(partial(embed_back_body, groups), len(after), 1 + 2...  26.8 us
  transfers between devices with their start and end apart: 150, of which 63 were waited for; matrix products, arithmetic and copies ran while one was open for 4% of the time, Pallas kernels for 36%

profile of v5, /device:TPU:0, one launch (start us, length us, event | category | flops | bytes accessed | tf_op | source)
XLA Modules:
  0.0 1009.6 jit_solution(14596387294802769785)
XLA Ops:
  40.8 9.0 embed.4
  53.6 9.3 embed.5
  73.1 8.4 embed.6
  81.5 12.8 %collective-permute-start.16 = (bf16[576,128]{1,0:T(8,128)(2,1)S(1)}, bf16[576,128]{1,0:T(8,128)(2,1)S(1)}, u32[]{:S(2)}, u32[]{:S(2)}) collective-permute-start(bf16[576,128]{1,0:T(8,128)(2,1)S(1)} %get-tuple-element.394.refs_7_), channel_id=1, source_target_pairs={{0,12},{4,8},{8,4},{12,0},{16,28},{20,24},{24,20},{28,16},{1,13},{... | collective-permute-start | bytes 442376 | tf_op jit(solution)/shard_map/ppermute | solution.py:972
  94.3 9.0 embed.7
  117.9 8.9 collective-permute-done.17.refs_4_
  130.8 8.6 self_forward.3
  169.2 8.6 self_forward.5
  189.0 9.0 collective-permute-done.30.refs_7_.refs_3_
  287.2 9.4 ffn_forward.3
  308.5 8.1 ffn_forward.4
  333.0 8.1 ffn_forward.5
  359.5 10.7 %head_forward.3 = (f32[768,2048]{1,0:T(8,128)}, f32[8,768]{1,0:T(8,128)S(1)}, bf16[384,1024]{1,0:T(8,128)(2,1)}, bf16[384,1024]{1,0:T(8,128)(2,1)}, f32[384,1024...) custom-call(s32[1]{0:T(128)} %bitcast.refs_0_, bf16[384,1024]{1,0:T(8,128)(2,1)S(1)} %get-tuple-element.490.refs_2_.refs_1_, ...), custom_call_target="tpu_custom_call" | custom-call | flops 1024 | bytes 1024 | tf_op jit(solution)/shard_map/head_forward/pallas_call | solution.py:264
  375.3 9.8 head_forward.4
  389.1 8.6 head_backward.3
  402.1 9.6 head_forward.5
  415.7 8.9 head_backward.4
  436.1 8.6 head_backward.5
  445.7 10.8 %collective-permute-done.72.refs_7_.refs_3_ = bf16[256,1024]{1,0:T(8,128)(2,1)S(1)} collective-permute-done((bf16[256,1024]{1,0:T(8,128)(2,1)S(1)}, bf16[256,1024]{1,0:T(8,128)(2,1)S(1)}, u32[]{:S(2)}, u32[]{:S(2)}) %collective-permute-start.72) | collective-permute-done | bytes 524320 | tf_op jit(solution)/shard_map/ppermute | solution.py:972
  478.5 15.8 %head_weights.1 = (bf16[8,4,128,512]{3,2,1,0:T(8,128)(2,1)}, f32[8,128]{1,0:T(8,128)S(1)}) custom-call(s32[1]{0:T(128)} %bitcast.refs_0_, bf16[384,1024]{1,0:T(8,128)(2,1)} %get-tuple-element.533.refs_1_, bf16[384,1024]{1,0:T(8,128)(2,1)} %get-tuple-element.534.refs_2_, bf16[384,1024]{1,0:T(8,128)(2,1)} %get-tuple-element.535.refs_3_, ...), custom_call_target="tpu_custom_call" | custom-call | flops 1024 | bytes 1024 | tf_op jit(solution)/shard_map/head_weights/pallas_call | solution.py:264
  505.6 8.0 collective-permute-done.80.refs_3_.refs_6_
  571.9 10.9 %ffn_two.1 = (bf16[8,2,128,1024]{3,2,1,0:T(8,128)(2,1)}, f32[8,128]{1,0:T(8,128)S(1)}) custom-call(s32[1]{0:T(128)} %bitcast.refs_0_, bf16[384,1024]{1,0:T(8,128)(2,1)} %get-tuple-element.577.refs_1_, bf16[384,1024]{1,0:T(8,128)(2,1)} %get-tuple-element.578.refs_2_, bf16[384,1024]{1,0:T(8,128)(2,1)} %get-tuple-element.579.refs_3_, ...), custom_call_target="tpu_custom_call" | custom-call | flops 1024 | bytes 1024 | tf_op jit(solution)/shard_map/ffn_two/pallas_call | solution.py:264
  603.6 10.9 %ffn_one.1 = (bf16[8,2,128,1024]{3,2,1,0:T(8,128)(2,1)}, f32[8,128]{1,0:T(8,128)S(1)}) custom-call(s32[1]{0:T(128)} %bitcast.refs_0_, bf16[384,1024]{1,0:T(8,128)(2,1)} %get-tuple-element.600.refs_1_, bf16[384,1024]{1,0:T(8,128)(2,1)} %get-tuple-element.601.refs_2_, bf16[384,1024]{1,0:T(8,128)(2,1)} %get-tuple-element.602.refs_3_, ...), custom_call_target="tpu_custom_call", output_to_operand_aliasing={{0}: (10, {})} | custom-call | flops 1024 | bytes 1024 | tf_op jit(solution)/shard_map/ffn_one/pallas_call | solution.py:264
  663.8 11.4 %self_backward.3 = (bf16[768,768]{1,0:T(8,128)(2,1)}, bf16[384,1024]{1,0:T(8,128)(2,1)S(1)}, bf16[384,1024]{1,0:T(8,128)(2,1)S(1)}, bf16[384,1024]{1,0:T(8,128)(...) custom-call(s32[1]{0:T(128)} %bitcast.refs_0_, ...), custom_call_target="tpu_custom_call" | custom-call | flops 1024 | bytes 1024 | tf_op jit(solution)/shard_map/self_backward/pallas_call | solution.py:264
  708.8 11.1 %self_backward.4 = (bf16[768,768]{1,0:T(8,128)(2,1)}, bf16[384,1024]{1,0:T(8,128)(2,1)S(1)}, bf16[384,1024]{1,0:T(8,128)(2,1)S(1)}, bf16[384,1024]{1,0:T(8,128)(...) custom-call(s32[1]{0:T(128)} %bitcast.refs_0_, ...), custom_call_target="tpu_custom_call" | custom-call | flops 1024 | bytes 1024 | tf_op jit(solution)/shard_map/self_backward/pallas_call | solution.py:264
  736.4 11.5 %self_backward.5 = (bf16[768,768]{1,0:T(8,128)(2,1)}, bf16[384,1024]{1,0:T(8,128)(2,1)S(1)}, bf16[384,1024]{1,0:T(8,128)(2,1)S(1)}, bf16[384,1024]{1,0:T(8,128)(...) custom-call(s32[1]{0:T(128)} %bitcast.refs_0_, ...), custom_call_target="tpu_custom_call" | custom-call | flops 1024 | bytes 1024 | tf_op jit(solution)/shard_map/self_backward/pallas_call | solution.py:264
  751.5 11.3 %collective-permute-done.117.refs_10_.refs_3_ = bf16[256,1024]{1,0:T(8,128)(2,1)S(1)} collective-permute-done((bf16[256,1024]{1,0:T(8,128)(2,1)S(1)}, bf16[256,1024]{1,0:T(8,128)(2,1)S(1)}, u32[]{:S(2)}, u32[]{:S(2)}) %collective-permute-start.117) | collective-permute-done | bytes 524320 | tf_op jit(solution)/shard_map/ppermute | solution.py:972
  788.5 9.8 self_in.1
  823.2 9.7 collective-permute-done.123.refs_11_
  839.6 9.4 collective-permute-done.126.refs_14_
  849.1 26.8 %embed_back.1 = bf16[4,4,128,512]{3,2,1,0:T(8,128)(2,1)S(1)} custom-call(s32[4]{0:T(128)S(1)} %copy-done.133, s32[8,640]{1,0:T(8,128)} %pad_select_fusion.refs_1_.refs_0_, s32[8,640]{1,0:T(8,128)} %collective-permute-done.refs_2_.refs_1_, s32[8,640]{1,0:T(8,128)S(1)} %copy-done.97, s32[8,640]{1,0:T(8,128)S(1)} %copy-done.113, s32[8,640]{1,0:T(8,128)S(1)} %copy-done.106, ...), custom_call_target="tpu_custom_call" | custom-call | flops 1024 | bytes 1024 | tf_op jit(solution)/shard_map/embed_back/pallas_call | solution.py:862
  922.6 37.9 %reduce-scatter.7.cloned.1.call-done = bf16[1,512,256]{2,1,0:T(8,128)(2,1)} async-done(((bf16[8,512,256]{2,1,0:T(8,128)(2,1)}), bf16[1,512,256]{2,1,0:T(8,128)(2,1)}) %reduce-scatter.7.cloned.1.call-update) | async-done | bytes 262160 | tf_op jit(solution)/shard_map/reduce_scatter | solution.py:1586
  (822 shorter events, 624.1 us)
Async XLA Ops:
  7.2 109.9 %all-gather.9.cloned.1.call-start = ((), (), s32[]{:S(2)}) async-start(), calls=%async_computation.8 | async-start | bytes 2433024 | tf_op jit(solution)/shard_map/all_gather | solution.py:1081
  11.8 129.6 %all-gather.11.cloned.1.call-start = ((), (), s32[]{:S(2)}) async-start(), calls=%async_computation.9 | async-start | bytes 2801664 | tf_op jit(solution)/shard_map/all_gather | solution.py:1082
  12.7 272.1 %all-gather.13.cloned.1.call-start = ((), (), s32[]{:S(2)}) async-start(), calls=%async_computation.10 | async-start | bytes 4718592 | tf_op jit(solution)/shard_map/all_gather | solution.py:1083
  13.7 344.4 %all-gather.15.cloned.1.call-start = ((), (), s32[]{:S(2)}) async-start(), calls=%async_computation.11 | async-start | bytes 4718592 | tf_op jit(solution)/shard_map/all_gather | solution.py:1084
  14.8 24.8 %collective-permute-start.1 = (bf16[4,128,512]{2,1,0:T(8,128)(2,1)S(1)}, bf16[4,128,512]{2,1,0:T(8,128)(2,1)S(1)}, u32[]{:S(2)}, u32[]{:S(2)}) collective-permute-start(bf16[4,128,512]{2,1,0:T(8,128)(2,1)S(1)} %get-tuple-element.791.refs_3_), channel_id=1, source_target_pairs={{0,1},{1,0},{2,3},{3,2},{4,5},{5,4},{6,7},{7,6},{8,9},{9,8},{10,11... | collective-permute-start | bytes 1572872 | tf_op jit(solution)/shard_map/ppermute | solution.py:972
  19.8 44.2 %collective-permute-start.4 = (s32[8,640]{1,0:T(8,128)}, s32[8,640]{1,0:T(8,128)S(1)}, u32[]{:S(2)}, u32[]{:S(2)}) collective-permute-start(s32[8,640]{1,0:T(8,128)} %pad_select_fusion.refs_1_.refs_0_), channel_id=1, source_target_pairs={{0,8},{4,12},{8,0},{12,4},{16,24},{20,28},{24,16},{28,20},{1,9},{5... | collective-permute-start | bytes 61448 | tf_op jit(solution)/shard_map/ppermute | solution.py:972
  39.6 27.9 %collective-permute-start.5 = (s32[8,640]{1,0:T(8,128)}, s32[8,640]{1,0:T(8,128)S(1)}, u32[]{:S(2)}, u32[]{:S(2)}) collective-permute-start(s32[8,640]{1,0:T(8,128)} %pad_select_fusion.refs_1_.refs_0_), channel_id=1, source_target_pairs={{0,12},{4,8},{8,4},{12,0},{16,28},{20,24},{24,20},{28,16},{1,13},{... | collective-permute-start | bytes 61448 | tf_op jit(solution)/shard_map/ppermute | solution.py:972
  49.9 21.2 %collective-permute-start.10 = (bf16[576,128]{1,0:T(8,128)(2,1)}, bf16[576,128]{1,0:T(8,128)(2,1)S(1)}, u32[]{:S(2)}, u32[]{:S(2)}) collective-permute-start(bf16[576,128]{1,0:T(8,128)(2,1)} %get-tuple-element.393), channel_id=1, source_target_pairs={{0,24},{4,28},{8,16},{12,20},{16,8},{20,12},{24,0},{28,4},{1,25},{... | collective-permute-start | bytes 442376 | tf_op jit(solution)/shard_map/ppermute | solution.py:972
  62.9 31.4 %collective-permute-start.12 = (bf16[576,128]{1,0:T(8,128)(2,1)}, bf16[576,128]{1,0:T(8,128)(2,1)}, u32[]{:S(2)}, u32[]{:S(2)}) collective-permute-start(bf16[576,128]{1,0:T(8,128)(2,1)} %get-tuple-element.395), channel_id=1, source_target_pairs={{0,16},{4,20},{8,24},{12,28},{16,0},{20,4},{24,8},{28,12},{1,17},{... | collective-permute-start | bytes 442376 | tf_op jit(solution)/shard_map/ppermute | solution.py:972
  64.0 30.4 %collective-permute-start.13 = (bf16[576,128]{1,0:T(8,128)(2,1)}, bf16[576,128]{1,0:T(8,128)(2,1)}, u32[]{:S(2)}, u32[]{:S(2)}) collective-permute-start(bf16[576,128]{1,0:T(8,128)(2,1)} %get-tuple-element.392.refs_7_), channel_id=1, source_target_pairs={{0,20},{4,16},{8,28},{12,24},{16,4},{20,0},{24,12},{28,8},{1,21},{... | collective-permute-start | bytes 442376 | tf_op jit(solution)/shard_map/ppermute | solution.py:972
  67.5 26.8 %collective-permute-start = (s32[8,640]{1,0:T(8,128)}, s32[8,640]{1,0:T(8,128)}, u32[]{:S(2)}, u32[]{:S(2)}) collective-permute-start(s32[8,640]{1,0:T(8,128)} %pad_select_fusion.refs_1_.refs_0_), channel_id=1, source_target_pairs={{0,4},{4,0},{8,12},{12,8},{16,20},{20,16},{24,28},{28,24},{1,5},{5... | collective-permute-start | bytes 61448 | tf_op jit(solution)/shard_map/ppermute | solution.py:972
  81.5 30.1 %collective-permute-start.16 = (bf16[576,128]{1,0:T(8,128)(2,1)S(1)}, bf16[576,128]{1,0:T(8,128)(2,1)S(1)}, u32[]{:S(2)}, u32[]{:S(2)}) collective-permute-start(bf16[576,128]{1,0:T(8,128)(2,1)S(1)} %get-tuple-element.394.refs_7_), channel_id=1, source_target_pairs={{0,12},{4,8},{8,4},{12,0},{16,28},{20,24},{24,20},{28,16},{1,13},{... | collective-permute-start | bytes 442376 | tf_op jit(solution)/shard_map/ppermute | solution.py:972
  160.7 28.3 %collective-permute-start.26 = (bf16[256,1024]{1,0:T(8,128)(2,1)}, bf16[256,1024]{1,0:T(8,128)(2,1)}, u32[]{:S(2)}, u32[]{:S(2)}) collective-permute-start(bf16[256,1024]{1,0:T(8,128)(2,1)} %get-tuple-element.429.refs_1_), channel_id=1, source_target_pairs={{0,2},{1,3},{2,0},{3,1},{4,6},{5,7},{6,4},{7,5},{8,10},{9,11},{10,... | collective-permute-start | bytes 1572872 | tf_op jit(solution)/shard_map/ppermute | solution.py:972
  168.1 29.9 %collective-permute-start.30 = (bf16[256,1024]{1,0:T(8,128)(2,1)S(1)}, bf16[256,1024]{1,0:T(8,128)(2,1)S(1)}, u32[]{:S(2)}, u32[]{:S(2)}) collective-permute-start(bf16[256,1024]{1,0:T(8,128)(2,1)S(1)} %get-tuple-element.433.refs_1_), channel_id=1, source_target_pairs={{0,2},{1,3},{2,0},{3,1},{4,6},{5,7},{6,4},{7,5},{8,10},{9,11},{10,... | collective-permute-start | bytes 1572872 | tf_op jit(solution)/shard_map/ppermute | solution.py:972
  179.9 28.9 %collective-permute-start.32 = (bf16[384,1024]{1,0:T(8,128)(2,1)}, bf16[384,1024]{1,0:T(8,128)(2,1)}, u32[]{:S(2)}, u32[]{:S(2)}) collective-permute-start(bf16[384,1024]{1,0:T(8,128)(2,1)} %get-tuple-element.440), channel_id=1, source_target_pairs={{0,1},{1,0},{2,3},{3,2},{4,5},{5,4},{6,7},{7,6},{8,9},{9,8},{10,11... | collective-permute-start | bytes 2359304 | tf_op jit(solution)/shard_map/ppermute | solution.py:972
  180.5 718.8 %reduce-scatter.11.cloned.1.call-start = ((), (), s32[]{:S(2)}) async-start(), calls=%async_computation.7 | async-start | bytes 4718592 | tf_op jit(solution)/shard_map/reduce_scatter | solution.py:1489
  373.1 24.8 %collective-permute-start.63 = (bf16[128,1024]{1,0:T(8,128)(2,1)S(1)}, bf16[128,1024]{1,0:T(8,128)(2,1)S(1)}, u32[]{:S(2)}, u32[]{:S(2)}) collective-permute-start(bf16[128,1024]{1,0:T(8,128)(2,1)S(1)} %get-tuple-element.495.refs_10_.refs_2_), channel_id=1, source_target_pairs={{0,2},{1,3},{2,0},{3,1},{4,6},{5,7},{6,4},{7,5},{8,10},{9,11},{10,... | collective-permute-start | bytes 786440 | tf_op jit(solution)/shard_map/ppermute | solution.py:972
  434.7 21.8 %collective-permute-start.72 = (bf16[256,1024]{1,0:T(8,128)(2,1)S(1)}, bf16[256,1024]{1,0:T(8,128)(2,1)S(1)}, u32[]{:S(2)}, u32[]{:S(2)}) collective-permute-start(bf16[256,1024]{1,0:T(8,128)(2,1)S(1)} %get-tuple-element.524.refs_1_), channel_id=1, source_target_pairs={{0,2},{1,3},{2,0},{3,1},{4,6},{5,7},{6,4},{7,5},{8,10},{9,11},{10,... | collective-permute-start | bytes 1572872 | tf_op jit(solution)/shard_map/ppermute | solution.py:972
  444.8 22.3 %collective-permute-start.74 = (bf16[384,1024]{1,0:T(8,128)(2,1)S(1)}, bf16[384,1024]{1,0:T(8,128)(2,1)S(1)}, u32[]{:S(2)}, u32[]{:S(2)}) collective-permute-start(bf16[384,1024]{1,0:T(8,128)(2,1)S(1)} %get-tuple-element.530), channel_id=1, source_target_pairs={{0,1},{1,0},{2,3},{3,2},{4,5},{5,4},{6,7},{7,6},{8,9},{9,8},{10,11... | collective-permute-start | bytes 2359304 | tf_op jit(solution)/shard_map/ppermute | solution.py:972
  494.3 423.7 %reduce-scatter.9.cloned.1.call-start = ((), (), s32[]{:S(2)}) async-start(), calls=%async_computation.6 | async-start | bytes 4718592 | tf_op jit(solution)/shard_map/reduce_scatter | solution.py:1524
  571.8 21.2 %collective-permute-start.92 = (bf16[384,1024]{1,0:T(8,128)(2,1)S(1)}, bf16[384,1024]{1,0:T(8,128)(2,1)S(1)}, u32[]{:S(2)}, u32[]{:S(2)}) collective-permute-start(bf16[384,1024]{1,0:T(8,128)(2,1)S(1)} %get-tuple-element.596), channel_id=1, source_target_pairs={{0,1},{1,0},{2,3},{3,2},{4,5},{5,4},{6,7},{7,6},{8,9},{9,8},{10,11... | collective-permute-start | bytes 2359304 | tf_op jit(solution)/shard_map/ppermute | solution.py:972
  614.5 305.6 %reduce-scatter.5.cloned.1.call-start = ((), (), s32[]{:S(2)}) async-start(), calls=%async_computation.4 | async-start | bytes 2801664 | tf_op jit(solution)/shard_map/reduce_scatter | solution.py:1612
  614.7 24.9 %collective-permute-start.97 = (bf16[384,1024]{1,0:T(8,128)(2,1)}, bf16[384,1024]{1,0:T(8,128)(2,1)S(1)}, u32[]{:S(2)}, u32[]{:S(2)}) collective-permute-start(bf16[384,1024]{1,0:T(8,128)(2,1)} %copy-done.142), channel_id=1, source_target_pairs={{0,1},{1,0},{2,3},{3,2},{4,5},{5,4},{6,7},{7,6},{8,9},{9,8},{10,11... | collective-permute-start | bytes 2359304 | tf_op jit(solution)/shard_map/ppermute | solution.py:972
  683.3 23.3 %collective-permute-start.108 = (bf16[384,1024]{1,0:T(8,128)(2,1)S(1)}, bf16[384,1024]{1,0:T(8,128)(2,1)S(1)}, u32[]{:S(2)}, u32[]{:S(2)}) collective-permute-start(bf16[384,1024]{1,0:T(8,128)(2,1)S(1)} %get-tuple-element.673), channel_id=1, source_target_pairs={{0,1},{1,0},{2,3},{3,2},{4,5},{5,4},{6,7},{7,6},{8,9},{9,8},{10,11... | collective-permute-start | bytes 2359304 | tf_op jit(solution)/shard_map/ppermute | solution.py:972
  750.1 26.7 %collective-permute-start.115 = (bf16[768,256]{1,0:T(8,128)(2,1)S(1)}, bf16[768,256]{1,0:T(8,128)(2,1)S(1)}, u32[]{:S(2)}, u32[]{:S(2)}) collective-permute-start(bf16[768,256]{1,0:T(8,128)(2,1)S(1)} %add.356.refs_11_), channel_id=1, source_target_pairs={{0,2},{1,3},{2,0},{3,1},{4,6},{5,7},{6,4},{7,5},{8,10},{9,11},{10,... | collective-permute-start | bytes 1179656 | tf_op jit(solution)/shard_map/ppermute | solution.py:972
  798.4 162.1 %reduce-scatter.7.cloned.1.call-start = ((), (), s32[]{:S(2)}) async-start(), calls=%async_computation.5 | async-start | bytes 2359296 | tf_op jit(solution)/shard_map/reduce_scatter | solution.py:1586
  815.9 23.7 %collective-permute-start.124 = (bf16[576,128]{1,0:T(8,128)(2,1)S(1)}, bf16[576,128]{1,0:T(8,128)(2,1)S(1)}, u32[]{:S(2)}, u32[]{:S(2)}) collective-permute-start(bf16[576,128]{1,0:T(8,128)(2,1)S(1)} %get-tuple-element.738), channel_id=1, source_target_pairs={{0,12},{4,8},{8,4},{12,0},{16,28},{20,24},{24,20},{28,16},{1,13},{... | collective-permute-start | bytes 442376 | tf_op jit(solution)/shard_map/ppermute | solution.py:972
  817.6 22.0 %collective-permute-start.125 = (bf16[576,128]{1,0:T(8,128)(2,1)S(1)}, bf16[576,128]{1,0:T(8,128)(2,1)S(1)}, u32[]{:S(2)}, u32[]{:S(2)}) collective-permute-start(bf16[576,128]{1,0:T(8,128)(2,1)S(1)} %get-tuple-element.739), channel_id=1, source_target_pairs={{0,16},{4,20},{8,24},{12,28},{16,0},{20,4},{24,8},{28,12},{1,17},{... | collective-permute-start | bytes 442376 | tf_op jit(solution)/shard_map/ppermute | solution.py:972
  819.3 29.7 %collective-permute-start.126 = (bf16[576,128]{1,0:T(8,128)(2,1)S(1)}, bf16[576,128]{1,0:T(8,128)(2,1)S(1)}, u32[]{:S(2)}, u32[]{:S(2)}) collective-permute-start(bf16[576,128]{1,0:T(8,128)(2,1)S(1)} %get-tuple-element.740), channel_id=1, source_target_pairs={{0,20},{4,16},{8,28},{12,24},{16,4},{20,0},{24,12},{28,8},{1,21},{... | collective-permute-start | bytes 442376 | tf_op jit(solution)/shard_map/ppermute | solution.py:972
  821.0 28.0 %collective-permute-start.127 = (bf16[576,128]{1,0:T(8,128)(2,1)S(1)}, bf16[576,128]{1,0:T(8,128)(2,1)S(1)}, u32[]{:S(2)}, u32[]{:S(2)}) collective-permute-start(bf16[576,128]{1,0:T(8,128)(2,1)S(1)} %get-tuple-element.741), channel_id=1, source_target_pairs={{0,24},{4,28},{8,16},{12,20},{16,8},{20,12},{24,0},{28,4},{1,25},{... | collective-permute-start | bytes 442376 | tf_op jit(solution)/shard_map/ppermute | solution.py:972
  884.5 30.5 %collective-permute-start.129 = (bf16[4,128,512]{2,1,0:T(8,128)(2,1)}, bf16[4,128,512]{2,1,0:T(8,128)(2,1)}, u32[]{:S(2)}, u32[]{:S(2)}) collective-permute-start(bf16[4,128,512]{2,1,0:T(8,128)(2,1)} %get-tuple-element.785), channel_id=1, source_target_pairs={{0,1},{1,0},{2,3},{3,2},{4,5},{5,4},{6,7},{7,6},{8,9},{9,8},{10,11... | collective-permute-start | bytes 1572872 | tf_op jit(solution)/shard_map/ppermute | solution.py:972
  885.4 29.5 %collective-permute-start.131 = (bf16[4,128,512]{2,1,0:T(8,128)(2,1)}, bf16[4,128,512]{2,1,0:T(8,128)(2,1)}, u32[]{:S(2)}, u32[]{:S(2)}) collective-permute-start(bf16[4,128,512]{2,1,0:T(8,128)(2,1)} %fusion.6), channel_id=1, source_target_pairs={{0,2},{1,3},{2,0},{3,1},{4,6},{5,7},{6,4},{7,5},{8,10},{9,11},{10,... | collective-permute-start | bytes 1572872 | tf_op jit(solution)/shard_map/ppermute | solution.py:972
  (297 other events, 3229.0 us)
Sparse Core Ops, SparseCore 0:
  12.0 68.6 all-gather.8
  83.4 57.9 all-gather.10
  143.6 71.9 all-gather.12
  218.2 71.6 all-gather.14
  494.5 85.7 reduce-scatter.10
  614.6 86.5 reduce-scatter.8
  798.5 88.0 reduce-scatter.4
  891.1 69.2 reduce-scatter.6

commit v6 on v5

--- a/solution.py
+++ b/solution.py
@@ -20,8 +20,7 @@
 
 SMALL = pl.CostEstimate(flops=1024, bytes_accessed=1024, transcendentals=0)
 
-PIECES = (2, 1)
-MORE_PIECES = (1, 1, 1)
+PIECES = (1, 1)
 
 clip_limit = 0.004
 stability_offset = 1e-08
@@ -743,21 +742,23 @@
         return pl.ds(pl.multiple_of(c * frames + at * height, 128), height)
 
     if turn_left:
-        for m, out_ref in enumerate(outs):
+        step = min(group, 512)
+        for m, v in [(m, v) for m in range(len(outs)) for v in range(0, group, step)]:
             total = None
             for c in range(clips):
-                if m == 0:
+                if m == 0 and v == 0:
                     for j, at in ((0, core), (1, 1 - core)):
                         need(1 + 2 * c + j)
                         turned[:, place(c, at)] = jnp.transpose(lefts[2 * c + j][...])
                     need(1 + 2 * clips + c)
                 part = nn(
                     turned[:, c * frames : (c + 1) * frames],
-                    rights[c][:, m * group : (m + 1) * group],
+                    rights[c][:, m * group + v : m * group + v + step],
                 )
                 total = part if total is None else total + part
-            out_ref[...] = total.astype(LOW).reshape(out_ref.shape)
-            put(m)
+            outs[m][:, :, v : v + step] = total.astype(LOW).reshape(-1, outs[m].shape[1], step)
+            if v + step == group:
+                put(m)
     else:
         total = None
         for c in range(clips):
@@ -788,29 +789,27 @@
     )(*(hold(a, pltpu.VMEM) for a in operands), *after)
 
 
-def turned_codes(packet):
-    lines = packet.astype(F32)
-    wide = jnp.concatenate([lines, jnp.zeros((120, lines.shape[1]), F32)], axis=0)
-    return jnp.transpose(wide)
+def equal_to(code, local):
+    local = jnp.clip(local, -1.0, 256.0).astype(LOW)
+    return jnp.where(code == local, jnp.asarray(1, LOW), jnp.asarray(0, LOW))
 
 
 def embed_body(count, books, base_ref, *refs):
     packets, tables, outs = refs[:count], refs[count : len(refs) - count], refs[len(refs) - count :]
     features, vocab = tables[0].shape[1:]
     rows = outs[0].shape[0]
+    padded = packets[0].shape[1]
     chunk = min(256, vocab)
-    code = lax.broadcasted_iota(jnp.int32, (rows, chunk), 1).astype(F32)
+    code = lax.broadcasted_iota(jnp.int32, (chunk, padded), 0).astype(F32).astype(LOW)
     for packet, out_ref in zip(packets, outs):
-        columns = turned_codes(packet[...])
-        acc = jnp.zeros((rows, features), F32)
+        lines = packet[...].astype(F32)
+        acc = jnp.zeros((features, padded), F32)
         for k in range(books):
-            column = columns[:rows, k : k + 1]
             for b, table in enumerate(tables):
-                local = column - base_ref[b].astype(F32)
+                local = lines[k : k + 1, :] - base_ref[b].astype(F32)
                 for v in range(0, vocab, chunk):
-                    hit = jnp.where(code == local - float(v), 1.0, 0.0).astype(LOW)
-                    acc = acc + nt(hit, table[k, :, v : v + chunk])
-        out_ref[...] = acc.astype(LOW)
+                    acc = acc + nn(table[k, :, v : v + chunk], equal_to(code, local - float(v)))
+        out_ref[...] = jnp.transpose(acc)[:rows, :].astype(LOW)
 
 
 def embed(base, packets, tables, rows, after):
@@ -829,47 +828,51 @@
     )(base, *packets, *tables, *after)
 
 
-def embed_back_body(groups, base_ref, *refs):
-    packets, grads = refs[:groups], refs[groups : 2 * groups]
-    out_ref, all_ref = refs[-2:]
+def embed_back_body(groups, base_ref, line_ref, *refs):
+    grads, (out_ref, turned, columns) = refs[:groups], refs[groups:]
     rows, features = grads[0].shape
-    padded = packets[0].shape[1]
     vocab = out_ref.shape[3]
     chunk = min(256, vocab)
-    book = pl.program_id(1)
-
-    @pl.when((pl.program_id(0) == 0) & (book == 0))
+    total = line_ref.shape[1]
+
+    @pl.when((pl.program_id(0) == 0) & (pl.program_id(1) == 0))
     def _():
-        for j, g in enumerate(grads):
-            all_ref[j * padded : j * padded + rows, :] = g[...]
-            if padded > rows:
-                all_ref[j * padded + rows : (j + 1) * padded, :] = jnp.zeros(
-                    (padded - rows, features), LOW
-                )
-
-    base = base_ref[pl.program_id(0)]
-    line = jnp.concatenate([p[pl.ds(book, 1), :] for p in packets], axis=1)
-    code = lax.broadcasted_iota(jnp.int32, (chunk, line.shape[1]), 0)
+        whole_rows = jnp.concatenate([g[...] for g in grads], axis=0)
+        turned[...] = jnp.transpose(whole_rows)
+        wide = jnp.concatenate(
+            [line_ref[...].astype(F32), jnp.zeros((128 - line_ref.shape[0], total), F32)], axis=0
+        )
+        columns[...] = jnp.transpose(wide)
+
+    base = base_ref[pl.program_id(0)].astype(F32)
+    lane = lax.broadcasted_iota(jnp.int32, (total, 128), 1)
+    column = jnp.sum(
+        jnp.where(lane == pl.program_id(1), columns[...], 0.0), axis=1, keepdims=True
+    )
+    code = lax.broadcasted_iota(jnp.int32, (total, chunk), 1).astype(F32).astype(LOW)
     for v in range(0, vocab, chunk):
-        hit = jnp.where(code == line - (base + v), 1.0, 0.0).astype(LOW)
-        out_ref[0, 0, :, v : v + chunk] = jnp.transpose(nn(hit, all_ref[...])).astype(LOW)
-
-
-def embed_back(base, packets, grads, books, vocab, after):
+        hit = equal_to(code, column - (base + float(v)))
+        out_ref[0, 0, :, v : v + chunk] = nn(turned[...], hit).astype(LOW)
+
+
+def embed_back(base, lines, grads, books, vocab, after):
     parts = base.shape[0]
-    groups = len(packets)
-    features = grads[0].shape[1]
+    groups = len(grads)
+    rows, features = grads[0].shape
     return pl.pallas_call(
-        later(partial(embed_back_body, groups), len(after), 1 + 2 * groups),
+        later(partial(embed_back_body, groups), len(after), 2 + groups),
         out_shape=sds((parts, books, features, vocab), LOW),
         grid=(parts, books),
-        in_specs=[scalars()] + [in_vmem()] * (2 * groups) + [anywhere()] * len(after),
+        in_specs=[scalars()] + [in_vmem()] * (1 + groups) + [anywhere()] * len(after),
         out_specs=pl.BlockSpec((1, 1, features, vocab), lambda i, k: (i, k, 0, 0)),
-        scratch_shapes=[pltpu.VMEM((groups * packets[0].shape[1], features), LOW)],
-        compiler_params=pltpu.CompilerParams(vmem_limit_bytes=24 << 20),
+        scratch_shapes=[
+            pltpu.VMEM((features, groups * rows), LOW),
+            pltpu.VMEM((groups * rows, 128), F32),
+        ],
+        compiler_params=pltpu.CompilerParams(vmem_limit_bytes=32 << 20),
         cost_estimate=SMALL,
         name="embed_back",
-    )(base, *packets, *grads, *after)
+    )(base, lines, *grads, *after)
 
 
 def gather_features_body(need, put, where_ref, *refs):
@@ -1120,7 +1123,8 @@
     (counted,) = norm_rows_kernel(
         partial(count_body, books), [sds((8, 128), F32)], packets, None, last, name="count"
     )
-    last[:] = bias_lines + bias_columns + targets + loss_weight + [placed, counted]
+    back_lines = jnp.concatenate([p[:, :count] for p in packets], axis=1)
+    last[:] = bias_lines + bias_columns + targets + loss_weight + [placed, counted, back_lines]
     last += [a for a in arrived if a is not None]
     aligned = share % 128 == 0
     if aligned:
@@ -1183,25 +1187,24 @@
         last[:] = [out]
         return new, (out, swap_core(free(out))), free(sums)
 
-    waiting, soon, middle = [], [], []
+    waiting, soon = [], []
     moving = [None] * clips
 
-    def flush(pieces=PIECES):
+    def flush():
         if waiting:
             c, keep, got = waiting.pop()
             parts = norm_rows_kernel(
                 add_parts_body,
-                [sds((height * part // sum(pieces), width), LOW) for part in pieces],
+                [sds((height * part // sum(PIECES), width), LOW) for part in PIECES],
                 [keep, got],
                 None,
-                last + middle,
+                last,
                 name="add",
             )
             last[:] = [parts[-1]]
             fars = [across(free(part))[1] for part in parts]
             moving[c] = (*parts, *fars)
             soon[:] = fars[:-1]
-            middle[:] = fars[-1:]
 
     def reduce_rows(c, keep, send):
         waiting.append((c, keep, swap_core(free(send))))
@@ -1442,7 +1445,7 @@
             flops=2 * clips * frames * width * total,
             scratch=[pltpu.VMEM((width if turn_left else total, clips * frames), LOW)],
             name=name,
-            margin=26,
+            margin=16,
         )
 
     logit_grads = [None] * clips
@@ -1481,7 +1484,7 @@
     for c in every:
         grads[c], back_pairs[3][c], s = norm_back(3, c, moving[c], None)
         sums[3].append(s)
-        flush(MORE_PIECES if c == 0 else PIECES)
+        flush()
         inner_grads[c] = ffn_back_step(c, back_pairs[3][c])
         if c == 0:
             head_into = [member_into(head_shared, k) for k in range(books)]
@@ -1513,7 +1516,7 @@
     for c in every:
         grads[c], back_pairs[2][c], s = norm_back(2, c, moving[c], grads[c])
         sums[2].append(s)
-        flush(MORE_PIECES if c < 2 else PIECES)
+        flush()
         cross_grads[c] = cross_back_step(c, back_pairs[2][c])
         if c == 0:
             weights(
@@ -1573,10 +1576,11 @@
         return grad
 
     self_grads = [None] * clips
+    last.append(head_sum)
     for c in every:
         grads[c], back_pairs[1][c], s = norm_back(1, c, moving[c], grads[c])
         sums[1].append(s)
-        flush(MORE_PIECES if c < 2 else PIECES)
+        flush()
         self_grads[c] = self_back_step(c, back_pairs[1][c])
         if c == 0:
             text_grad = text_back_step()
@@ -1594,7 +1598,7 @@
         sums[0].append(s)
 
     zero_step(0)
-    flush(MORE_PIECES)
+    flush()
     text_into = Into(
         self_shared,
         (dp, text_share, columns),
@@ -1604,12 +1608,11 @@
         text_weight_body,
         [text_into, Flow(sds((8, columns), F32))],
         [fetch(text_rows), *text_grad],
+        after=[ffn_sum],
         flops=2 * clips * text_len * text_width * columns,
         name="text_weight",
     )
     weights(back_pairs[1], [k[3] for k in kept[0]], [attn_into(6)], "self_out")
-    weights(pairs[0], self_grads, [attn_into(n) for n in range(3)], "self_in")
-    self_sum = lax.psum_scatter(free(self_shared.array), "dp", scatter_dimension=0, tiled=False)
     for c in range(1, clips):
         zero_step(c)
 
@@ -1622,6 +1625,7 @@
                 Scalar(jnp.broadcast_to(side.astype(jnp.int32), (clips + 1,))),
             ]
             + zero_lows,
+            after=[cross_sum],
             name="split_features",
         )))
     else:
@@ -1630,8 +1634,10 @@
         )
         rows = jnp.transpose(rows.reshape(clips * strip, dp, share), (1, 0, 2))
         pieces = list(jnp.take(rows, group_order, axis=0))
+    weights(pairs[0], self_grads, [attn_into(n) for n in range(3)], "self_in")
+    self_sum = lax.psum_scatter(free(self_shared.array), "dp", scatter_dimension=0, tiled=False)
     rows_all = [pieces[0]] + [swap(pieces[m], "dp", m) for m in range(1, dp)]
-    embed_parts = embed_back(vocab_base, packets, rows_all, books, vocab, list(last))
+    embed_parts = embed_back(vocab_base, back_lines, rows_all, books, vocab, list(last))
     grad_embed = collect_tensor([embed_parts[m] for m in range(tensor)])
 
     norm_part = jnp.concatenate(
@@ -1645,21 +1651,20 @@
     )
     grad_norm_rows = lax.dynamic_slice_in_dim(norm_total, group * share, share, 1)
 
-    parts = [None] * attention.shape[0]
-    for at, n in enumerate(SELF):
-        parts[n] = self_sum[at * share : (at + 1) * share]
-    for at, n in enumerate(CROSS):
-        parts[n] = cross_sum[at * share : (at + 1) * share]
-    grad_attention = jnp.stack(parts).astype(F32)
+    own_self = self_sum[: 4 * share].reshape(4, share, columns)
+    own_cross = cross_sum.reshape(4, share, columns)
+    grad_attention = jnp.concatenate(
+        [own_self[:3], own_cross[:3], own_self[3:], own_cross[3:]], axis=0
+    ).astype(F32)
     grad_text_proj = jnp.transpose(self_sum[4 * share :]).astype(F32)
     grad_feedforward = ffn_sum.astype(F32)
     grad_heads = head_sum.astype(F32)
     local_square = (
-        jnp.sum(grad_attention * grad_attention)
+        jnp.sum(jnp.square(self_sum.astype(F32)))
+        + jnp.sum(jnp.square(cross_sum.astype(F32)))
         + jnp.sum(grad_feedforward * grad_feedforward)
         + jnp.sum(grad_heads * grad_heads)
         + jnp.sum(grad_embed * grad_embed)
-        + jnp.sum(grad_text_proj * grad_text_proj)
         + jnp.sum(grad_norm_rows * grad_norm_rows) / tensor
     )
     both = total_over(

time: 1010 us -> 928 us (0.919)
  waiting for transfers between devices: 356 us -> 284 us
  Pallas kernels: 392 us -> 377 us
    reduce_scatter x1, waiting for transfers between devices: 37.9 us -> 0.01 us  [on_device(): lax.psum_scatter(free(cross_shared.array), 'dp', scatter_dimension=0, til...]
    ppermute x142 -> x136, waiting for transfers between devices: 317 us -> 283 us  [swap(): return lax.ppermute(values, axis, [(i, i ^ mask) for i in range(size)])]
    pallas_call x4, Pallas kernels: 35.7 us -> 20.1 us  [embed(): pl.pallas_call(later(partial(embed_body, count, books), len(after), 1 + c...]
    unnamed x367 -> x286, local copies, waits for them, and re-layouts: 43.1 us -> 51.3 us
    ppermute x142 -> x136, starting transfers between devices: 139 us -> 134 us  [swap(): return lax.ppermute(values, axis, [(i, i ^ mask) for i in range(size)])]
  transfers between devices with their start and end apart: 150 -> 144, of which waited for: 63 -> 65; matrix products, arithmetic and copies ran while one was open for 4% -> 4% of each run, Pallas kernels for 36% -> 37%
where the time goes in v6:
time: 928 us; the launch traced here: 923 us
  Pallas kernels  377 us (41%)
  waiting for transfers between devices  284 us (31%)
  starting transfers between devices  135 us (15%)
  local copies, waits for them, and re-layouts  67.4 us (7%)
  other arithmetic  36.5 us (4%)
  between operations  24.2 us (3%)
    pallas_call x40, Pallas kernels, kernel(): pl.pallas_call(run_body, out_shape=tuple(out_shapes), in_specs=specs + [a...  295 us
    ppermute x136, waiting for transfers between devices, swap(): return lax.ppermute(values, axis, [(i, i ^ mask) for i in range(size)])  283 us
    ppermute x136, starting transfers between devices, swap(): return lax.ppermute(values, axis, [(i, i ^ mask) for i in range(size)])  134 us
    unnamed x286, local copies, waits for them, and re-layouts  51.3 us
    pallas_call x51, Pallas kernels, norm_rows_kernel(): pl.pallas_call(later(body, len(after), len(operands)), out_shape=tuple((p...  43.5 us
    pallas_call x4, Pallas kernels, embed(): pl.pallas_call(later(partial(embed_body, count, books), len(after), 1 + c...  20.1 us
  transfers between devices with their start and end apart: 144, of which 65 were waited for; matrix products, arithmetic and copies ran while one was open for 4% of the time, Pallas kernels for 37%

profile of v6, /device:TPU:0, one launch (start us, length us, event | category | flops | bytes accessed | tf_op | source)
XLA Modules:
  0.0 923.3 jit_solution(7009327613453990204)
XLA Ops:
  67.4 20.3 %collective-permute-start.16 = (bf16[576,128]{1,0:T(8,128)(2,1)}, bf16[576,128]{1,0:T(8,128)(2,1)}, u32[]{:S(2)}, u32[]{:S(2)}) collective-permute-start(bf16[576,128]{1,0:T(8,128)(2,1)} %get-tuple-element.388.refs_7_), channel_id=1, source_target_pairs={{0,12},{4,8},{8,4},{12,0},{16,28},{20,24},{24,20},{28,16},{1,13},{... | collective-permute-start | bytes 442376 | tf_op jit(solution)/shard_map/ppermute | solution.py:975
  118.2 8.8 collective-permute-done.17.refs_4_
  131.1 8.6 self_forward.3
  149.4 8.9 self_forward.4
  162.1 10.9 %collective-permute-done.28.refs_3_ = bf16[768,256]{1,0:T(8,128)(2,1)} collective-permute-done((bf16[768,256]{1,0:T(8,128)(2,1)}, bf16[768,256]{1,0:T(8,128)(2,1)}, u32[]{:S(2)}, u32[]{:S(2)}) %collective-permute-start.28) | collective-permute-done | bytes 393248 | tf_op jit(solution)/shard_map/ppermute | solution.py:975
  178.1 9.1 self_forward.5
  270.1 9.4 %ffn_forward.3 = (bf16[768,1024]{1,0:T(8,128)(2,1)}, bf16[768,1024]{1,0:T(8,128)(2,1)}, bf16[384,1024]{1,0:T(8,128)(2,1)S(1)}, bf16[384,1024]{1,0:T(8,128)(2,1)S...) custom-call(s32[1]{0:T(128)} %bitcast.refs_0_, ...), custom_call_target="tpu_custom_call" | custom-call | flops 1024 | bytes 1024 | tf_op jit(solution)/shard_map/ffn_forward/pallas_call | solution.py:263
  289.9 8.1 ffn_forward.4
  312.7 8.1 ffn_forward.5
  336.0 10.9 %head_forward.3 = (f32[768,2048]{1,0:T(8,128)}, f32[8,768]{1,0:T(8,128)S(1)}, bf16[384,1024]{1,0:T(8,128)(2,1)}, bf16[384,1024]{1,0:T(8,128)(2,1)}, f32[384,1024...) custom-call(s32[1]{0:T(128)} %bitcast.refs_0_, bf16[384,1024]{1,0:T(8,128)(2,1)S(1)} %get-tuple-element.484.refs_2_.refs_1_, ...), custom_call_target="tpu_custom_call" | custom-call | flops 1024 | bytes 1024 | tf_op jit(solution)/shard_map/head_forward/pallas_call | solution.py:263
  355.9 9.6 %head_forward.4 = (f32[768,2048]{1,0:T(8,128)}, f32[8,768]{1,0:T(8,128)S(1)}, bf16[384,1024]{1,0:T(8,128)(2,1)}, bf16[384,1024]{1,0:T(8,128)(2,1)}, f32[384,1024...) custom-call(s32[1]{0:T(128)} %bitcast.refs_0_, bf16[384,1024]{1,0:T(8,128)(2,1)S(1)} %get-tuple-element.495.refs_1_.refs_10_, ...), custom_call_target="tpu_custom_call" | custom-call | flops 1024 | bytes 1024 | tf_op jit(solution)/shard_map/head_forward/pallas_call | solution.py:263
  369.5 8.6 head_backward.3
  382.7 9.6 %head_forward.5 = (f32[768,2048]{1,0:T(8,128)}, f32[8,768]{1,0:T(8,128)S(1)}, bf16[384,1024]{1,0:T(8,128)(2,1)}, bf16[384,1024]{1,0:T(8,128)(2,1)}, f32[384,1024]{1,0:T(8,128)}, /*index=5*/f32[8,128]{1,0:T(8,128)S(1)}) custom-call(s32[1]{0:T(128)} %bitcast.refs_0_, bf16[384,1024]{1,0:T(8,128)(2,1)S(1)} %get-tuple-element.504.refs_2_.refs_1_, ...), custom_call_target="tpu_custom_call" | custom-call | flops 1024 | bytes 1024 | tf_op jit(solution)/shard_map/head_forward/pallas_call | solution.py:263
  396.3 8.5 head_backward.4
  412.0 8.8 head_backward.5
  448.9 16.3 %head_weights.1 = (bf16[8,4,128,512]{3,2,1,0:T(8,128)(2,1)}, f32[8,128]{1,0:T(8,128)S(1)}) custom-call(s32[1]{0:T(128)} %bitcast.refs_0_, bf16[384,1024]{1,0:T(8,128)(2,1)} %get-tuple-element.527.refs_1_, bf16[384,1024]{1,0:T(8,128)(2,1)} %get-tuple-element.528.refs_2_, bf16[384,1024]{1,0:T(8,128)(2,1)} %get-tuple-element.529.refs_3_, ...), custom_call_target="tpu_custom_call" | custom-call | flops 1024 | bytes 1024 | tf_op jit(solution)/shard_map/head_weights/pallas_call | solution.py:263
  466.6 9.5 %collective-permute-done.75.refs_4_ = bf16[192,1024]{1,0:T(8,128)(2,1)S(1)} collective-permute-done((bf16[192,1024]{1,0:T(8,128)(2,1)S(1)}, bf16[192,1024]{1,0:T(8,128)(2,1)S(1)}, u32[]{:S(2)}, u32[]{:S(2)}) %collective-permute-start.75) | collective-permute-done | bytes 393248 | tf_op jit(solution)/shard_map/ppermute | solution.py:975
  533.2 10.8 %ffn_two.1 = (bf16[8,2,128,1024]{3,2,1,0:T(8,128)(2,1)}, f32[8,128]{1,0:T(8,128)S(1)}) custom-call(s32[1]{0:T(128)} %bitcast.refs_0_, bf16[384,1024]{1,0:T(8,128)(2,1)} %get-tuple-element.570.refs_1_, bf16[384,1024]{1,0:T(8,128)(2,1)} %get-tuple-element.571.refs_2_, bf16[384,1024]{1,0:T(8,128)(2,1)} %get-tuple-element.572.refs_3_, ...), custom_call_target="tpu_custom_call" | custom-call | flops 1024 | bytes 1024 | tf_op jit(solution)/shard_map/ffn_two/pallas_call | solution.py:263
  558.7 10.6 %ffn_one.1 = (bf16[8,2,128,1024]{3,2,1,0:T(8,128)(2,1)}, f32[8,128]{1,0:T(8,128)S(1)}) custom-call(s32[1]{0:T(128)} %bitcast.refs_0_, bf16[384,1024]{1,0:T(8,128)(2,1)} %get-tuple-element.592.refs_1_, bf16[384,1024]{1,0:T(8,128)(2,1)} %get-tuple-element.593.refs_2_, bf16[384,1024]{1,0:T(8,128)(2,1)} %get-tuple-element.594.refs_3_, ...), custom_call_target="tpu_custom_call", output_to_operand_aliasing={{0}: (10, {})} | custom-call | flops 1024 | bytes 1024 | tf_op jit(solution)/shard_map/ffn_one/pallas_call | solution.py:263
  570.8 9.7 %collective-permute-done.91.refs_4_ = bf16[192,1024]{1,0:T(8,128)(2,1)S(1)} collective-permute-done((bf16[192,1024]{1,0:T(8,128)(2,1)S(1)}, bf16[192,1024]{1,0:T(8,128)(2,1)S(1)}, u32[]{:S(2)}, u32[]{:S(2)}) %collective-permute-start.91) | collective-permute-done | bytes 393248 | tf_op jit(solution)/shard_map/ppermute | solution.py:975
  586.7 9.3 %cross_backward.5 = (bf16[768,256]{1,0:T(8,128)(2,1)}, bf16[256,256]{1,0:T(8,128)(2,1)}, bf16[256,256]{1,0:T(8,128)(2,1)}, bf16[384,1024]{1,0:T(8,128)(2,1)S(1)}...) custom-call(s32[1]{0:T(128)} %bitcast.refs_0_, ...), custom_call_target="tpu_custom_call" | custom-call | flops 1024 | bytes 1024 | tf_op jit(solution)/shard_map/cross_backward/pallas_call | solution.py:263
  612.5 11.1 %self_backward.3 = (bf16[768,768]{1,0:T(8,128)(2,1)}, bf16[384,1024]{1,0:T(8,128)(2,1)S(1)}, bf16[384,1024]{1,0:T(8,128)(2,1)S(1)}, bf16[384,1024]{1,0:T(8,128)(...) custom-call(s32[1]{0:T(128)} %bitcast.refs_0_, ...), custom_call_target="tpu_custom_call" | custom-call | flops 1024 | bytes 1024 | tf_op jit(solution)/shard_map/self_backward/pallas_call | solution.py:263
  631.9 9.7 %collective-permute-done.102.refs_12_.refs_3_ = bf16[192,1024]{1,0:T(8,128)(2,1)S(1)} collective-permute-done((bf16[192,1024]{1,0:T(8,128)(2,1)S(1)}, bf16[192,1024]{1,0:T(8,128)(2,1)S(1)}, u32[]{:S(2)}, u32[]{:S(2)}) %collective-permute-start.102) | collective-permute-done | bytes 393248 | tf_op jit(solution)/shard_map/ppermute | solution.py:975
  652.9 11.3 %self_backward.4 = (bf16[768,768]{1,0:T(8,128)(2,1)}, bf16[384,1024]{1,0:T(8,128)(2,1)S(1)}, bf16[384,1024]{1,0:T(8,128)(2,1)S(1)}, bf16[384,1024]{1,0:T(8,128)(...) custom-call(s32[1]{0:T(128)} %bitcast.refs_0_, ...), custom_call_target="tpu_custom_call" | custom-call | flops 1024 | bytes 1024 | tf_op jit(solution)/shard_map/self_backward/pallas_call | solution.py:263
  674.5 9.7 %collective-permute-done.105.refs_4_ = bf16[192,1024]{1,0:T(8,128)(2,1)S(1)} collective-permute-done((bf16[192,1024]{1,0:T(8,128)(2,1)S(1)}, bf16[192,1024]{1,0:T(8,128)(2,1)S(1)}, u32[]{:S(2)}, u32[]{:S(2)}) %collective-permute-start.105) | collective-permute-done | bytes 393248 | tf_op jit(solution)/shard_map/ppermute | solution.py:975
  690.3 11.0 %self_backward.5 = (bf16[768,768]{1,0:T(8,128)(2,1)}, bf16[384,1024]{1,0:T(8,128)(2,1)S(1)}, bf16[384,1024]{1,0:T(8,128)(2,1)S(1)}, bf16[384,1024]{1,0:T(8,128)(...) custom-call(s32[1]{0:T(128)} %bitcast.refs_0_, ...), custom_call_target="tpu_custom_call" | custom-call | flops 1024 | bytes 1024 | tf_op jit(solution)/shard_map/self_backward/pallas_call | solution.py:263
  705.0 8.5 collective-permute-done.111.refs_4_
  713.5 8.4 collective-permute-done.112.refs_8_.refs_3_
  763.9 9.6 %self_in.1 = (bf16[8,608,256]{2,1,0:T(8,128)(2,1)}, f32[8,128]{1,0:T(8,128)S(1)}) custom-call(s32[1]{0:T(128)} %bitcast.refs_0_, bf16[384,1024]{1,0:T(8,128)(2,1)} %get-tuple-element.398.refs_1_, bf16[384,1024]{1,0:T(8,128)(2,1)} %get-tuple-element.399.refs_2_, bf16[384,1024]{1,0:T(8,128)(2,1)} %get-tuple-element.409.refs_3_, ...), custom_call_target="tpu_custom_call", output_to_operand_aliasing={{0}: (10, {})} | custom-call | flops 1024 | bytes 1024 | tf_op jit(solution)/shard_map/self_in/pallas_call | solution.py:263
  792.3 20.0 %collective-permute-done.120.refs_7_ = bf16[576,128]{1,0:T(8,128)(2,1)S(1)} collective-permute-done((bf16[576,128]{1,0:T(8,128)(2,1)S(1)}, bf16[576,128]{1,0:T(8,128)(2,1)S(1)}, u32[]{:S(2)}, u32[]{:S(2)}) %collective-permute-start.120) | collective-permute-done | bytes 147488 | tf_op jit(solution)/shard_map/ppermute | solution.py:975
  812.3 18.1 %embed_back.1 = bf16[4,4,128,512]{3,2,1,0:T(8,128)(2,1)S(1)} custom-call(s32[4]{0:T(128)S(1)} %copy-done.92, s32[8,4608]{1,0:T(8,128)S(1)} %copy-done.39, bf16[576,128]{1,0:T(8,128)(2,1)S(1)} %get-tuple-element.723.refs_2_, bf16[576,128]{1,0:T(8,128)(2,1)S(1)} %collective-permute-done.116.refs_3_, bf16[576,128]{1,0:T(8,128)(2,1)S(1)} %collective-permute-done.117.refs_4_, ...), custom_call_target="tpu_custom_call" | custom-call | flops 1024 | bytes 1024 | tf_op jit(solution)/shard_map/embed_back/pallas_call | solution.py:862
  842.2 15.7 %collective-permute-start.129 = (f32[9,1024]{1,0:T(8,128)S(1)}, f32[9,1024]{1,0:T(8,128)S(1)}, u32[]{:S(2)}, u32[]{:S(2)}) collective-permute-start(f32[9,1024]{1,0:T(8,128)S(1)} %add.235), channel_id=1, source_target_pairs={{0,8},{4,12},{8,0},{12,4},{16,24},{20,28},{24,16},{28,20},{1,9},{5... | collective-permute-start | bytes 110600 | tf_op jit(solution)/shard_map/ppermute | solution.py:975
  (735 shorter events, 551.5 us)
Async XLA Ops:
  7.2 110.3 %all-gather.9.cloned.1.call-start = ((), (), s32[]{:S(2)}) async-start(), calls=%async_computation.8 | async-start | bytes 2433024 | tf_op jit(solution)/shard_map/all_gather | solution.py:1084
  11.8 129.3 %all-gather.11.cloned.1.call-start = ((), (), s32[]{:S(2)}) async-start(), calls=%async_computation.9 | async-start | bytes 2801664 | tf_op jit(solution)/shard_map/all_gather | solution.py:1085
  12.7 256.0 %all-gather.13.cloned.1.call-start = ((), (), s32[]{:S(2)}) async-start(), calls=%async_computation.10 | async-start | bytes 4718592 | tf_op jit(solution)/shard_map/all_gather | solution.py:1086
  13.6 320.9 %all-gather.15.cloned.1.call-start = ((), (), s32[]{:S(2)}) async-start(), calls=%async_computation.11 | async-start | bytes 4718592 | tf_op jit(solution)/shard_map/all_gather | solution.py:1087
  14.7 23.5 %collective-permute-start.1 = (bf16[4,128,512]{2,1,0:T(8,128)(2,1)S(1)}, bf16[4,128,512]{2,1,0:T(8,128)(2,1)S(1)}, u32[]{:S(2)}, u32[]{:S(2)}) collective-permute-start(bf16[4,128,512]{2,1,0:T(8,128)(2,1)S(1)} %get-tuple-element.779.refs_3_), channel_id=1, source_target_pairs={{0,1},{1,0},{2,3},{3,2},{4,5},{5,4},{6,7},{7,6},{8,9},{9,8},{10,11... | collective-permute-start | bytes 1572872 | tf_op jit(solution)/shard_map/ppermute | solution.py:975
  19.2 34.6 %collective-permute-start.4 = (s32[8,640]{1,0:T(8,128)S(1)}, s32[8,640]{1,0:T(8,128)S(1)}, u32[]{:S(2)}, u32[]{:S(2)}) collective-permute-start(s32[8,640]{1,0:T(8,128)S(1)} %pad_select_fusion.refs_1_.refs_0_), channel_id=1, source_target_pairs={{0,8},{4,12},{8,0},{12,4},{16,24},{20,28},{24,16},{28,20},{1,9},{5... | collective-permute-start | bytes 61448 | tf_op jit(solution)/shard_map/ppermute | solution.py:975
  52.8 35.0 %collective-permute-start.12 = (bf16[576,128]{1,0:T(8,128)(2,1)}, bf16[576,128]{1,0:T(8,128)(2,1)}, u32[]{:S(2)}, u32[]{:S(2)}) collective-permute-start(bf16[576,128]{1,0:T(8,128)(2,1)} %get-tuple-element.389), channel_id=1, source_target_pairs={{0,16},{4,20},{8,24},{12,28},{16,0},{20,4},{24,8},{28,12},{1,17},{... | collective-permute-start | bytes 442376 | tf_op jit(solution)/shard_map/ppermute | solution.py:975
  53.8 34.8 %collective-permute-start.13 = (bf16[576,128]{1,0:T(8,128)(2,1)}, bf16[576,128]{1,0:T(8,128)(2,1)}, u32[]{:S(2)}, u32[]{:S(2)}) collective-permute-start(bf16[576,128]{1,0:T(8,128)(2,1)} %get-tuple-element.386.refs_7_), channel_id=1, source_target_pairs={{0,20},{4,16},{8,28},{12,24},{16,4},{20,0},{24,12},{28,8},{1,21},{... | collective-permute-start | bytes 442376 | tf_op jit(solution)/shard_map/ppermute | solution.py:975
  57.3 30.5 %collective-permute-start = (s32[8,640]{1,0:T(8,128)S(1)}, s32[8,640]{1,0:T(8,128)}, u32[]{:S(2)}, u32[]{:S(2)}) collective-permute-start(s32[8,640]{1,0:T(8,128)S(1)} %pad_select_fusion.refs_1_.refs_0_), channel_id=1, source_target_pairs={{0,4},{4,0},{8,12},{12,8},{16,20},{20,16},{24,28},{28,24},{1,5},{5... | collective-permute-start | bytes 61448 | tf_op jit(solution)/shard_map/ppermute | solution.py:975
  67.4 36.9 %collective-permute-start.16 = (bf16[576,128]{1,0:T(8,128)(2,1)}, bf16[576,128]{1,0:T(8,128)(2,1)}, u32[]{:S(2)}, u32[]{:S(2)}) collective-permute-start(bf16[576,128]{1,0:T(8,128)(2,1)} %get-tuple-element.388.refs_7_), channel_id=1, source_target_pairs={{0,12},{4,8},{8,4},{12,0},{16,28},{20,24},{24,20},{28,16},{1,13},{... | collective-permute-start | bytes 442376 | tf_op jit(solution)/shard_map/ppermute | solution.py:975
  162.0 25.2 %collective-permute-start.27 = (bf16[768,256]{1,0:T(8,128)(2,1)}, bf16[768,256]{1,0:T(8,128)(2,1)}, u32[]{:S(2)}, u32[]{:S(2)}) collective-permute-start(bf16[768,256]{1,0:T(8,128)(2,1)} %get-tuple-element.424.refs_1_), channel_id=1, source_target_pairs={{0,1},{1,0},{2,3},{3,2},{4,5},{5,4},{6,7},{7,6},{8,9},{9,8},{10,11... | collective-permute-start | bytes 1179656 | tf_op jit(solution)/shard_map/ppermute | solution.py:975
  162.0 442.3 %reduce-scatter.5.cloned.1.call-start = ((), (), s32[]{:S(2)}) async-start(), calls=%async_computation.4 | async-start | bytes 4718592 | tf_op jit(solution)/shard_map/reduce_scatter | solution.py:1492
  173.0 20.6 %collective-permute-start.26 = (bf16[192,1024]{1,0:T(8,128)(2,1)}, bf16[192,1024]{1,0:T(8,128)(2,1)S(1)}, u32[]{:S(2)}, u32[]{:S(2)}) collective-permute-start(bf16[192,1024]{1,0:T(8,128)(2,1)} %copy-done.13), channel_id=1, source_target_pairs={{0,2},{1,3},{2,0},{3,1},{4,6},{5,7},{6,4},{7,5},{8,10},{9,11},{10,... | collective-permute-start | bytes 1179656 | tf_op jit(solution)/shard_map/ppermute | solution.py:975
  173.5 20.0 %collective-permute-start.25 = (bf16[192,1024]{1,0:T(8,128)(2,1)}, bf16[192,1024]{1,0:T(8,128)(2,1)S(1)}, u32[]{:S(2)}, u32[]{:S(2)}) collective-permute-start(bf16[192,1024]{1,0:T(8,128)(2,1)} %copy-done.67), channel_id=1, source_target_pairs={{0,2},{1,3},{2,0},{3,1},{4,6},{5,7},{6,4},{7,5},{8,10},{9,11},{10,... | collective-permute-start | bytes 1179656 | tf_op jit(solution)/shard_map/ppermute | solution.py:975
  177.5 24.0 %collective-permute-start.30 = (bf16[192,1024]{1,0:T(8,128)(2,1)S(1)}, bf16[192,1024]{1,0:T(8,128)(2,1)S(1)}, u32[]{:S(2)}, u32[]{:S(2)}) collective-permute-start(bf16[192,1024]{1,0:T(8,128)(2,1)S(1)} %get-tuple-element.427.refs_1_), channel_id=1, source_target_pairs={{0,2},{1,3},{2,0},{3,1},{4,6},{5,7},{6,4},{7,5},{8,10},{9,11},{10,... | collective-permute-start | bytes 1179656 | tf_op jit(solution)/shard_map/ppermute | solution.py:975
  353.6 24.5 %collective-permute-start.63 = (bf16[192,1024]{1,0:T(8,128)(2,1)S(1)}, bf16[192,1024]{1,0:T(8,128)(2,1)S(1)}, u32[]{:S(2)}, u32[]{:S(2)}) collective-permute-start(bf16[192,1024]{1,0:T(8,128)(2,1)S(1)} %get-tuple-element.489.refs_10_.refs_2_), channel_id=1, source_target_pairs={{0,2},{1,3},{2,0},{3,1},{4,6},{5,7},{6,4},{7,5},{8,10},{9,11},{10,... | collective-permute-start | bytes 1179656 | tf_op jit(solution)/shard_map/ppermute | solution.py:975
  407.8 20.5 %collective-permute-start.65 = (bf16[192,1024]{1,0:T(8,128)(2,1)S(1)}, bf16[192,1024]{1,0:T(8,128)(2,1)S(1)}, u32[]{:S(2)}, u32[]{:S(2)}) collective-permute-start(bf16[192,1024]{1,0:T(8,128)(2,1)S(1)} %get-tuple-element.506.refs_9_.refs_2_), channel_id=1, source_target_pairs={{0,2},{1,3},{2,0},{3,1},{4,6},{5,7},{6,4},{7,5},{8,10},{9,11},{10,... | collective-permute-start | bytes 1179656 | tf_op jit(solution)/shard_map/ppermute | solution.py:975
  411.6 24.2 %collective-permute-start.72 = (bf16[192,1024]{1,0:T(8,128)(2,1)S(1)}, bf16[192,1024]{1,0:T(8,128)(2,1)S(1)}, u32[]{:S(2)}, u32[]{:S(2)}) collective-permute-start(bf16[192,1024]{1,0:T(8,128)(2,1)S(1)} %get-tuple-element.518.refs_1_), channel_id=1, source_target_pairs={{0,2},{1,3},{2,0},{3,1},{4,6},{5,7},{6,4},{7,5},{8,10},{9,11},{10,... | collective-permute-start | bytes 1179656 | tf_op jit(solution)/shard_map/ppermute | solution.py:975
  465.2 265.9 %reduce-scatter.7.cloned.1.call-start = ((), (), s32[]{:S(2)}) async-start(), calls=%async_computation.5 | async-start | bytes 4718592 | tf_op jit(solution)/shard_map/reduce_scatter | solution.py:1527
  522.5 21.5 %collective-permute-start.87 = (bf16[192,1024]{1,0:T(8,128)(2,1)S(1)}, bf16[192,1024]{1,0:T(8,128)(2,1)S(1)}, u32[]{:S(2)}, u32[]{:S(2)}) collective-permute-start(bf16[192,1024]{1,0:T(8,128)(2,1)S(1)} %get-tuple-element.555.refs_9_.refs_2_), channel_id=1, source_target_pairs={{0,2},{1,3},{2,0},{3,1},{4,6},{5,7},{6,4},{7,5},{8,10},{9,11},{10,... | collective-permute-start | bytes 1179656 | tf_op jit(solution)/shard_map/ppermute | solution.py:975
  569.3 190.1 %reduce-scatter.9.cloned.1.call-start = ((), (), s32[]{:S(2)}) async-start(), calls=%async_computation.6 | async-start | bytes 2359296 | tf_op jit(solution)/shard_map/reduce_scatter | solution.py:1590
  672.2 205.4 %reduce-scatter.11.cloned.1.call-start = ((), (), s32[]{:S(2)}) async-start(), calls=%async_computation.7 | async-start | bytes 2801664 | tf_op jit(solution)/shard_map/reduce_scatter | solution.py:1638
  701.3 23.1 %collective-permute-start.110 = (bf16[384,1024]{1,0:T(8,128)(2,1)S(1)}, bf16[384,1024]{1,0:T(8,128)(2,1)S(1)}, u32[]{:S(2)}, u32[]{:S(2)}) collective-permute-start(bf16[384,1024]{1,0:T(8,128)(2,1)S(1)} %get-tuple-element.703), channel_id=1, source_target_pairs={{0,1},{1,0},{2,3},{3,2},{4,5},{5,4},{6,7},{7,6},{8,9},{9,8},{10,11... | collective-permute-start | bytes 2359304 | tf_op jit(solution)/shard_map/ppermute | solution.py:975
  703.6 26.8 %collective-permute-start.109 = (bf16[768,256]{1,0:T(8,128)(2,1)S(1)}, bf16[768,256]{1,0:T(8,128)(2,1)S(1)}, u32[]{:S(2)}, u32[]{:S(2)}) collective-permute-start(bf16[768,256]{1,0:T(8,128)(2,1)S(1)} %add.356.refs_11_), channel_id=1, source_target_pairs={{0,2},{1,3},{2,0},{3,1},{4,6},{5,7},{6,4},{7,5},{8,10},{9,11},{10,... | collective-permute-start | bytes 1179656 | tf_op jit(solution)/shard_map/ppermute | solution.py:975
  726.7 20.6 %collective-permute-start.114 = (bf16[192,1024]{1,0:T(8,128)(2,1)S(1)}, bf16[192,1024]{1,0:T(8,128)(2,1)}, u32[]{:S(2)}, u32[]{:S(2)}) collective-permute-start(bf16[192,1024]{1,0:T(8,128)(2,1)S(1)} %get-tuple-element.691.refs_14_.refs_2_), channel_id=1, source_target_pairs={{0,2},{1,3},{2,0},{3,1},{4,6},{5,7},{6,4},{7,5},{8,10},{9,11},{10,... | collective-permute-start | bytes 1179656 | tf_op jit(solution)/shard_map/ppermute | solution.py:975
  727.3 27.8 %collective-permute-start.115 = (bf16[192,1024]{1,0:T(8,128)(2,1)S(1)}, bf16[192,1024]{1,0:T(8,128)(2,1)}, u32[]{:S(2)}, u32[]{:S(2)}) collective-permute-start(bf16[192,1024]{1,0:T(8,128)(2,1)S(1)} %get-tuple-element.709.refs_3_.refs_2_), channel_id=1, source_target_pairs={{0,2},{1,3},{2,0},{3,1},{4,6},{5,7},{6,4},{7,5},{8,10},{9,11},{10,... | collective-permute-start | bytes 1179656 | tf_op jit(solution)/shard_map/ppermute | solution.py:975
  780.2 32.1 %collective-permute-start.120 = (bf16[576,128]{1,0:T(8,128)(2,1)S(1)}, bf16[576,128]{1,0:T(8,128)(2,1)S(1)}, u32[]{:S(2)}, u32[]{:S(2)}) collective-permute-start(bf16[576,128]{1,0:T(8,128)(2,1)S(1)} %get-tuple-element.728), channel_id=1, source_target_pairs={{0,20},{4,16},{8,28},{12,24},{16,4},{20,0},{24,12},{28,8},{1,21},{... | collective-permute-start | bytes 442376 | tf_op jit(solution)/shard_map/ppermute | solution.py:975
  781.9 30.4 %collective-permute-start.121 = (bf16[576,128]{1,0:T(8,128)(2,1)S(1)}, bf16[576,128]{1,0:T(8,128)(2,1)S(1)}, u32[]{:S(2)}, u32[]{:S(2)}) collective-permute-start(bf16[576,128]{1,0:T(8,128)(2,1)S(1)} %get-tuple-element.729), channel_id=1, source_target_pairs={{0,24},{4,28},{8,16},{12,20},{16,8},{20,12},{24,0},{28,4},{1,25},{... | collective-permute-start | bytes 442376 | tf_op jit(solution)/shard_map/ppermute | solution.py:975
  790.6 21.7 %collective-permute-start.122 = (bf16[576,128]{1,0:T(8,128)(2,1)S(1)}, bf16[576,128]{1,0:T(8,128)(2,1)S(1)}, u32[]{:S(2)}, u32[]{:S(2)}) collective-permute-start(bf16[576,128]{1,0:T(8,128)(2,1)S(1)} %get-tuple-element.730), channel_id=1, source_target_pairs={{0,28},{4,24},{8,20},{12,16},{16,12},{20,8},{24,4},{28,0},{1,29},{... | collective-permute-start | bytes 442376 | tf_op jit(solution)/shard_map/ppermute | solution.py:975
  791.9 39.5 %collective-permute-start.126 = (f32[9,1024]{1,0:T(8,128)S(1)}, f32[9,1024]{1,0:T(8,128)S(1)}, u32[]{:S(2)}, u32[]{:S(2)}) collective-permute-start(f32[9,1024]{1,0:T(8,128)S(1)} %pad_maximum_fusion.2), channel_id=1, source_target_pairs={{0,1},{1,0},{2,3},{3,2},{4,5},{5,4},{6,7},{7,6},{8,9},{9,8},{10,11... | collective-permute-start | bytes 110600 | tf_op jit(solution)/shard_map/ppermute | solution.py:975
  831.4 26.5 %collective-permute-start.124 = (bf16[4,128,512]{2,1,0:T(8,128)(2,1)}, bf16[4,128,512]{2,1,0:T(8,128)(2,1)}, u32[]{:S(2)}, u32[]{:S(2)}) collective-permute-start(bf16[4,128,512]{2,1,0:T(8,128)(2,1)} %get-tuple-element.774), channel_id=1, source_target_pairs={{0,1},{1,0},{2,3},{3,2},{4,5},{5,4},{6,7},{7,6},{8,9},{9,8},{10,11... | collective-permute-start | bytes 1572872 | tf_op jit(solution)/shard_map/ppermute | solution.py:975
  842.2 20.1 %collective-permute-start.129 = (f32[9,1024]{1,0:T(8,128)S(1)}, f32[9,1024]{1,0:T(8,128)S(1)}, u32[]{:S(2)}, u32[]{:S(2)}) collective-permute-start(f32[9,1024]{1,0:T(8,128)S(1)} %add.235), channel_id=1, source_target_pairs={{0,8},{4,12},{8,0},{12,4},{16,24},{20,28},{24,16},{28,20},{1,9},{5... | collective-permute-start | bytes 110600 | tf_op jit(solution)/shard_map/ppermute | solution.py:975
  (256 other events, 2213.9 us)
Sparse Core Ops, SparseCore 0:
  12.0 70.4 all-gather.8
  85.2 55.9 all-gather.10
  143.9 71.9 all-gather.12
  218.4 71.6 all-gather.14
  465.4 88.6 reduce-scatter.4
  569.4 88.9 reduce-scatter.6
  672.3 68.5 reduce-scatter.8
  773.7 89.6 reduce-scatter.10

commit v7 on v6

--- a/solution.py
+++ b/solution.py
@@ -703,6 +703,7 @@
 
 def norm_back_body(which, parts, hidden_ref, *refs):
     *before, norm_ref, new_ref, low_ref, sums_ref = refs[parts:]
+    sums = before.pop() if before and before[-1].shape[0] == sums_ref.shape[0] else None
     values = hidden_ref[...]
     grad = joined(refs[:parts])
     gain = norm_ref[which : which + 1, :]
@@ -718,14 +719,9 @@
         new = before[0][...] + new
     new_ref[...] = new
     low_ref[...] = new.astype(LOW)
-    sums_ref[...] = jnp.concatenate(
-        [
-            jnp.sum(grad * unit, axis=0, keepdims=True),
-            jnp.sum(grad, axis=0, keepdims=True),
-            jnp.zeros((6, values.shape[1]), F32),
-        ],
-        axis=0,
-    )
+    sums_ref[...] = jnp.zeros(sums_ref.shape, F32) if sums is None else sums[...]
+    sums_ref[which : which + 1, :] += jnp.sum(grad * unit, axis=0, keepdims=True)
+    sums_ref[which + 4 : which + 5, :] += jnp.sum(grad, axis=0, keepdims=True)
 
 
 def weight_grad_body(clips, turn_left, need, put, core_ref, *refs):
@@ -1073,8 +1069,11 @@
         return run(*args, **rest)
 
     def run_weight(*args, **rest):
-        results = run(*args, after=soon[:1], **rest)
-        del soon[:1]
+        results = run(*args, after=older[:1] or soon[:1], **rest)
+        if older:
+            older.clear()
+        else:
+            soon.clear()
         return results
 
     norm_pad = jnp.pad(norm_params.astype(LOW), ((0, 16 - norm_params.shape[0]), (0, columns - share)))
@@ -1175,8 +1174,8 @@
         rows = near.get((which, c, "back"), hidden[which][c])
         if before is not None:
             before = near_grad.get((which, c), before)
-        operands = [rows, *parts] + ([before] if before is not None else [])
-        new, out, sums = norm_rows_kernel(
+        operands = [rows, *parts] + ([before] if before is not None else []) + sums
+        new, out, total = norm_rows_kernel(
             partial(norm_back_body, which, len(parts)),
             [half_sds, half_low, sds((8, width), F32)],
             operands,
@@ -1185,9 +1184,11 @@
         )
         soon[:] = []
         last[:] = [out]
-        return new, (out, swap_core(free(out))), free(sums)
-
-    waiting, soon = [], []
+        sums[:] = [total]
+        return new, (out, swap_core(free(out)))
+
+    sums = []
+    waiting, soon, older, newest = [], [], [], []
     moving = [None] * clips
 
     def flush():
@@ -1205,6 +1206,8 @@
             fars = [across(free(part))[1] for part in parts]
             moving[c] = (*parts, *fars)
             soon[:] = fars[:-1]
+            older[:] = newest
+            newest[:] = fars[-1:]
 
     def reduce_rows(c, keep, send):
         waiting.append((c, keep, swap_core(free(send))))
@@ -1365,7 +1368,6 @@
         kept[2][c] = ffn_step(c, pairs[2][c])
 
     loss_part = [None] * clips
-    sums = [[], [], [], []]
 
     def head_step(c, pair):
         own, got = pair
@@ -1435,13 +1437,28 @@
     def member_into(shared, n):
         return Into(shared, (dp,) + shared.full.shape[2:], lambda ref: ref.at[:, n])
 
+    def halves(rights, shared, n):
+        step = rights[0].shape[1] // 2
+        found = []
+        for at in (0, step):
+            windows = [
+                Window(a, (frames, step), lambda ref, at=at: ref.at[:, pl.ds(at, step)])
+                for a in rights
+            ]
+            into = Into(
+                shared, (dp, share, step), lambda ref, at=at: ref.at[:, n, :, pl.ds(at, step)]
+            )
+            found.append((windows, [into]))
+        return found
+
     def weights(lefts, rights, outs, name):
+        rights = [a if isinstance(a, Window) else fetch(a) for a in rights]
         total = rights[0].shape[1]
         turn_left = 2 * total > width
         run_weight(
             partial(weight_grad_body, clips, turn_left),
             outs,
-            [core_arg] + [fetch(half) for pair in lefts for half in pair] + [fetch(a) for a in rights],
+            [core_arg] + [fetch(half) for pair in lefts for half in pair] + rights,
             flops=2 * clips * frames * width * total,
             scratch=[pltpu.VMEM((width if turn_left else total, clips * frames), LOW)],
             name=name,
@@ -1482,13 +1499,20 @@
     back_pairs = [[None] * clips for _ in range(4)]
     inner_grads = [None] * clips
     for c in every:
-        grads[c], back_pairs[3][c], s = norm_back(3, c, moving[c], None)
-        sums[3].append(s)
+        grads[c], back_pairs[3][c] = norm_back(3, c, moving[c], None)
         flush()
         inner_grads[c] = ffn_back_step(c, back_pairs[3][c])
         if c == 0:
-            head_into = [member_into(head_shared, k) for k in range(books)]
-            weights(pairs[3], logit_grads, head_into, "head_weights")
+            step = books // 2 * vocab
+            for at in (0, 1):
+                windows = [
+                    Window(a, (frames, step), lambda ref, at=at: ref.at[:, pl.ds(at * step, step)])
+                    for a in logit_grads
+                ]
+                into = [
+                    member_into(head_shared, k) for k in range(at * books // 2, (at + 1) * books // 2)
+                ]
+                weights(pairs[3], windows, into, "head_weights")
     head_sum = lax.psum_scatter(free(head_shared.array), "dp", scatter_dimension=0, tiled=False)
 
     acc_text = [pltpu.VMEM((text_len, columns), F32)] * 2
@@ -1514,20 +1538,19 @@
 
     cross_grads = [None] * clips
     for c in every:
-        grads[c], back_pairs[2][c], s = norm_back(2, c, moving[c], grads[c])
-        sums[2].append(s)
+        grads[c], back_pairs[2][c] = norm_back(2, c, moving[c], grads[c])
         flush()
         cross_grads[c] = cross_back_step(c, back_pairs[2][c])
         if c == 0:
-            weights(
-                back_pairs[3], [k[0] for k in kept[2]], [member_into(ffn_shared, 1)], "ffn_two"
-            )
+            for windows, into in halves([k[0] for k in kept[2]], ffn_shared, 1):
+                weights(back_pairs[3], windows, into, "ffn_two")
         if c == min(1, clips - 1):
-            weights(pairs[2], inner_grads, [member_into(ffn_shared, 0)], "ffn_one")
+            for windows, into in halves(inner_grads, ffn_shared, 0):
+                weights(pairs[2], windows, into, "ffn_one")
     ffn_sum = lax.psum_scatter(free(ffn_shared.array), "dp", scatter_dimension=0, tiled=False)
 
     def text_back_step():
-        results = run(
+        results = run_weight(
             partial(text_back_body, clips),
             [Flow(text_cols)] * tensor + [attn_into(4), attn_into(5)],
             [Scalar(place_order)]
@@ -1578,14 +1601,12 @@
     self_grads = [None] * clips
     last.append(head_sum)
     for c in every:
-        grads[c], back_pairs[1][c], s = norm_back(1, c, moving[c], grads[c])
-        sums[1].append(s)
+        grads[c], back_pairs[1][c] = norm_back(1, c, moving[c], grads[c])
         flush()
         self_grads[c] = self_back_step(c, back_pairs[1][c])
         if c == 0:
             text_grad = text_back_step()
             weights(back_pairs[2], [k[3] for k in kept[1]], [attn_into(7)], "cross_out")
-        if c == min(1, clips - 1):
             weights(pairs[1], [g[0] for g in cross_grads], [attn_into(3)], "cross_query")
             cross_sum = lax.psum_scatter(
                 free(cross_shared.array), "dp", scatter_dimension=0, tiled=False
@@ -1594,10 +1615,10 @@
     zero_lows = [None] * clips
 
     def zero_step(c):
-        _, (zero_lows[c], _), s = norm_back(0, c, moving[c], grads[c])
-        sums[0].append(s)
-
-    zero_step(0)
+        _, (zero_lows[c], _) = norm_back(0, c, moving[c], grads[c])
+
+    weights(back_pairs[1], [k[3] for k in kept[0]], [attn_into(6)], "self_out")
+    first = list(soon)
     flush()
     text_into = Into(
         self_shared,
@@ -1608,12 +1629,22 @@
         text_weight_body,
         [text_into, Flow(sds((8, columns), F32))],
         [fetch(text_rows), *text_grad],
-        after=[ffn_sum],
+        after=[ffn_sum] + first,
         flops=2 * clips * text_len * text_width * columns,
         name="text_weight",
     )
-    weights(back_pairs[1], [k[3] for k in kept[0]], [attn_into(6)], "self_out")
-    for c in range(1, clips):
+    for members in ((0, 1), (2,)):
+        size = len(members) * columns
+        windows = [
+            Window(
+                a, (frames, size), lambda ref: ref.at[:, pl.ds(members[0] * columns, size)]
+            )
+            for a in self_grads
+        ]
+        weights(pairs[0], windows, [attn_into(n) for n in members], "self_in")
+    soon[:] = newest
+    self_sum = lax.psum_scatter(free(self_shared.array), "dp", scatter_dimension=0, tiled=False)
+    for c in every:
         zero_step(c)
 
     if aligned:
@@ -1634,15 +1665,11 @@
         )
         rows = jnp.transpose(rows.reshape(clips * strip, dp, share), (1, 0, 2))
         pieces = list(jnp.take(rows, group_order, axis=0))
-    weights(pairs[0], self_grads, [attn_into(n) for n in range(3)], "self_in")
-    self_sum = lax.psum_scatter(free(self_shared.array), "dp", scatter_dimension=0, tiled=False)
     rows_all = [pieces[0]] + [swap(pieces[m], "dp", m) for m in range(1, dp)]
     embed_parts = embed_back(vocab_base, back_lines, rows_all, books, vocab, list(last))
     grad_embed = collect_tensor([embed_parts[m] for m in range(tensor)])
 
-    norm_part = jnp.concatenate(
-        [sum(s)[0:1] for s in sums] + [sum(s)[1:2] for s in sums], axis=0
-    ) * (1.0 / sides)
+    norm_part = free(sums[0]) * (1.0 / sides)
     bias_row = lax.dynamic_update_slice_in_dim(
         jnp.zeros((width,), F32), free(bias_grad)[0], place * columns, 0
     )

time: 928 us -> 905 us (0.975)
  waiting for transfers between devices: 284 us -> 240 us
  Pallas kernels: 377 us -> 398 us
    ppermute x136, waiting for transfers between devices: 283 us -> 240 us  [swap(): return lax.ppermute(values, axis, [(i, i ^ mask) for i in range(size)])]
    pallas_call x40 -> x44, Pallas kernels: 295 us -> 316 us  [kernel(): pl.pallas_call(run_body, out_shape=tuple(out_shapes), in_specs=specs + [a...]
    unnamed x286 -> x282, local copies, waits for them, and re-layouts: 51.3 us -> 59.6 us
  transfers between devices with their start and end apart: 144 -> 144, of which waited for: 65 -> 54; matrix products, arithmetic and copies ran while one was open for 4% -> 3% of each run, Pallas kernels for 37% -> 42%
where the time goes in v7:
time: 905 us; the launch traced here: 900 us
  Pallas kernels  398 us (44%)
  waiting for transfers between devices  240 us (27%)
  starting transfers between devices  128 us (14%)
  local copies, waits for them, and re-layouts  73.5 us (8%)
  other arithmetic  36.3 us (4%)
  between operations  24.2 us (3%)
    pallas_call x44, Pallas kernels, kernel(): pl.pallas_call(run_body, out_shape=tuple(out_shapes), in_specs=specs + [a...  316 us
    ppermute x136, waiting for transfers between devices, swap(): return lax.ppermute(values, axis, [(i, i ^ mask) for i in range(size)])  240 us
    ppermute x136, starting transfers between devices, swap(): return lax.ppermute(values, axis, [(i, i ^ mask) for i in range(size)])  127 us
    unnamed x282, local copies, waits for them, and re-layouts  59.6 us
    pallas_call x51, Pallas kernels, norm_rows_kernel(): pl.pallas_call(later(body, len(after), len(operands)), out_shape=tuple((p...  44.4 us
    pallas_call x4, Pallas kernels, embed(): pl.pallas_call(later(partial(embed_body, count, books), len(after), 1 + c...  19.9 us
  transfers between devices with their start and end apart: 144, of which 54 were waited for; matrix products, arithmetic and copies ran while one was open for 3% of the time, Pallas kernels for 42%

profile of v7, /device:TPU:0, one launch (start us, length us, event | category | flops | bytes accessed | tf_op | source)
XLA Modules:
  0.0 899.8 jit_solution(116389201565480774)
XLA Ops:
  67.3 20.5 %collective-permute-start.16 = (bf16[576,128]{1,0:T(8,128)(2,1)}, bf16[576,128]{1,0:T(8,128)(2,1)}, u32[]{:S(2)}, u32[]{:S(2)}) collective-permute-start(bf16[576,128]{1,0:T(8,128)(2,1)} %get-tuple-element.396.refs_7_), channel_id=1, source_target_pairs={{0,12},{4,8},{8,4},{12,0},{16,28},{20,24},{24,20},{28,16},{1,13},{... | collective-permute-start | bytes 442376 | tf_op jit(solution)/shard_map/ppermute | solution.py:971
  118.3 9.1 %collective-permute-done.17.refs_4_ = bf16[192,1024]{1,0:T(8,128)(2,1)} collective-permute-done((bf16[192,1024]{1,0:T(8,128)(2,1)}, bf16[192,1024]{1,0:T(8,128)(2,1)}, u32[]{:S(2)}, u32[]{:S(2)}) %collective-permute-start.17) | collective-permute-done | bytes 393248 | tf_op jit(solution)/shard_map/ppermute | solution.py:971
  131.4 8.6 self_forward.3
  149.4 8.8 self_forward.4
  162.3 10.6 %collective-permute-done.28.refs_3_ = bf16[768,256]{1,0:T(8,128)(2,1)} collective-permute-done((bf16[768,256]{1,0:T(8,128)(2,1)}, bf16[768,256]{1,0:T(8,128)(2,1)}, u32[]{:S(2)}, u32[]{:S(2)}) %collective-permute-start.28) | collective-permute-done | bytes 393248 | tf_op jit(solution)/shard_map/ppermute | solution.py:971
  178.3 9.1 %self_forward.5 = (bf16[768,256]{1,0:T(8,128)(2,1)}, bf16[768,256]{1,0:T(8,128)(2,1)}, bf16[768,256]{1,0:T(8,128)(2,1)}, bf16[768,256]{1,0:T(8,128)(2,1)}, f32[8...) custom-call(s32[1]{0:T(128)} %bitcast.refs_0_, ...), custom_call_target="tpu_custom_call" | custom-call | flops 1024 | bytes 1024 | tf_op jit(solution)/shard_map/self_forward/pallas_call | solution.py:263
  193.5 8.0 collective-permute-done.30.refs_7_.refs_3_
  214.3 8.0 collective-permute-done.34.refs_7_.refs_3_
  270.0 9.4 %ffn_forward.3 = (bf16[768,1024]{1,0:T(8,128)(2,1)}, bf16[768,1024]{1,0:T(8,128)(2,1)}, bf16[384,1024]{1,0:T(8,128)(2,1)S(1)}, bf16[384,1024]{1,0:T(8,128)(2,1)S...) custom-call(s32[1]{0:T(128)} %bitcast.refs_0_, ...), custom_call_target="tpu_custom_call" | custom-call | flops 1024 | bytes 1024 | tf_op jit(solution)/shard_map/ffn_forward/pallas_call | solution.py:263
  289.9 8.2 ffn_forward.4
  312.6 8.1 ffn_forward.5
  335.9 10.9 %head_forward.3 = (f32[768,2048]{1,0:T(8,128)}, f32[8,768]{1,0:T(8,128)S(1)}, bf16[384,1024]{1,0:T(8,128)(2,1)}, bf16[384,1024]{1,0:T(8,128)(2,1)}, f32[384,1024...) custom-call(s32[1]{0:T(128)} %bitcast.refs_0_, bf16[384,1024]{1,0:T(8,128)(2,1)S(1)} %get-tuple-element.492.refs_2_.refs_1_, ...), custom_call_target="tpu_custom_call" | custom-call | flops 1024 | bytes 1024 | tf_op jit(solution)/shard_map/head_forward/pallas_call | solution.py:263
  355.9 9.6 %head_forward.4 = (f32[768,2048]{1,0:T(8,128)}, f32[8,768]{1,0:T(8,128)S(1)}, bf16[384,1024]{1,0:T(8,128)(2,1)}, bf16[384,1024]{1,0:T(8,128)(2,1)}, f32[384,1024...) custom-call(s32[1]{0:T(128)} %bitcast.refs_0_, bf16[384,1024]{1,0:T(8,128)(2,1)S(1)} %get-tuple-element.503.refs_1_.refs_10_, ...), custom_call_target="tpu_custom_call" | custom-call | flops 1024 | bytes 1024 | tf_op jit(solution)/shard_map/head_forward/pallas_call | solution.py:263
  369.4 8.6 head_backward.3
  382.7 9.6 %head_forward.5 = (f32[768,2048]{1,0:T(8,128)}, f32[8,768]{1,0:T(8,128)S(1)}, bf16[384,1024]{1,0:T(8,128)(2,1)}, bf16[384,1024]{1,0:T(8,128)(2,1)}, f32[384,1024]{1,0:T(8,128)}, /*index=5*/f32[8,128]{1,0:T(8,128)S(1)}) custom-call(s32[1]{0:T(128)} %bitcast.refs_0_, bf16[384,1024]{1,0:T(8,128)(2,1)S(1)} %get-tuple-element.512.refs_2_.refs_1_, ...), custom_call_target="tpu_custom_call" | custom-call | flops 1024 | bytes 1024 | tf_op jit(solution)/shard_map/head_forward/pallas_call | solution.py:263
  396.3 8.5 head_backward.4
  412.1 8.8 head_backward.5
  449.2 10.2 %head_weights.2 = (bf16[8,4,128,512]{3,2,1,0:T(8,128)(2,1)}, f32[8,128]{1,0:T(8,128)S(1)}) custom-call(s32[1]{0:T(128)} %bitcast.refs_0_, bf16[384,1024]{1,0:T(8,128)(2,1)} %get-tuple-element.536.refs_1_, bf16[384,1024]{1,0:T(8,128)(2,1)} %get-tuple-element.537.refs_2_, bf16[384,1024]{1,0:T(8,128)(2,1)} %get-tuple-element.538.refs_3_, ...), custom_call_target="tpu_custom_call" | custom-call | flops 1024 | bytes 1024 | tf_op jit(solution)/shard_map/head_weights/pallas_call | solution.py:263
  459.4 10.8 %head_weights.3 = (bf16[8,4,128,512]{3,2,1,0:T(8,128)(2,1)}, f32[8,128]{1,0:T(8,128)S(1)}) custom-call(s32[1]{0:T(128)} %bitcast.refs_0_, bf16[384,1024]{1,0:T(8,128)(2,1)} %get-tuple-element.536.refs_1_, bf16[384,1024]{1,0:T(8,128)(2,1)} %get-tuple-element.537.refs_2_, ...), custom_call_target="tpu_custom_call", output_to_operand_aliasing={{0}: (10, {})} | custom-call | flops 1024 | bytes 1024 | tf_op jit(solution)/shard_map/head_weights/pallas_call | solution.py:263
  527.4 8.2 ffn_two.2
  535.6 8.2 ffn_two.3
  559.5 8.2 ffn_one.2
  567.7 8.2 ffn_one.3
  583.5 9.2 %cross_backward.5 = (bf16[768,256]{1,0:T(8,128)(2,1)}, bf16[256,256]{1,0:T(8,128)(2,1)}, bf16[256,256]{1,0:T(8,128)(2,1)}, bf16[384,1024]{1,0:T(8,128)(2,1)S(1)}...) custom-call(s32[1]{0:T(128)} %bitcast.refs_0_, ...), custom_call_target="tpu_custom_call" | custom-call | flops 1024 | bytes 1024 | tf_op jit(solution)/shard_map/cross_backward/pallas_call | solution.py:263
  609.7 11.1 %self_backward.3 = (bf16[768,768]{1,0:T(8,128)(2,1)}, bf16[384,1024]{1,0:T(8,128)(2,1)S(1)}, bf16[384,1024]{1,0:T(8,128)(2,1)S(1)}, bf16[384,1024]{1,0:T(8,128)(...) custom-call(s32[1]{0:T(128)} %bitcast.refs_0_, ...), custom_call_target="tpu_custom_call" | custom-call | flops 1024 | bytes 1024 | tf_op jit(solution)/shard_map/self_backward/pallas_call | solution.py:263
  629.9 9.3 %collective-permute-done.102.refs_12_.refs_3_ = bf16[192,1024]{1,0:T(8,128)(2,1)S(1)} collective-permute-done((bf16[192,1024]{1,0:T(8,128)(2,1)S(1)}, bf16[192,1024]{1,0:T(8,128)(2,1)S(1)}, u32[]{:S(2)}, u32[]{:S(2)}) %collective-permute-start.102) | collective-permute-done | bytes 393248 | tf_op jit(solution)/shard_map/ppermute | solution.py:971
  659.6 10.9 %self_backward.4 = (bf16[768,768]{1,0:T(8,128)(2,1)}, bf16[384,1024]{1,0:T(8,128)(2,1)S(1)}, bf16[384,1024]{1,0:T(8,128)(2,1)S(1)}, bf16[384,1024]{1,0:T(8,128)(...) custom-call(s32[1]{0:T(128)} %bitcast.refs_0_, ...), custom_call_target="tpu_custom_call" | custom-call | flops 1024 | bytes 1024 | tf_op jit(solution)/shard_map/self_backward/pallas_call | solution.py:263
  680.9 11.3 %self_backward.5 = (bf16[768,768]{1,0:T(8,128)(2,1)}, bf16[384,1024]{1,0:T(8,128)(2,1)S(1)}, bf16[384,1024]{1,0:T(8,128)(2,1)S(1)}, bf16[384,1024]{1,0:T(8,128)(...) custom-call(s32[1]{0:T(128)} %bitcast.refs_0_, ...), custom_call_target="tpu_custom_call" | custom-call | flops 1024 | bytes 1024 | tf_op jit(solution)/shard_map/self_backward/pallas_call | solution.py:263
  730.8 8.3 self_in.2
  747.2 9.0 collective-permute-done.115.refs_9_.refs_4_
  789.6 11.6 %collective-permute-done.120.refs_7_ = bf16[576,128]{1,0:T(8,128)(2,1)S(1)} collective-permute-done((bf16[576,128]{1,0:T(8,128)(2,1)S(1)}, bf16[576,128]{1,0:T(8,128)(2,1)S(1)}, u32[]{:S(2)}, u32[]{:S(2)}) %collective-permute-start.120) | collective-permute-done | bytes 147488 | tf_op jit(solution)/shard_map/ppermute | solution.py:971
  801.2 18.1 %embed_back.1 = bf16[4,4,128,512]{3,2,1,0:T(8,128)(2,1)S(1)} custom-call(s32[4]{0:T(128)S(1)} %copy-done.102, s32[8,4608]{1,0:T(8,128)S(1)} %copy-done.55, bf16[576,128]{1,0:T(8,128)(2,1)S(1)} %get-tuple-element.750.refs_2_, bf16[576,128]{1,0:T(8,128)(2,1)S(1)} %collective-permute-done.116.refs_3_, bf16[576,128]{1,0:T(8,128)(2,1)S(1)} %collective-permute-done.117.refs_4_, ...), custom_call_target="tpu_custom_call" | custom-call | flops 1024 | bytes 1024 | tf_op jit(solution)/shard_map/embed_back/pallas_call | solution.py:858
  (726 shorter events, 558.6 us)
Async XLA Ops:
  7.2 110.3 %all-gather.9.cloned.1.call-start = ((), (), s32[]{:S(2)}) async-start(), calls=%async_computation.8 | async-start | bytes 2433024 | tf_op jit(solution)/shard_map/all_gather | solution.py:1083
  11.8 129.3 %all-gather.11.cloned.1.call-start = ((), (), s32[]{:S(2)}) async-start(), calls=%async_computation.9 | async-start | bytes 2801664 | tf_op jit(solution)/shard_map/all_gather | solution.py:1084
  12.7 256.0 %all-gather.13.cloned.1.call-start = ((), (), s32[]{:S(2)}) async-start(), calls=%async_computation.10 | async-start | bytes 4718592 | tf_op jit(solution)/shard_map/all_gather | solution.py:1085
  13.6 320.9 %all-gather.15.cloned.1.call-start = ((), (), s32[]{:S(2)}) async-start(), calls=%async_computation.11 | async-start | bytes 4718592 | tf_op jit(solution)/shard_map/all_gather | solution.py:1086
  14.7 23.4 %collective-permute-start.1 = (bf16[4,128,512]{2,1,0:T(8,128)(2,1)S(1)}, bf16[4,128,512]{2,1,0:T(8,128)(2,1)S(1)}, u32[]{:S(2)}, u32[]{:S(2)}) collective-permute-start(bf16[4,128,512]{2,1,0:T(8,128)(2,1)S(1)} %get-tuple-element.795.refs_3_), channel_id=1, source_target_pairs={{0,1},{1,0},{2,3},{3,2},{4,5},{5,4},{6,7},{7,6},{8,9},{9,8},{10,11... | collective-permute-start | bytes 1572872 | tf_op jit(solution)/shard_map/ppermute | solution.py:971
  19.2 34.5 %collective-permute-start.4 = (s32[8,640]{1,0:T(8,128)S(1)}, s32[8,640]{1,0:T(8,128)S(1)}, u32[]{:S(2)}, u32[]{:S(2)}) collective-permute-start(s32[8,640]{1,0:T(8,128)S(1)} %pad_select_fusion.refs_1_.refs_0_), channel_id=1, source_target_pairs={{0,8},{4,12},{8,0},{12,4},{16,24},{20,28},{24,16},{28,20},{1,9},{5... | collective-permute-start | bytes 61448 | tf_op jit(solution)/shard_map/ppermute | solution.py:971
  52.7 35.1 %collective-permute-start.12 = (bf16[576,128]{1,0:T(8,128)(2,1)}, bf16[576,128]{1,0:T(8,128)(2,1)}, u32[]{:S(2)}, u32[]{:S(2)}) collective-permute-start(bf16[576,128]{1,0:T(8,128)(2,1)} %get-tuple-element.397), channel_id=1, source_target_pairs={{0,16},{4,20},{8,24},{12,28},{16,0},{20,4},{24,8},{28,12},{1,17},{... | collective-permute-start | bytes 442376 | tf_op jit(solution)/shard_map/ppermute | solution.py:971
  53.7 35.0 %collective-permute-start.13 = (bf16[576,128]{1,0:T(8,128)(2,1)}, bf16[576,128]{1,0:T(8,128)(2,1)}, u32[]{:S(2)}, u32[]{:S(2)}) collective-permute-start(bf16[576,128]{1,0:T(8,128)(2,1)} %get-tuple-element.394.refs_7_), channel_id=1, source_target_pairs={{0,20},{4,16},{8,28},{12,24},{16,4},{20,0},{24,12},{28,8},{1,21},{... | collective-permute-start | bytes 442376 | tf_op jit(solution)/shard_map/ppermute | solution.py:971
  57.1 30.7 %collective-permute-start = (s32[8,640]{1,0:T(8,128)S(1)}, s32[8,640]{1,0:T(8,128)}, u32[]{:S(2)}, u32[]{:S(2)}) collective-permute-start(s32[8,640]{1,0:T(8,128)S(1)} %pad_select_fusion.refs_1_.refs_0_), channel_id=1, source_target_pairs={{0,4},{4,0},{8,12},{12,8},{16,20},{20,16},{24,28},{28,24},{1,5},{5... | collective-permute-start | bytes 61448 | tf_op jit(solution)/shard_map/ppermute | solution.py:971
  67.3 37.1 %collective-permute-start.16 = (bf16[576,128]{1,0:T(8,128)(2,1)}, bf16[576,128]{1,0:T(8,128)(2,1)}, u32[]{:S(2)}, u32[]{:S(2)}) collective-permute-start(bf16[576,128]{1,0:T(8,128)(2,1)} %get-tuple-element.396.refs_7_), channel_id=1, source_target_pairs={{0,12},{4,8},{8,4},{12,0},{16,28},{20,24},{24,20},{28,16},{1,13},{... | collective-permute-start | bytes 442376 | tf_op jit(solution)/shard_map/ppermute | solution.py:971
  162.3 25.1 %collective-permute-start.27 = (bf16[768,256]{1,0:T(8,128)(2,1)}, bf16[768,256]{1,0:T(8,128)(2,1)}, u32[]{:S(2)}, u32[]{:S(2)}) collective-permute-start(bf16[768,256]{1,0:T(8,128)(2,1)} %get-tuple-element.432.refs_1_), channel_id=1, source_target_pairs={{0,1},{1,0},{2,3},{3,2},{4,5},{5,4},{6,7},{7,6},{8,9},{9,8},{10,11... | collective-permute-start | bytes 1179656 | tf_op jit(solution)/shard_map/ppermute | solution.py:971
  162.3 438.8 %reduce-scatter.5.cloned.1.call-start = ((), (), s32[]{:S(2)}) async-start(), calls=%async_computation.4 | async-start | bytes 4718592 | tf_op jit(solution)/shard_map/reduce_scatter | solution.py:1516
  172.9 20.6 %collective-permute-start.26 = (bf16[192,1024]{1,0:T(8,128)(2,1)}, bf16[192,1024]{1,0:T(8,128)(2,1)S(1)}, u32[]{:S(2)}, u32[]{:S(2)}) collective-permute-start(bf16[192,1024]{1,0:T(8,128)(2,1)} %copy-done.13), channel_id=1, source_target_pairs={{0,2},{1,3},{2,0},{3,1},{4,6},{5,7},{6,4},{7,5},{8,10},{9,11},{10,... | collective-permute-start | bytes 1179656 | tf_op jit(solution)/shard_map/ppermute | solution.py:971
  173.6 19.8 %collective-permute-start.25 = (bf16[192,1024]{1,0:T(8,128)(2,1)}, bf16[192,1024]{1,0:T(8,128)(2,1)S(1)}, u32[]{:S(2)}, u32[]{:S(2)}) collective-permute-start(bf16[192,1024]{1,0:T(8,128)(2,1)} %copy-done.85), channel_id=1, source_target_pairs={{0,2},{1,3},{2,0},{3,1},{4,6},{5,7},{6,4},{7,5},{8,10},{9,11},{10,... | collective-permute-start | bytes 1179656 | tf_op jit(solution)/shard_map/ppermute | solution.py:971
  177.6 23.9 %collective-permute-start.30 = (bf16[192,1024]{1,0:T(8,128)(2,1)S(1)}, bf16[192,1024]{1,0:T(8,128)(2,1)S(1)}, u32[]{:S(2)}, u32[]{:S(2)}) collective-permute-start(bf16[192,1024]{1,0:T(8,128)(2,1)S(1)} %get-tuple-element.435.refs_1_), channel_id=1, source_target_pairs={{0,2},{1,3},{2,0},{3,1},{4,6},{5,7},{6,4},{7,5},{8,10},{9,11},{10,... | collective-permute-start | bytes 1179656 | tf_op jit(solution)/shard_map/ppermute | solution.py:971
  288.5 19.2 %collective-permute-start.50 = (bf16[192,1024]{1,0:T(8,128)(2,1)S(1)}, bf16[192,1024]{1,0:T(8,128)(2,1)S(1)}, u32[]{:S(2)}, u32[]{:S(2)}) collective-permute-start(bf16[192,1024]{1,0:T(8,128)(2,1)S(1)} %get-tuple-element.482.refs_1_), channel_id=1, source_target_pairs={{0,2},{1,3},{2,0},{3,1},{4,6},{5,7},{6,4},{7,5},{8,10},{9,11},{10,... | collective-permute-start | bytes 1179656 | tf_op jit(solution)/shard_map/ppermute | solution.py:971
  353.6 24.5 %collective-permute-start.63 = (bf16[192,1024]{1,0:T(8,128)(2,1)S(1)}, bf16[192,1024]{1,0:T(8,128)(2,1)S(1)}, u32[]{:S(2)}, u32[]{:S(2)}) collective-permute-start(bf16[192,1024]{1,0:T(8,128)(2,1)S(1)} %get-tuple-element.497.refs_10_.refs_2_), channel_id=1, source_target_pairs={{0,2},{1,3},{2,0},{3,1},{4,6},{5,7},{6,4},{7,5},{8,10},{9,11},{10,... | collective-permute-start | bytes 1179656 | tf_op jit(solution)/shard_map/ppermute | solution.py:971
  407.9 20.4 %collective-permute-start.65 = (bf16[192,1024]{1,0:T(8,128)(2,1)S(1)}, bf16[192,1024]{1,0:T(8,128)(2,1)S(1)}, u32[]{:S(2)}, u32[]{:S(2)}) collective-permute-start(bf16[192,1024]{1,0:T(8,128)(2,1)S(1)} %get-tuple-element.514.refs_9_.refs_2_), channel_id=1, source_target_pairs={{0,2},{1,3},{2,0},{3,1},{4,6},{5,7},{6,4},{7,5},{8,10},{9,11},{10,... | collective-permute-start | bytes 1179656 | tf_op jit(solution)/shard_map/ppermute | solution.py:971
  411.4 24.5 %collective-permute-start.72 = (bf16[192,1024]{1,0:T(8,128)(2,1)S(1)}, bf16[192,1024]{1,0:T(8,128)(2,1)S(1)}, u32[]{:S(2)}, u32[]{:S(2)}) collective-permute-start(bf16[192,1024]{1,0:T(8,128)(2,1)S(1)} %get-tuple-element.526.refs_1_), channel_id=1, source_target_pairs={{0,2},{1,3},{2,0},{3,1},{4,6},{5,7},{6,4},{7,5},{8,10},{9,11},{10,... | collective-permute-start | bytes 1179656 | tf_op jit(solution)/shard_map/ppermute | solution.py:971
  438.6 20.8 %collective-permute-start.76 = (bf16[192,1024]{1,0:T(8,128)(2,1)S(1)}, bf16[192,1024]{1,0:T(8,128)(2,1)S(1)}, u32[]{:S(2)}, u32[]{:S(2)}) collective-permute-start(bf16[192,1024]{1,0:T(8,128)(2,1)S(1)} %get-tuple-element.548.refs_1_), channel_id=1, source_target_pairs={{0,2},{1,3},{2,0},{3,1},{4,6},{5,7},{6,4},{7,5},{8,10},{9,11},{10,... | collective-permute-start | bytes 1179656 | tf_op jit(solution)/shard_map/ppermute | solution.py:971
  470.3 252.8 %reduce-scatter.7.cloned.1.call-start = ((), (), s32[]{:S(2)}) async-start(), calls=%async_computation.5 | async-start | bytes 4718592 | tf_op jit(solution)/shard_map/reduce_scatter | solution.py:1550
  525.5 21.0 %collective-permute-start.90 = (bf16[384,1024]{1,0:T(8,128)(2,1)S(1)}, bf16[384,1024]{1,0:T(8,128)(2,1)S(1)}, u32[]{:S(2)}, u32[]{:S(2)}) collective-permute-start(bf16[384,1024]{1,0:T(8,128)(2,1)S(1)} %get-tuple-element.604), channel_id=1, source_target_pairs={{0,1},{1,0},{2,3},{3,2},{4,5},{5,4},{6,7},{7,6},{8,9},{9,8},{10,11... | collective-permute-start | bytes 2359304 | tf_op jit(solution)/shard_map/ppermute | solution.py:971
  546.6 21.1 %collective-permute-start.92 = (bf16[192,1024]{1,0:T(8,128)(2,1)S(1)}, bf16[192,1024]{1,0:T(8,128)(2,1)S(1)}, u32[]{:S(2)}, u32[]{:S(2)}) collective-permute-start(bf16[192,1024]{1,0:T(8,128)(2,1)S(1)} %get-tuple-element.622.refs_1_), channel_id=1, source_target_pairs={{0,2},{1,3},{2,0},{3,1},{4,6},{5,7},{6,4},{7,5},{8,10},{9,11},{10,... | collective-permute-start | bytes 1179656 | tf_op jit(solution)/shard_map/ppermute | solution.py:971
  576.0 195.3 %reduce-scatter.11.cloned.1.call-start = ((), (), s32[]{:S(2)}) async-start(), calls=%async_computation.7 | async-start | bytes 2359296 | tf_op jit(solution)/shard_map/reduce_scatter | solution.py:1611
  651.0 203.0 %reduce-scatter.9.cloned.1.call-start = ((), (), s32[]{:S(2)}) async-start(), calls=%async_computation.6 | async-start | bytes 2801664 | tf_op jit(solution)/shard_map/reduce_scatter | solution.py:1646
  694.6 19.6 %collective-permute-start.109 = (bf16[768,256]{1,0:T(8,128)(2,1)S(1)}, bf16[768,256]{1,0:T(8,128)(2,1)S(1)}, u32[]{:S(2)}, u32[]{:S(2)}) collective-permute-start(bf16[768,256]{1,0:T(8,128)(2,1)S(1)} %add.308.refs_11_), channel_id=1, source_target_pairs={{0,2},{1,3},{2,0},{3,1},{4,6},{5,7},{6,4},{7,5},{8,10},{9,11},{10,... | collective-permute-start | bytes 1179656 | tf_op jit(solution)/shard_map/ppermute | solution.py:971
  695.5 26.8 %collective-permute-start.112 = (bf16[192,1024]{1,0:T(8,128)(2,1)S(1)}, bf16[192,1024]{1,0:T(8,128)(2,1)S(1)}, u32[]{:S(2)}, u32[]{:S(2)}) collective-permute-start(bf16[192,1024]{1,0:T(8,128)(2,1)S(1)} %get-tuple-element.731.refs_1_), channel_id=1, source_target_pairs={{0,2},{1,3},{2,0},{3,1},{4,6},{5,7},{6,4},{7,5},{8,10},{9,11},{10,... | collective-permute-start | bytes 1179656 | tf_op jit(solution)/shard_map/ppermute | solution.py:971
  696.6 34.2 %collective-permute-start.113 = (bf16[192,1024]{1,0:T(8,128)(2,1)}, bf16[192,1024]{1,0:T(8,128)(2,1)}, u32[]{:S(2)}, u32[]{:S(2)}) collective-permute-start(bf16[192,1024]{1,0:T(8,128)(2,1)} %get-tuple-element.713.refs_14_.refs_2_), channel_id=1, source_target_pairs={{0,2},{1,3},{2,0},{3,1},{4,6},{5,7},{6,4},{7,5},{8,10},{9,11},{10,... | collective-permute-start | bytes 1179656 | tf_op jit(solution)/shard_map/ppermute | solution.py:971
  713.1 26.1 %collective-permute-start.114 = (bf16[192,1024]{1,0:T(8,128)(2,1)}, bf16[192,1024]{1,0:T(8,128)(2,1)}, u32[]{:S(2)}, u32[]{:S(2)}) collective-permute-start(bf16[192,1024]{1,0:T(8,128)(2,1)} %get-tuple-element.736.refs_1_), channel_id=1, source_target_pairs={{0,2},{1,3},{2,0},{3,1},{4,6},{5,7},{6,4},{7,5},{8,10},{9,11},{10,... | collective-permute-start | bytes 1179656 | tf_op jit(solution)/shard_map/ppermute | solution.py:971
  779.1 22.1 %collective-permute-start.120 = (bf16[576,128]{1,0:T(8,128)(2,1)S(1)}, bf16[576,128]{1,0:T(8,128)(2,1)S(1)}, u32[]{:S(2)}, u32[]{:S(2)}) collective-permute-start(bf16[576,128]{1,0:T(8,128)(2,1)S(1)} %get-tuple-element.755), channel_id=1, source_target_pairs={{0,20},{4,16},{8,28},{12,24},{16,4},{20,0},{24,12},{28,8},{1,21},{... | collective-permute-start | bytes 442376 | tf_op jit(solution)/shard_map/ppermute | solution.py:971
  780.6 20.6 %collective-permute-start.121 = (bf16[576,128]{1,0:T(8,128)(2,1)S(1)}, bf16[576,128]{1,0:T(8,128)(2,1)S(1)}, u32[]{:S(2)}, u32[]{:S(2)}) collective-permute-start(bf16[576,128]{1,0:T(8,128)(2,1)S(1)} %get-tuple-element.756), channel_id=1, source_target_pairs={{0,24},{4,28},{8,16},{12,20},{16,8},{20,12},{24,0},{28,4},{1,25},{... | collective-permute-start | bytes 442376 | tf_op jit(solution)/shard_map/ppermute | solution.py:971
  789.5 30.9 %collective-permute-start.126 = (f32[9,1024]{1,0:T(8,128)S(1)}, f32[9,1024]{1,0:T(8,128)S(1)}, u32[]{:S(2)}, u32[]{:S(2)}) collective-permute-start(f32[9,1024]{1,0:T(8,128)S(1)} %pad_maximum_fusion.2), channel_id=1, source_target_pairs={{0,1},{1,0},{2,3},{3,2},{4,5},{5,4},{6,7},{7,6},{8,9},{9,8},{10,11... | collective-permute-start | bytes 110600 | tf_op jit(solution)/shard_map/ppermute | solution.py:971
  (254 other events, 2031.3 us)
Sparse Core Ops, SparseCore 0:
  12.0 70.5 all-gather.8
  85.3 55.5 all-gather.10
  143.6 71.9 all-gather.12
  218.2 71.6 all-gather.14
  470.4 88.6 reduce-scatter.4
  576.1 88.7 reduce-scatter.6
  669.0 67.5 reduce-scatter.10
  745.3 78.8 reduce-scatter.8

commit v8 on v7

--- a/solution.py
+++ b/solution.py
@@ -826,14 +826,14 @@
 
 def embed_back_body(groups, base_ref, line_ref, *refs):
     grads, (out_ref, turned, columns) = refs[:groups], refs[groups:]
-    rows, features = grads[0].shape
     vocab = out_ref.shape[3]
     chunk = min(256, vocab)
     total = line_ref.shape[1]
+    rows = total // groups
 
     @pl.when((pl.program_id(0) == 0) & (pl.program_id(1) == 0))
     def _():
-        whole_rows = jnp.concatenate([g[...] for g in grads], axis=0)
+        whole_rows = jnp.concatenate([g[:rows, :] for g in grads], axis=0)
         turned[...] = jnp.transpose(whole_rows)
         wide = jnp.concatenate(
             [line_ref[...].astype(F32), jnp.zeros((128 - line_ref.shape[0], total), F32)], axis=0
@@ -854,7 +854,8 @@
 def embed_back(base, lines, grads, books, vocab, after):
     parts = base.shape[0]
     groups = len(grads)
-    rows, features = grads[0].shape
+    features = grads[0].shape[1]
+    rows = lines.shape[1] // groups
     return pl.pallas_call(
         later(partial(embed_back_body, groups), len(after), 2 + groups),
         out_shape=sds((parts, books, features, vocab), LOW),
@@ -882,18 +883,29 @@
             out_ref[:, at] = part[c * strip : (c + 1) * strip, :]
 
 
-def split_features_body(need, put, where_ref, side_ref, *refs):
+def split_features_body(scale, need, put, where_ref, side_ref, place_ref, sums_ref, bias_ref, *refs):
     clips = side_ref.shape[0] - 1
+    *refs, extra_ref = refs
     grads, outs = refs[:clips], refs[clips:]
     features = outs[0].shape[1]
-    rows = outs[0].shape[0] // clips
+    columns = bias_ref.shape[1]
+    rows = (outs[0].shape[0] - extra_ref.shape[0]) // clips
     at_rows = pl.ds(pl.multiple_of(side_ref[0] * rows, rows), rows)
-    need(*range(2, 2 + clips))
-    for m, out_ref in reversed(list(enumerate(outs))):
+    extra_ref[...] = jnp.zeros(extra_ref.shape, F32)
+    extra_ref[:8, :] = sums_ref[...] * scale
+    at = pl.ds(pl.multiple_of(place_ref[0] * columns, columns), columns)
+    extra_ref[8:9, at] = bias_ref[0:1, :]
+    for m, out_ref in enumerate(outs):
         at = pl.ds(pl.multiple_of(where_ref[m] * features, features), features)
         for c in range(clips):
             out_ref[c * rows : (c + 1) * rows, :] = grads[c][at_rows, at]
-        put(m)
+        out_ref[clips * rows :, :] = extra_ref[:, at].astype(LOW)
+
+
+def extra_body(*refs):
+    *part_refs, out_ref = refs
+    count = out_ref.shape[0]
+    out_ref[...] = sum(p[p.shape[0] - count :, :].astype(F32) for p in part_refs)
 
 
 def text_body(need, put, where_ref, *refs):
@@ -1106,7 +1118,6 @@
     targets = (jnp.roll(audio_codes, -1, axis=1) - place * vocab).astype(jnp.int32)
     targets = [targets[c] for c in range(clips)]
     loss_weight = [weight_int[c].astype(F32) for c in range(clips)]
-    placed = positions_rows(core * height, height, width)
 
     table_parts = spread_tensor(tables[:books].astype(LOW))
     step = max(1, dp // 4)
@@ -1116,6 +1127,9 @@
             vocab_base, packets[low_end : low_end + step], table_parts, count, list(last)
         )
         last[:] = [embedded[-1]]
+        if low_end + step == dp:
+            begin, _ = lax.optimization_barrier((core * height, embedded[0]))
+            placed = positions_rows(begin, height, width)
         for m, piece in enumerate(embedded, low_end):
             arrived[m] = swap(piece, "dp", m) if m else piece
         last += [a for a in arrived[low_end + step : low_end + 2 * step] if a is not None]
@@ -1406,7 +1420,7 @@
             mask *= 2
         return stats
 
-    def head_back_step(c, logits, stats):
+    def head_back_step(c, logits, stats, pieces):
         grad, keep, send, loss = run_block(
             head_backward_body,
             [sds((frames, books * vocab), LOW), flow, flow, Flow(sds((8, 128), F32))],
@@ -1415,6 +1429,7 @@
             + [counted],
             flops=2 * frames * width * books * vocab,
             scratch=tot,
+            after=pieces,
             name="head_backward",
         )
         loss_part[c] = free(loss)[0, 0]
@@ -1472,13 +1487,15 @@
         flush()
         ready[c] = head_step(c, pairs[3][c])
         if c:
+            pieces = list(soon)
             flush()
             logits, stats = ready[c - 1]
-            logit_grads[c - 1] = head_back_step(c - 1, logits, merge_step(stats))
+            logit_grads[c - 1] = head_back_step(c - 1, logits, merge_step(stats), pieces)
     logits, stats = ready[-1]
     stats = merge_step(stats)
+    pieces = list(newest)
     flush()
-    logit_grads[-1] = head_back_step(clips - 1, logits, stats)
+    logit_grads[-1] = head_back_step(clips - 1, logits, stats, pieces)
 
     def ffn_back_step(c, pair):
         own, got = pair
@@ -1633,32 +1650,41 @@
         flops=2 * clips * text_len * text_width * columns,
         name="text_weight",
     )
-    for members in ((0, 1), (2,)):
+    def self_in(members):
         size = len(members) * columns
         windows = [
-            Window(
-                a, (frames, size), lambda ref: ref.at[:, pl.ds(members[0] * columns, size)]
-            )
+            Window(a, (frames, size), lambda ref: ref.at[:, pl.ds(members[0] * columns, size)])
             for a in self_grads
         ]
         weights(pairs[0], windows, [attn_into(n) for n in members], "self_in")
-    soon[:] = newest
-    self_sum = lax.psum_scatter(free(self_shared.array), "dp", scatter_dimension=0, tiled=False)
+
+    self_in((0, 1))
     for c in every:
+        if c == clips - 1:
+            older[:] = newest
+            self_in((2,))
+            self_sum = lax.psum_scatter(
+                free(self_shared.array), "dp", scatter_dimension=0, tiled=False
+            )
         zero_step(c)
 
     if aligned:
-        pieces = list(map(free, run(
-            split_features_body,
-            [Flow(sds((clips * strip, share), LOW))] * dp,
+        pieces = run(
+            partial(split_features_body, 1.0 / sides),
+            [Flow(sds((clips * strip + 16, share), LOW))] * dp,
             [
                 Scalar(group_order),
                 Scalar(jnp.broadcast_to(side.astype(jnp.int32), (clips + 1,))),
+                Scalar(place.astype(jnp.int32).reshape(1)),
+                sums[0],
+                bias_grad,
             ]
             + zero_lows,
+            scratch=[pltpu.VMEM((16, width), F32)],
             after=[cross_sum],
             name="split_features",
-        )))
+        )
+        pieces = [free(p) for p in pieces]
     else:
         rows = jnp.concatenate(
             [lax.dynamic_slice_in_dim(free(a), side * strip, strip, 0) for a in zero_lows], axis=0
@@ -1669,14 +1695,20 @@
     embed_parts = embed_back(vocab_base, back_lines, rows_all, books, vocab, list(last))
     grad_embed = collect_tensor([embed_parts[m] for m in range(tensor)])
 
-    norm_part = free(sums[0]) * (1.0 / sides)
-    bias_row = lax.dynamic_update_slice_in_dim(
-        jnp.zeros((width,), F32), free(bias_grad)[0], place * columns, 0
-    )
-    norm_total = total_over(
-        jnp.concatenate([norm_part, bias_row[None]], axis=0), ("tensor", "dp")
-    )
-    grad_norm_rows = lax.dynamic_slice_in_dim(norm_total, group * share, share, 1)
+    if aligned:
+        (extra,) = norm_rows_kernel(
+            extra_body, [sds((16, share), F32)], rows_all, None, last, name="extra"
+        )
+        grad_norm_rows = total_over(free(extra), ("tensor",))[: norm_params.shape[0]]
+    else:
+        norm_part = free(sums[0]) * (1.0 / sides)
+        bias_row = lax.dynamic_update_slice_in_dim(
+            jnp.zeros((width,), F32), free(bias_grad)[0], place * columns, 0
+        )
+        norm_total = total_over(
+            jnp.concatenate([norm_part, bias_row[None]], axis=0), ("tensor", "dp")
+        )
+        grad_norm_rows = lax.dynamic_slice_in_dim(norm_total, group * share, share, 1)
 
     own_self = self_sum[: 4 * share].reshape(4, share, columns)
     own_cross = cross_sum.reshape(4, share, columns)

time: 905 us -> 905 us (level)
  waiting for transfers between devices: 240 us -> 258 us
  local copies, waits for them, and re-layouts: 73.5 us -> 63 us
  starting transfers between devices: 128 us -> 118 us
    ppermute x136 -> x133, starting transfers between devices: 127 us -> 117 us  [swap(): return lax.ppermute(values, axis, [(i, i ^ mask) for i in range(size)])]
    all_gather x1, waiting for transfers between devices: 0.01 us -> 9.57 us  [on_device(): cross_all = lax.all_gather(cross_flat, 'dp', axis=0)]
    unnamed x282 -> x274, local copies, waits for them, and re-layouts: 59.6 us -> 50.7 us
    ppermute x136 -> x133, waiting for transfers between devices: 240 us -> 248 us  [swap(): return lax.ppermute(values, axis, [(i, i ^ mask) for i in range(size)])]
    pallas_call x51 -> x52, Pallas kernels: 44.4 us -> 44.4 us  [norm_rows_kernel(): pl.pallas_call(later(body, len(after), len(operands)), out_shape=tuple((p...]
  transfers between devices with their start and end apart: 144 -> 141, of which waited for: 54 -> 55; matrix products, arithmetic and copies ran while one was open for 3% -> 3% of each run, Pallas kernels for 42% -> 42%
where the time goes in v8:
time: 905 us; the launch traced here: 893 us
  Pallas kernels  395 us (44%)
  waiting for transfers between devices  258 us (29%)
  starting transfers between devices  118 us (13%)
  local copies, waits for them, and re-layouts  63 us (7%)
  other arithmetic  35.2 us (4%)
  between operations  24.6 us (3%)
    pallas_call x44, Pallas kernels, kernel(): pl.pallas_call(run_body, out_shape=tuple(out_shapes), in_specs=specs + [a...  316 us
    ppermute x133, waiting for transfers between devices, swap(): return lax.ppermute(values, axis, [(i, i ^ mask) for i in range(size)])  248 us
    ppermute x133, starting transfers between devices, swap(): return lax.ppermute(values, axis, [(i, i ^ mask) for i in range(size)])  117 us
    unnamed x274, local copies, waits for them, and re-layouts  50.7 us
    pallas_call x52, Pallas kernels, norm_rows_kernel(): pl.pallas_call(later(body, len(after), len(operands)), out_shape=tuple((p...  44.4 us
    pallas_call x1, Pallas kernels, embed_back(): pl.pallas_call(later(partial(embed_back_body, groups), len(after), 2 + gr...  18.1 us
  transfers between devices with their start and end apart: 141, of which 55 were waited for; matrix products, arithmetic and copies ran while one was open for 3% of the time, Pallas kernels for 42%

profile of v8, /device:TPU:0, one launch (start us, length us, event | category | flops | bytes accessed | tf_op | source)
XLA Modules:
  0.0 893.4 jit_solution(2942616730224895797)
XLA Ops:
  77.2 12.7 %collective-permute-start.16 = (bf16[576,128]{1,0:T(8,128)(2,1)S(1)}, bf16[576,128]{1,0:T(8,128)(2,1)S(1)}, u32[]{:S(2)}, u32[]{:S(2)}) collective-permute-start(bf16[576,128]{1,0:T(8,128)(2,1)S(1)} %get-tuple-element.398.refs_7_), channel_id=1, source_target_pairs={{0,12},{4,8},{8,4},{12,0},{16,28},{20,24},{24,20},{28,16},{1,13},{... | collective-permute-start | bytes 442376 | tf_op jit(solution)/shard_map/ppermute | solution.py:983
  119.4 9.0 %self_forward.3 = (bf16[768,256]{1,0:T(8,128)(2,1)}, bf16[768,256]{1,0:T(8,128)(2,1)}, bf16[768,256]{1,0:T(8,128)(2,1)}, bf16[768,256]{1,0:T(8,128)(2,1)}, f32[8...) custom-call(s32[1]{0:T(128)} %bitcast.refs_0_, ...), custom_call_target="tpu_custom_call" | custom-call | flops 1024 | bytes 1024 | tf_op jit(solution)/shard_map/self_forward/pallas_call | solution.py:263
  129.5 9.6 %all-gather.11.cloned.1.call-done = bf16[4864,256]{1,0:T(8,128)(2,1)} async-done(((bf16[608,256]{1,0:T(8,128)(2,1)}), bf16[4864,256]{1,0:T(8,128)(2,1)}) %all-gather.11.cloned.1.call-update) | async-done | bytes 2490384 | tf_op jit(solution)/shard_map/all_gather | solution.py:1096
  147.3 8.7 self_forward.4
  160.0 10.7 %collective-permute-done.28.refs_3_ = bf16[768,256]{1,0:T(8,128)(2,1)} collective-permute-done((bf16[768,256]{1,0:T(8,128)(2,1)}, bf16[768,256]{1,0:T(8,128)(2,1)}, u32[]{:S(2)}, u32[]{:S(2)}) %collective-permute-start.28) | collective-permute-done | bytes 393248 | tf_op jit(solution)/shard_map/ppermute | solution.py:983
  175.8 9.1 %self_forward.5 = (bf16[768,256]{1,0:T(8,128)(2,1)}, bf16[768,256]{1,0:T(8,128)(2,1)}, bf16[768,256]{1,0:T(8,128)(2,1)}, bf16[768,256]{1,0:T(8,128)(2,1)}, f32[8...) custom-call(s32[1]{0:T(128)} %bitcast.refs_0_, ...), custom_call_target="tpu_custom_call" | custom-call | flops 1024 | bytes 1024 | tf_op jit(solution)/shard_map/self_forward/pallas_call | solution.py:263
  267.8 9.4 %ffn_forward.3 = (bf16[768,1024]{1,0:T(8,128)(2,1)}, bf16[768,1024]{1,0:T(8,128)(2,1)}, bf16[384,1024]{1,0:T(8,128)(2,1)S(1)}, bf16[384,1024]{1,0:T(8,128)(2,1)S...) custom-call(s32[1]{0:T(128)} %bitcast.refs_0_, ...), custom_call_target="tpu_custom_call" | custom-call | flops 1024 | bytes 1024 | tf_op jit(solution)/shard_map/ffn_forward/pallas_call | solution.py:263
  287.9 8.2 ffn_forward.4
  310.7 8.2 ffn_forward.5
  333.9 10.8 %head_forward.3 = (f32[768,2048]{1,0:T(8,128)}, f32[8,768]{1,0:T(8,128)S(1)}, bf16[384,1024]{1,0:T(8,128)(2,1)}, bf16[384,1024]{1,0:T(8,128)(2,1)}, f32[384,1024...) custom-call(s32[1]{0:T(128)} %bitcast.refs_0_, bf16[384,1024]{1,0:T(8,128)(2,1)S(1)} %get-tuple-element.494.refs_2_.refs_1_, ...), custom_call_target="tpu_custom_call" | custom-call | flops 1024 | bytes 1024 | tf_op jit(solution)/shard_map/head_forward/pallas_call | solution.py:263
  353.9 9.6 %head_forward.4 = (f32[768,2048]{1,0:T(8,128)}, f32[8,768]{1,0:T(8,128)S(1)}, bf16[384,1024]{1,0:T(8,128)(2,1)}, bf16[384,1024]{1,0:T(8,128)(2,1)}, f32[384,1024...) custom-call(s32[1]{0:T(128)} %bitcast.refs_0_, bf16[384,1024]{1,0:T(8,128)(2,1)S(1)} %get-tuple-element.505.refs_1_.refs_10_, ...), custom_call_target="tpu_custom_call" | custom-call | flops 1024 | bytes 1024 | tf_op jit(solution)/shard_map/head_forward/pallas_call | solution.py:263
  367.4 8.6 head_backward.3
  380.5 9.6 %head_forward.5 = (f32[768,2048]{1,0:T(8,128)}, f32[8,768]{1,0:T(8,128)S(1)}, bf16[384,1024]{1,0:T(8,128)(2,1)}, bf16[384,1024]{1,0:T(8,128)(2,1)}, f32[384,1024]{1,0:T(8,128)}, /*index=5*/f32[8,128]{1,0:T(8,128)S(1)}) custom-call(s32[1]{0:T(128)} %bitcast.refs_0_, bf16[384,1024]{1,0:T(8,128)(2,1)S(1)} %get-tuple-element.514.refs_2_.refs_1_, ...), custom_call_target="tpu_custom_call" | custom-call | flops 1024 | bytes 1024 | tf_op jit(solution)/shard_map/head_forward/pallas_call | solution.py:263
  394.1 8.5 head_backward.4
  406.0 8.7 collective-permute-done.70.refs_1_
  415.5 9.1 %head_backward.5 = (bf16[768,2048]{1,0:T(8,128)(2,1)}, bf16[384,1024]{1,0:T(8,128)(2,1)S(1)}, bf16[384,1024]{1,0:T(8,128)(2,1)S(1)}, f32[8,128]{1,0:T(8,128)S(1)}, f32[8,128]{1,0:T(8,128)S(1)}) custom-call(s32[1]{0:T(128)} %bitcast.refs_0_, f32[8,768]{1,0:T(8,128)S(1)} %merge.11.refs_2_.refs_1_, f32[768,4]{1,0:T(8,128)S(1)} %copy-done.6, ...), custom_call_target="tpu_custom_call" | custom-call | flops 1024 | bytes 1024 | tf_op jit(solution)/shard_map/head_backward/pallas_call | solution.py:263
  439.0 10.2 %head_weights.2 = (bf16[8,4,128,512]{3,2,1,0:T(8,128)(2,1)}, f32[8,128]{1,0:T(8,128)S(1)}) custom-call(s32[1]{0:T(128)} %bitcast.refs_0_, bf16[384,1024]{1,0:T(8,128)(2,1)} %get-tuple-element.538.refs_1_, bf16[384,1024]{1,0:T(8,128)(2,1)} %get-tuple-element.539.refs_2_, bf16[384,1024]{1,0:T(8,128)(2,1)} %get-tuple-element.540.refs_3_, ...), custom_call_target="tpu_custom_call" | custom-call | flops 1024 | bytes 1024 | tf_op jit(solution)/shard_map/head_weights/pallas_call | solution.py:263
  449.2 10.5 %head_weights.3 = (bf16[8,4,128,512]{3,2,1,0:T(8,128)(2,1)}, f32[8,128]{1,0:T(8,128)S(1)}) custom-call(s32[1]{0:T(128)} %bitcast.refs_0_, bf16[384,1024]{1,0:T(8,128)(2,1)} %get-tuple-element.538.refs_1_, bf16[384,1024]{1,0:T(8,128)(2,1)} %get-tuple-element.539.refs_2_, ...), custom_call_target="tpu_custom_call", output_to_operand_aliasing={{0}: (10, {})} | custom-call | flops 1024 | bytes 1024 | tf_op jit(solution)/shard_map/head_weights/pallas_call | solution.py:263
  516.9 8.3 ffn_two.2
  525.2 8.4 ffn_two.3
  549.5 8.2 ffn_one.2
  557.7 8.2 ffn_one.3
  573.5 9.2 %cross_backward.5 = (bf16[768,256]{1,0:T(8,128)(2,1)}, bf16[256,256]{1,0:T(8,128)(2,1)}, bf16[256,256]{1,0:T(8,128)(2,1)}, bf16[384,1024]{1,0:T(8,128)(2,1)S(1)}...) custom-call(s32[1]{0:T(128)} %bitcast.refs_0_, ...), custom_call_target="tpu_custom_call" | custom-call | flops 1024 | bytes 1024 | tf_op jit(solution)/shard_map/cross_backward/pallas_call | solution.py:263
  600.6 11.2 %self_backward.3 = (bf16[768,768]{1,0:T(8,128)(2,1)}, bf16[384,1024]{1,0:T(8,128)(2,1)S(1)}, bf16[384,1024]{1,0:T(8,128)(2,1)S(1)}, bf16[384,1024]{1,0:T(8,128)(...) custom-call(s32[1]{0:T(128)} %bitcast.refs_0_, ...), custom_call_target="tpu_custom_call" | custom-call | flops 1024 | bytes 1024 | tf_op jit(solution)/shard_map/self_backward/pallas_call | solution.py:263
  620.8 9.3 %collective-permute-done.102.refs_12_.refs_3_ = bf16[192,1024]{1,0:T(8,128)(2,1)S(1)} collective-permute-done((bf16[192,1024]{1,0:T(8,128)(2,1)S(1)}, bf16[192,1024]{1,0:T(8,128)(2,1)S(1)}, u32[]{:S(2)}, u32[]{:S(2)}) %collective-permute-start.102) | collective-permute-done | bytes 393248 | tf_op jit(solution)/shard_map/ppermute | solution.py:983
  651.0 10.9 %self_backward.4 = (bf16[768,768]{1,0:T(8,128)(2,1)}, bf16[384,1024]{1,0:T(8,128)(2,1)S(1)}, bf16[384,1024]{1,0:T(8,128)(2,1)S(1)}, bf16[384,1024]{1,0:T(8,128)(...) custom-call(s32[1]{0:T(128)} %bitcast.refs_0_, ...), custom_call_target="tpu_custom_call" | custom-call | flops 1024 | bytes 1024 | tf_op jit(solution)/shard_map/self_backward/pallas_call | solution.py:263
  672.2 11.1 %self_backward.5 = (bf16[768,768]{1,0:T(8,128)(2,1)}, bf16[384,1024]{1,0:T(8,128)(2,1)S(1)}, bf16[384,1024]{1,0:T(8,128)(2,1)S(1)}, bf16[384,1024]{1,0:T(8,128)(...) custom-call(s32[1]{0:T(128)} %bitcast.refs_0_, ...), custom_call_target="tpu_custom_call" | custom-call | flops 1024 | bytes 1024 | tf_op jit(solution)/shard_map/self_backward/pallas_call | solution.py:263
  707.4 15.6 %collective-permute-done.112.refs_6_.refs_3_ = bf16[192,1024]{1,0:T(8,128)(2,1)S(1)} collective-permute-done((bf16[192,1024]{1,0:T(8,128)(2,1)S(1)}, bf16[192,1024]{1,0:T(8,128)(2,1)S(1)}, u32[]{:S(2)}, u32[]{:S(2)}) %collective-permute-start.112) | collective-permute-done | bytes 393248 | tf_op jit(solution)/shard_map/ppermute | solution.py:983
  727.7 8.5 self_in.2
  769.2 11.5 %collective-permute-done.117.refs_4_.refs_2_ = bf16[592,128]{1,0:T(8,128)(2,1)S(1)} collective-permute-done((bf16[592,128]{1,0:T(8,128)(2,1)S(1)}, bf16[592,128]{1,0:T(8,128)(2,1)S(1)}, u32[]{:S(2)}, u32[]{:S(2)}) %collective-permute-start.117) | collective-permute-done | bytes 151584 | tf_op jit(solution)/shard_map/ppermute | solution.py:983
  797.9 18.1 %embed_back.1 = bf16[4,4,128,512]{3,2,1,0:T(8,128)(2,1)S(1)} custom-call(s32[4]{0:T(128)S(1)} %copy-done.100, s32[8,4608]{1,0:T(8,128)S(1)} %concatenate.29.refs_23_.refs_1_, bf16[592,128]{1,0:T(8,128)(2,1)S(1)} %get-tuple-element.754.refs_2_.refs_0_, bf16[592,128]{1,0:T(8,128)(2,1)S(1)} %collective-permute-done.116.refs_3_.refs_1_, ...), custom_call_target="tpu_custom_call" | custom-call | flops 1024 | bytes 1024 | tf_op jit(solution)/shard_map/embed_back/pallas_call | solution.py:859
  828.3 9.1 %collective-permute-done.127 = f32[16,128]{1,0:T(8,128)S(1)} collective-permute-done((f32[16,128]{1,0:T(8,128)S(1)}, f32[16,128]{1,0:T(8,128)S(1)}, u32[]{:S(2)}, u32[]{:S(2)}) %collective-permute-start.127) | collective-permute-done | bytes 8224 | tf_op jit(solution)/shard_map/ppermute | solution.py:983
  (706 shorter events, 549.8 us)
Async XLA Ops:
  7.2 99.9 %all-gather.9.cloned.1.call-start = ((), (), s32[]{:S(2)}) async-start(), calls=%async_computation.8 | async-start | bytes 2433024 | tf_op jit(solution)/shard_map/all_gather | solution.py:1095
  11.8 127.2 %all-gather.11.cloned.1.call-start = ((), (), s32[]{:S(2)}) async-start(), calls=%async_computation.9 | async-start | bytes 2801664 | tf_op jit(solution)/shard_map/all_gather | solution.py:1096
  13.5 252.8 %all-gather.13.cloned.1.call-start = ((), (), s32[]{:S(2)}) async-start(), calls=%async_computation.10 | async-start | bytes 4718592 | tf_op jit(solution)/shard_map/all_gather | solution.py:1097
  14.5 318.0 %all-gather.15.cloned.1.call-start = ((), (), s32[]{:S(2)}) async-start(), calls=%async_computation.11 | async-start | bytes 4718592 | tf_op jit(solution)/shard_map/all_gather | solution.py:1098
  16.8 22.2 %collective-permute-start = (s32[8,640]{1,0:T(8,128)S(1)}, s32[8,640]{1,0:T(8,128)S(1)}, u32[]{:S(2)}, u32[]{:S(2)}) collective-permute-start(s32[8,640]{1,0:T(8,128)S(1)} %pad_select_fusion.refs_1_.refs_0_), channel_id=1, source_target_pairs={{0,24},{4,28},{8,16},{12,20},{16,8},{20,12},{24,0},{28,4},{1,25},{... | collective-permute-start | bytes 61448 | tf_op jit(solution)/shard_map/ppermute | solution.py:983
  24.1 27.3 %collective-permute-start.2 = (bf16[4,128,512]{2,1,0:T(8,128)(2,1)S(1)}, bf16[4,128,512]{2,1,0:T(8,128)(2,1)S(1)}, u32[]{:S(2)}, u32[]{:S(2)}) collective-permute-start(bf16[4,128,512]{2,1,0:T(8,128)(2,1)S(1)} %get-tuple-element.795.refs_3_), channel_id=1, source_target_pairs={{0,1},{1,0},{2,3},{3,2},{4,5},{5,4},{6,7},{7,6},{8,9},{9,8},{10,11... | collective-permute-start | bytes 1572872 | tf_op jit(solution)/shard_map/ppermute | solution.py:983
  64.9 25.1 %collective-permute-start.12 = (bf16[576,128]{1,0:T(8,128)(2,1)S(1)}, bf16[576,128]{1,0:T(8,128)(2,1)S(1)}, u32[]{:S(2)}, u32[]{:S(2)}) collective-permute-start(bf16[576,128]{1,0:T(8,128)(2,1)S(1)} %get-tuple-element.399), channel_id=1, source_target_pairs={{0,16},{4,20},{8,24},{12,28},{16,0},{20,4},{24,8},{28,12},{1,17},{... | collective-permute-start | bytes 442376 | tf_op jit(solution)/shard_map/ppermute | solution.py:983
  64.9 25.3 %collective-permute-start.13 = (bf16[576,128]{1,0:T(8,128)(2,1)S(1)}, bf16[576,128]{1,0:T(8,128)(2,1)S(1)}, u32[]{:S(2)}, u32[]{:S(2)}) collective-permute-start(bf16[576,128]{1,0:T(8,128)(2,1)S(1)} %get-tuple-element.397.refs_7_), channel_id=1, source_target_pairs={{0,20},{4,16},{8,28},{12,24},{16,4},{20,0},{24,12},{28,8},{1,21},{... | collective-permute-start | bytes 442376 | tf_op jit(solution)/shard_map/ppermute | solution.py:983
  77.2 25.0 %collective-permute-start.16 = (bf16[576,128]{1,0:T(8,128)(2,1)S(1)}, bf16[576,128]{1,0:T(8,128)(2,1)S(1)}, u32[]{:S(2)}, u32[]{:S(2)}) collective-permute-start(bf16[576,128]{1,0:T(8,128)(2,1)S(1)} %get-tuple-element.398.refs_7_), channel_id=1, source_target_pairs={{0,12},{4,8},{8,4},{12,0},{16,28},{20,24},{24,20},{28,16},{1,13},{... | collective-permute-start | bytes 442376 | tf_op jit(solution)/shard_map/ppermute | solution.py:983
  117.2 24.6 %collective-permute-start.19 = (bf16[192,1024]{1,0:T(8,128)(2,1)}, bf16[192,1024]{1,0:T(8,128)(2,1)}, u32[]{:S(2)}, u32[]{:S(2)}) collective-permute-start(bf16[192,1024]{1,0:T(8,128)(2,1)} %get-tuple-element.410.refs_3_), channel_id=1, source_target_pairs={{0,2},{1,3},{2,0},{3,1},{4,6},{5,7},{6,4},{7,5},{8,10},{9,11},{10,... | collective-permute-start | bytes 1179656 | tf_op jit(solution)/shard_map/ppermute | solution.py:983
  159.7 25.2 %collective-permute-start.27 = (bf16[768,256]{1,0:T(8,128)(2,1)}, bf16[768,256]{1,0:T(8,128)(2,1)}, u32[]{:S(2)}, u32[]{:S(2)}) collective-permute-start(bf16[768,256]{1,0:T(8,128)(2,1)} %get-tuple-element.434.refs_1_), channel_id=1, source_target_pairs={{0,1},{1,0},{2,3},{3,2},{4,5},{5,4},{6,7},{7,6},{8,9},{9,8},{10,11... | collective-permute-start | bytes 1179656 | tf_op jit(solution)/shard_map/ppermute | solution.py:983
  159.8 431.4 %reduce-scatter.5.cloned.1.call-start = ((), (), s32[]{:S(2)}) async-start(), calls=%async_computation.4 | async-start | bytes 4718592 | tf_op jit(solution)/shard_map/reduce_scatter | solution.py:1533
  170.7 20.6 %collective-permute-start.26 = (bf16[192,1024]{1,0:T(8,128)(2,1)}, bf16[192,1024]{1,0:T(8,128)(2,1)S(1)}, u32[]{:S(2)}, u32[]{:S(2)}) collective-permute-start(bf16[192,1024]{1,0:T(8,128)(2,1)} %copy-done.15), channel_id=1, source_target_pairs={{0,2},{1,3},{2,0},{3,1},{4,6},{5,7},{6,4},{7,5},{8,10},{9,11},{10,... | collective-permute-start | bytes 1179656 | tf_op jit(solution)/shard_map/ppermute | solution.py:983
  171.2 20.0 %collective-permute-start.25 = (bf16[192,1024]{1,0:T(8,128)(2,1)}, bf16[192,1024]{1,0:T(8,128)(2,1)S(1)}, u32[]{:S(2)}, u32[]{:S(2)}) collective-permute-start(bf16[192,1024]{1,0:T(8,128)(2,1)} %copy-done.81), channel_id=1, source_target_pairs={{0,2},{1,3},{2,0},{3,1},{4,6},{5,7},{6,4},{7,5},{8,10},{9,11},{10,... | collective-permute-start | bytes 1179656 | tf_op jit(solution)/shard_map/ppermute | solution.py:983
  175.3 24.0 %collective-permute-start.30 = (bf16[192,1024]{1,0:T(8,128)(2,1)S(1)}, bf16[192,1024]{1,0:T(8,128)(2,1)S(1)}, u32[]{:S(2)}, u32[]{:S(2)}) collective-permute-start(bf16[192,1024]{1,0:T(8,128)(2,1)S(1)} %get-tuple-element.437.refs_1_), channel_id=1, source_target_pairs={{0,2},{1,3},{2,0},{3,1},{4,6},{5,7},{6,4},{7,5},{8,10},{9,11},{10,... | collective-permute-start | bytes 1179656 | tf_op jit(solution)/shard_map/ppermute | solution.py:983
  286.3 19.4 %collective-permute-start.50 = (bf16[192,1024]{1,0:T(8,128)(2,1)S(1)}, bf16[192,1024]{1,0:T(8,128)(2,1)S(1)}, u32[]{:S(2)}, u32[]{:S(2)}) collective-permute-start(bf16[192,1024]{1,0:T(8,128)(2,1)S(1)} %get-tuple-element.484.refs_1_), channel_id=1, source_target_pairs={{0,2},{1,3},{2,0},{3,1},{4,6},{5,7},{6,4},{7,5},{8,10},{9,11},{10,... | collective-permute-start | bytes 1179656 | tf_op jit(solution)/shard_map/ppermute | solution.py:983
  352.1 24.0 %collective-permute-start.63 = (bf16[192,1024]{1,0:T(8,128)(2,1)S(1)}, bf16[192,1024]{1,0:T(8,128)(2,1)S(1)}, u32[]{:S(2)}, u32[]{:S(2)}) collective-permute-start(bf16[192,1024]{1,0:T(8,128)(2,1)S(1)} %get-tuple-element.499.refs_10_.refs_2_), channel_id=1, source_target_pairs={{0,2},{1,3},{2,0},{3,1},{4,6},{5,7},{6,4},{7,5},{8,10},{9,11},{10,... | collective-permute-start | bytes 1179656 | tf_op jit(solution)/shard_map/ppermute | solution.py:983
  428.3 20.9 %collective-permute-start.76 = (bf16[192,1024]{1,0:T(8,128)(2,1)S(1)}, bf16[192,1024]{1,0:T(8,128)(2,1)S(1)}, u32[]{:S(2)}, u32[]{:S(2)}) collective-permute-start(bf16[192,1024]{1,0:T(8,128)(2,1)S(1)} %get-tuple-element.550.refs_1_), channel_id=1, source_target_pairs={{0,2},{1,3},{2,0},{3,1},{4,6},{5,7},{6,4},{7,5},{8,10},{9,11},{10,... | collective-permute-start | bytes 1179656 | tf_op jit(solution)/shard_map/ppermute | solution.py:983
  459.8 263.2 %reduce-scatter.7.cloned.1.call-start = ((), (), s32[]{:S(2)}) async-start(), calls=%async_computation.5 | async-start | bytes 4718592 | tf_op jit(solution)/shard_map/reduce_scatter | solution.py:1567
  515.1 21.3 %collective-permute-start.90 = (bf16[384,1024]{1,0:T(8,128)(2,1)S(1)}, bf16[384,1024]{1,0:T(8,128)(2,1)S(1)}, u32[]{:S(2)}, u32[]{:S(2)}) collective-permute-start(bf16[384,1024]{1,0:T(8,128)(2,1)S(1)} %get-tuple-element.606), channel_id=1, source_target_pairs={{0,1},{1,0},{2,3},{3,2},{4,5},{5,4},{6,7},{7,6},{8,9},{9,8},{10,11... | collective-permute-start | bytes 2359304 | tf_op jit(solution)/shard_map/ppermute | solution.py:983
  536.5 21.2 %collective-permute-start.92 = (bf16[192,1024]{1,0:T(8,128)(2,1)S(1)}, bf16[192,1024]{1,0:T(8,128)(2,1)S(1)}, u32[]{:S(2)}, u32[]{:S(2)}) collective-permute-start(bf16[192,1024]{1,0:T(8,128)(2,1)S(1)} %get-tuple-element.624.refs_1_), channel_id=1, source_target_pairs={{0,2},{1,3},{2,0},{3,1},{4,6},{5,7},{6,4},{7,5},{8,10},{9,11},{10,... | collective-permute-start | bytes 1179656 | tf_op jit(solution)/shard_map/ppermute | solution.py:983
  566.0 192.7 %reduce-scatter.11.cloned.1.call-start = ((), (), s32[]{:S(2)}) async-start(), calls=%async_computation.7 | async-start | bytes 2359296 | tf_op jit(solution)/shard_map/reduce_scatter | solution.py:1628
  642.4 199.3 %reduce-scatter.9.cloned.1.call-start = ((), (), s32[]{:S(2)}) async-start(), calls=%async_computation.6 | async-start | bytes 2801664 | tf_op jit(solution)/shard_map/reduce_scatter | solution.py:1666
  686.3 20.3 %collective-permute-start.109 = (bf16[768,256]{1,0:T(8,128)(2,1)S(1)}, bf16[768,256]{1,0:T(8,128)(2,1)S(1)}, u32[]{:S(2)}, u32[]{:S(2)}) collective-permute-start(bf16[768,256]{1,0:T(8,128)(2,1)S(1)} %add.294.refs_11_), channel_id=1, source_target_pairs={{0,2},{1,3},{2,0},{3,1},{4,6},{5,7},{6,4},{7,5},{8,10},{9,11},{10,... | collective-permute-start | bytes 1179656 | tf_op jit(solution)/shard_map/ppermute | solution.py:983
  687.8 39.9 %collective-permute-start.113 = (bf16[192,1024]{1,0:T(8,128)(2,1)}, bf16[192,1024]{1,0:T(8,128)(2,1)}, u32[]{:S(2)}, u32[]{:S(2)}) collective-permute-start(bf16[192,1024]{1,0:T(8,128)(2,1)} %get-tuple-element.715.refs_14_.refs_2_), channel_id=1, source_target_pairs={{0,2},{1,3},{2,0},{3,1},{4,6},{5,7},{6,4},{7,5},{8,10},{9,11},{10,... | collective-permute-start | bytes 1179656 | tf_op jit(solution)/shard_map/ppermute | solution.py:983
  688.3 34.7 %collective-permute-start.112 = (bf16[192,1024]{1,0:T(8,128)(2,1)S(1)}, bf16[192,1024]{1,0:T(8,128)(2,1)S(1)}, u32[]{:S(2)}, u32[]{:S(2)}) collective-permute-start(bf16[192,1024]{1,0:T(8,128)(2,1)S(1)} %get-tuple-element.733.refs_1_), channel_id=1, source_target_pairs={{0,2},{1,3},{2,0},{3,1},{4,6},{5,7},{6,4},{7,5},{8,10},{9,11},{10,... | collective-permute-start | bytes 1179656 | tf_op jit(solution)/shard_map/ppermute | solution.py:983
  704.6 31.7 %collective-permute-start.114 = (bf16[192,1024]{1,0:T(8,128)(2,1)}, bf16[192,1024]{1,0:T(8,128)(2,1)S(1)}, u32[]{:S(2)}, u32[]{:S(2)}) collective-permute-start(bf16[192,1024]{1,0:T(8,128)(2,1)} %get-tuple-element.742.refs_1_), channel_id=1, source_target_pairs={{0,2},{1,3},{2,0},{3,1},{4,6},{5,7},{6,4},{7,5},{8,10},{9,11},{10,... | collective-permute-start | bytes 1179656 | tf_op jit(solution)/shard_map/ppermute | solution.py:983
  705.1 37.6 %collective-permute-start.115 = (bf16[192,1024]{1,0:T(8,128)(2,1)S(1)}, bf16[192,1024]{1,0:T(8,128)(2,1)S(1)}, u32[]{:S(2)}, u32[]{:S(2)}) collective-permute-start(bf16[192,1024]{1,0:T(8,128)(2,1)S(1)} %get-tuple-element.731.refs_4_.refs_2_), channel_id=1, source_target_pairs={{0,2},{1,3},{2,0},{3,1},{4,6},{5,7},{6,4},{7,5},{8,10},{9,11},{10,... | collective-permute-start | bytes 1179656 | tf_op jit(solution)/shard_map/ppermute | solution.py:983
  763.3 25.4 %collective-permute-start.118 = (bf16[592,128]{1,0:T(8,128)(2,1)S(1)}, bf16[592,128]{1,0:T(8,128)(2,1)S(1)}, u32[]{:S(2)}, u32[]{:S(2)}) collective-permute-start(bf16[592,128]{1,0:T(8,128)(2,1)S(1)} %get-tuple-element.757), channel_id=1, source_target_pairs={{0,12},{4,8},{8,4},{12,0},{16,28},{20,24},{24,20},{28,16},{1,13},{... | collective-permute-start | bytes 454664 | tf_op jit(solution)/shard_map/ppermute | solution.py:983
  765.3 23.4 %collective-permute-start.119 = (bf16[592,128]{1,0:T(8,128)(2,1)S(1)}, bf16[592,128]{1,0:T(8,128)(2,1)S(1)}, u32[]{:S(2)}, u32[]{:S(2)}) collective-permute-start(bf16[592,128]{1,0:T(8,128)(2,1)S(1)} %get-tuple-element.758), channel_id=1, source_target_pairs={{0,16},{4,20},{8,24},{12,28},{16,0},{20,4},{24,8},{28,12},{1,17},{... | collective-permute-start | bytes 454664 | tf_op jit(solution)/shard_map/ppermute | solution.py:983
  766.8 21.9 %collective-permute-start.120 = (bf16[592,128]{1,0:T(8,128)(2,1)S(1)}, bf16[592,128]{1,0:T(8,128)(2,1)S(1)}, u32[]{:S(2)}, u32[]{:S(2)}) collective-permute-start(bf16[592,128]{1,0:T(8,128)(2,1)S(1)} %get-tuple-element.759), channel_id=1, source_target_pairs={{0,20},{4,16},{8,28},{12,24},{16,4},{20,0},{24,12},{28,8},{1,21},{... | collective-permute-start | bytes 454664 | tf_op jit(solution)/shard_map/ppermute | solution.py:983
  767.7 27.3 %collective-permute-start.121 = (bf16[592,128]{1,0:T(8,128)(2,1)S(1)}, bf16[592,128]{1,0:T(8,128)(2,1)S(1)}, u32[]{:S(2)}, u32[]{:S(2)}) collective-permute-start(bf16[592,128]{1,0:T(8,128)(2,1)S(1)} %get-tuple-element.760), channel_id=1, source_target_pairs={{0,24},{4,28},{8,16},{12,20},{16,8},{20,12},{24,0},{28,4},{1,25},{... | collective-permute-start | bytes 454664 | tf_op jit(solution)/shard_map/ppermute | solution.py:983
  (247 other events, 1877.8 us)
Sparse Core Ops, SparseCore 0:
  11.9 69.7 all-gather.8
  84.5 54.5 all-gather.10
  141.8 71.9 all-gather.12
  216.3 71.6 all-gather.14
  459.9 86.0 reduce-scatter.4
  566.1 86.3 reduce-scatter.6
  656.6 67.4 reduce-scatter.10
  749.5 89.1 reduce-scatter.8

commit v9 on v8

--- a/solution.py
+++ b/solution.py
@@ -1369,7 +1369,7 @@
         hidden[0][c], pairs[0][c] = embed_step(c)
         flush()
         kept[0][c] = self_step(c, pairs[0][c])
-        if c == 0:
+        if c == min(1, clips - 1):
             text_parts = text_in_step()
     text_hidden, text_key, text_value = text_step()
     for c in every:

time: 905 us -> 894 us (0.988)
  waiting for transfers between devices: 258 us -> 236 us
  starting transfers between devices: 118 us -> 132 us
    ppermute x133, starting transfers between devices: 117 us -> 131 us  [swap(): return lax.ppermute(values, axis, [(i, i ^ mask) for i in range(size)])]
    ppermute x133, waiting for transfers between devices: 248 us -> 236 us  [swap(): return lax.ppermute(values, axis, [(i, i ^ mask) for i in range(size)])]
    all_gather x1, waiting for transfers between devices: 9.57 us -> 0.01 us  [on_device(): cross_all = lax.all_gather(cross_flat, 'dp', axis=0)]
    unnamed x274 -> x270, local copies, waits for them, and re-layouts: 50.7 us -> 50.2 us
where the time goes in v9:
time: 894 us; the launch traced here: 883 us
  Pallas kernels  392 us (44%)
  waiting for transfers between devices  236 us (26%)
  starting transfers between devices  132 us (15%)
  local copies, waits for them, and re-layouts  62.5 us (7%)
  other arithmetic  35.2 us (4%)
  between operations  24.5 us (3%)
    pallas_call x44, Pallas kernels, kernel(): pl.pallas_call(run_body, out_shape=tuple(out_shapes), in_specs=specs + [a...  315 us
    ppermute x133, waiting for transfers between devices, swap(): return lax.ppermute(values, axis, [(i, i ^ mask) for i in range(size)])  236 us
    ppermute x133, starting transfers between devices, swap(): return lax.ppermute(values, axis, [(i, i ^ mask) for i in range(size)])  131 us
    unnamed x270, local copies, waits for them, and re-layouts  50.2 us
    pallas_call x52, Pallas kernels, norm_rows_kernel(): pl.pallas_call(later(body, len(after), len(operands)), out_shape=tuple((p...  43.1 us
    pallas_call x1, Pallas kernels, embed_back(): pl.pallas_call(later(partial(embed_back_body, groups), len(after), 2 + gr...  18.1 us
  transfers between devices with their start and end apart: 141, of which 55 were waited for; matrix products, arithmetic and copies ran while one was open for 3% of the time, Pallas kernels for 42%

profile of v9, /device:TPU:0, one launch (start us, length us, event | category | flops | bytes accessed | tf_op | source)
XLA Modules:
  0.0 882.8 jit_solution(108717528095090075)
XLA Ops:
  77.2 12.7 %collective-permute-start.16 = (bf16[576,128]{1,0:T(8,128)(2,1)S(1)}, bf16[576,128]{1,0:T(8,128)(2,1)S(1)}, u32[]{:S(2)}, u32[]{:S(2)}) collective-permute-start(bf16[576,128]{1,0:T(8,128)(2,1)S(1)} %get-tuple-element.398.refs_7_), channel_id=1, source_target_pairs={{0,12},{4,8},{8,4},{12,0},{16,28},{20,24},{24,20},{28,16},{1,13},{... | collective-permute-start | bytes 442376 | tf_op jit(solution)/shard_map/ppermute | solution.py:983
  119.4 8.2 self_forward.3
  131.8 8.6 self_forward.4
  150.6 9.9 %collective-permute-done.28.refs_3_ = bf16[768,256]{1,0:T(8,128)(2,1)} collective-permute-done((bf16[768,256]{1,0:T(8,128)(2,1)}, bf16[768,256]{1,0:T(8,128)(2,1)}, u32[]{:S(2)}, u32[]{:S(2)}) %collective-permute-start.28) | collective-permute-done | bytes 393248 | tf_op jit(solution)/shard_map/ppermute | solution.py:983
  165.1 9.1 %self_forward.5 = (bf16[768,256]{1,0:T(8,128)(2,1)}, bf16[768,256]{1,0:T(8,128)(2,1)}, bf16[768,256]{1,0:T(8,128)(2,1)}, bf16[768,256]{1,0:T(8,128)(2,1)}, f32[8...) custom-call(s32[1]{0:T(128)} %bitcast.refs_0_, ...), custom_call_target="tpu_custom_call" | custom-call | flops 1024 | bytes 1024 | tf_op jit(solution)/shard_map/self_forward/pallas_call | solution.py:263
  253.4 9.4 %ffn_forward.3 = (bf16[768,1024]{1,0:T(8,128)(2,1)}, bf16[768,1024]{1,0:T(8,128)(2,1)}, bf16[384,1024]{1,0:T(8,128)(2,1)S(1)}, bf16[384,1024]{1,0:T(8,128)(2,1)S...) custom-call(s32[1]{0:T(128)} %bitcast.refs_0_, ...), custom_call_target="tpu_custom_call" | custom-call | flops 1024 | bytes 1024 | tf_op jit(solution)/shard_map/ffn_forward/pallas_call | solution.py:263
  273.5 8.2 ffn_forward.4
  296.3 8.2 ffn_forward.5
  319.5 10.9 %head_forward.3 = (f32[768,2048]{1,0:T(8,128)}, f32[8,768]{1,0:T(8,128)S(1)}, bf16[384,1024]{1,0:T(8,128)(2,1)}, bf16[384,1024]{1,0:T(8,128)(2,1)}, f32[384,1024...) custom-call(s32[1]{0:T(128)} %bitcast.refs_0_, bf16[384,1024]{1,0:T(8,128)(2,1)S(1)} %get-tuple-element.494.refs_2_.refs_1_, ...), custom_call_target="tpu_custom_call" | custom-call | flops 1024 | bytes 1024 | tf_op jit(solution)/shard_map/head_forward/pallas_call | solution.py:263
  339.5 9.6 %head_forward.4 = (f32[768,2048]{1,0:T(8,128)}, f32[8,768]{1,0:T(8,128)S(1)}, bf16[384,1024]{1,0:T(8,128)(2,1)}, bf16[384,1024]{1,0:T(8,128)(2,1)}, f32[384,1024...) custom-call(s32[1]{0:T(128)} %bitcast.refs_0_, bf16[384,1024]{1,0:T(8,128)(2,1)S(1)} %get-tuple-element.505.refs_1_.refs_10_, ...), custom_call_target="tpu_custom_call" | custom-call | flops 1024 | bytes 1024 | tf_op jit(solution)/shard_map/head_forward/pallas_call | solution.py:263
  353.1 8.6 head_backward.3
  366.2 9.6 %head_forward.5 = (f32[768,2048]{1,0:T(8,128)}, f32[8,768]{1,0:T(8,128)S(1)}, bf16[384,1024]{1,0:T(8,128)(2,1)}, bf16[384,1024]{1,0:T(8,128)(2,1)}, f32[384,1024]{1,0:T(8,128)}, /*index=5*/f32[8,128]{1,0:T(8,128)S(1)}) custom-call(s32[1]{0:T(128)} %bitcast.refs_0_, bf16[384,1024]{1,0:T(8,128)(2,1)S(1)} %get-tuple-element.514.refs_2_.refs_1_, ...), custom_call_target="tpu_custom_call" | custom-call | flops 1024 | bytes 1024 | tf_op jit(solution)/shard_map/head_forward/pallas_call | solution.py:263
  379.8 8.5 head_backward.4
  392.0 8.4 collective-permute-done.70.refs_1_
  401.9 9.1 %head_backward.5 = (bf16[768,2048]{1,0:T(8,128)(2,1)}, bf16[384,1024]{1,0:T(8,128)(2,1)S(1)}, bf16[384,1024]{1,0:T(8,128)(2,1)S(1)}, f32[8,128]{1,0:T(8,128)S(1)}, f32[8,128]{1,0:T(8,128)S(1)}) custom-call(s32[1]{0:T(128)} %bitcast.refs_0_, f32[8,768]{1,0:T(8,128)S(1)} %merge.11.refs_2_.refs_1_, f32[768,4]{1,0:T(8,128)S(1)} %copy-done.6, ...), custom_call_target="tpu_custom_call" | custom-call | flops 1024 | bytes 1024 | tf_op jit(solution)/shard_map/head_backward/pallas_call | solution.py:263
  425.0 10.2 %head_weights.2 = (bf16[8,4,128,512]{3,2,1,0:T(8,128)(2,1)}, f32[8,128]{1,0:T(8,128)S(1)}) custom-call(s32[1]{0:T(128)} %bitcast.refs_0_, bf16[384,1024]{1,0:T(8,128)(2,1)} %get-tuple-element.538.refs_1_, bf16[384,1024]{1,0:T(8,128)(2,1)} %get-tuple-element.539.refs_2_, bf16[384,1024]{1,0:T(8,128)(2,1)} %get-tuple-element.540.refs_3_, ...), custom_call_target="tpu_custom_call" | custom-call | flops 1024 | bytes 1024 | tf_op jit(solution)/shard_map/head_weights/pallas_call | solution.py:263
  435.2 10.5 %head_weights.3 = (bf16[8,4,128,512]{3,2,1,0:T(8,128)(2,1)}, f32[8,128]{1,0:T(8,128)S(1)}) custom-call(s32[1]{0:T(128)} %bitcast.refs_0_, bf16[384,1024]{1,0:T(8,128)(2,1)} %get-tuple-element.538.refs_1_, bf16[384,1024]{1,0:T(8,128)(2,1)} %get-tuple-element.539.refs_2_, ...), custom_call_target="tpu_custom_call", output_to_operand_aliasing={{0}: (10, {})} | custom-call | flops 1024 | bytes 1024 | tf_op jit(solution)/shard_map/head_weights/pallas_call | solution.py:263
  502.9 8.2 ffn_two.2
  511.1 8.2 ffn_two.3
  535.2 8.2 ffn_one.2
  543.5 8.2 ffn_one.3
  559.3 9.3 %cross_backward.5 = (bf16[768,256]{1,0:T(8,128)(2,1)}, bf16[256,256]{1,0:T(8,128)(2,1)}, bf16[256,256]{1,0:T(8,128)(2,1)}, bf16[384,1024]{1,0:T(8,128)(2,1)S(1)}...) custom-call(s32[1]{0:T(128)} %bitcast.refs_0_, ...), custom_call_target="tpu_custom_call" | custom-call | flops 1024 | bytes 1024 | tf_op jit(solution)/shard_map/cross_backward/pallas_call | solution.py:263
  586.0 11.2 %self_backward.3 = (bf16[768,768]{1,0:T(8,128)(2,1)}, bf16[384,1024]{1,0:T(8,128)(2,1)S(1)}, bf16[384,1024]{1,0:T(8,128)(2,1)S(1)}, bf16[384,1024]{1,0:T(8,128)(...) custom-call(s32[1]{0:T(128)} %bitcast.refs_0_, ...), custom_call_target="tpu_custom_call" | custom-call | flops 1024 | bytes 1024 | tf_op jit(solution)/shard_map/self_backward/pallas_call | solution.py:263
  606.3 9.3 %collective-permute-done.102.refs_12_.refs_3_ = bf16[192,1024]{1,0:T(8,128)(2,1)S(1)} collective-permute-done((bf16[192,1024]{1,0:T(8,128)(2,1)S(1)}, bf16[192,1024]{1,0:T(8,128)(2,1)S(1)}, u32[]{:S(2)}, u32[]{:S(2)}) %collective-permute-start.102) | collective-permute-done | bytes 393248 | tf_op jit(solution)/shard_map/ppermute | solution.py:983
  636.0 10.9 %self_backward.4 = (bf16[768,768]{1,0:T(8,128)(2,1)}, bf16[384,1024]{1,0:T(8,128)(2,1)S(1)}, bf16[384,1024]{1,0:T(8,128)(2,1)S(1)}, bf16[384,1024]{1,0:T(8,128)(...) custom-call(s32[1]{0:T(128)} %bitcast.refs_0_, ...), custom_call_target="tpu_custom_call" | custom-call | flops 1024 | bytes 1024 | tf_op jit(solution)/shard_map/self_backward/pallas_call | solution.py:263
  657.3 11.1 %self_backward.5 = (bf16[768,768]{1,0:T(8,128)(2,1)}, bf16[384,1024]{1,0:T(8,128)(2,1)S(1)}, bf16[384,1024]{1,0:T(8,128)(2,1)S(1)}, bf16[384,1024]{1,0:T(8,128)(...) custom-call(s32[1]{0:T(128)} %bitcast.refs_0_, ...), custom_call_target="tpu_custom_call" | custom-call | flops 1024 | bytes 1024 | tf_op jit(solution)/shard_map/self_backward/pallas_call | solution.py:263
  692.4 15.7 %collective-permute-done.112.refs_6_.refs_3_ = bf16[192,1024]{1,0:T(8,128)(2,1)S(1)} collective-permute-done((bf16[192,1024]{1,0:T(8,128)(2,1)S(1)}, bf16[192,1024]{1,0:T(8,128)(2,1)S(1)}, u32[]{:S(2)}, u32[]{:S(2)}) %collective-permute-start.112) | collective-permute-done | bytes 393248 | tf_op jit(solution)/shard_map/ppermute | solution.py:983
  712.8 8.5 self_in.2
  758.7 9.8 %collective-permute-done.117.refs_4_.refs_2_ = bf16[592,128]{1,0:T(8,128)(2,1)S(1)} collective-permute-done((bf16[592,128]{1,0:T(8,128)(2,1)S(1)}, bf16[592,128]{1,0:T(8,128)(2,1)S(1)}, u32[]{:S(2)}, u32[]{:S(2)}) %collective-permute-start.117) | collective-permute-done | bytes 151584 | tf_op jit(solution)/shard_map/ppermute | solution.py:983
  784.6 18.1 %embed_back.1 = bf16[4,4,128,512]{3,2,1,0:T(8,128)(2,1)S(1)} custom-call(s32[4]{0:T(128)S(1)} %copy-done.98, s32[8,4608]{1,0:T(8,128)S(1)} %concatenate.29.refs_23_.refs_1_, bf16[592,128]{1,0:T(8,128)(2,1)S(1)} %get-tuple-element.754.refs_2_.refs_0_, bf16[592,128]{1,0:T(8,128)(2,1)S(1)} %collective-permute-done.116.refs_3_.refs_1_, ...), custom_call_target="tpu_custom_call" | custom-call | flops 1024 | bytes 1024 | tf_op jit(solution)/shard_map/embed_back/pallas_call | solution.py:859
  815.0 9.1 %collective-permute-done.127 = f32[16,128]{1,0:T(8,128)S(1)} collective-permute-done((f32[16,128]{1,0:T(8,128)S(1)}, f32[16,128]{1,0:T(8,128)S(1)}, u32[]{:S(2)}, u32[]{:S(2)}) %collective-permute-start.127) | collective-permute-done | bytes 8224 | tf_op jit(solution)/shard_map/ppermute | solution.py:983
  842.3 9.9 %collective-permute-start.131 = (f32[1,2]{1,0:T(1,128)S(1)}, f32[1,2]{1,0:T(1,128)S(1)}, u32[]{:S(2)}, u32[]{:S(2)}) collective-permute-start(f32[1,2]{1,0:T(1,128)S(1)} %add.184), channel_id=1, source_target_pairs={{0,8},{4,12},{8,0},{12,4},{16,24},{20,28},{24,16},{28,20},{1,9},{5... | collective-permute-start | bytes 32 | tf_op jit(solution)/shard_map/ppermute | solution.py:983
  (702 shorter events, 542.7 us)
Async XLA Ops:
  7.2 99.9 %all-gather.9.cloned.1.call-start = ((), (), s32[]{:S(2)}) async-start(), calls=%async_computation.8 | async-start | bytes 2433024 | tf_op jit(solution)/shard_map/all_gather | solution.py:1095
  11.8 129.7 %all-gather.11.cloned.1.call-start = ((), (), s32[]{:S(2)}) async-start(), calls=%async_computation.9 | async-start | bytes 2801664 | tf_op jit(solution)/shard_map/all_gather | solution.py:1096
  13.5 238.5 %all-gather.13.cloned.1.call-start = ((), (), s32[]{:S(2)}) async-start(), calls=%async_computation.10 | async-start | bytes 4718592 | tf_op jit(solution)/shard_map/all_gather | solution.py:1097
  14.5 303.6 %all-gather.15.cloned.1.call-start = ((), (), s32[]{:S(2)}) async-start(), calls=%async_computation.11 | async-start | bytes 4718592 | tf_op jit(solution)/shard_map/all_gather | solution.py:1098
  16.8 22.2 %collective-permute-start = (s32[8,640]{1,0:T(8,128)S(1)}, s32[8,640]{1,0:T(8,128)S(1)}, u32[]{:S(2)}, u32[]{:S(2)}) collective-permute-start(s32[8,640]{1,0:T(8,128)S(1)} %pad_select_fusion.refs_1_.refs_0_), channel_id=1, source_target_pairs={{0,24},{4,28},{8,16},{12,20},{16,8},{20,12},{24,0},{28,4},{1,25},{... | collective-permute-start | bytes 61448 | tf_op jit(solution)/shard_map/ppermute | solution.py:983
  24.1 27.3 %collective-permute-start.2 = (bf16[4,128,512]{2,1,0:T(8,128)(2,1)S(1)}, bf16[4,128,512]{2,1,0:T(8,128)(2,1)S(1)}, u32[]{:S(2)}, u32[]{:S(2)}) collective-permute-start(bf16[4,128,512]{2,1,0:T(8,128)(2,1)S(1)} %get-tuple-element.795.refs_3_), channel_id=1, source_target_pairs={{0,1},{1,0},{2,3},{3,2},{4,5},{5,4},{6,7},{7,6},{8,9},{9,8},{10,11... | collective-permute-start | bytes 1572872 | tf_op jit(solution)/shard_map/ppermute | solution.py:983
  64.9 25.1 %collective-permute-start.12 = (bf16[576,128]{1,0:T(8,128)(2,1)S(1)}, bf16[576,128]{1,0:T(8,128)(2,1)S(1)}, u32[]{:S(2)}, u32[]{:S(2)}) collective-permute-start(bf16[576,128]{1,0:T(8,128)(2,1)S(1)} %get-tuple-element.399), channel_id=1, source_target_pairs={{0,16},{4,20},{8,24},{12,28},{16,0},{20,4},{24,8},{28,12},{1,17},{... | collective-permute-start | bytes 442376 | tf_op jit(solution)/shard_map/ppermute | solution.py:983
  64.9 25.3 %collective-permute-start.13 = (bf16[576,128]{1,0:T(8,128)(2,1)S(1)}, bf16[576,128]{1,0:T(8,128)(2,1)S(1)}, u32[]{:S(2)}, u32[]{:S(2)}) collective-permute-start(bf16[576,128]{1,0:T(8,128)(2,1)S(1)} %get-tuple-element.397.refs_7_), channel_id=1, source_target_pairs={{0,20},{4,16},{8,28},{12,24},{16,4},{20,0},{24,12},{28,8},{1,21},{... | collective-permute-start | bytes 442376 | tf_op jit(solution)/shard_map/ppermute | solution.py:983
  77.2 25.0 %collective-permute-start.16 = (bf16[576,128]{1,0:T(8,128)(2,1)S(1)}, bf16[576,128]{1,0:T(8,128)(2,1)S(1)}, u32[]{:S(2)}, u32[]{:S(2)}) collective-permute-start(bf16[576,128]{1,0:T(8,128)(2,1)S(1)} %get-tuple-element.398.refs_7_), channel_id=1, source_target_pairs={{0,12},{4,8},{8,4},{12,0},{16,28},{20,24},{24,20},{28,16},{1,13},{... | collective-permute-start | bytes 442376 | tf_op jit(solution)/shard_map/ppermute | solution.py:983
  141.3 20.5 %collective-permute-start.24 = (bf16[384,1024]{1,0:T(8,128)(2,1)}, bf16[384,1024]{1,0:T(8,128)(2,1)}, u32[]{:S(2)}, u32[]{:S(2)}) collective-permute-start(bf16[384,1024]{1,0:T(8,128)(2,1)} %get-tuple-element.427), channel_id=1, source_target_pairs={{0,1},{1,0},{2,3},{3,2},{4,5},{5,4},{6,7},{7,6},{8,9},{9,8},{10,11... | collective-permute-start | bytes 2359304 | tf_op jit(solution)/shard_map/ppermute | solution.py:983
  149.5 24.7 %collective-permute-start.27 = (bf16[768,256]{1,0:T(8,128)(2,1)}, bf16[768,256]{1,0:T(8,128)(2,1)}, u32[]{:S(2)}, u32[]{:S(2)}) collective-permute-start(bf16[768,256]{1,0:T(8,128)(2,1)} %get-tuple-element.434.refs_1_), channel_id=1, source_target_pairs={{0,1},{1,0},{2,3},{3,2},{4,5},{5,4},{6,7},{7,6},{8,9},{9,8},{10,11... | collective-permute-start | bytes 1179656 | tf_op jit(solution)/shard_map/ppermute | solution.py:983
  149.6 427.3 %reduce-scatter.5.cloned.1.call-start = ((), (), s32[]{:S(2)}) async-start(), calls=%async_computation.4 | async-start | bytes 4718592 | tf_op jit(solution)/shard_map/reduce_scatter | solution.py:1533
  149.8 29.9 %collective-permute-start.26 = (bf16[192,1024]{1,0:T(8,128)(2,1)}, bf16[192,1024]{1,0:T(8,128)(2,1)S(1)}, u32[]{:S(2)}, u32[]{:S(2)}) collective-permute-start(bf16[192,1024]{1,0:T(8,128)(2,1)} %copy-done.15), channel_id=1, source_target_pairs={{0,2},{1,3},{2,0},{3,1},{4,6},{5,7},{6,4},{7,5},{8,10},{9,11},{10,... | collective-permute-start | bytes 1179656 | tf_op jit(solution)/shard_map/ppermute | solution.py:983
  160.5 19.1 %collective-permute-start.25 = (bf16[192,1024]{1,0:T(8,128)(2,1)}, bf16[192,1024]{1,0:T(8,128)(2,1)S(1)}, u32[]{:S(2)}, u32[]{:S(2)}) collective-permute-start(bf16[192,1024]{1,0:T(8,128)(2,1)} %copy-done.79), channel_id=1, source_target_pairs={{0,2},{1,3},{2,0},{3,1},{4,6},{5,7},{6,4},{7,5},{8,10},{9,11},{10,... | collective-permute-start | bytes 1179656 | tf_op jit(solution)/shard_map/ppermute | solution.py:983
  164.3 20.6 %collective-permute-start.30 = (bf16[192,1024]{1,0:T(8,128)(2,1)S(1)}, bf16[192,1024]{1,0:T(8,128)(2,1)S(1)}, u32[]{:S(2)}, u32[]{:S(2)}) collective-permute-start(bf16[192,1024]{1,0:T(8,128)(2,1)S(1)} %get-tuple-element.437.refs_1_), channel_id=1, source_target_pairs={{0,2},{1,3},{2,0},{3,1},{4,6},{5,7},{6,4},{7,5},{8,10},{9,11},{10,... | collective-permute-start | bytes 1179656 | tf_op jit(solution)/shard_map/ppermute | solution.py:983
  337.7 24.1 %collective-permute-start.63 = (bf16[192,1024]{1,0:T(8,128)(2,1)S(1)}, bf16[192,1024]{1,0:T(8,128)(2,1)S(1)}, u32[]{:S(2)}, u32[]{:S(2)}) collective-permute-start(bf16[192,1024]{1,0:T(8,128)(2,1)S(1)} %get-tuple-element.499.refs_10_.refs_2_), channel_id=1, source_target_pairs={{0,2},{1,3},{2,0},{3,1},{4,6},{5,7},{6,4},{7,5},{8,10},{9,11},{10,... | collective-permute-start | bytes 1179656 | tf_op jit(solution)/shard_map/ppermute | solution.py:983
  414.2 21.0 %collective-permute-start.76 = (bf16[192,1024]{1,0:T(8,128)(2,1)S(1)}, bf16[192,1024]{1,0:T(8,128)(2,1)S(1)}, u32[]{:S(2)}, u32[]{:S(2)}) collective-permute-start(bf16[192,1024]{1,0:T(8,128)(2,1)S(1)} %get-tuple-element.550.refs_1_), channel_id=1, source_target_pairs={{0,2},{1,3},{2,0},{3,1},{4,6},{5,7},{6,4},{7,5},{8,10},{9,11},{10,... | collective-permute-start | bytes 1179656 | tf_op jit(solution)/shard_map/ppermute | solution.py:983
  445.8 262.3 %reduce-scatter.7.cloned.1.call-start = ((), (), s32[]{:S(2)}) async-start(), calls=%async_computation.5 | async-start | bytes 4718592 | tf_op jit(solution)/shard_map/reduce_scatter | solution.py:1567
  501.0 20.8 %collective-permute-start.90 = (bf16[384,1024]{1,0:T(8,128)(2,1)S(1)}, bf16[384,1024]{1,0:T(8,128)(2,1)S(1)}, u32[]{:S(2)}, u32[]{:S(2)}) collective-permute-start(bf16[384,1024]{1,0:T(8,128)(2,1)S(1)} %get-tuple-element.606), channel_id=1, source_target_pairs={{0,1},{1,0},{2,3},{3,2},{4,5},{5,4},{6,7},{7,6},{8,9},{9,8},{10,11... | collective-permute-start | bytes 2359304 | tf_op jit(solution)/shard_map/ppermute | solution.py:983
  522.0 21.5 %collective-permute-start.92 = (bf16[192,1024]{1,0:T(8,128)(2,1)S(1)}, bf16[192,1024]{1,0:T(8,128)(2,1)S(1)}, u32[]{:S(2)}, u32[]{:S(2)}) collective-permute-start(bf16[192,1024]{1,0:T(8,128)(2,1)S(1)} %get-tuple-element.624.refs_1_), channel_id=1, source_target_pairs={{0,2},{1,3},{2,0},{3,1},{4,6},{5,7},{6,4},{7,5},{8,10},{9,11},{10,... | collective-permute-start | bytes 1179656 | tf_op jit(solution)/shard_map/ppermute | solution.py:983
  551.7 192.0 %reduce-scatter.11.cloned.1.call-start = ((), (), s32[]{:S(2)}) async-start(), calls=%async_computation.7 | async-start | bytes 2359296 | tf_op jit(solution)/shard_map/reduce_scatter | solution.py:1628
  627.5 200.9 %reduce-scatter.9.cloned.1.call-start = ((), (), s32[]{:S(2)}) async-start(), calls=%async_computation.6 | async-start | bytes 2801664 | tf_op jit(solution)/shard_map/reduce_scatter | solution.py:1666
  672.1 19.5 %collective-permute-start.109 = (bf16[768,256]{1,0:T(8,128)(2,1)S(1)}, bf16[768,256]{1,0:T(8,128)(2,1)S(1)}, u32[]{:S(2)}, u32[]{:S(2)}) collective-permute-start(bf16[768,256]{1,0:T(8,128)(2,1)S(1)} %add.294.refs_11_), channel_id=1, source_target_pairs={{0,2},{1,3},{2,0},{3,1},{4,6},{5,7},{6,4},{7,5},{8,10},{9,11},{10,... | collective-permute-start | bytes 1179656 | tf_op jit(solution)/shard_map/ppermute | solution.py:983
  672.9 39.9 %collective-permute-start.113 = (bf16[192,1024]{1,0:T(8,128)(2,1)}, bf16[192,1024]{1,0:T(8,128)(2,1)}, u32[]{:S(2)}, u32[]{:S(2)}) collective-permute-start(bf16[192,1024]{1,0:T(8,128)(2,1)} %get-tuple-element.715.refs_14_.refs_2_), channel_id=1, source_target_pairs={{0,2},{1,3},{2,0},{3,1},{4,6},{5,7},{6,4},{7,5},{8,10},{9,11},{10,... | collective-permute-start | bytes 1179656 | tf_op jit(solution)/shard_map/ppermute | solution.py:983
  674.2 33.9 %collective-permute-start.112 = (bf16[192,1024]{1,0:T(8,128)(2,1)S(1)}, bf16[192,1024]{1,0:T(8,128)(2,1)S(1)}, u32[]{:S(2)}, u32[]{:S(2)}) collective-permute-start(bf16[192,1024]{1,0:T(8,128)(2,1)S(1)} %get-tuple-element.733.refs_1_), channel_id=1, source_target_pairs={{0,2},{1,3},{2,0},{3,1},{4,6},{5,7},{6,4},{7,5},{8,10},{9,11},{10,... | collective-permute-start | bytes 1179656 | tf_op jit(solution)/shard_map/ppermute | solution.py:983
  689.7 31.7 %collective-permute-start.114 = (bf16[192,1024]{1,0:T(8,128)(2,1)}, bf16[192,1024]{1,0:T(8,128)(2,1)S(1)}, u32[]{:S(2)}, u32[]{:S(2)}) collective-permute-start(bf16[192,1024]{1,0:T(8,128)(2,1)} %get-tuple-element.742.refs_1_), channel_id=1, source_target_pairs={{0,2},{1,3},{2,0},{3,1},{4,6},{5,7},{6,4},{7,5},{8,10},{9,11},{10,... | collective-permute-start | bytes 1179656 | tf_op jit(solution)/shard_map/ppermute | solution.py:983
  690.9 36.9 %collective-permute-start.115 = (bf16[192,1024]{1,0:T(8,128)(2,1)S(1)}, bf16[192,1024]{1,0:T(8,128)(2,1)S(1)}, u32[]{:S(2)}, u32[]{:S(2)}) collective-permute-start(bf16[192,1024]{1,0:T(8,128)(2,1)S(1)} %get-tuple-element.731.refs_4_.refs_2_), channel_id=1, source_target_pairs={{0,2},{1,3},{2,0},{3,1},{4,6},{5,7},{6,4},{7,5},{8,10},{9,11},{10,... | collective-permute-start | bytes 1179656 | tf_op jit(solution)/shard_map/ppermute | solution.py:983
  748.4 20.2 %collective-permute-start.117 = (bf16[592,128]{1,0:T(8,128)(2,1)S(1)}, bf16[592,128]{1,0:T(8,128)(2,1)S(1)}, u32[]{:S(2)}, u32[]{:S(2)}) collective-permute-start(bf16[592,128]{1,0:T(8,128)(2,1)S(1)} %get-tuple-element.756), channel_id=1, source_target_pairs={{0,8},{4,12},{8,0},{12,4},{16,24},{20,28},{24,16},{28,20},{1,9},{5... | collective-permute-start | bytes 454664 | tf_op jit(solution)/shard_map/ppermute | solution.py:983
  750.4 24.1 %collective-permute-start.118 = (bf16[592,128]{1,0:T(8,128)(2,1)S(1)}, bf16[592,128]{1,0:T(8,128)(2,1)S(1)}, u32[]{:S(2)}, u32[]{:S(2)}) collective-permute-start(bf16[592,128]{1,0:T(8,128)(2,1)S(1)} %get-tuple-element.757), channel_id=1, source_target_pairs={{0,12},{4,8},{8,4},{12,0},{16,28},{20,24},{24,20},{28,16},{1,13},{... | collective-permute-start | bytes 454664 | tf_op jit(solution)/shard_map/ppermute | solution.py:983
  750.8 23.7 %collective-permute-start.119 = (bf16[592,128]{1,0:T(8,128)(2,1)S(1)}, bf16[592,128]{1,0:T(8,128)(2,1)S(1)}, u32[]{:S(2)}, u32[]{:S(2)}) collective-permute-start(bf16[592,128]{1,0:T(8,128)(2,1)S(1)} %get-tuple-element.758), channel_id=1, source_target_pairs={{0,16},{4,20},{8,24},{12,28},{16,0},{20,4},{24,8},{28,12},{1,17},{... | collective-permute-start | bytes 454664 | tf_op jit(solution)/shard_map/ppermute | solution.py:983
  753.5 23.5 %collective-permute-start.120 = (bf16[592,128]{1,0:T(8,128)(2,1)S(1)}, bf16[592,128]{1,0:T(8,128)(2,1)S(1)}, u32[]{:S(2)}, u32[]{:S(2)}) collective-permute-start(bf16[592,128]{1,0:T(8,128)(2,1)S(1)} %get-tuple-element.759), channel_id=1, source_target_pairs={{0,20},{4,16},{8,28},{12,24},{16,4},{20,0},{24,12},{28,8},{1,21},{... | collective-permute-start | bytes 454664 | tf_op jit(solution)/shard_map/ppermute | solution.py:983
  754.4 27.4 %collective-permute-start.121 = (bf16[592,128]{1,0:T(8,128)(2,1)S(1)}, bf16[592,128]{1,0:T(8,128)(2,1)S(1)}, u32[]{:S(2)}, u32[]{:S(2)}) collective-permute-start(bf16[592,128]{1,0:T(8,128)(2,1)S(1)} %get-tuple-element.760), channel_id=1, source_target_pairs={{0,24},{4,28},{8,16},{12,20},{16,8},{20,12},{24,0},{28,4},{1,25},{... | collective-permute-start | bytes 454664 | tf_op jit(solution)/shard_map/ppermute | solution.py:983
  (245 other events, 1854.5 us)
Sparse Core Ops, SparseCore 0:
  11.9 69.7 all-gather.8
  84.5 54.5 all-gather.10
  141.8 71.9 all-gather.12
  216.3 71.6 all-gather.14
  445.9 89.5 reduce-scatter.4
  551.9 89.5 reduce-scatter.6
  645.5 67.4 reduce-scatter.10
  734.7 93.3 reduce-scatter.8

commit v10 on v9

--- a/solution.py
+++ b/solution.py
@@ -1487,13 +1487,13 @@
         flush()
         ready[c] = head_step(c, pairs[3][c])
         if c:
-            pieces = list(soon)
+            pieces = soon + (newest if c == clips - 1 else [])
             flush()
             logits, stats = ready[c - 1]
             logit_grads[c - 1] = head_back_step(c - 1, logits, merge_step(stats), pieces)
     logits, stats = ready[-1]
     stats = merge_step(stats)
-    pieces = list(newest)
+    pieces = []
     flush()
     logit_grads[-1] = head_back_step(clips - 1, logits, stats, pieces)
 

time: 894 us -> 895 us (level)
    unnamed x270 -> x268, local copies, waits for them, and re-layouts: 50.2 us -> 49.8 us
  transfers between devices with their start and end apart: 141 -> 141, of which waited for: 55 -> 52; matrix products, arithmetic and copies ran while one was open for 3% -> 3% of each run, Pallas kernels for 42% -> 42%
where the time goes in v10:
time: 895 us; the launch traced here: 883 us
  Pallas kernels  393 us (44%)
  waiting for transfers between devices  241 us (27%)
  starting transfers between devices  127 us (14%)
  local copies, waits for them, and re-layouts  62.1 us (7%)
  other arithmetic  36 us (4%)
  between operations  24.5 us (3%)
    pallas_call x44, Pallas kernels, kernel(): pl.pallas_call(run_body, out_shape=tuple(out_shapes), in_specs=specs + [a...  315 us
    ppermute x133, waiting for transfers between devices, swap(): return lax.ppermute(values, axis, [(i, i ^ mask) for i in range(size)])  241 us
    ppermute x133, starting transfers between devices, swap(): return lax.ppermute(values, axis, [(i, i ^ mask) for i in range(size)])  126 us
    unnamed x268, local copies, waits for them, and re-layouts  49.8 us
    pallas_call x52, Pallas kernels, norm_rows_kernel(): pl.pallas_call(later(body, len(after), len(operands)), out_shape=tuple((p...  43.1 us
    pallas_call x1, Pallas kernels, embed_back(): pl.pallas_call(later(partial(embed_back_body, groups), len(after), 2 + gr...  18.1 us
  transfers between devices with their start and end apart: 141, of which 52 were waited for; matrix products, arithmetic and copies ran while one was open for 3% of the time, Pallas kernels for 42%

profile of v10, /device:TPU:0, one launch (start us, length us, event | category | flops | bytes accessed | tf_op | source)
XLA Modules:
  0.0 883.4 jit_solution(13965297729319821059)
XLA Ops:
  77.6 11.6 %collective-permute-start.16 = (bf16[576,128]{1,0:T(8,128)(2,1)S(1)}, bf16[576,128]{1,0:T(8,128)(2,1)S(1)}, u32[]{:S(2)}, u32[]{:S(2)}) collective-permute-start(bf16[576,128]{1,0:T(8,128)(2,1)S(1)} %get-tuple-element.398.refs_7_), channel_id=1, source_target_pairs={{0,12},{4,8},{8,4},{12,0},{16,28},{20,24},{24,20},{28,16},{1,13},{... | collective-permute-start | bytes 442376 | tf_op jit(solution)/shard_map/ppermute | solution.py:983
  120.3 8.2 self_forward.3
  132.7 8.6 self_forward.4
  151.5 9.9 %collective-permute-done.28.refs_3_ = bf16[768,256]{1,0:T(8,128)(2,1)} collective-permute-done((bf16[768,256]{1,0:T(8,128)(2,1)}, bf16[768,256]{1,0:T(8,128)(2,1)}, u32[]{:S(2)}, u32[]{:S(2)}) %collective-permute-start.28) | collective-permute-done | bytes 393248 | tf_op jit(solution)/shard_map/ppermute | solution.py:983
  166.0 9.1 %self_forward.5 = (bf16[768,256]{1,0:T(8,128)(2,1)}, bf16[768,256]{1,0:T(8,128)(2,1)}, bf16[768,256]{1,0:T(8,128)(2,1)}, bf16[768,256]{1,0:T(8,128)(2,1)}, f32[8...) custom-call(s32[1]{0:T(128)} %bitcast.refs_0_, ...), custom_call_target="tpu_custom_call" | custom-call | flops 1024 | bytes 1024 | tf_op jit(solution)/shard_map/self_forward/pallas_call | solution.py:263
  254.3 9.3 %ffn_forward.3 = (bf16[768,1024]{1,0:T(8,128)(2,1)}, bf16[768,1024]{1,0:T(8,128)(2,1)}, bf16[384,1024]{1,0:T(8,128)(2,1)S(1)}, bf16[384,1024]{1,0:T(8,128)(2,1)S...) custom-call(s32[1]{0:T(128)} %bitcast.refs_0_, ...), custom_call_target="tpu_custom_call" | custom-call | flops 1024 | bytes 1024 | tf_op jit(solution)/shard_map/ffn_forward/pallas_call | solution.py:263
  274.4 8.2 ffn_forward.4
  297.2 8.2 ffn_forward.5
  320.4 10.9 %head_forward.3 = (f32[768,2048]{1,0:T(8,128)}, f32[8,768]{1,0:T(8,128)S(1)}, bf16[384,1024]{1,0:T(8,128)(2,1)}, bf16[384,1024]{1,0:T(8,128)(2,1)}, f32[384,1024...) custom-call(s32[1]{0:T(128)} %bitcast.refs_0_, bf16[384,1024]{1,0:T(8,128)(2,1)S(1)} %get-tuple-element.494.refs_2_.refs_1_, ...), custom_call_target="tpu_custom_call" | custom-call | flops 1024 | bytes 1024 | tf_op jit(solution)/shard_map/head_forward/pallas_call | solution.py:263
  340.4 9.6 %head_forward.4 = (f32[768,2048]{1,0:T(8,128)}, f32[8,768]{1,0:T(8,128)S(1)}, bf16[384,1024]{1,0:T(8,128)(2,1)}, bf16[384,1024]{1,0:T(8,128)(2,1)}, f32[384,1024...) custom-call(s32[1]{0:T(128)} %bitcast.refs_0_, bf16[384,1024]{1,0:T(8,128)(2,1)S(1)} %get-tuple-element.505.refs_1_.refs_10_, ...), custom_call_target="tpu_custom_call" | custom-call | flops 1024 | bytes 1024 | tf_op jit(solution)/shard_map/head_forward/pallas_call | solution.py:263
  354.0 8.6 head_backward.3
  367.4 9.6 %head_forward.5 = (f32[768,2048]{1,0:T(8,128)}, f32[8,768]{1,0:T(8,128)S(1)}, bf16[384,1024]{1,0:T(8,128)(2,1)}, bf16[384,1024]{1,0:T(8,128)(2,1)}, f32[384,1024]{1,0:T(8,128)}, /*index=5*/f32[8,128]{1,0:T(8,128)S(1)}) custom-call(s32[1]{0:T(128)} %bitcast.refs_0_, bf16[384,1024]{1,0:T(8,128)(2,1)S(1)} %get-tuple-element.514.refs_2_.refs_1_, ...), custom_call_target="tpu_custom_call" | custom-call | flops 1024 | bytes 1024 | tf_op jit(solution)/shard_map/head_forward/pallas_call | solution.py:263
  385.5 8.5 head_backward.4
  401.8 9.1 %head_backward.5 = (bf16[768,2048]{1,0:T(8,128)(2,1)}, bf16[384,1024]{1,0:T(8,128)(2,1)S(1)}, bf16[384,1024]{1,0:T(8,128)(2,1)S(1)}, f32[8,128]{1,0:T(8,128)S(1)}, f32[8,128]{1,0:T(8,128)S(1)}) custom-call(s32[1]{0:T(128)} %bitcast.refs_0_, f32[8,768]{1,0:T(8,128)S(1)} %merge.11.refs_2_.refs_1_, f32[768,4]{1,0:T(8,128)S(1)} %copy-done.6, ...), custom_call_target="tpu_custom_call" | custom-call | flops 1024 | bytes 1024 | tf_op jit(solution)/shard_map/head_backward/pallas_call | solution.py:263
  424.8 10.3 %head_weights.2 = (bf16[8,4,128,512]{3,2,1,0:T(8,128)(2,1)}, f32[8,128]{1,0:T(8,128)S(1)}) custom-call(s32[1]{0:T(128)} %bitcast.refs_0_, bf16[384,1024]{1,0:T(8,128)(2,1)} %get-tuple-element.538.refs_1_, bf16[384,1024]{1,0:T(8,128)(2,1)} %get-tuple-element.539.refs_2_, bf16[384,1024]{1,0:T(8,128)(2,1)} %get-tuple-element.540.refs_3_, ...), custom_call_target="tpu_custom_call" | custom-call | flops 1024 | bytes 1024 | tf_op jit(solution)/shard_map/head_weights/pallas_call | solution.py:263
  435.1 10.5 %head_weights.3 = (bf16[8,4,128,512]{3,2,1,0:T(8,128)(2,1)}, f32[8,128]{1,0:T(8,128)S(1)}) custom-call(s32[1]{0:T(128)} %bitcast.refs_0_, bf16[384,1024]{1,0:T(8,128)(2,1)} %get-tuple-element.538.refs_1_, bf16[384,1024]{1,0:T(8,128)(2,1)} %get-tuple-element.539.refs_2_, ...), custom_call_target="tpu_custom_call", output_to_operand_aliasing={{0}: (10, {})} | custom-call | flops 1024 | bytes 1024 | tf_op jit(solution)/shard_map/head_weights/pallas_call | solution.py:263
  502.7 8.2 ffn_two.2
  511.0 8.2 ffn_two.3
  535.1 8.3 ffn_one.2
  543.4 8.2 ffn_one.3
  559.2 9.4 %cross_backward.5 = (bf16[768,256]{1,0:T(8,128)(2,1)}, bf16[256,256]{1,0:T(8,128)(2,1)}, bf16[256,256]{1,0:T(8,128)(2,1)}, bf16[384,1024]{1,0:T(8,128)(2,1)S(1)}...) custom-call(s32[1]{0:T(128)} %bitcast.refs_0_, ...), custom_call_target="tpu_custom_call" | custom-call | flops 1024 | bytes 1024 | tf_op jit(solution)/shard_map/cross_backward/pallas_call | solution.py:263
  585.8 11.2 %self_backward.3 = (bf16[768,768]{1,0:T(8,128)(2,1)}, bf16[384,1024]{1,0:T(8,128)(2,1)S(1)}, bf16[384,1024]{1,0:T(8,128)(2,1)S(1)}, bf16[384,1024]{1,0:T(8,128)(...) custom-call(s32[1]{0:T(128)} %bitcast.refs_0_, ...), custom_call_target="tpu_custom_call" | custom-call | flops 1024 | bytes 1024 | tf_op jit(solution)/shard_map/self_backward/pallas_call | solution.py:263
  606.1 9.3 %collective-permute-done.102.refs_12_.refs_3_ = bf16[192,1024]{1,0:T(8,128)(2,1)S(1)} collective-permute-done((bf16[192,1024]{1,0:T(8,128)(2,1)S(1)}, bf16[192,1024]{1,0:T(8,128)(2,1)S(1)}, u32[]{:S(2)}, u32[]{:S(2)}) %collective-permute-start.102) | collective-permute-done | bytes 393248 | tf_op jit(solution)/shard_map/ppermute | solution.py:983
  636.1 10.9 %self_backward.4 = (bf16[768,768]{1,0:T(8,128)(2,1)}, bf16[384,1024]{1,0:T(8,128)(2,1)S(1)}, bf16[384,1024]{1,0:T(8,128)(2,1)S(1)}, bf16[384,1024]{1,0:T(8,128)(...) custom-call(s32[1]{0:T(128)} %bitcast.refs_0_, ...), custom_call_target="tpu_custom_call" | custom-call | flops 1024 | bytes 1024 | tf_op jit(solution)/shard_map/self_backward/pallas_call | solution.py:263
  657.4 11.1 %self_backward.5 = (bf16[768,768]{1,0:T(8,128)(2,1)}, bf16[384,1024]{1,0:T(8,128)(2,1)S(1)}, bf16[384,1024]{1,0:T(8,128)(2,1)S(1)}, bf16[384,1024]{1,0:T(8,128)(...) custom-call(s32[1]{0:T(128)} %bitcast.refs_0_, ...), custom_call_target="tpu_custom_call" | custom-call | flops 1024 | bytes 1024 | tf_op jit(solution)/shard_map/self_backward/pallas_call | solution.py:263
  692.5 15.7 %collective-permute-done.112.refs_6_.refs_3_ = bf16[192,1024]{1,0:T(8,128)(2,1)S(1)} collective-permute-done((bf16[192,1024]{1,0:T(8,128)(2,1)S(1)}, bf16[192,1024]{1,0:T(8,128)(2,1)S(1)}, u32[]{:S(2)}, u32[]{:S(2)}) %collective-permute-start.112) | collective-permute-done | bytes 393248 | tf_op jit(solution)/shard_map/ppermute | solution.py:983
  712.9 8.5 self_in.2
  759.6 11.4 %collective-permute-done.117.refs_4_.refs_2_ = bf16[592,128]{1,0:T(8,128)(2,1)S(1)} collective-permute-done((bf16[592,128]{1,0:T(8,128)(2,1)S(1)}, bf16[592,128]{1,0:T(8,128)(2,1)S(1)}, u32[]{:S(2)}, u32[]{:S(2)}) %collective-permute-start.117) | collective-permute-done | bytes 151584 | tf_op jit(solution)/shard_map/ppermute | solution.py:983
  776.5 10.8 %collective-permute-done.120.refs_7_.refs_5_ = bf16[592,128]{1,0:T(8,128)(2,1)S(1)} collective-permute-done((bf16[592,128]{1,0:T(8,128)(2,1)S(1)}, bf16[592,128]{1,0:T(8,128)(2,1)S(1)}, u32[]{:S(2)}, u32[]{:S(2)}) %collective-permute-start.120) | collective-permute-done | bytes 151584 | tf_op jit(solution)/shard_map/ppermute | solution.py:983
  787.3 18.1 %embed_back.1 = bf16[4,4,128,512]{3,2,1,0:T(8,128)(2,1)S(1)} custom-call(s32[4]{0:T(128)S(1)} %copy-done.98, s32[8,4608]{1,0:T(8,128)S(1)} %concatenate.29.refs_23_.refs_1_, bf16[592,128]{1,0:T(8,128)(2,1)S(1)} %get-tuple-element.754.refs_2_.refs_0_, bf16[592,128]{1,0:T(8,128)(2,1)S(1)} %collective-permute-done.116.refs_3_.refs_1_, ...), custom_call_target="tpu_custom_call" | custom-call | flops 1024 | bytes 1024 | tf_op jit(solution)/shard_map/embed_back/pallas_call | solution.py:859
  817.7 9.1 %collective-permute-done.127 = f32[16,128]{1,0:T(8,128)S(1)} collective-permute-done((f32[16,128]{1,0:T(8,128)S(1)}, f32[16,128]{1,0:T(8,128)S(1)}, u32[]{:S(2)}, u32[]{:S(2)}) %collective-permute-start.127) | collective-permute-done | bytes 8224 | tf_op jit(solution)/shard_map/ppermute | solution.py:983
  844.6 8.7 collective-permute-start.131
  (700 shorter events, 541.6 us)
Async XLA Ops:
  7.2 100.7 %all-gather.9.cloned.1.call-start = ((), (), s32[]{:S(2)}) async-start(), calls=%async_computation.8 | async-start | bytes 2433024 | tf_op jit(solution)/shard_map/all_gather | solution.py:1095
  12.5 129.9 %all-gather.11.cloned.1.call-start = ((), (), s32[]{:S(2)}) async-start(), calls=%async_computation.9 | async-start | bytes 2801664 | tf_op jit(solution)/shard_map/all_gather | solution.py:1096
  14.2 238.7 %all-gather.13.cloned.1.call-start = ((), (), s32[]{:S(2)}) async-start(), calls=%async_computation.10 | async-start | bytes 4718592 | tf_op jit(solution)/shard_map/all_gather | solution.py:1097
  15.1 303.8 %all-gather.15.cloned.1.call-start = ((), (), s32[]{:S(2)}) async-start(), calls=%async_computation.11 | async-start | bytes 4718592 | tf_op jit(solution)/shard_map/all_gather | solution.py:1098
  17.5 21.4 %collective-permute-start.9 = (s32[8,640]{1,0:T(8,128)S(1)}, s32[8,640]{1,0:T(8,128)S(1)}, u32[]{:S(2)}, u32[]{:S(2)}) collective-permute-start(s32[8,640]{1,0:T(8,128)S(1)} %pad_select_fusion.refs_1_.refs_0_), channel_id=1, source_target_pairs={{0,20},{4,16},{8,28},{12,24},{16,4},{20,0},{24,12},{28,8},{1,21},{... | collective-permute-start | bytes 61448 | tf_op jit(solution)/shard_map/ppermute | solution.py:983
  26.9 24.5 %collective-permute-start.2 = (bf16[4,128,512]{2,1,0:T(8,128)(2,1)S(1)}, bf16[4,128,512]{2,1,0:T(8,128)(2,1)S(1)}, u32[]{:S(2)}, u32[]{:S(2)}) collective-permute-start(bf16[4,128,512]{2,1,0:T(8,128)(2,1)S(1)} %get-tuple-element.795.refs_3_), channel_id=1, source_target_pairs={{0,1},{1,0},{2,3},{3,2},{4,5},{5,4},{6,7},{7,6},{8,9},{9,8},{10,11... | collective-permute-start | bytes 1572872 | tf_op jit(solution)/shard_map/ppermute | solution.py:983
  64.8 24.4 %collective-permute-start.12 = (bf16[576,128]{1,0:T(8,128)(2,1)S(1)}, bf16[576,128]{1,0:T(8,128)(2,1)S(1)}, u32[]{:S(2)}, u32[]{:S(2)}) collective-permute-start(bf16[576,128]{1,0:T(8,128)(2,1)S(1)} %get-tuple-element.399), channel_id=1, source_target_pairs={{0,16},{4,20},{8,24},{12,28},{16,0},{20,4},{24,8},{28,12},{1,17},{... | collective-permute-start | bytes 442376 | tf_op jit(solution)/shard_map/ppermute | solution.py:983
  64.8 25.6 %collective-permute-start.13 = (bf16[576,128]{1,0:T(8,128)(2,1)S(1)}, bf16[576,128]{1,0:T(8,128)(2,1)S(1)}, u32[]{:S(2)}, u32[]{:S(2)}) collective-permute-start(bf16[576,128]{1,0:T(8,128)(2,1)S(1)} %get-tuple-element.397.refs_7_), channel_id=1, source_target_pairs={{0,20},{4,16},{8,28},{12,24},{16,4},{20,0},{24,12},{28,8},{1,21},{... | collective-permute-start | bytes 442376 | tf_op jit(solution)/shard_map/ppermute | solution.py:983
  77.6 25.4 %collective-permute-start.16 = (bf16[576,128]{1,0:T(8,128)(2,1)S(1)}, bf16[576,128]{1,0:T(8,128)(2,1)S(1)}, u32[]{:S(2)}, u32[]{:S(2)}) collective-permute-start(bf16[576,128]{1,0:T(8,128)(2,1)S(1)} %get-tuple-element.398.refs_7_), channel_id=1, source_target_pairs={{0,12},{4,8},{8,4},{12,0},{16,28},{20,24},{24,20},{28,16},{1,13},{... | collective-permute-start | bytes 442376 | tf_op jit(solution)/shard_map/ppermute | solution.py:983
  142.2 20.5 %collective-permute-start.24 = (bf16[384,1024]{1,0:T(8,128)(2,1)}, bf16[384,1024]{1,0:T(8,128)(2,1)}, u32[]{:S(2)}, u32[]{:S(2)}) collective-permute-start(bf16[384,1024]{1,0:T(8,128)(2,1)} %get-tuple-element.427), channel_id=1, source_target_pairs={{0,1},{1,0},{2,3},{3,2},{4,5},{5,4},{6,7},{7,6},{8,9},{9,8},{10,11... | collective-permute-start | bytes 2359304 | tf_op jit(solution)/shard_map/ppermute | solution.py:983
  150.4 24.7 %collective-permute-start.27 = (bf16[768,256]{1,0:T(8,128)(2,1)}, bf16[768,256]{1,0:T(8,128)(2,1)}, u32[]{:S(2)}, u32[]{:S(2)}) collective-permute-start(bf16[768,256]{1,0:T(8,128)(2,1)} %get-tuple-element.434.refs_1_), channel_id=1, source_target_pairs={{0,1},{1,0},{2,3},{3,2},{4,5},{5,4},{6,7},{7,6},{8,9},{9,8},{10,11... | collective-permute-start | bytes 1179656 | tf_op jit(solution)/shard_map/ppermute | solution.py:983
  150.4 426.3 %reduce-scatter.5.cloned.1.call-start = ((), (), s32[]{:S(2)}) async-start(), calls=%async_computation.4 | async-start | bytes 4718592 | tf_op jit(solution)/shard_map/reduce_scatter | solution.py:1533
  150.7 29.9 %collective-permute-start.26 = (bf16[192,1024]{1,0:T(8,128)(2,1)}, bf16[192,1024]{1,0:T(8,128)(2,1)S(1)}, u32[]{:S(2)}, u32[]{:S(2)}) collective-permute-start(bf16[192,1024]{1,0:T(8,128)(2,1)} %copy-done.15), channel_id=1, source_target_pairs={{0,2},{1,3},{2,0},{3,1},{4,6},{5,7},{6,4},{7,5},{8,10},{9,11},{10,... | collective-permute-start | bytes 1179656 | tf_op jit(solution)/shard_map/ppermute | solution.py:983
  165.2 20.7 %collective-permute-start.30 = (bf16[192,1024]{1,0:T(8,128)(2,1)S(1)}, bf16[192,1024]{1,0:T(8,128)(2,1)S(1)}, u32[]{:S(2)}, u32[]{:S(2)}) collective-permute-start(bf16[192,1024]{1,0:T(8,128)(2,1)S(1)} %get-tuple-element.437.refs_1_), channel_id=1, source_target_pairs={{0,2},{1,3},{2,0},{3,1},{4,6},{5,7},{6,4},{7,5},{8,10},{9,11},{10,... | collective-permute-start | bytes 1179656 | tf_op jit(solution)/shard_map/ppermute | solution.py:983
  338.6 24.0 %collective-permute-start.63 = (bf16[192,1024]{1,0:T(8,128)(2,1)S(1)}, bf16[192,1024]{1,0:T(8,128)(2,1)S(1)}, u32[]{:S(2)}, u32[]{:S(2)}) collective-permute-start(bf16[192,1024]{1,0:T(8,128)(2,1)S(1)} %get-tuple-element.499.refs_10_.refs_2_), channel_id=1, source_target_pairs={{0,2},{1,3},{2,0},{3,1},{4,6},{5,7},{6,4},{7,5},{8,10},{9,11},{10,... | collective-permute-start | bytes 1179656 | tf_op jit(solution)/shard_map/ppermute | solution.py:983
  365.3 20.1 %collective-permute-start.64 = (bf16[192,1024]{1,0:T(8,128)(2,1)S(1)}, bf16[192,1024]{1,0:T(8,128)(2,1)S(1)}, u32[]{:S(2)}, u32[]{:S(2)}) collective-permute-start(bf16[192,1024]{1,0:T(8,128)(2,1)S(1)} %get-tuple-element.515.refs_1_), channel_id=1, source_target_pairs={{0,2},{1,3},{2,0},{3,1},{4,6},{5,7},{6,4},{7,5},{8,10},{9,11},{10,... | collective-permute-start | bytes 1179656 | tf_op jit(solution)/shard_map/ppermute | solution.py:983
  413.8 21.2 %collective-permute-start.76 = (bf16[192,1024]{1,0:T(8,128)(2,1)S(1)}, bf16[192,1024]{1,0:T(8,128)(2,1)S(1)}, u32[]{:S(2)}, u32[]{:S(2)}) collective-permute-start(bf16[192,1024]{1,0:T(8,128)(2,1)S(1)} %get-tuple-element.550.refs_1_), channel_id=1, source_target_pairs={{0,2},{1,3},{2,0},{3,1},{4,6},{5,7},{6,4},{7,5},{8,10},{9,11},{10,... | collective-permute-start | bytes 1179656 | tf_op jit(solution)/shard_map/ppermute | solution.py:983
  445.6 262.5 %reduce-scatter.7.cloned.1.call-start = ((), (), s32[]{:S(2)}) async-start(), calls=%async_computation.5 | async-start | bytes 4718592 | tf_op jit(solution)/shard_map/reduce_scatter | solution.py:1567
  500.9 20.7 %collective-permute-start.90 = (bf16[384,1024]{1,0:T(8,128)(2,1)S(1)}, bf16[384,1024]{1,0:T(8,128)(2,1)S(1)}, u32[]{:S(2)}, u32[]{:S(2)}) collective-permute-start(bf16[384,1024]{1,0:T(8,128)(2,1)S(1)} %get-tuple-element.606), channel_id=1, source_target_pairs={{0,1},{1,0},{2,3},{3,2},{4,5},{5,4},{6,7},{7,6},{8,9},{9,8},{10,11... | collective-permute-start | bytes 2359304 | tf_op jit(solution)/shard_map/ppermute | solution.py:983
  521.7 21.6 %collective-permute-start.92 = (bf16[192,1024]{1,0:T(8,128)(2,1)S(1)}, bf16[192,1024]{1,0:T(8,128)(2,1)S(1)}, u32[]{:S(2)}, u32[]{:S(2)}) collective-permute-start(bf16[192,1024]{1,0:T(8,128)(2,1)S(1)} %get-tuple-element.624.refs_1_), channel_id=1, source_target_pairs={{0,2},{1,3},{2,0},{3,1},{4,6},{5,7},{6,4},{7,5},{8,10},{9,11},{10,... | collective-permute-start | bytes 1179656 | tf_op jit(solution)/shard_map/ppermute | solution.py:983
  551.6 192.2 %reduce-scatter.11.cloned.1.call-start = ((), (), s32[]{:S(2)}) async-start(), calls=%async_computation.7 | async-start | bytes 2359296 | tf_op jit(solution)/shard_map/reduce_scatter | solution.py:1628
  627.5 203.7 %reduce-scatter.9.cloned.1.call-start = ((), (), s32[]{:S(2)}) async-start(), calls=%async_computation.6 | async-start | bytes 2801664 | tf_op jit(solution)/shard_map/reduce_scatter | solution.py:1666
  672.2 19.5 %collective-permute-start.109 = (bf16[768,256]{1,0:T(8,128)(2,1)S(1)}, bf16[768,256]{1,0:T(8,128)(2,1)S(1)}, u32[]{:S(2)}, u32[]{:S(2)}) collective-permute-start(bf16[768,256]{1,0:T(8,128)(2,1)S(1)} %add.294.refs_11_), channel_id=1, source_target_pairs={{0,2},{1,3},{2,0},{3,1},{4,6},{5,7},{6,4},{7,5},{8,10},{9,11},{10,... | collective-permute-start | bytes 1179656 | tf_op jit(solution)/shard_map/ppermute | solution.py:983
  672.9 39.9 %collective-permute-start.113 = (bf16[192,1024]{1,0:T(8,128)(2,1)}, bf16[192,1024]{1,0:T(8,128)(2,1)}, u32[]{:S(2)}, u32[]{:S(2)}) collective-permute-start(bf16[192,1024]{1,0:T(8,128)(2,1)} %get-tuple-element.715.refs_14_.refs_2_), channel_id=1, source_target_pairs={{0,2},{1,3},{2,0},{3,1},{4,6},{5,7},{6,4},{7,5},{8,10},{9,11},{10,... | collective-permute-start | bytes 1179656 | tf_op jit(solution)/shard_map/ppermute | solution.py:983
  674.2 33.9 %collective-permute-start.112 = (bf16[192,1024]{1,0:T(8,128)(2,1)S(1)}, bf16[192,1024]{1,0:T(8,128)(2,1)S(1)}, u32[]{:S(2)}, u32[]{:S(2)}) collective-permute-start(bf16[192,1024]{1,0:T(8,128)(2,1)S(1)} %get-tuple-element.733.refs_1_), channel_id=1, source_target_pairs={{0,2},{1,3},{2,0},{3,1},{4,6},{5,7},{6,4},{7,5},{8,10},{9,11},{10,... | collective-permute-start | bytes 1179656 | tf_op jit(solution)/shard_map/ppermute | solution.py:983
  689.7 31.7 %collective-permute-start.114 = (bf16[192,1024]{1,0:T(8,128)(2,1)}, bf16[192,1024]{1,0:T(8,128)(2,1)S(1)}, u32[]{:S(2)}, u32[]{:S(2)}) collective-permute-start(bf16[192,1024]{1,0:T(8,128)(2,1)} %get-tuple-element.742.refs_1_), channel_id=1, source_target_pairs={{0,2},{1,3},{2,0},{3,1},{4,6},{5,7},{6,4},{7,5},{8,10},{9,11},{10,... | collective-permute-start | bytes 1179656 | tf_op jit(solution)/shard_map/ppermute | solution.py:983
  691.0 36.9 %collective-permute-start.115 = (bf16[192,1024]{1,0:T(8,128)(2,1)S(1)}, bf16[192,1024]{1,0:T(8,128)(2,1)S(1)}, u32[]{:S(2)}, u32[]{:S(2)}) collective-permute-start(bf16[192,1024]{1,0:T(8,128)(2,1)S(1)} %get-tuple-element.731.refs_4_.refs_2_), channel_id=1, source_target_pairs={{0,2},{1,3},{2,0},{3,1},{4,6},{5,7},{6,4},{7,5},{8,10},{9,11},{10,... | collective-permute-start | bytes 1179656 | tf_op jit(solution)/shard_map/ppermute | solution.py:983
  750.9 20.0 %collective-permute-start.117 = (bf16[592,128]{1,0:T(8,128)(2,1)S(1)}, bf16[592,128]{1,0:T(8,128)(2,1)S(1)}, u32[]{:S(2)}, u32[]{:S(2)}) collective-permute-start(bf16[592,128]{1,0:T(8,128)(2,1)S(1)} %get-tuple-element.756), channel_id=1, source_target_pairs={{0,8},{4,12},{8,0},{12,4},{16,24},{20,28},{24,16},{28,20},{1,9},{5... | collective-permute-start | bytes 454664 | tf_op jit(solution)/shard_map/ppermute | solution.py:983
  751.0 25.5 %collective-permute-start.118 = (bf16[592,128]{1,0:T(8,128)(2,1)S(1)}, bf16[592,128]{1,0:T(8,128)(2,1)S(1)}, u32[]{:S(2)}, u32[]{:S(2)}) collective-permute-start(bf16[592,128]{1,0:T(8,128)(2,1)S(1)} %get-tuple-element.757), channel_id=1, source_target_pairs={{0,12},{4,8},{8,4},{12,0},{16,28},{20,24},{24,20},{28,16},{1,13},{... | collective-permute-start | bytes 454664 | tf_op jit(solution)/shard_map/ppermute | solution.py:983
  752.5 24.0 %collective-permute-start.119 = (bf16[592,128]{1,0:T(8,128)(2,1)S(1)}, bf16[592,128]{1,0:T(8,128)(2,1)S(1)}, u32[]{:S(2)}, u32[]{:S(2)}) collective-permute-start(bf16[592,128]{1,0:T(8,128)(2,1)S(1)} %get-tuple-element.758), channel_id=1, source_target_pairs={{0,16},{4,20},{8,24},{12,28},{16,0},{20,4},{24,8},{28,12},{1,17},{... | collective-permute-start | bytes 454664 | tf_op jit(solution)/shard_map/ppermute | solution.py:983
  754.3 33.0 %collective-permute-start.120 = (bf16[592,128]{1,0:T(8,128)(2,1)S(1)}, bf16[592,128]{1,0:T(8,128)(2,1)S(1)}, u32[]{:S(2)}, u32[]{:S(2)}) collective-permute-start(bf16[592,128]{1,0:T(8,128)(2,1)S(1)} %get-tuple-element.759), channel_id=1, source_target_pairs={{0,20},{4,16},{8,28},{12,24},{16,4},{20,0},{24,12},{28,8},{1,21},{... | collective-permute-start | bytes 454664 | tf_op jit(solution)/shard_map/ppermute | solution.py:983
  756.8 30.5 %collective-permute-start.121 = (bf16[592,128]{1,0:T(8,128)(2,1)S(1)}, bf16[592,128]{1,0:T(8,128)(2,1)S(1)}, u32[]{:S(2)}, u32[]{:S(2)}) collective-permute-start(bf16[592,128]{1,0:T(8,128)(2,1)S(1)} %get-tuple-element.760), channel_id=1, source_target_pairs={{0,24},{4,28},{8,16},{12,20},{16,8},{20,12},{24,0},{28,4},{1,25},{... | collective-permute-start | bytes 454664 | tf_op jit(solution)/shard_map/ppermute | solution.py:983
  (244 other events, 1884.4 us)
Sparse Core Ops, SparseCore 0:
  12.6 68.9 all-gather.8
  84.4 54.7 all-gather.10
  141.9 71.9 all-gather.12
  216.4 71.6 all-gather.14
  445.8 90.5 reduce-scatter.4
  551.8 90.3 reduce-scatter.6
  646.3 67.7 reduce-scatter.10
  734.7 94.4 reduce-scatter.8
